TPU v7x, 256 devices: a whole 4x4x8 slice. The times are simulated.
256 devices in a mesh: group: 16 (over z, y_lo), tp: 16 (over x, y_hi, core).
Axes of the slice: x: 4, y: 4 (y_hi: 2, y_lo: 2; y = y_hi * 2 + y_lo), z: 8, core: 2. Of those that a mesh axis runs over, the one named last changes fastest.
Arguments:
- token_ids: int32 [2, 512], P(None, 'group'), may hold values from 0 to 1023
- row_counts: int32 [16], P('group'), may hold values from 8 to 32, as said below
- code_table: bfloat16 [1024, 5120], P(None, 'tp'), may hold values from -6 to 6
- x_weight: bfloat16 [5120, 10240], P('group', 'tp'), may hold values from -0.078125 to 0.078125
- z_weight: bfloat16 [5120, 10240], P('group', 'tp'), may hold values from -0.078125 to 0.078125
- dt_weight: bfloat16 [5120, 160], P('group', 'tp'), may hold values from -0.078125 to 0.078125
- bc_weight: bfloat16 [5120, 512], P('group', 'tp'), may hold values from -0.078125 to 0.078125
- dt_bias: float32 [160], P('tp'), may hold values from -3 to 0.5
- head_rate: float32 [160], P('tp'), may hold values from 0.05 to 8
- skip_gain: float32 [160], P('tp'), may hold values from 0.5 to 2
- norm_gain: float32 [10240], P('tp'), may hold values from 0.25 to 1.75
- out_weight: bfloat16 [10240, 5120], P('tp', 'group'), may hold values from -0.078125 to 0.078125
- ssm_state: bfloat16 [512, 160, 64, 256], P('group', 'tp')
Outputs:
- layer_out: bfloat16 [2, 512, 5120], P(None, 'group', 'tp')
Inputs may be any that keep to these rules, and one draw needn't show every extreme that they name: `row_counts`: each count is a multiple of 8, and in every draw some group has all 32 rows live.
All inputs are finite; a program needn't handle non-finite values.
Results may differ from a plain program's by a relative error of at most 0.013.
Values may be sent and summed in bfloat16 or wider, within the bound.
No kernel may reach another device: no remote copies, remote signals or barrier semaphores. Data moves between devices by JAX's collectives and lax.ppermute only.
A program may use at most 128 MiB of HBM per device.

v0:
```python
import functools

import jax
import jax.numpy as jnp
from jax import lax
from jax.experimental import pallas as pl
from jax.experimental.pallas import tpu as pltpu
from jax.sharding import Mesh
from jax.sharding import PartitionSpec as P


BF = jnp.bfloat16
F32 = jnp.float32
SCALE = 2.0**-20
GROUP = ("z", "yl")
TP = ("x", "yh", "core")
ALL = GROUP + TP
VMEM_LIMIT = 48 * 1024 * 1024

FAR_FIRST = (4, 3, 5, 2, 6, 1, 7)


def nt(a, b):
    return lax.dot_general(a, b, (((1,), (1,)), ((), ())), preferred_element_type=F32)


def nn(a, b):
    return jnp.dot(a, b, preferred_element_type=F32)


def call(body, out_shape, args, in_smem=0, flops=1 << 20, grid=None, in_specs=None, out_specs=None, scratch=()):
    if in_specs is None:
        in_specs = [pl.BlockSpec(memory_space=pltpu.SMEM)] * in_smem + [
            pl.BlockSpec(memory_space=pltpu.VMEM)
        ] * (len(args) - in_smem)
        out_specs = jax.tree.map(lambda _: pl.BlockSpec(memory_space=pltpu.VMEM), out_shape)
    kwargs = {} if grid is None else {"grid": grid}
    return pl.pallas_call(
        body,
        out_shape=out_shape,
        in_specs=in_specs,
        out_specs=out_specs,
        scratch_shapes=scratch,
        compiler_params=pltpu.CompilerParams(vmem_limit_bytes=VMEM_LIMIT),
        cost_estimate=pl.CostEstimate(flops=flops, bytes_accessed=1 << 20, transcendentals=0),
        **kwargs,
    )(*args)


def split2(v):
    hi = v.astype(BF)
    return hi, (v - hi.astype(F32)).astype(BF)


def project_small_kernel(flag, e_own, e_oth, s_own, s_oth, out):
    groups, rows, width = out.shape

    def run(ea, eb):
        ps = nt(ea[...], s_own[...]) + nt(eb[...], s_oth[...])
        hi, lo = split2(ps)
        out[...] = jnp.concatenate([hi, lo], 1).reshape(groups, rows, width)

    @pl.when(flag[0] == 1)
    def _():
        run(e_own, e_oth)

    @pl.when(flag[0] == 0)
    def _():
        run(e_oth, e_own)


def project_kernel(place, e_own, e_oth, x_own, x_oth, z_own, z_oth, *outs):
    inner = x_own.shape[1]
    rows = outs[0].shape[0]
    groups = len(outs)

    def turned(ref):
        blocks = []
        for k in range(groups):
            at = lax.rem(place[1] + k, groups) * rows
            blocks.append(ref[pl.ds(pl.multiple_of(at, rows), rows), :])
        return jnp.concatenate(blocks, 0)

    def run(ea, eb):
        a = turned(ea)
        b = turned(eb)
        px = (nn(a, x_own[...]) + nn(b, x_oth[...])).astype(BF)
        for k in range(groups):
            outs[k][:, :inner] = px[k * rows : (k + 1) * rows]
        pz = (nn(a, z_own[...]) + nn(b, z_oth[...])).astype(BF)
        for k in range(groups):
            outs[k][:, inner:] = pz[k * rows : (k + 1) * rows]

    @pl.when(place[0] == 1)
    def _():
        run(e_own, e_oth)

    @pl.when(place[0] == 0)
    def _():
        run(e_oth, e_own)


def small_kernel(part, bc, small):
    total = part[0].astype(F32)
    for k in range(1, part.shape[0]):
        total = total + part[k].astype(F32)
    total = total[:, :64] + total[:, 64:]
    hi, lo = split2(total)
    both = jnp.concatenate([hi, lo], 1)
    for k in range(bc.shape[0]):
        bc[k] = both
    small[...] = total


def state_kernel(bc, s, out, dots, cmat):
    rows = cmat.shape[0]

    @pl.when(pl.program_id(0) == 0)
    def _():
        pieces = [bc[t] for t in range(bc.shape[0])]
        pieces = [p[:, :32].astype(F32) + p[:, 64:96].astype(F32) for p in pieces]
        b = jnp.concatenate(pieces[:8], 1)
        c = jnp.concatenate(pieces[8:], 1)
        b1, b2, c1, c2 = b[:rows], b[rows:], c[:rows], c[rows:]
        lane = lax.broadcasted_iota(jnp.int32, dots.shape, 1)
        b11 = jnp.sum(b1 * c1, axis=1, keepdims=True)
        b12 = jnp.sum(b1 * c2, axis=1, keepdims=True)
        b22 = jnp.sum(b2 * c2, axis=1, keepdims=True)
        dots[...] = jnp.where(lane == 0, b11, jnp.where(lane == 1, b12, b22))
        cmat[...] = jnp.zeros_like(cmat)
        for k, v in enumerate((c1, c2)):
            v = v * SCALE
            hi = v.astype(BF).astype(F32)
            cmat[:, 2 * k, :] = hi
            cmat[:, 2 * k + 1, :] = v - hi

    for r in range(s.shape[0]):
        m = s[r].reshape(s.shape[1] * s.shape[2], s.shape[3])
        g = nt(cmat[pl.program_id(0) * s.shape[0] + r].astype(BF), m)
        out[r] = g


def decode_kernel(*refs):
    parts, (small, dots, g, bias, rate, skip, gain, out) = refs[:8], refs[8:]
    heads = bias.shape[1]
    inner = gain.shape[1]
    half = parts[0].shape[0] // 2
    total = parts[0][...].astype(F32)
    for part in parts[1:]:
        total = total + part[...].astype(F32)
    x_pre = total[:, :inner]
    z_pre = total[:, inner:]
    pick = (
        lax.broadcasted_iota(jnp.int32, (heads, inner), 0)
        == lax.broadcasted_iota(jnp.int32, (heads, inner), 1) // (inner // heads)
    ).astype(F32)
    expand = functools.partial(
        jnp.dot, preferred_element_type=F32, precision=lax.Precision.HIGHEST
    )
    dt_pre = expand(small[:, 32 : 32 + heads], pick)
    bias_e = expand(bias[...], pick)
    rate_e = expand(rate[...], pick)
    skip_e = expand(skip[...], pick)
    pre = dt_pre + bias_e
    dt = jnp.maximum(pre, 0.0) + jnp.log1p(jnp.exp(-jnp.abs(pre)))
    decay = jnp.exp(-dt * rate_e)
    inputs = x_pre * jax.nn.sigmoid(x_pre)
    upd = dt * inputs
    gate = z_pre * jax.nn.sigmoid(z_pre)
    b11 = dots[:, 0:1]
    b12 = dots[:, 1:2]
    b22 = dots[:, 2:3]
    gs = g[...]
    g1 = gs[:, 0, :] + gs[:, 1, :]
    g2 = gs[:, 2, :] + gs[:, 3, :]
    d1, d2 = decay[:half], decay[half:]
    u1, u2 = upd[:half], upd[half:]
    read1 = (d1 * g1) * (1.0 / SCALE) + u1 * b11 + skip_e * inputs[:half]
    read2 = d2 * ((d1 * g2) * (1.0 / SCALE) + u1 * b12) + u2 * b22 + skip_e * inputs[half:]
    lim = 1e30
    gg1 = jnp.clip(read1 * gate[:half] * gain[...], -lim, lim)
    gg2 = jnp.clip(read2 * gate[half:] * gain[...], -lim, lim)
    both = jnp.concatenate([gg1, gg2], 0).astype(BF)
    for k in range(out.shape[0]):
        out[k] = both


def output_kernel(place, gg, w_own, w_oth, gain, keep, send):
    y = place[0]
    core = place[1]
    groups, rows, inner = gg.shape
    cols = w_own.shape[0]
    v = gg[...].reshape(groups * rows, inner)
    raw = v.astype(F32) / gain[...]
    ss = jnp.sum(raw * raw, axis=1, keepdims=True)
    hi = ss.astype(BF).astype(F32)
    lo = ss - hi
    lane = lax.broadcasted_iota(jnp.int32, (groups * rows, 64), 1)
    tail = jnp.where(lane == 0, hi, jnp.where(lane == 1, lo, 0.0))

    def block(w):
        o = jnp.concatenate([nt(v, w[...]), tail], 1)
        return o.reshape(groups, rows, cols + 64)

    @pl.when(y == core)
    def _():
        keep[...] = block(w_own)
        send[...] = block(w_oth).astype(BF)

    @pl.when(y != core)
    def _():
        keep[...] = block(w_oth)
        send[...] = block(w_own).astype(BF)


def pair_kernel(keep, got, out):
    total = keep[...] + got[...].astype(F32)
    cols = out.shape[2] - 64
    lane = lax.broadcasted_iota(jnp.int32, total.shape, 2)
    ss = total[:, :, cols : cols + 1] + total[:, :, cols + 1 : cols + 2]
    hi = ss.astype(BF).astype(F32)
    total = jnp.where(lane == cols, hi, jnp.where(lane == cols + 1, ss - hi, total))
    out[...] = total.astype(BF)


def reduce_kernel(part, out, *, count):
    total = part[0].astype(F32)
    for k in range(1, part.shape[0]):
        total = total + part[k].astype(F32)
    cols = out.shape[1]
    ss = total[:, cols : cols + 1] + total[:, cols + 1 : cols + 2]
    out[...] = (total[:, :cols] * lax.rsqrt(ss / count + 1e-05)).astype(BF)


def per_device(
    token_ids,
    row_counts,
    code_table,
    x_weight,
    z_weight,
    dt_weight,
    bc_weight,
    dt_bias,
    head_rate,
    skip_gain,
    norm_gain,
    out_weight,
    ssm_state,
):
    rows = token_ids.shape[1]
    heads = dt_bias.shape[0]
    inner = x_weight.shape[1]
    wide = code_table.shape[1]
    y = lax.axis_index("yl")
    core = lax.axis_index("core")
    swap = []
    for z in range(8):
        for yy in range(2):
            for w in range(8):
                for c in range(2):
                    swap.append(((z * 2 + yy) * 16 + w * 2 + c, (w * 2 + yy) * 16 + z * 2 + c))
    pair = [(0, 1), (1, 0)]

    x_oth = lax.ppermute(x_weight, "yl", pair)
    z_oth = lax.ppermute(z_weight, "yl", pair)
    small_own = jnp.concatenate(
        [bc_weight.T, dt_weight.T, jnp.zeros((64 - 32 - heads, wide), BF)], 0
    )
    small_oth = lax.ppermute(small_own, "yl", pair)
    out_own = out_weight.T
    out_oth = lax.ppermute(out_own, "yl", pair)

    flat_ids = token_ids.reshape(-1)
    codes = jnp.arange(code_table.shape[0], dtype=jnp.int32)
    one_hot = (flat_ids[:, None] == codes[None, :]).astype(BF)
    own_embed = jnp.dot(one_hot, code_table, preferred_element_type=F32).astype(BF)
    moved = lax.ppermute(own_embed, ALL, swap)
    e_own = lax.all_to_all(
        jnp.broadcast_to(moved[None], (8,) + moved.shape), ("x", "yh"), 0, 0
    ).reshape(8 * 2 * rows, wide)
    e_oth = lax.ppermute(e_own, "core", pair)
    flag = (y == core).astype(jnp.int32).reshape(1)
    part_small = call(
        project_small_kernel,
        jax.ShapeDtypeStruct((8, 2 * rows, 128), BF),
        (flag, e_own, e_oth, small_own, small_oth),
        in_smem=1,
        flops=2 * 16 * rows * 2 * wide * 128,
    )
    part_small = lax.all_to_all(part_small, "z", 0, 0)
    blocks = call(
        project_kernel,
        tuple(jax.ShapeDtypeStruct((2 * rows, 2 * inner), BF) for _ in range(8)),
        (
            jnp.stack([(y == core).astype(jnp.int32), lax.axis_index("z")]),
            e_own,
            e_oth,
            x_weight,
            x_oth,
            z_weight,
            z_oth,
        ),
        in_smem=1,
        flops=2 * 16 * rows * 2 * wide * 2 * inner,
    )
    parts = [blocks[0]]
    for k in FAR_FIRST:
        parts.append(lax.ppermute(blocks[k], "z", [(i, (i + k) % 8) for i in range(8)]))
    bc, small = call(
        small_kernel,
        (jax.ShapeDtypeStruct((16, 2 * rows, 128), BF), jax.ShapeDtypeStruct((2 * rows, 64), F32)),
        (part_small,),
    )
    bc_all = lax.all_to_all(bc, TP, 0, 0)
    step = 4
    g, dots = call(
        state_kernel,
        (jax.ShapeDtypeStruct((rows, 8, inner), F32), jax.ShapeDtypeStruct((rows, 128), F32)),
        (bc_all, ssm_state),
        grid=(rows // step,),
        in_specs=[
            pl.BlockSpec(bc_all.shape, lambda i: (0, 0, 0)),
            pl.BlockSpec((step,) + ssm_state.shape[1:], lambda i: (i, 0, 0, 0)),
        ],
        out_specs=(
            pl.BlockSpec((step, 8, inner), lambda i: (i, 0, 0)),
            pl.BlockSpec((rows, 128), lambda i: (0, 0)),
        ),
        scratch=[pltpu.VMEM((rows, 8, 256), F32)],
        flops=2 * 8 * rows * inner * 256,
    )
    gain = norm_gain.reshape(1, inner)
    gg = call(
        decode_kernel,
        jax.ShapeDtypeStruct((8, 2 * rows, inner), BF),
        (
            *parts,
            small,
            dots,
            g,
            dt_bias.reshape(1, heads),
            head_rate.reshape(1, heads),
            skip_gain.reshape(1, heads),
            gain,
        ),
    )
    gg_all = lax.all_to_all(gg, "z", 0, 0)
    keep, send = call(
        output_kernel,
        (
            jax.ShapeDtypeStruct((8, 2 * rows, wide + 64), F32),
            jax.ShapeDtypeStruct((8, 2 * rows, wide + 64), BF),
        ),
        (jnp.stack([y, core]), gg_all, out_own, out_oth, gain),
        in_smem=1,
        flops=2 * 16 * rows * inner * 2 * wide,
    )
    got = lax.ppermute(send, "core", pair)
    paired = call(pair_kernel, jax.ShapeDtypeStruct((8, 2 * rows, wide + 64), BF), (keep, got))
    partial_out = lax.all_to_all(paired, ("x", "yh"), 0, 0)
    mine = call(
        functools.partial(reduce_kernel, count=float(16 * inner)),
        jax.ShapeDtypeStruct((2 * rows, wide), BF),
        (partial_out,),
    )
    back = lax.ppermute(mine, ALL, swap)
    result = (own_embed.astype(F32) + back.astype(F32)).reshape(2, rows, wide)
    live = jnp.arange(rows, dtype=jnp.int32) < row_counts[0]
    return jnp.where(live[None, :, None], result, 0.0).astype(BF)


def solution(mesh):
    fine = Mesh(mesh.devices.reshape(8, 2, 4, 2, 2), ALL)
    return jax.shard_map(
        per_device,
        mesh=fine,
        in_specs=(
            P(None, GROUP),
            P(GROUP),
            P(None, TP),
            P(GROUP, TP),
            P(GROUP, TP),
            P(GROUP, TP),
            P(GROUP, TP),
            P(TP),
            P(TP),
            P(TP),
            P(TP),
            P(TP, GROUP),
            P(GROUP, TP, None, None),
        ),
        out_specs=P(None, GROUP, TP),
        check_vma=False,
    )
```

profile of v0, /device:TPU:30, one launch (start us, length us, event | category | flops | bytes accessed | tf_op | source)
XLA Modules:
  0.0 165.5 jit_solution(15856675031027295271)
XLA Ops:
  1.5 8.5 %collective-permute-start = (bf16[64,320]{1,0:T(8,128)(2,1)S(1)}, bf16[64,320]{1,0:T(8,128)(2,1)S(1)}, u32[]{:S(2)}, u32[]{:S(2)}) collective-permute-start(bf16[64,320]{1,0:T(8,128)(2,1)S(1)} %convolution_convert_fusion), channel_id=1, source_target_pairs={{0,0},{1,1},{2,32},{3,33},{4,64},{5,65},{6,96},{7,97},{8,128},{9,1... | collective-permute-start | bytes 122888 | tf_op jit(solution)/shard_map/ppermute | solution.py:277
  10.0 5.5 %collective-permute-done = bf16[64,320]{1,0:T(8,128)(2,1)S(1)} collective-permute-done((bf16[64,320]{1,0:T(8,128)(2,1)S(1)}, bf16[64,320]{1,0:T(8,128)(2,1)S(1)}, u32[]{:S(2)}, u32[]{:S(2)}) %collective-permute-start) | collective-permute-done | bytes 40992 | tf_op jit(solution)/shard_map/ppermute | solution.py:277
  15.5 12.3 %all_to_all.25 = bf16[8,64,320]{2,1,0:T(8,128)(2,1)S(1)} all-to-all(bf16[8,64,320]{2,1,0:T(8,128)(2,1)S(1)} %broadcast_in_dim.24), channel_id=1, replica_groups=mesh['z'=8,'yl'=2,'x'=4,'yh'=2,'core'=2] {'x','yh'}, dimensions={0} | all-to-all | bytes 655360 | tf_op jit(solution)/shard_map/all_to_all | solution.py:278
  31.5 18.2 %collective-permute-done.11.s_oth = bf16[64,320]{1,0:T(8,128)(2,1)S(1)} collective-permute-done((bf16[64,320]{1,0:T(8,128)(2,1)S(1)}, bf16[64,320]{1,0:T(8,128)(2,1)S(1)}, u32[]{:S(2)}, u32[]{:S(2)}) %collective-permute-start.11) | collective-permute-done | bytes 40992 | tf_op jit(solution)/shard_map/ppermute | solution.py:269
  50.8 6.7 %all-to-all-start.1 = ((bf16[8,64,128]{2,1,0:T(8,128)(2,1)}), bf16[8,64,128]{2,1,0:T(8,128)(2,1)S(1)}, u32[]{:S(2)}, u32[]{:S(2)}) async-start(bf16[8,64,128]{2,1,0:T(8,128)(2,1)} %shard_map.128), calls=%async_computation.1 | async-start | bytes 262144 | tf_op jit(solution)/shard_map/all_to_all | solution.py:290
  61.3 3.1 %shard_map.127 = (bf16[64,1280]{1,0:T(8,128)(2,1)S(1)}, bf16[64,1280]{1,0:T(8,128)(2,1)S(1)}, bf16[64,1280]{1,0:T(8,128)(2,1)}, bf16[64,1280]{1,0:T(8,128)(2,1)S...) custom-call(s32[2]{0:T(128)S(1)} %pad_add_fusion.1.place, ...), custom_call_target="tpu_custom_call" | custom-call | flops 838860800 | bytes 1048576 | tf_op jit(solution)/shard_map/pallas_call | solution.py:38
  64.4 5.9 %collective-permute-start.4 = (bf16[64,1280]{1,0:T(8,128)(2,1)}, bf16[64,1280]{1,0:T(8,128)(2,1)S(1)}, u32[]{:S(2)}, u32[]{:S(2)}) collective-permute-start(bf16[64,1280]{1,0:T(8,128)(2,1)} %get-tuple-element.20), channel_id=1, source_target_pairs={{0,128},{32,160},{64,192},{96,224},{128,0},{160,32},{192,64},{224,... | collective-permute-start | bytes 491528 | tf_op jit(solution)/shard_map/ppermute | solution.py:308
  71.8 7.5 %all-to-all-start.2 = ((bf16[16,64,128]{2,1,0:T(8,128)(2,1)}), bf16[16,64,128]{2,1,0:T(8,128)(2,1)S(1)}, u32[]{:S(2)}, u32[]{:S(2)}) async-start(bf16[16,64,128]{2,1,0:T(8,128)(2,1)} %get-tuple-element.28), calls=%async_computation.2 | async-start | bytes 524288 | tf_op jit(solution)/shard_map/all_to_all | solution.py:314
  79.3 4.5 %collective-permute-start.6 = (bf16[64,1280]{1,0:T(8,128)(2,1)}, bf16[64,1280]{1,0:T(8,128)(2,1)S(1)}, u32[]{:S(2)}, u32[]{:S(2)}) collective-permute-start(bf16[64,1280]{1,0:T(8,128)(2,1)} %get-tuple-element.22), channel_id=1, source_target_pairs={{0,160},{32,192},{64,224},{96,0},{128,32},{160,64},{192,96},{224,1... | collective-permute-start | bytes 491528 | tf_op jit(solution)/shard_map/ppermute | solution.py:308
  84.3 3.6 %collective-permute-start.8 = (bf16[64,1280]{1,0:T(8,128)(2,1)}, bf16[64,1280]{1,0:T(8,128)(2,1)S(1)}, u32[]{:S(2)}, u32[]{:S(2)}) collective-permute-start(bf16[64,1280]{1,0:T(8,128)(2,1)} %get-tuple-element.24), channel_id=1, source_target_pairs={{0,192},{32,224},{64,0},{96,32},{128,64},{160,96},{192,128},{224,1... | collective-permute-start | bytes 491528 | tf_op jit(solution)/shard_map/ppermute | solution.py:308
  88.5 2.7 %collective-permute-start.10 = (bf16[64,1280]{1,0:T(8,128)(2,1)S(1)}, bf16[64,1280]{1,0:T(8,128)(2,1)S(1)}, u32[]{:S(2)}, u32[]{:S(2)}) collective-permute-start(bf16[64,1280]{1,0:T(8,128)(2,1)S(1)} %get-tuple-element.26), channel_id=1, source_target_pairs={{0,224},{32,0},{64,32},{96,64},{128,96},{160,128},{192,160},{224,1... | collective-permute-start | bytes 491528 | tf_op jit(solution)/shard_map/ppermute | solution.py:308
  91.8 8.1 %shard_map.130 = (f32[32,8,640]{2,1,0:T(8,128)S(1)}, f32[32,128]{1,0:T(8,128)S(1)}) custom-call(bf16[16,64,128]{2,1,0:T(8,128)(2,1)S(1)} %all-to-all-done.2.bc, bf16[32,10,64,256]{3,2,1,0:T(8,128)(2,1)} %s.1), custom_call_target="tpu_custom_call" | custom-call | flops 83886080 | bytes 1048576 | tf_op jit(solution)/shard_map/pallas_call | solution.py:38
  100.0 1.7 %collective-permute-done.8.refs_5_ = bf16[64,1280]{1,0:T(8,128)(2,1)S(1)} collective-permute-done((bf16[64,1280]{1,0:T(8,128)(2,1)}, bf16[64,1280]{1,0:T(8,128)(2,1)S(1)}, u32[]{:S(2)}, u32[]{:S(2)}) %collective-permute-start.8) | collective-permute-done | bytes 163872 | tf_op jit(solution)/shard_map/ppermute | solution.py:308
  101.7 3.9 %collective-permute-done.10.refs_7_ = bf16[64,1280]{1,0:T(8,128)(2,1)S(1)} collective-permute-done((bf16[64,1280]{1,0:T(8,128)(2,1)S(1)}, bf16[64,1280]{1,0:T(8,128)(2,1)S(1)}, u32[]{:S(2)}, u32[]{:S(2)}) %collective-permute-start.10) | collective-permute-done | bytes 163872 | tf_op jit(solution)/shard_map/ppermute | solution.py:308
  105.5 1.6 shard_map.131
  107.2 4.7 %all-to-all-start.3 = ((bf16[8,64,640]{2,1,0:T(8,128)(2,1)}), bf16[8,64,640]{2,1,0:T(8,128)(2,1)S(1)}, u32[]{:S(2)}, u32[]{:S(2)}) async-start(bf16[8,64,640]{2,1,0:T(8,128)(2,1)} %shard_map.131), calls=%async_computation.3 | async-start | bytes 1310720 | tf_op jit(solution)/shard_map/all_to_all | solution.py:347
  112.3 10.7 %collective-permute-done.12.w_oth = bf16[320,640]{1,0:T(8,128)(2,1)S(1)} collective-permute-done((bf16[320,640]{1,0:T(8,128)(2,1)S(1)}, bf16[320,640]{1,0:T(8,128)(2,1)S(1)}, u32[]{:S(2)}, u32[]{:S(2)}) %collective-permute-start.12) | collective-permute-done | bytes 409632 | tf_op jit(solution)/shard_map/ppermute | solution.py:271
  123.0 9.3 %all-to-all-done.3.gg = bf16[8,64,640]{2,1,0:T(8,128)(2,1)S(1)} async-done(((bf16[8,64,640]{2,1,0:T(8,128)(2,1)}), bf16[8,64,640]{2,1,0:T(8,128)(2,1)S(1)}, u32[]{:S(2)}, u32[]{:S(2)}) %all-to-all-start.3) | async-done | bytes 655392 | tf_op jit(solution)/shard_map/all_to_all | solution.py:347
  132.3 1.7 %shard_map.132 = (f32[8,64,384]{2,1,0:T(8,128)S(1)}, bf16[8,64,384]{2,1,0:T(8,128)(2,1)S(1)}) custom-call(s32[2]{0:T(128)S(1)} %pad_add_fusion.place, bf16[8,64,640]{2,1,0:T(8,128)(2,1)S(1)} %all-to-all-done.3.gg, bf16[320,640]{1,0:T(8,128)(2,1)S(1)} %bitcast.22, bf16[320,640]{1,0:T(8,128)(2,1)S(1)} %collective-permute-done.12.w_oth, ...), custom_call_target="tpu_custom_call" | custom-call | flops 419430400 | bytes 1048576 | tf_op jit(solution)/shard_map/pallas_call | solution.py:38
  134.1 1.7 %collective-permute-done.13.got = bf16[8,64,384]{2,1,0:T(8,128)(2,1)S(1)} collective-permute-done((bf16[8,64,384]{2,1,0:T(8,128)(2,1)S(1)}, bf16[8,64,384]{2,1,0:T(8,128)(2,1)S(1)}, u32[]{:S(2)}, u32[]{:S(2)}) %collective-permute-start.13) | collective-permute-done | bytes 393248 | tf_op jit(solution)/shard_map/ppermute | solution.py:358
  136.9 7.2 %all-to-all-start.4 = ((bf16[8,64,384]{2,1,0:T(8,128)(2,1)}), bf16[8,64,384]{2,1,0:T(8,128)(2,1)S(1)}, u32[]{:S(2)}, u32[]{:S(2)}) async-start(bf16[8,64,384]{2,1,0:T(8,128)(2,1)} %shard_map.133), calls=%async_computation.4 | async-start | bytes 786432 | tf_op jit(solution)/shard_map/all_to_all | solution.py:360
  144.8 5.7 %all-to-all-done.4.part = bf16[8,64,384]{2,1,0:T(8,128)(2,1)S(1)} async-done(((bf16[8,64,384]{2,1,0:T(8,128)(2,1)}), bf16[8,64,384]{2,1,0:T(8,128)(2,1)S(1)}, u32[]{:S(2)}, u32[]{:S(2)}) %all-to-all-start.4) | async-done | bytes 393248 | tf_op jit(solution)/shard_map/all_to_all | solution.py:360
  150.6 3.8 %collective-permute-start.14 = (bf16[64,320]{1,0:T(8,128)(2,1)S(1)}, bf16[64,320]{1,0:T(8,128)(2,1)S(1)}, u32[]{:S(2)}, u32[]{:S(2)}) collective-permute-start(bf16[64,320]{1,0:T(8,128)(2,1)S(1)} %shard_map.134), channel_id=1, source_target_pairs={{0,0},{1,1},{2,32},{3,33},{4,64},{5,65},{6,96},{7,97},{8,128},{9,1... | collective-permute-start | bytes 122888 | tf_op jit(solution)/shard_map/ppermute | solution.py:366
  154.4 10.3 %collective-permute-done.14 = bf16[64,320]{1,0:T(8,128)(2,1)S(1)} collective-permute-done((bf16[64,320]{1,0:T(8,128)(2,1)S(1)}, bf16[64,320]{1,0:T(8,128)(2,1)S(1)}, u32[]{:S(2)}, u32[]{:S(2)}) %collective-permute-start.14) | collective-permute-done | bytes 40992 | tf_op jit(solution)/shard_map/ppermute | solution.py:366
  (57 shorter events, 15.9 us)
Async XLA Ops:
  0.0 105.5 %copy-start.1 = (f32[10]{0:T(128)S(1)}, f32[10]{0:T(128)}, u32[]{:S(2)}) copy-start(f32[10]{0:T(128)} %param.20) | copy-start | bytes 124
  0.0 105.5 %copy-start.2 = (f32[10]{0:T(128)S(1)}, f32[10]{0:T(128)}, u32[]{:S(2)}) copy-start(f32[10]{0:T(128)} %param.21) | copy-start | bytes 124
  0.0 105.5 %copy-start.3 = (f32[10]{0:T(128)S(1)}, f32[10]{0:T(128)}, u32[]{:S(2)}) copy-start(f32[10]{0:T(128)} %param.22) | copy-start | bytes 124
  1.5 110.4 %copy-start.6 = (bf16[640,320]{0,1:T(8,128)(2,1)S(1)}, bf16[640,320]{0,1:T(8,128)(2,1)}, u32[]{:S(2)}) copy-start(bf16[640,320]{0,1:T(8,128)(2,1)} %param.24) | copy-start | bytes 1228804
  1.5 13.9 %collective-permute-start = (bf16[64,320]{1,0:T(8,128)(2,1)S(1)}, bf16[64,320]{1,0:T(8,128)(2,1)S(1)}, u32[]{:S(2)}, u32[]{:S(2)}) collective-permute-start(bf16[64,320]{1,0:T(8,128)(2,1)S(1)} %convolution_convert_fusion), channel_id=1, source_target_pairs={{0,0},{1,1},{2,32},{3,33},{4,64},{5,65},{6,96},{7,97},{8,128},{9,1... | collective-permute-start | bytes 122888 | tf_op jit(solution)/shard_map/ppermute | solution.py:277
  27.8 21.9 %collective-permute-start.1 = (bf16[512,320]{1,0:T(8,128)(2,1)S(1)}, bf16[512,320]{1,0:T(8,128)(2,1)S(1)}, u32[]{:S(2)}, u32[]{:S(2)}) collective-permute-start(bf16[512,320]{1,0:T(8,128)(2,1)S(1)} %bitcast.15), channel_id=1, source_target_pairs={{0,1},{1,0},{2,3},{3,2},{4,5},{5,4},{6,7},{7,6},{8,9},{9,8},{10,11... | collective-permute-start | bytes 983048 | tf_op jit(solution)/shard_map/ppermute | solution.py:281
  27.8 29.7 %collective-permute-start.2 = (bf16[320,640]{1,0:T(8,128)(2,1)}, bf16[320,640]{1,0:T(8,128)(2,1)S(1)}, u32[]{:S(2)}, u32[]{:S(2)}) collective-permute-start(bf16[320,640]{1,0:T(8,128)(2,1)} %x_own.1), channel_id=1, source_target_pairs={{0,16},{16,0},{1,17},{17,1},{2,18},{18,2},{3,19},{19,3},{4,20},{20... | collective-permute-start | bytes 1228808 | tf_op jit(solution)/shard_map/ppermute | solution.py:264
  28.5 29.1 %collective-permute-start.3 = (bf16[320,640]{1,0:T(8,128)(2,1)}, bf16[320,640]{1,0:T(8,128)(2,1)S(1)}, u32[]{:S(2)}, u32[]{:S(2)}) collective-permute-start(bf16[320,640]{1,0:T(8,128)(2,1)} %z_own.1), channel_id=1, source_target_pairs={{0,16},{16,0},{1,17},{17,1},{2,18},{18,2},{3,19},{19,3},{4,20},{20... | collective-permute-start | bytes 1228808 | tf_op jit(solution)/shard_map/ppermute | solution.py:265
  30.8 19.0 %collective-permute-start.11 = (bf16[64,320]{1,0:T(8,128)(2,1)S(1)}, bf16[64,320]{1,0:T(8,128)(2,1)S(1)}, u32[]{:S(2)}, u32[]{:S(2)}) collective-permute-start(bf16[64,320]{1,0:T(8,128)(2,1)S(1)} %maximum_maximum_fusion.s_own), channel_id=1, source_target_pairs={{0,16},{16,0},{1,17},{17,1},{2,18},{18,2},{3,19},{19,3},{4,20},{20... | collective-permute-start | bytes 122888 | tf_op jit(solution)/shard_map/ppermute | solution.py:269
  50.8 20.1 %all-to-all-start.1 = ((bf16[8,64,128]{2,1,0:T(8,128)(2,1)}), bf16[8,64,128]{2,1,0:T(8,128)(2,1)S(1)}, u32[]{:S(2)}, u32[]{:S(2)}) async-start(bf16[8,64,128]{2,1,0:T(8,128)(2,1)} %shard_map.128), calls=%async_computation.1 | async-start | bytes 262144 | tf_op jit(solution)/shard_map/all_to_all | solution.py:290
  64.4 100.4 %copy-start.10 = (bf16[64,320]{1,0:T(8,128)(2,1)S(1)}, bf16[64,320]{1,0:T(8,128)(2,1)}, u32[]{:S(2)}) copy-start(bf16[64,320]{1,0:T(8,128)(2,1)} %copy-done.9) | copy-start | bytes 122884
  64.4 23.5 %collective-permute-start.4 = (bf16[64,1280]{1,0:T(8,128)(2,1)}, bf16[64,1280]{1,0:T(8,128)(2,1)S(1)}, u32[]{:S(2)}, u32[]{:S(2)}) collective-permute-start(bf16[64,1280]{1,0:T(8,128)(2,1)} %get-tuple-element.20), channel_id=1, source_target_pairs={{0,128},{32,160},{64,192},{96,224},{128,0},{160,32},{192,64},{224,... | collective-permute-start | bytes 491528 | tf_op jit(solution)/shard_map/ppermute | solution.py:308
  70.3 18.1 %collective-permute-start.5 = (bf16[64,1280]{1,0:T(8,128)(2,1)S(1)}, bf16[64,1280]{1,0:T(8,128)(2,1)S(1)}, u32[]{:S(2)}, u32[]{:S(2)}) collective-permute-start(bf16[64,1280]{1,0:T(8,128)(2,1)S(1)} %get-tuple-element.21), channel_id=1, source_target_pairs={{0,96},{32,128},{64,160},{96,192},{128,224},{160,0},{192,32},{224,... | collective-permute-start | bytes 491528 | tf_op jit(solution)/shard_map/ppermute | solution.py:308
  71.8 20.1 %all-to-all-start.2 = ((bf16[16,64,128]{2,1,0:T(8,128)(2,1)}), bf16[16,64,128]{2,1,0:T(8,128)(2,1)S(1)}, u32[]{:S(2)}, u32[]{:S(2)}) async-start(bf16[16,64,128]{2,1,0:T(8,128)(2,1)} %get-tuple-element.28), calls=%async_computation.2 | async-start | bytes 524288 | tf_op jit(solution)/shard_map/all_to_all | solution.py:314
  79.3 20.7 %collective-permute-start.6 = (bf16[64,1280]{1,0:T(8,128)(2,1)}, bf16[64,1280]{1,0:T(8,128)(2,1)S(1)}, u32[]{:S(2)}, u32[]{:S(2)}) collective-permute-start(bf16[64,1280]{1,0:T(8,128)(2,1)} %get-tuple-element.22), channel_id=1, source_target_pairs={{0,160},{32,192},{64,224},{96,0},{128,32},{160,64},{192,96},{224,1... | collective-permute-start | bytes 491528 | tf_op jit(solution)/shard_map/ppermute | solution.py:308
  83.7 16.2 %collective-permute-start.7 = (bf16[64,1280]{1,0:T(8,128)(2,1)}, bf16[64,1280]{1,0:T(8,128)(2,1)S(1)}, u32[]{:S(2)}, u32[]{:S(2)}) collective-permute-start(bf16[64,1280]{1,0:T(8,128)(2,1)} %get-tuple-element.23), channel_id=1, source_target_pairs={{0,64},{32,96},{64,128},{96,160},{128,192},{160,224},{192,0},{224,... | collective-permute-start | bytes 491528 | tf_op jit(solution)/shard_map/ppermute | solution.py:308
  84.3 17.4 %collective-permute-start.8 = (bf16[64,1280]{1,0:T(8,128)(2,1)}, bf16[64,1280]{1,0:T(8,128)(2,1)S(1)}, u32[]{:S(2)}, u32[]{:S(2)}) collective-permute-start(bf16[64,1280]{1,0:T(8,128)(2,1)} %get-tuple-element.24), channel_id=1, source_target_pairs={{0,192},{32,224},{64,0},{96,32},{128,64},{160,96},{192,128},{224,1... | collective-permute-start | bytes 491528 | tf_op jit(solution)/shard_map/ppermute | solution.py:308
  87.9 13.8 %collective-permute-start.9 = (bf16[64,1280]{1,0:T(8,128)(2,1)S(1)}, bf16[64,1280]{1,0:T(8,128)(2,1)S(1)}, u32[]{:S(2)}, u32[]{:S(2)}) collective-permute-start(bf16[64,1280]{1,0:T(8,128)(2,1)S(1)} %get-tuple-element.25), channel_id=1, source_target_pairs={{0,32},{32,64},{64,96},{96,128},{128,160},{160,192},{192,224},{224... | collective-permute-start | bytes 491528 | tf_op jit(solution)/shard_map/ppermute | solution.py:308
  88.5 17.1 %collective-permute-start.10 = (bf16[64,1280]{1,0:T(8,128)(2,1)S(1)}, bf16[64,1280]{1,0:T(8,128)(2,1)S(1)}, u32[]{:S(2)}, u32[]{:S(2)}) collective-permute-start(bf16[64,1280]{1,0:T(8,128)(2,1)S(1)} %get-tuple-element.26), channel_id=1, source_target_pairs={{0,224},{32,0},{64,32},{96,64},{128,96},{160,128},{192,160},{224,1... | collective-permute-start | bytes 491528 | tf_op jit(solution)/shard_map/ppermute | solution.py:308
  107.2 25.2 %all-to-all-start.3 = ((bf16[8,64,640]{2,1,0:T(8,128)(2,1)}), bf16[8,64,640]{2,1,0:T(8,128)(2,1)S(1)}, u32[]{:S(2)}, u32[]{:S(2)}) async-start(bf16[8,64,640]{2,1,0:T(8,128)(2,1)} %shard_map.131), calls=%async_computation.3 | async-start | bytes 1310720 | tf_op jit(solution)/shard_map/all_to_all | solution.py:347
  111.9 11.2 %collective-permute-start.12 = (bf16[320,640]{1,0:T(8,128)(2,1)S(1)}, bf16[320,640]{1,0:T(8,128)(2,1)S(1)}, u32[]{:S(2)}, u32[]{:S(2)}) collective-permute-start(bf16[320,640]{1,0:T(8,128)(2,1)S(1)} %bitcast.21), channel_id=1, source_target_pairs={{0,16},{16,0},{1,17},{17,1},{2,18},{18,2},{3,19},{19,3},{4,20},{20... | collective-permute-start | bytes 1228808 | tf_op jit(solution)/shard_map/ppermute | solution.py:271
  134.0 1.8 %collective-permute-start.13 = (bf16[8,64,384]{2,1,0:T(8,128)(2,1)S(1)}, bf16[8,64,384]{2,1,0:T(8,128)(2,1)S(1)}, u32[]{:S(2)}, u32[]{:S(2)}) collective-permute-start(bf16[8,64,384]{2,1,0:T(8,128)(2,1)S(1)} %get-tuple-element.32), channel_id=1, source_target_pairs={{0,1},{1,0},{2,3},{3,2},{4,5},{5,4},{6,7},{7,6},{8,9},{9,8},{10,11... | collective-permute-start | bytes 1179656 | tf_op jit(solution)/shard_map/ppermute | solution.py:358
  136.9 13.5 %all-to-all-start.4 = ((bf16[8,64,384]{2,1,0:T(8,128)(2,1)}), bf16[8,64,384]{2,1,0:T(8,128)(2,1)S(1)}, u32[]{:S(2)}, u32[]{:S(2)}) async-start(bf16[8,64,384]{2,1,0:T(8,128)(2,1)} %shard_map.133), calls=%async_computation.4 | async-start | bytes 786432 | tf_op jit(solution)/shard_map/all_to_all | solution.py:360
  150.6 14.2 %collective-permute-start.14 = (bf16[64,320]{1,0:T(8,128)(2,1)S(1)}, bf16[64,320]{1,0:T(8,128)(2,1)S(1)}, u32[]{:S(2)}, u32[]{:S(2)}) collective-permute-start(bf16[64,320]{1,0:T(8,128)(2,1)S(1)} %shard_map.134), channel_id=1, source_target_pairs={{0,0},{1,1},{2,32},{3,33},{4,64},{5,65},{6,96},{7,97},{8,128},{9,1... | collective-permute-start | bytes 122888 | tf_op jit(solution)/shard_map/ppermute | solution.py:366
  (6 other events, 18.8 us)
where the time goes:
time: 166 us; the launch traced here: 165 us
  waiting for transfers between devices  67 us (40%)
  starting transfers between devices  59.9 us (36%)
  Pallas kernels  17.7 us (11%)
  blocking collectives  12.3 us (7%)
  local copies, waits for them, and re-layouts  5.68 us (3%)
  other arithmetic  1.7 us (1%)
    ppermute x7, starting transfers between devices, per_device(): lax.ppermute(blocks[k], 'z', [(i, (i + k) % 8) for i in range(8)])  18.3 us
    ppermute x1, waiting for transfers between devices, per_device(): small_oth = lax.ppermute(small_own, 'yl', pair)  18.2 us
    pallas_call x8, Pallas kernels, call(): pl.pallas_call(body, out_shape=out_shape, in_specs=in_specs, out_specs=ou...  17.7 us
    all_to_all x1, blocking collectives, per_device(): lax.all_to_all(jnp.broadcast_to(moved[None], (8,) + moved.shape), ('x', '...  12.3 us
    ppermute x1, waiting for transfers between devices, per_device(): out_oth = lax.ppermute(out_own, 'yl', pair)  10.7 us
    ppermute x1, waiting for transfers between devices, per_device(): back = lax.ppermute(mine, ALL, swap)  10.3 us
    all_to_all x1, waiting for transfers between devices, per_device(): gg_all = lax.all_to_all(gg, 'z', 0, 0)  9.29 us
    ppermute x1, starting transfers between devices, per_device(): moved = lax.ppermute(own_embed, ALL, swap)  8.48 us
  transfers between devices with their start and end apart: 19, of which 9 were waited for; matrix products, arithmetic and copies ran while one was open for 1% of the time, Pallas kernels for 8%

commit v1 on v0

--- a/solution.py
+++ b/solution.py
@@ -15,7 +15,7 @@
 GROUP = ("z", "yl")
 TP = ("x", "yh", "core")
 ALL = GROUP + TP
-VMEM_LIMIT = 48 * 1024 * 1024
+VMEM_LIMIT = 14 * 1024 * 1024
 
 FAR_FIRST = (4, 3, 5, 2, 6, 1, 7)
 
@@ -180,37 +180,27 @@
     lim = 1e30
     gg1 = jnp.clip(read1 * gate[:half] * gain[...], -lim, lim)
     gg2 = jnp.clip(read2 * gate[half:] * gain[...], -lim, lim)
-    both = jnp.concatenate([gg1, gg2], 0).astype(BF)
-    for k in range(out.shape[0]):
-        out[k] = both
-
-
-def output_kernel(place, gg, w_own, w_oth, gain, keep, send):
-    y = place[0]
-    core = place[1]
-    groups, rows, inner = gg.shape
-    cols = w_own.shape[0]
-    v = gg[...].reshape(groups * rows, inner)
+    out[...] = jnp.concatenate([gg1, gg2], 0).astype(BF)
+
+
+def output_kernel(place, mine, other, gain, own, r1, l1, r2, l2, r3, l3, r4, keep, send):
+    swapped = place[0]
+    z = place[1]
+    groups, rows, _ = keep.shape
+    m = mine[...]
+    o = other[...]
+    v = jnp.concatenate([jnp.where(swapped == 0, m, o), jnp.where(swapped == 0, o, m)], 0)
     raw = v.astype(F32) / gain[...]
     ss = jnp.sum(raw * raw, axis=1, keepdims=True)
     hi = ss.astype(BF).astype(F32)
-    lo = ss - hi
-    lane = lax.broadcasted_iota(jnp.int32, (groups * rows, 64), 1)
-    tail = jnp.where(lane == 0, hi, jnp.where(lane == 1, lo, 0.0))
-
-    def block(w):
-        o = jnp.concatenate([nt(v, w[...]), tail], 1)
-        return o.reshape(groups, rows, cols + 64)
-
-    @pl.when(y == core)
-    def _():
-        keep[...] = block(w_own)
-        send[...] = block(w_oth).astype(BF)
-
-    @pl.when(y != core)
-    def _():
-        keep[...] = block(w_oth)
-        send[...] = block(w_own).astype(BF)
+    lane = lax.broadcasted_iota(jnp.int32, (2 * rows, 64), 1)
+    tail = jnp.where(lane == 0, hi, jnp.where(lane == 1, ss - hi, 0.0))
+    order = ((0, own), (7, r1), (1, l1), (6, r2), (2, l2), (5, r3), (3, l3), (4, r4))
+    for shift, w in order:
+        block = jnp.concatenate([nt(v, w[...]), tail], 1)
+        at = lax.rem(z + shift, groups)
+        keep[at] = block[:rows]
+        send[at] = block[rows:].astype(BF)
 
 
 def pair_kernel(keep, got, out):
@@ -261,14 +251,22 @@
                     swap.append(((z * 2 + yy) * 16 + w * 2 + c, (w * 2 + yy) * 16 + z * 2 + c))
     pair = [(0, 1), (1, 0)]
 
+    gain = norm_gain.reshape(1, inner)
+    right = [(i, (i + 1) % 8) for i in range(8)]
+    left = [(i, (i + 7) % 8) for i in range(8)]
+    out_own = out_weight.T
+    ring_r = [out_own]
+    ring_l = [out_own]
+    for _ in range(1, 4):
+        ring_r.append(lax.ppermute(ring_r[-1], "z", right))
+        ring_l.append(lax.ppermute(ring_l[-1], "z", left))
+    ring_r.append(lax.ppermute(ring_r[-1], "z", right))
     x_oth = lax.ppermute(x_weight, "yl", pair)
     z_oth = lax.ppermute(z_weight, "yl", pair)
     small_own = jnp.concatenate(
         [bc_weight.T, dt_weight.T, jnp.zeros((64 - 32 - heads, wide), BF)], 0
     )
     small_oth = lax.ppermute(small_own, "yl", pair)
-    out_own = out_weight.T
-    out_oth = lax.ppermute(out_own, "yl", pair)
 
     flat_ids = token_ids.reshape(-1)
     codes = jnp.arange(code_table.shape[0], dtype=jnp.int32)
@@ -329,10 +327,9 @@
         scratch=[pltpu.VMEM((rows, 8, 256), F32)],
         flops=2 * 8 * rows * inner * 256,
     )
-    gain = norm_gain.reshape(1, inner)
     gg = call(
         decode_kernel,
-        jax.ShapeDtypeStruct((8, 2 * rows, inner), BF),
+        jax.ShapeDtypeStruct((2 * rows, inner), BF),
         (
             *parts,
             small,
@@ -344,16 +341,29 @@
             gain,
         ),
     )
-    gg_all = lax.all_to_all(gg, "z", 0, 0)
+    gg_oth = lax.ppermute(gg, "yl", pair)
     keep, send = call(
         output_kernel,
         (
             jax.ShapeDtypeStruct((8, 2 * rows, wide + 64), F32),
             jax.ShapeDtypeStruct((8, 2 * rows, wide + 64), BF),
         ),
-        (jnp.stack([y, core]), gg_all, out_own, out_oth, gain),
+        (
+            jnp.stack([(y != core).astype(jnp.int32), lax.axis_index("z")]),
+            gg,
+            gg_oth,
+            gain,
+            out_own,
+            ring_r[1],
+            ring_l[1],
+            ring_r[2],
+            ring_l[2],
+            ring_r[3],
+            ring_l[3],
+            ring_r[4],
+        ),
         in_smem=1,
-        flops=2 * 16 * rows * inner * 2 * wide,
+        flops=2 * 4 * rows * inner * 8 * wide,
     )
     got = lax.ppermute(send, "core", pair)
     paired = call(pair_kernel, jax.ShapeDtypeStruct((8, 2 * rows, wide + 64), BF), (keep, got))
@@ -363,7 +373,7 @@
         jax.ShapeDtypeStruct((2 * rows, wide), BF),
         (partial_out,),
     )
-    back = lax.ppermute(mine, ALL, swap)
+    back = lax.ppermute(mine, ("yl", "core"), [(0, 0), (1, 2), (2, 1), (3, 3)])
     result = (own_embed.astype(F32) + back.astype(F32)).reshape(2, rows, wide)
     live = jnp.arange(rows, dtype=jnp.int32) < row_counts[0]
     return jnp.where(live[None, :, None], result, 0.0).astype(BF)

time: 166 us -> 160 us (0.964)
  the two profiles are of different devices: /device:TPU:30 before, /device:TPU:1 now
where the time goes in v1:
time: 160 us; the launch traced here: 159 us
  starting transfers between devices  84.2 us (53%)
  waiting for transfers between devices  40.6 us (25%)
  Pallas kernels  15.5 us (10%)
  local copies, waits for them, and re-layouts  14.8 us (9%)
  other arithmetic  2.48 us (2%)
    all_to_all x1, starting transfers between devices, per_device(): lax.all_to_all(jnp.broadcast_to(moved[None], (8,) + moved.shape), ('x', '...  19 us
    pallas_call x8, Pallas kernels, call(): pl.pallas_call(body, out_shape=out_shape, in_specs=in_specs, out_specs=ou...  15.5 us
    ppermute x7, starting transfers between devices, per_device(): lax.ppermute(blocks[k], 'z', [(i, (i + k) % 8) for i in range(8)])  14.6 us
    all_to_all x1, starting transfers between devices, per_device(): bc_all = lax.all_to_all(bc, TP, 0, 0)  12.8 us
    unnamed x40, local copies, waits for them, and re-layouts  12 us
    ppermute x4, waiting for transfers between devices, per_device(): ring_r.append(lax.ppermute(ring_r[-1], 'z', right))  8.57 us
    all_to_all x1, waiting for transfers between devices, per_device(): partial_out = lax.all_to_all(paired, ('x', 'yh'), 0, 0)  8.5 us
    all_to_all x1, starting transfers between devices, per_device(): partial_out = lax.all_to_all(paired, ('x', 'yh'), 0, 0)  7.48 us
  transfers between devices with their start and end apart: 26, of which 9 were waited for; matrix products, arithmetic and copies ran while one was open for 3% of the time, Pallas kernels for 7%

profile of v1, /device:TPU:1, one launch (start us, length us, event | category | flops | bytes accessed | tf_op | source)
XLA Modules:
  0.0 158.8 jit_solution(1663558714247393050)
XLA Ops:
  0.0 2.5 %collective-permute-start.13 = (bf16[320,640]{1,0:T(8,128)(2,1)}, bf16[320,640]{1,0:T(8,128)(2,1)S(1)}, u32[]{:S(2)}, u32[]{:S(2)}) collective-permute-start(bf16[320,640]{1,0:T(8,128)(2,1)} %bitcast.17), channel_id=1, source_target_pairs={{0,32},{32,64},{64,96},{96,128},{128,160},{160,192},{192,224},{224... | collective-permute-start | bytes 1228808 | tf_op jit(solution)/shard_map/ppermute | solution.py:261
  2.5 4.0 %collective-permute-start.14 = (bf16[320,640]{1,0:T(8,128)(2,1)}, bf16[320,640]{1,0:T(8,128)(2,1)S(1)}, u32[]{:S(2)}, u32[]{:S(2)}) collective-permute-start(bf16[320,640]{1,0:T(8,128)(2,1)} %bitcast.18), channel_id=1, source_target_pairs={{0,224},{32,0},{64,32},{96,64},{128,96},{160,128},{192,160},{224,1... | collective-permute-start | bytes 1228808 | tf_op jit(solution)/shard_map/ppermute | solution.py:262
  7.2 8.6 %collective-permute-done.13.r1 = bf16[320,640]{1,0:T(8,128)(2,1)S(1)} collective-permute-done((bf16[320,640]{1,0:T(8,128)(2,1)}, bf16[320,640]{1,0:T(8,128)(2,1)S(1)}, u32[]{:S(2)}, u32[]{:S(2)}) %collective-permute-start.13) | collective-permute-done | bytes 409632 | tf_op jit(solution)/shard_map/ppermute | solution.py:261
  17.7 19.0 %all-to-all-start = ((bf16[8,64,320]{2,1,0:T(8,128)(2,1)}), bf16[8,64,320]{2,1,0:T(8,128)(2,1)S(1)}, u32[]{:S(2)}, u32[]{:S(2)}) async-start(bf16[8,64,320]{2,1,0:T(8,128)(2,1)} %broadcast_in_dim.24), calls=%async_computation | async-start | bytes 786432 | tf_op jit(solution)/shard_map/all_to_all | solution.py:276
  38.7 5.8 %all-to-all-done = bf16[8,64,320]{2,1,0:T(8,128)(2,1)S(1)} async-done(((bf16[8,64,320]{2,1,0:T(8,128)(2,1)}), bf16[8,64,320]{2,1,0:T(8,128)(2,1)S(1)}, u32[]{:S(2)}, u32[]{:S(2)}) %all-to-all-start) | async-done | bytes 327712 | tf_op jit(solution)/shard_map/all_to_all | solution.py:276
  44.5 4.8 %collective-permute-start.1 = (bf16[512,320]{1,0:T(8,128)(2,1)S(1)}, bf16[512,320]{1,0:T(8,128)(2,1)}, u32[]{:S(2)}, u32[]{:S(2)}) collective-permute-start(bf16[512,320]{1,0:T(8,128)(2,1)S(1)} %bitcast.14), channel_id=1, source_target_pairs={{0,1},{1,0},{2,3},{3,2},{4,5},{5,4},{6,7},{7,6},{8,9},{9,8},{10,11... | collective-permute-start | bytes 983048 | tf_op jit(solution)/shard_map/ppermute | solution.py:279
  52.9 5.2 %collective-permute-done.3.z_oth = bf16[320,640]{1,0:T(8,128)(2,1)} collective-permute-done((bf16[320,640]{1,0:T(8,128)(2,1)}, bf16[320,640]{1,0:T(8,128)(2,1)}, u32[]{:S(2)}, u32[]{:S(2)}) %collective-permute-start.3) | collective-permute-done | bytes 409632 | tf_op jit(solution)/shard_map/ppermute | solution.py:265
  60.2 3.6 %shard_map.127 = (bf16[64,1280]{1,0:T(8,128)(2,1)S(1)}, bf16[64,1280]{1,0:T(8,128)(2,1)S(1)}, bf16[64,1280]{1,0:T(8,128)(2,1)S(1)}, bf16[64,1280]{1,0:T(8,128)(2...) custom-call(s32[2]{0:T(128)S(1)} %pad_add_fusion.1.place, ...), custom_call_target="tpu_custom_call" | custom-call | flops 838860800 | bytes 1048576 | tf_op jit(solution)/shard_map/pallas_call | solution.py:38
  71.4 6.0 %all-to-all-start.1 = ((bf16[8,64,128]{2,1,0:T(8,128)(2,1)}), bf16[8,64,128]{2,1,0:T(8,128)(2,1)S(1)}, u32[]{:S(2)}, u32[]{:S(2)}) async-start(bf16[8,64,128]{2,1,0:T(8,128)(2,1)} %shard_map.128), calls=%async_computation.1 | async-start | bytes 262144 | tf_op jit(solution)/shard_map/all_to_all | solution.py:288
  77.4 5.4 %collective-permute-start.4 = (bf16[64,1280]{1,0:T(8,128)(2,1)}, bf16[64,1280]{1,0:T(8,128)(2,1)}, u32[]{:S(2)}, u32[]{:S(2)}) collective-permute-start(bf16[64,1280]{1,0:T(8,128)(2,1)} %copy-done.18), channel_id=1, source_target_pairs={{0,128},{32,160},{64,192},{96,224},{128,0},{160,32},{192,64},{224,... | collective-permute-start | bytes 491528 | tf_op jit(solution)/shard_map/ppermute | solution.py:306
  83.0 4.2 %collective-permute-start.6 = (bf16[64,1280]{1,0:T(8,128)(2,1)}, bf16[64,1280]{1,0:T(8,128)(2,1)}, u32[]{:S(2)}, u32[]{:S(2)}) collective-permute-start(bf16[64,1280]{1,0:T(8,128)(2,1)} %copy-done.16), channel_id=1, source_target_pairs={{0,160},{32,192},{64,224},{96,0},{128,32},{160,64},{192,96},{224,1... | collective-permute-start | bytes 491528 | tf_op jit(solution)/shard_map/ppermute | solution.py:306
  90.2 12.8 %all-to-all-start.2 = ((bf16[16,64,128]{2,1,0:T(8,128)(2,1)}), bf16[16,64,128]{2,1,0:T(8,128)(2,1)S(1)}, u32[]{:S(2)}, u32[]{:S(2)}) async-start(bf16[16,64,128]{2,1,0:T(8,128)(2,1)} %copy-done.3), calls=%async_computation.2 | async-start | bytes 524288 | tf_op jit(solution)/shard_map/all_to_all | solution.py:312
  103.4 3.3 %collective-permute-start.8 = (bf16[64,1280]{1,0:T(8,128)(2,1)}, bf16[64,1280]{1,0:T(8,128)(2,1)}, u32[]{:S(2)}, u32[]{:S(2)}) collective-permute-start(bf16[64,1280]{1,0:T(8,128)(2,1)} %copy-done.14), channel_id=1, source_target_pairs={{0,192},{32,224},{64,0},{96,32},{128,64},{160,96},{192,128},{224,1... | collective-permute-start | bytes 491528 | tf_op jit(solution)/shard_map/ppermute | solution.py:306
  107.6 4.2 %all-to-all-done.2.bc = bf16[16,64,128]{2,1,0:T(8,128)(2,1)S(1)} async-done(((bf16[16,64,128]{2,1,0:T(8,128)(2,1)}), bf16[16,64,128]{2,1,0:T(8,128)(2,1)S(1)}, u32[]{:S(2)}, u32[]{:S(2)}) %all-to-all-start.2) | async-done | bytes 262176 | tf_op jit(solution)/shard_map/all_to_all | solution.py:312
  111.9 4.0 %copy-done.1 = bf16[32,10,64,256]{3,2,1,0:T(8,128)(2,1)S(1)} copy-done((bf16[32,10,64,256]{3,2,1,0:T(8,128)(2,1)S(1)}, bf16[32,10,64,256]{3,2,1,0:T(8,128)(2,1)}, u32[]{:S(2)}) %copy-start.1) | copy-done | bytes 10485784
  115.8 4.0 %shard_map.130 = (f32[32,8,640]{2,1,0:T(8,128)S(1)}, f32[32,128]{1,0:T(8,128)S(1)}) custom-call(bf16[16,64,128]{2,1,0:T(8,128)(2,1)S(1)} %all-to-all-done.2.bc, bf16[32,10,64,256]{3,2,1,0:T(8,128)(2,1)S(1)} %copy-done.1), custom_call_target="tpu_custom_call" | custom-call | flops 83886080 | bytes 1048576 | tf_op jit(solution)/shard_map/pallas_call | solution.py:38
  119.8 2.1 %collective-permute-done.9.refs_6_ = bf16[64,1280]{1,0:T(8,128)(2,1)} collective-permute-done((bf16[64,1280]{1,0:T(8,128)(2,1)}, bf16[64,1280]{1,0:T(8,128)(2,1)}, u32[]{:S(2)}, u32[]{:S(2)}) %collective-permute-start.9) | collective-permute-done | bytes 163872 | tf_op jit(solution)/shard_map/ppermute | solution.py:306
  122.0 2.1 %shard_map.131.mine = bf16[64,640]{1,0:T(8,128)(2,1)S(1)} custom-call(bf16[64,1280]{1,0:T(8,128)(2,1)S(1)} %copy-done.5, bf16[64,1280]{1,0:T(8,128)(2,1)} %collective-permute-done.4.refs_1_, bf16[64,1280]{1,0:T(8,128)(2,1)} %collective-permute-done.5.refs_2_, bf16[64,1280]{1,0:T(8,128)(2,1)} %collective-permute-done.6.refs_3_, ...), custom_call_target="tpu_custom_call" | custom-call | flops 1048576 | bytes 1048576 | tf_op jit(solution)/shard_map/pallas_call | solution.py:38
  127.6 2.4 %shard_map.132 = (f32[8,64,384]{2,1,0:T(8,128)S(1)}, bf16[8,64,384]{2,1,0:T(8,128)(2,1)S(1)}) custom-call(s32[2]{0:T(128)S(1)} %pad_add_fusion.place, bf16[64,640]{1,0:T(8,128)(2,1)S(1)} %shard_map.131.mine, bf16[64,640]{1,0:T(8,128)(2,1)S(1)} %collective-permute-done.12.other, f32[1,640]{1,0:T(1,128)S(1)} %reshape.29.refs_14_.gain, ...), custom_call_target="tpu_custom_call" | custom-call | flops 419430400 | bytes 1048576 | tf_op jit(solution)/shard_map/pallas_call | solution.py:38
  130.0 2.6 %collective-permute-start.20 = (bf16[8,64,384]{2,1,0:T(8,128)(2,1)S(1)}, bf16[8,64,384]{2,1,0:T(8,128)(2,1)S(1)}, u32[]{:S(2)}, u32[]{:S(2)}) collective-permute-start(bf16[8,64,384]{2,1,0:T(8,128)(2,1)S(1)} %get-tuple-element.32), channel_id=1, source_target_pairs={{0,1},{1,0},{2,3},{3,2},{4,5},{5,4},{6,7},{7,6},{8,9},{9,8},{10,11... | collective-permute-start | bytes 1179656 | tf_op jit(solution)/shard_map/ppermute | solution.py:368
  135.1 7.5 %all-to-all-start.3 = ((bf16[8,64,384]{2,1,0:T(8,128)(2,1)}), bf16[8,64,384]{2,1,0:T(8,128)(2,1)S(1)}, u32[]{:S(2)}, u32[]{:S(2)}) async-start(bf16[8,64,384]{2,1,0:T(8,128)(2,1)} %shard_map.133), calls=%async_computation.3 | async-start | bytes 786432 | tf_op jit(solution)/shard_map/all_to_all | solution.py:370
  143.2 8.5 %all-to-all-done.3.part = bf16[8,64,384]{2,1,0:T(8,128)(2,1)S(1)} async-done(((bf16[8,64,384]{2,1,0:T(8,128)(2,1)}), bf16[8,64,384]{2,1,0:T(8,128)(2,1)S(1)}, u32[]{:S(2)}, u32[]{:S(2)}) %all-to-all-start.3) | async-done | bytes 393248 | tf_op jit(solution)/shard_map/all_to_all | solution.py:370
  151.9 2.4 %collective-permute-start.21 = (bf16[64,320]{1,0:T(8,128)(2,1)S(1)}, bf16[64,320]{1,0:T(8,128)(2,1)S(1)}, u32[]{:S(2)}, u32[]{:S(2)}) collective-permute-start(bf16[64,320]{1,0:T(8,128)(2,1)S(1)} %shard_map.134), channel_id=1, source_target_pairs={{0,0},{1,16},{16,1},{17,17},{2,2},{3,18},{18,3},{19,19},{4,4},{5,2... | collective-permute-start | bytes 122888 | tf_op jit(solution)/shard_map/ppermute | solution.py:376
  154.3 3.0 %collective-permute-done.21 = bf16[64,320]{1,0:T(8,128)(2,1)S(1)} collective-permute-done((bf16[64,320]{1,0:T(8,128)(2,1)S(1)}, bf16[64,320]{1,0:T(8,128)(2,1)S(1)}, u32[]{:S(2)}, u32[]{:S(2)}) %collective-permute-start.21) | collective-permute-done | bytes 40992 | tf_op jit(solution)/shard_map/ppermute | solution.py:376
  (88 shorter events, 30.2 us)
Async XLA Ops:
  0.0 15.8 %collective-permute-start.13 = (bf16[320,640]{1,0:T(8,128)(2,1)}, bf16[320,640]{1,0:T(8,128)(2,1)S(1)}, u32[]{:S(2)}, u32[]{:S(2)}) collective-permute-start(bf16[320,640]{1,0:T(8,128)(2,1)} %bitcast.17), channel_id=1, source_target_pairs={{0,32},{32,64},{64,96},{96,128},{128,160},{160,192},{192,224},{224... | collective-permute-start | bytes 1228808 | tf_op jit(solution)/shard_map/ppermute | solution.py:261
  2.5 46.8 %collective-permute-start.14 = (bf16[320,640]{1,0:T(8,128)(2,1)}, bf16[320,640]{1,0:T(8,128)(2,1)S(1)}, u32[]{:S(2)}, u32[]{:S(2)}) collective-permute-start(bf16[320,640]{1,0:T(8,128)(2,1)} %bitcast.18), channel_id=1, source_target_pairs={{0,224},{32,0},{64,32},{96,64},{128,96},{160,128},{192,160},{224,1... | collective-permute-start | bytes 1228808 | tf_op jit(solution)/shard_map/ppermute | solution.py:262
  15.8 33.5 %collective-permute-start.15 = (bf16[320,640]{1,0:T(8,128)(2,1)S(1)}, bf16[320,640]{1,0:T(8,128)(2,1)S(1)}, u32[]{:S(2)}, u32[]{:S(2)}) collective-permute-start(bf16[320,640]{1,0:T(8,128)(2,1)S(1)} %collective-permute-done.13.r1), channel_id=1, source_target_pairs={{0,32},{32,64},{64,96},{96,128},{128,160},{160,192},{192,224},{224... | collective-permute-start | bytes 1228808 | tf_op jit(solution)/shard_map/ppermute | solution.py:261
  17.7 26.8 %all-to-all-start = ((bf16[8,64,320]{2,1,0:T(8,128)(2,1)}), bf16[8,64,320]{2,1,0:T(8,128)(2,1)S(1)}, u32[]{:S(2)}, u32[]{:S(2)}) async-start(bf16[8,64,320]{2,1,0:T(8,128)(2,1)} %broadcast_in_dim.24), calls=%async_computation | async-start | bytes 786432 | tf_op jit(solution)/shard_map/all_to_all | solution.py:276
  36.6 15.0 %collective-permute-start.2 = (bf16[320,640]{1,0:T(8,128)(2,1)}, bf16[320,640]{1,0:T(8,128)(2,1)}, u32[]{:S(2)}, u32[]{:S(2)}) collective-permute-start(bf16[320,640]{1,0:T(8,128)(2,1)} %x_own.1), channel_id=1, source_target_pairs={{0,16},{16,0},{1,17},{17,1},{2,18},{18,2},{3,19},{19,3},{4,20},{20... | collective-permute-start | bytes 1228808 | tf_op jit(solution)/shard_map/ppermute | solution.py:264
  37.6 20.5 %collective-permute-start.3 = (bf16[320,640]{1,0:T(8,128)(2,1)}, bf16[320,640]{1,0:T(8,128)(2,1)}, u32[]{:S(2)}, u32[]{:S(2)}) collective-permute-start(bf16[320,640]{1,0:T(8,128)(2,1)} %z_own.1), channel_id=1, source_target_pairs={{0,16},{16,0},{1,17},{17,1},{2,18},{18,2},{3,19},{19,3},{4,20},{20... | collective-permute-start | bytes 1228808 | tf_op jit(solution)/shard_map/ppermute | solution.py:265
  44.5 13.7 %collective-permute-start.1 = (bf16[512,320]{1,0:T(8,128)(2,1)S(1)}, bf16[512,320]{1,0:T(8,128)(2,1)}, u32[]{:S(2)}, u32[]{:S(2)}) collective-permute-start(bf16[512,320]{1,0:T(8,128)(2,1)S(1)} %bitcast.14), channel_id=1, source_target_pairs={{0,1},{1,0},{2,3},{3,2},{4,5},{5,4},{6,7},{7,6},{8,9},{9,8},{10,11... | collective-permute-start | bytes 983048 | tf_op jit(solution)/shard_map/ppermute | solution.py:279
  49.2 38.0 %collective-permute-start.16 = (bf16[320,640]{1,0:T(8,128)(2,1)S(1)}, bf16[320,640]{1,0:T(8,128)(2,1)S(1)}, u32[]{:S(2)}, u32[]{:S(2)}) collective-permute-start(bf16[320,640]{1,0:T(8,128)(2,1)S(1)} %collective-permute-done.14.l1), channel_id=1, source_target_pairs={{0,224},{32,0},{64,32},{96,64},{128,96},{160,128},{192,160},{224,1... | collective-permute-start | bytes 1228808 | tf_op jit(solution)/shard_map/ppermute | solution.py:262
  49.4 37.9 %collective-permute-start.17 = (bf16[320,640]{1,0:T(8,128)(2,1)S(1)}, bf16[320,640]{1,0:T(8,128)(2,1)S(1)}, u32[]{:S(2)}, u32[]{:S(2)}) collective-permute-start(bf16[320,640]{1,0:T(8,128)(2,1)S(1)} %collective-permute-done.15.r2), channel_id=1, source_target_pairs={{0,32},{32,64},{64,96},{96,128},{128,160},{160,192},{192,224},{224... | collective-permute-start | bytes 1228808 | tf_op jit(solution)/shard_map/ppermute | solution.py:261
  51.6 17.7 %collective-permute-start.11 = (bf16[64,320]{1,0:T(8,128)(2,1)S(1)}, bf16[64,320]{1,0:T(8,128)(2,1)S(1)}, u32[]{:S(2)}, u32[]{:S(2)}) collective-permute-start(bf16[64,320]{1,0:T(8,128)(2,1)S(1)} %maximum_maximum_fusion.s_own), channel_id=1, source_target_pairs={{0,16},{16,0},{1,17},{17,1},{2,18},{18,2},{3,19},{19,3},{4,20},{20... | collective-permute-start | bytes 122888 | tf_op jit(solution)/shard_map/ppermute | solution.py:269
  68.5 14.5 %collective-permute-start.10 = (bf16[64,1280]{1,0:T(8,128)(2,1)}, bf16[64,1280]{1,0:T(8,128)(2,1)}, u32[]{:S(2)}, u32[]{:S(2)}) collective-permute-start(bf16[64,1280]{1,0:T(8,128)(2,1)} %get-tuple-element.26), channel_id=1, source_target_pairs={{0,224},{32,0},{64,32},{96,64},{128,96},{160,128},{192,160},{224,1... | collective-permute-start | bytes 491528 | tf_op jit(solution)/shard_map/ppermute | solution.py:306
  71.4 17.3 %all-to-all-start.1 = ((bf16[8,64,128]{2,1,0:T(8,128)(2,1)}), bf16[8,64,128]{2,1,0:T(8,128)(2,1)S(1)}, u32[]{:S(2)}, u32[]{:S(2)}) async-start(bf16[8,64,128]{2,1,0:T(8,128)(2,1)} %shard_map.128), calls=%async_computation.1 | async-start | bytes 262144 | tf_op jit(solution)/shard_map/all_to_all | solution.py:288
  77.4 25.6 %collective-permute-start.4 = (bf16[64,1280]{1,0:T(8,128)(2,1)}, bf16[64,1280]{1,0:T(8,128)(2,1)}, u32[]{:S(2)}, u32[]{:S(2)}) collective-permute-start(bf16[64,1280]{1,0:T(8,128)(2,1)} %copy-done.18), channel_id=1, source_target_pairs={{0,128},{32,160},{64,192},{96,224},{128,0},{160,32},{192,64},{224,... | collective-permute-start | bytes 491528 | tf_op jit(solution)/shard_map/ppermute | solution.py:306
  82.7 20.6 %collective-permute-start.5 = (bf16[64,1280]{1,0:T(8,128)(2,1)}, bf16[64,1280]{1,0:T(8,128)(2,1)}, u32[]{:S(2)}, u32[]{:S(2)}) collective-permute-start(bf16[64,1280]{1,0:T(8,128)(2,1)} %copy-done.17), channel_id=1, source_target_pairs={{0,96},{32,128},{64,160},{96,192},{128,224},{160,0},{192,32},{224,... | collective-permute-start | bytes 491528 | tf_op jit(solution)/shard_map/ppermute | solution.py:306
  83.0 23.6 %collective-permute-start.6 = (bf16[64,1280]{1,0:T(8,128)(2,1)}, bf16[64,1280]{1,0:T(8,128)(2,1)}, u32[]{:S(2)}, u32[]{:S(2)}) collective-permute-start(bf16[64,1280]{1,0:T(8,128)(2,1)} %copy-done.16), channel_id=1, source_target_pairs={{0,160},{32,192},{64,224},{96,0},{128,32},{160,64},{192,96},{224,1... | collective-permute-start | bytes 491528 | tf_op jit(solution)/shard_map/ppermute | solution.py:306
  87.2 40.4 %collective-permute-start.18 = (bf16[320,640]{1,0:T(8,128)(2,1)S(1)}, bf16[320,640]{1,0:T(8,128)(2,1)}, u32[]{:S(2)}, u32[]{:S(2)}) collective-permute-start(bf16[320,640]{1,0:T(8,128)(2,1)S(1)} %collective-permute-done.16.l2), channel_id=1, source_target_pairs={{0,224},{32,0},{64,32},{96,64},{128,96},{160,128},{192,160},{224,1... | collective-permute-start | bytes 1228808 | tf_op jit(solution)/shard_map/ppermute | solution.py:262
  87.2 40.4 %collective-permute-start.19 = (bf16[320,640]{1,0:T(8,128)(2,1)S(1)}, bf16[320,640]{1,0:T(8,128)(2,1)}, u32[]{:S(2)}, u32[]{:S(2)}) collective-permute-start(bf16[320,640]{1,0:T(8,128)(2,1)S(1)} %collective-permute-done.17.r3), channel_id=1, source_target_pairs={{0,32},{32,64},{64,96},{96,128},{128,160},{160,192},{192,224},{224... | collective-permute-start | bytes 1228808 | tf_op jit(solution)/shard_map/ppermute | solution.py:263
  90.2 21.7 %all-to-all-start.2 = ((bf16[16,64,128]{2,1,0:T(8,128)(2,1)}), bf16[16,64,128]{2,1,0:T(8,128)(2,1)S(1)}, u32[]{:S(2)}, u32[]{:S(2)}) async-start(bf16[16,64,128]{2,1,0:T(8,128)(2,1)} %copy-done.3), calls=%async_computation.2 | async-start | bytes 524288 | tf_op jit(solution)/shard_map/all_to_all | solution.py:312
  103.0 16.8 %collective-permute-start.7 = (bf16[64,1280]{1,0:T(8,128)(2,1)}, bf16[64,1280]{1,0:T(8,128)(2,1)}, u32[]{:S(2)}, u32[]{:S(2)}) collective-permute-start(bf16[64,1280]{1,0:T(8,128)(2,1)} %copy-done.15), channel_id=1, source_target_pairs={{0,64},{32,96},{64,128},{96,160},{128,192},{160,224},{192,0},{224,... | collective-permute-start | bytes 491528 | tf_op jit(solution)/shard_map/ppermute | solution.py:306
  103.4 16.4 %collective-permute-start.8 = (bf16[64,1280]{1,0:T(8,128)(2,1)}, bf16[64,1280]{1,0:T(8,128)(2,1)}, u32[]{:S(2)}, u32[]{:S(2)}) collective-permute-start(bf16[64,1280]{1,0:T(8,128)(2,1)} %copy-done.14), channel_id=1, source_target_pairs={{0,192},{32,224},{64,0},{96,32},{128,64},{160,96},{192,128},{224,1... | collective-permute-start | bytes 491528 | tf_op jit(solution)/shard_map/ppermute | solution.py:306
  106.7 15.3 %collective-permute-start.9 = (bf16[64,1280]{1,0:T(8,128)(2,1)}, bf16[64,1280]{1,0:T(8,128)(2,1)}, u32[]{:S(2)}, u32[]{:S(2)}) collective-permute-start(bf16[64,1280]{1,0:T(8,128)(2,1)} %copy-done.13), channel_id=1, source_target_pairs={{0,32},{32,64},{64,96},{96,128},{128,160},{160,192},{192,224},{224... | collective-permute-start | bytes 491528 | tf_op jit(solution)/shard_map/ppermute | solution.py:306
  130.0 4.0 %collective-permute-start.20 = (bf16[8,64,384]{2,1,0:T(8,128)(2,1)S(1)}, bf16[8,64,384]{2,1,0:T(8,128)(2,1)S(1)}, u32[]{:S(2)}, u32[]{:S(2)}) collective-permute-start(bf16[8,64,384]{2,1,0:T(8,128)(2,1)S(1)} %get-tuple-element.32), channel_id=1, source_target_pairs={{0,1},{1,0},{2,3},{3,2},{4,5},{5,4},{6,7},{7,6},{8,9},{9,8},{10,11... | collective-permute-start | bytes 1179656 | tf_op jit(solution)/shard_map/ppermute | solution.py:368
  135.1 16.6 %all-to-all-start.3 = ((bf16[8,64,384]{2,1,0:T(8,128)(2,1)}), bf16[8,64,384]{2,1,0:T(8,128)(2,1)S(1)}, u32[]{:S(2)}, u32[]{:S(2)}) async-start(bf16[8,64,384]{2,1,0:T(8,128)(2,1)} %shard_map.133), calls=%async_computation.3 | async-start | bytes 786432 | tf_op jit(solution)/shard_map/all_to_all | solution.py:370
  151.9 5.4 %collective-permute-start.21 = (bf16[64,320]{1,0:T(8,128)(2,1)S(1)}, bf16[64,320]{1,0:T(8,128)(2,1)S(1)}, u32[]{:S(2)}, u32[]{:S(2)}) collective-permute-start(bf16[64,320]{1,0:T(8,128)(2,1)S(1)} %shard_map.134), channel_id=1, source_target_pairs={{0,0},{1,16},{16,1},{17,17},{2,2},{3,18},{18,3},{19,19},{4,4},{5,2... | collective-permute-start | bytes 122888 | tf_op jit(solution)/shard_map/ppermute | solution.py:376
  (22 other events, 401.1 us)

commit v2 on v1

--- a/solution.py
+++ b/solution.py
@@ -16,6 +16,8 @@
 TP = ("x", "yh", "core")
 ALL = GROUP + TP
 VMEM_LIMIT = 14 * 1024 * 1024
+PROJECT_LIMIT = 58 * 1024 * 1024
+STATE_LIMIT = 52 * 1024 * 1024
 
 FAR_FIRST = (4, 3, 5, 2, 6, 1, 7)
 
@@ -28,7 +30,7 @@
     return jnp.dot(a, b, preferred_element_type=F32)
 
 
-def call(body, out_shape, args, in_smem=0, flops=1 << 20, grid=None, in_specs=None, out_specs=None, scratch=()):
+def call(body, out_shape, args, in_smem=0, flops=1 << 20, grid=None, in_specs=None, out_specs=None, scratch=(), limit=VMEM_LIMIT):
     if in_specs is None:
         in_specs = [pl.BlockSpec(memory_space=pltpu.SMEM)] * in_smem + [
             pl.BlockSpec(memory_space=pltpu.VMEM)
@@ -41,7 +43,7 @@
         in_specs=in_specs,
         out_specs=out_specs,
         scratch_shapes=scratch,
-        compiler_params=pltpu.CompilerParams(vmem_limit_bytes=VMEM_LIMIT),
+        compiler_params=pltpu.CompilerParams(vmem_limit_bytes=limit),
         cost_estimate=pl.CostEstimate(flops=flops, bytes_accessed=1 << 20, transcendentals=0),
         **kwargs,
     )(*args)
@@ -69,8 +71,15 @@
         run(e_oth, e_own)
 
 
-def project_kernel(place, e_own, e_oth, x_own, x_oth, z_own, z_oth, *outs):
+def project_kernel(place, e_own, e_oth, *refs):
+    outs, held, sems = refs[4:12], refs[12:16], refs[16]
+    x_own, x_oth, z_own, z_oth = held
     inner = x_own.shape[1]
+    copies = [
+        pltpu.make_async_copy(refs[k], held[k], sems.at[k]) for k in range(4)
+    ]
+    for copy in copies:
+        copy.start()
     rows = outs[0].shape[0]
     groups = len(outs)
 
@@ -84,9 +93,13 @@
     def run(ea, eb):
         a = turned(ea)
         b = turned(eb)
+        copies[0].wait()
+        copies[1].wait()
         px = (nn(a, x_own[...]) + nn(b, x_oth[...])).astype(BF)
         for k in range(groups):
             outs[k][:, :inner] = px[k * rows : (k + 1) * rows]
+        copies[2].wait()
+        copies[3].wait()
         pz = (nn(a, z_own[...]) + nn(b, z_oth[...])).astype(BF)
         for k in range(groups):
             outs[k][:, inner:] = pz[k * rows : (k + 1) * rows]
@@ -112,32 +125,39 @@
     small[...] = total
 
 
-def state_kernel(bc, s, out, dots, cmat):
+def state_kernel(bc, s, out, dots, cmat, held, sems):
     rows = cmat.shape[0]
-
-    @pl.when(pl.program_id(0) == 0)
-    def _():
-        pieces = [bc[t] for t in range(bc.shape[0])]
-        pieces = [p[:, :32].astype(F32) + p[:, 64:96].astype(F32) for p in pieces]
-        b = jnp.concatenate(pieces[:8], 1)
-        c = jnp.concatenate(pieces[8:], 1)
-        b1, b2, c1, c2 = b[:rows], b[rows:], c[:rows], c[rows:]
-        lane = lax.broadcasted_iota(jnp.int32, dots.shape, 1)
-        b11 = jnp.sum(b1 * c1, axis=1, keepdims=True)
-        b12 = jnp.sum(b1 * c2, axis=1, keepdims=True)
-        b22 = jnp.sum(b2 * c2, axis=1, keepdims=True)
-        dots[...] = jnp.where(lane == 0, b11, jnp.where(lane == 1, b12, b22))
-        cmat[...] = jnp.zeros_like(cmat)
-        for k, v in enumerate((c1, c2)):
-            v = v * SCALE
-            hi = v.astype(BF).astype(F32)
-            cmat[:, 2 * k, :] = hi
-            cmat[:, 2 * k + 1, :] = v - hi
-
-    for r in range(s.shape[0]):
-        m = s[r].reshape(s.shape[1] * s.shape[2], s.shape[3])
-        g = nt(cmat[pl.program_id(0) * s.shape[0] + r].astype(BF), m)
-        out[r] = g
+    chunks = sems.shape[0]
+    step = rows // chunks
+    copies = [
+        pltpu.make_async_copy(
+            s.at[pl.ds(k * step, step)], held.at[pl.ds(k * step, step)], sems.at[k]
+        )
+        for k in range(chunks)
+    ]
+    for copy in copies:
+        copy.start()
+    pieces = [bc[t] for t in range(bc.shape[0])]
+    pieces = [p[:, :32].astype(F32) + p[:, 64:96].astype(F32) for p in pieces]
+    b = jnp.concatenate(pieces[:8], 1)
+    c = jnp.concatenate(pieces[8:], 1)
+    b1, b2, c1, c2 = b[:rows], b[rows:], c[:rows], c[rows:]
+    lane = lax.broadcasted_iota(jnp.int32, dots.shape, 1)
+    b11 = jnp.sum(b1 * c1, axis=1, keepdims=True)
+    b12 = jnp.sum(b1 * c2, axis=1, keepdims=True)
+    b22 = jnp.sum(b2 * c2, axis=1, keepdims=True)
+    dots[...] = jnp.where(lane == 0, b11, jnp.where(lane == 1, b12, b22))
+    cmat[...] = jnp.zeros_like(cmat)
+    for k, v in enumerate((c1, c2)):
+        v = v * SCALE
+        hi = v.astype(BF).astype(F32)
+        cmat[:, 2 * k, :] = hi
+        cmat[:, 2 * k + 1, :] = v - hi
+    for k in range(chunks):
+        copies[k].wait()
+        for r in range(k * step, (k + 1) * step):
+            m = held[r].reshape(s.shape[1] * s.shape[2], s.shape[3])
+            out[r] = nt(cmat[r].astype(BF), m)
 
 
 def decode_kernel(*refs):
@@ -184,12 +204,12 @@
 
 
 def output_kernel(place, mine, other, gain, own, r1, l1, r2, l2, r3, l3, r4, keep, send):
-    swapped = place[0]
+    same = place[0]
     z = place[1]
     groups, rows, _ = keep.shape
     m = mine[...]
     o = other[...]
-    v = jnp.concatenate([jnp.where(swapped == 0, m, o), jnp.where(swapped == 0, o, m)], 0)
+    v = jnp.concatenate([jnp.where(same == 1, m, o), jnp.where(same == 1, o, m)], 0)
     raw = v.astype(F32) / gain[...]
     ss = jnp.sum(raw * raw, axis=1, keepdims=True)
     hi = ss.astype(BF).astype(F32)
@@ -277,11 +297,11 @@
         jnp.broadcast_to(moved[None], (8,) + moved.shape), ("x", "yh"), 0, 0
     ).reshape(8 * 2 * rows, wide)
     e_oth = lax.ppermute(e_own, "core", pair)
-    flag = (y == core).astype(jnp.int32).reshape(1)
+    place = jnp.stack([(y == core).astype(jnp.int32), lax.axis_index("z")])
     part_small = call(
         project_small_kernel,
         jax.ShapeDtypeStruct((8, 2 * rows, 128), BF),
-        (flag, e_own, e_oth, small_own, small_oth),
+        (place, e_own, e_oth, small_own, small_oth),
         in_smem=1,
         flops=2 * 16 * rows * 2 * wide * 128,
     )
@@ -290,7 +310,7 @@
         project_kernel,
         tuple(jax.ShapeDtypeStruct((2 * rows, 2 * inner), BF) for _ in range(8)),
         (
-            jnp.stack([(y == core).astype(jnp.int32), lax.axis_index("z")]),
+            place,
             e_own,
             e_oth,
             x_weight,
@@ -298,7 +318,12 @@
             z_weight,
             z_oth,
         ),
-        in_smem=1,
+        in_specs=[pl.BlockSpec(memory_space=pltpu.SMEM)]
+        + [pl.BlockSpec(memory_space=pltpu.VMEM)] * 2
+        + [pl.BlockSpec(memory_space=pltpu.HBM)] * 4,
+        out_specs=tuple(pl.BlockSpec(memory_space=pltpu.VMEM) for _ in range(8)),
+        scratch=[pltpu.VMEM((wide, inner), BF)] * 4 + [pltpu.SemaphoreType.DMA((4,))],
+        limit=PROJECT_LIMIT,
         flops=2 * 16 * rows * 2 * wide * 2 * inner,
     )
     parts = [blocks[0]]
@@ -310,21 +335,21 @@
         (part_small,),
     )
     bc_all = lax.all_to_all(bc, TP, 0, 0)
-    step = 4
     g, dots = call(
         state_kernel,
         (jax.ShapeDtypeStruct((rows, 8, inner), F32), jax.ShapeDtypeStruct((rows, 128), F32)),
         (bc_all, ssm_state),
-        grid=(rows // step,),
         in_specs=[
-            pl.BlockSpec(bc_all.shape, lambda i: (0, 0, 0)),
-            pl.BlockSpec((step,) + ssm_state.shape[1:], lambda i: (i, 0, 0, 0)),
+            pl.BlockSpec(memory_space=pltpu.VMEM),
+            pl.BlockSpec(memory_space=pl.ANY),
         ],
-        out_specs=(
-            pl.BlockSpec((step, 8, inner), lambda i: (i, 0, 0)),
-            pl.BlockSpec((rows, 128), lambda i: (0, 0)),
-        ),
-        scratch=[pltpu.VMEM((rows, 8, 256), F32)],
+        out_specs=(pl.BlockSpec(memory_space=pltpu.VMEM), pl.BlockSpec(memory_space=pltpu.VMEM)),
+        scratch=[
+            pltpu.VMEM((rows, 8, 256), F32),
+            pltpu.VMEM(ssm_state.shape, BF),
+            pltpu.SemaphoreType.DMA((8,)),
+        ],
+        limit=STATE_LIMIT,
         flops=2 * 8 * rows * inner * 256,
     )
     gg = call(
@@ -349,7 +374,7 @@
             jax.ShapeDtypeStruct((8, 2 * rows, wide + 64), BF),
         ),
         (
-            jnp.stack([(y != core).astype(jnp.int32), lax.axis_index("z")]),
+            place,
             gg,
             gg_oth,
             gain,

time: 160 us -> 156 us (0.975)
  local copies, waits for them, and re-layouts: 14.8 us -> 5.9 us
  Pallas kernels: 15.5 us -> 18.4 us
  waiting for transfers between devices: 40.6 us -> 42.8 us
    unnamed x40 -> x28, local copies, waits for them, and re-layouts: 12 us -> 3.02 us
    pallas_call x8, Pallas kernels: 15.5 us -> 18.4 us  [call(): pl.pallas_call(body, out_shape=out_shape, in_specs=in_specs, out_specs=ou...]
    ppermute x7, waiting for transfers between devices: 2.15 us -> 4.86 us  [per_device(): lax.ppermute(blocks[k], 'z', [(i, (i + k) % 8) for i in range(8)])]
  transfers between devices with their start and end apart: 26 -> 26, of which waited for: 9 -> 10; matrix products, arithmetic and copies ran while one was open for 3% -> 3% of each run, Pallas kernels for 7% -> 10%
where the time goes in v2:
time: 156 us
  starting transfers between devices  84.3 us (54%)
  waiting for transfers between devices  42.8 us (27%)
  Pallas kernels  18.4 us (12%)
  local copies, waits for them, and re-layouts  5.9 us (4%)
  other arithmetic  2.98 us (2%)
    all_to_all x1, starting transfers between devices, per_device(): lax.all_to_all(jnp.broadcast_to(moved[None], (8,) + moved.shape), ('x', '...  19 us
    pallas_call x8, Pallas kernels, call(): pl.pallas_call(body, out_shape=out_shape, in_specs=in_specs, out_specs=ou...  18.4 us
    ppermute x7, starting transfers between devices, per_device(): lax.ppermute(blocks[k], 'z', [(i, (i + k) % 8) for i in range(8)])  14.7 us
    all_to_all x1, starting transfers between devices, per_device(): bc_all = lax.all_to_all(bc, TP, 0, 0)  12.8 us
    ppermute x4, waiting for transfers between devices, per_device(): ring_r.append(lax.ppermute(ring_r[-1], 'z', right))  8.57 us
    all_to_all x1, waiting for transfers between devices, per_device(): partial_out = lax.all_to_all(paired, ('x', 'yh'), 0, 0)  8.5 us
    all_to_all x1, starting transfers between devices, per_device(): partial_out = lax.all_to_all(paired, ('x', 'yh'), 0, 0)  7.51 us
    all_to_all x1, starting transfers between devices, per_device(): part_small = lax.all_to_all(part_small, 'z', 0, 0)  5.95 us
  transfers between devices with their start and end apart: 26, of which 10 were waited for; matrix products, arithmetic and copies ran while one was open for 3% of the time, Pallas kernels for 10%

profile of v2, /device:TPU:1, one launch (start us, length us, event | category | flops | bytes accessed | tf_op | source)
XLA Modules:
  0.0 155.5 jit_solution(1540434833641421891)
XLA Ops:
  0.0 2.5 %collective-permute-start.13 = (bf16[320,640]{1,0:T(8,128)(2,1)}, bf16[320,640]{1,0:T(8,128)(2,1)S(1)}, u32[]{:S(2)}, u32[]{:S(2)}) collective-permute-start(bf16[320,640]{1,0:T(8,128)(2,1)} %bitcast.16), channel_id=1, source_target_pairs={{0,32},{32,64},{64,96},{96,128},{128,160},{160,192},{192,224},{224... | collective-permute-start | bytes 1228808 | tf_op jit(solution)/shard_map/ppermute | solution.py:281
  2.5 4.0 %collective-permute-start.14 = (bf16[320,640]{1,0:T(8,128)(2,1)}, bf16[320,640]{1,0:T(8,128)(2,1)S(1)}, u32[]{:S(2)}, u32[]{:S(2)}) collective-permute-start(bf16[320,640]{1,0:T(8,128)(2,1)} %bitcast.17), channel_id=1, source_target_pairs={{0,224},{32,0},{64,32},{96,64},{128,96},{160,128},{192,160},{224,1... | collective-permute-start | bytes 1228808 | tf_op jit(solution)/shard_map/ppermute | solution.py:282
  7.2 8.6 %collective-permute-done.13.r1 = bf16[320,640]{1,0:T(8,128)(2,1)S(1)} collective-permute-done((bf16[320,640]{1,0:T(8,128)(2,1)}, bf16[320,640]{1,0:T(8,128)(2,1)S(1)}, u32[]{:S(2)}, u32[]{:S(2)}) %collective-permute-start.13) | collective-permute-done | bytes 409632 | tf_op jit(solution)/shard_map/ppermute | solution.py:281
  17.6 19.0 %all-to-all-start = ((bf16[8,64,320]{2,1,0:T(8,128)(2,1)}), bf16[8,64,320]{2,1,0:T(8,128)(2,1)S(1)}, u32[]{:S(2)}, u32[]{:S(2)}) async-start(bf16[8,64,320]{2,1,0:T(8,128)(2,1)} %broadcast_in_dim.24), calls=%async_computation | async-start | bytes 786432 | tf_op jit(solution)/shard_map/all_to_all | solution.py:296
  38.8 5.7 %all-to-all-done = bf16[8,64,320]{2,1,0:T(8,128)(2,1)S(1)} async-done(((bf16[8,64,320]{2,1,0:T(8,128)(2,1)}), bf16[8,64,320]{2,1,0:T(8,128)(2,1)S(1)}, u32[]{:S(2)}, u32[]{:S(2)}) %all-to-all-start) | async-done | bytes 327712 | tf_op jit(solution)/shard_map/all_to_all | solution.py:296
  44.5 4.8 %collective-permute-start.1 = (bf16[512,320]{1,0:T(8,128)(2,1)S(1)}, bf16[512,320]{1,0:T(8,128)(2,1)}, u32[]{:S(2)}, u32[]{:S(2)}) collective-permute-start(bf16[512,320]{1,0:T(8,128)(2,1)S(1)} %bitcast.13), channel_id=1, source_target_pairs={{0,1},{1,0},{2,3},{3,2},{4,5},{5,4},{6,7},{7,6},{8,9},{9,8},{10,11... | collective-permute-start | bytes 983048 | tf_op jit(solution)/shard_map/ppermute | solution.py:299
  53.5 4.7 %collective-permute-done.3.refs_3_ = bf16[320,640]{1,0:T(8,128)(2,1)} collective-permute-done((bf16[320,640]{1,0:T(8,128)(2,1)}, bf16[320,640]{1,0:T(8,128)(2,1)}, u32[]{:S(2)}, u32[]{:S(2)}) %collective-permute-start.3) | collective-permute-done | bytes 409632 | tf_op jit(solution)/shard_map/ppermute | solution.py:285
  58.2 5.2 %shard_map.127 = (bf16[64,1280]{1,0:T(8,128)(2,1)}, bf16[64,1280]{1,0:T(8,128)(2,1)}, bf16[64,1280]{1,0:T(8,128)(2,1)}, bf16[64,1280]{1,0:T(8,128)(2,1)}, bf16[6...) custom-call(s32[2]{0:T(128)} %pad_add_fusion.place.flag, ...), custom_call_target="tpu_custom_call" | custom-call | flops 838860800 | bytes 1048576 | tf_op jit(solution)/shard_map/pallas_call | solution.py:40
  66.0 2.1 %shard_map.128 = bf16[8,64,128]{2,1,0:T(8,128)(2,1)} custom-call(s32[2]{0:T(128)S(1)} %copy-done.8, bf16[512,320]{1,0:T(8,128)(2,1)S(1)} %bitcast.15, bf16[512,320]{1,0:T(8,128)(2,1)} %collective-permute-done.1.e_oth, bf16[64,320]{1,0:T(8,128)(2,1)S(1)} %maximum_maximum_fusion.s_own, bf16[64,320]{1,0:T(8,128)(2,1)S(1)} %collective-permute-done.11.s_oth), custom_call_target="tpu_custom_call" | custom-call | flops 83886080 | bytes 1048576 | tf_op jit(solution)/shard_map/pallas_call | solution.py:40
  68.1 5.9 %all-to-all-start.1 = ((bf16[8,64,128]{2,1,0:T(8,128)(2,1)}), bf16[8,64,128]{2,1,0:T(8,128)(2,1)S(1)}, u32[]{:S(2)}, u32[]{:S(2)}) async-start(bf16[8,64,128]{2,1,0:T(8,128)(2,1)} %shard_map.128), calls=%async_computation.1 | async-start | bytes 262144 | tf_op jit(solution)/shard_map/all_to_all | solution.py:308
  74.1 5.4 %collective-permute-start.4 = (bf16[64,1280]{1,0:T(8,128)(2,1)}, bf16[64,1280]{1,0:T(8,128)(2,1)}, u32[]{:S(2)}, u32[]{:S(2)}) collective-permute-start(bf16[64,1280]{1,0:T(8,128)(2,1)} %get-tuple-element.20), channel_id=1, source_target_pairs={{0,128},{32,160},{64,192},{96,224},{128,0},{160,32},{192,64},{224,... | collective-permute-start | bytes 491528 | tf_op jit(solution)/shard_map/ppermute | solution.py:331
  79.7 4.2 %collective-permute-start.6 = (bf16[64,1280]{1,0:T(8,128)(2,1)}, bf16[64,1280]{1,0:T(8,128)(2,1)}, u32[]{:S(2)}, u32[]{:S(2)}) collective-permute-start(bf16[64,1280]{1,0:T(8,128)(2,1)} %get-tuple-element.22), channel_id=1, source_target_pairs={{0,160},{32,192},{64,224},{96,0},{128,32},{160,64},{192,96},{224,1... | collective-permute-start | bytes 491528 | tf_op jit(solution)/shard_map/ppermute | solution.py:331
  86.9 12.8 %all-to-all-start.2 = ((bf16[16,64,128]{2,1,0:T(8,128)(2,1)}), bf16[16,64,128]{2,1,0:T(8,128)(2,1)S(1)}, u32[]{:S(2)}, u32[]{:S(2)}) async-start(bf16[16,64,128]{2,1,0:T(8,128)(2,1)} %copy-done.4), calls=%async_computation.2 | async-start | bytes 524288 | tf_op jit(solution)/shard_map/all_to_all | solution.py:337
  100.1 3.3 %collective-permute-start.8 = (bf16[64,1280]{1,0:T(8,128)(2,1)}, bf16[64,1280]{1,0:T(8,128)(2,1)}, u32[]{:S(2)}, u32[]{:S(2)}) collective-permute-start(bf16[64,1280]{1,0:T(8,128)(2,1)} %get-tuple-element.24), channel_id=1, source_target_pairs={{0,192},{32,224},{64,0},{96,32},{128,64},{160,96},{192,128},{224,1... | collective-permute-start | bytes 491528 | tf_op jit(solution)/shard_map/ppermute | solution.py:331
  104.4 4.2 %all-to-all-done.2.bc = bf16[16,64,128]{2,1,0:T(8,128)(2,1)S(1)} async-done(((bf16[16,64,128]{2,1,0:T(8,128)(2,1)}), bf16[16,64,128]{2,1,0:T(8,128)(2,1)S(1)}, u32[]{:S(2)}, u32[]{:S(2)}) %all-to-all-start.2) | async-done | bytes 262176 | tf_op jit(solution)/shard_map/all_to_all | solution.py:337
  108.6 5.2 %shard_map.130 = (f32[32,8,640]{2,1,0:T(8,128)S(1)}, f32[32,128]{1,0:T(8,128)S(1)}) custom-call(bf16[16,64,128]{2,1,0:T(8,128)(2,1)S(1)} %all-to-all-done.2.bc, bf16[32,10,64,256]{3,2,1,0:T(8,128)(2,1)} %s.1), custom_call_target="tpu_custom_call" | custom-call | flops 83886080 | bytes 1048576 | tf_op jit(solution)/shard_map/pallas_call | solution.py:40
  115.7 2.9 %collective-permute-done.9.refs_6_ = bf16[64,1280]{1,0:T(8,128)(2,1)} collective-permute-done((bf16[64,1280]{1,0:T(8,128)(2,1)}, bf16[64,1280]{1,0:T(8,128)(2,1)}, u32[]{:S(2)}, u32[]{:S(2)}) %collective-permute-start.9) | collective-permute-done | bytes 163872 | tf_op jit(solution)/shard_map/ppermute | solution.py:331
  118.7 2.1 %shard_map.131.mine = bf16[64,640]{1,0:T(8,128)(2,1)S(1)} custom-call(bf16[64,1280]{1,0:T(8,128)(2,1)S(1)} %copy-done.5, bf16[64,1280]{1,0:T(8,128)(2,1)} %collective-permute-done.4.refs_1_, bf16[64,1280]{1,0:T(8,128)(2,1)} %collective-permute-done.5.refs_2_, bf16[64,1280]{1,0:T(8,128)(2,1)} %collective-permute-done.6.refs_3_, ...), custom_call_target="tpu_custom_call" | custom-call | flops 1048576 | bytes 1048576 | tf_op jit(solution)/shard_map/pallas_call | solution.py:40
  124.3 2.4 %shard_map.132 = (f32[8,64,384]{2,1,0:T(8,128)S(1)}, bf16[8,64,384]{2,1,0:T(8,128)(2,1)S(1)}) custom-call(s32[2]{0:T(128)S(1)} %copy-done.9, bf16[64,640]{1,0:T(8,128)(2,1)S(1)} %shard_map.131.mine, bf16[64,640]{1,0:T(8,128)(2,1)S(1)} %collective-permute-done.12.other, f32[1,640]{1,0:T(1,128)S(1)} %reshape.28.refs_14_.gain, bf16[320,640]{1,0:T(8,128)(2,1)S(1)} %bitcast.18, ...), custom_call_target="tpu_custom_call" | custom-call | flops 419430400 | bytes 1048576 | tf_op jit(solution)/shard_map/pallas_call | solution.py:40
  126.7 2.6 %collective-permute-start.20 = (bf16[8,64,384]{2,1,0:T(8,128)(2,1)S(1)}, bf16[8,64,384]{2,1,0:T(8,128)(2,1)S(1)}, u32[]{:S(2)}, u32[]{:S(2)}) collective-permute-start(bf16[8,64,384]{2,1,0:T(8,128)(2,1)S(1)} %get-tuple-element.32), channel_id=1, source_target_pairs={{0,1},{1,0},{2,3},{3,2},{4,5},{5,4},{6,7},{7,6},{8,9},{9,8},{10,11... | collective-permute-start | bytes 1179656 | tf_op jit(solution)/shard_map/ppermute | solution.py:393
  131.8 7.5 %all-to-all-start.3 = ((bf16[8,64,384]{2,1,0:T(8,128)(2,1)}), bf16[8,64,384]{2,1,0:T(8,128)(2,1)S(1)}, u32[]{:S(2)}, u32[]{:S(2)}) async-start(bf16[8,64,384]{2,1,0:T(8,128)(2,1)} %shard_map.133), calls=%async_computation.3 | async-start | bytes 786432 | tf_op jit(solution)/shard_map/all_to_all | solution.py:395
  139.9 8.5 %all-to-all-done.3.part = bf16[8,64,384]{2,1,0:T(8,128)(2,1)S(1)} async-done(((bf16[8,64,384]{2,1,0:T(8,128)(2,1)}), bf16[8,64,384]{2,1,0:T(8,128)(2,1)S(1)}, u32[]{:S(2)}, u32[]{:S(2)}) %all-to-all-start.3) | async-done | bytes 393248 | tf_op jit(solution)/shard_map/all_to_all | solution.py:395
  148.6 2.4 %collective-permute-start.21 = (bf16[64,320]{1,0:T(8,128)(2,1)S(1)}, bf16[64,320]{1,0:T(8,128)(2,1)S(1)}, u32[]{:S(2)}, u32[]{:S(2)}) collective-permute-start(bf16[64,320]{1,0:T(8,128)(2,1)S(1)} %shard_map.134), channel_id=1, source_target_pairs={{0,0},{1,16},{16,1},{17,17},{2,2},{3,18},{18,3},{19,19},{4,4},{5,2... | collective-permute-start | bytes 122888 | tf_op jit(solution)/shard_map/ppermute | solution.py:401
  151.0 3.0 %collective-permute-done.21 = bf16[64,320]{1,0:T(8,128)(2,1)S(1)} collective-permute-done((bf16[64,320]{1,0:T(8,128)(2,1)S(1)}, bf16[64,320]{1,0:T(8,128)(2,1)S(1)}, u32[]{:S(2)}, u32[]{:S(2)}) %collective-permute-start.21) | collective-permute-done | bytes 40992 | tf_op jit(solution)/shard_map/ppermute | solution.py:401
  (75 shorter events, 25.6 us)
Async XLA Ops:
  0.0 15.8 %collective-permute-start.13 = (bf16[320,640]{1,0:T(8,128)(2,1)}, bf16[320,640]{1,0:T(8,128)(2,1)S(1)}, u32[]{:S(2)}, u32[]{:S(2)}) collective-permute-start(bf16[320,640]{1,0:T(8,128)(2,1)} %bitcast.16), channel_id=1, source_target_pairs={{0,32},{32,64},{64,96},{96,128},{128,160},{160,192},{192,224},{224... | collective-permute-start | bytes 1228808 | tf_op jit(solution)/shard_map/ppermute | solution.py:281
  2.5 46.8 %collective-permute-start.14 = (bf16[320,640]{1,0:T(8,128)(2,1)}, bf16[320,640]{1,0:T(8,128)(2,1)S(1)}, u32[]{:S(2)}, u32[]{:S(2)}) collective-permute-start(bf16[320,640]{1,0:T(8,128)(2,1)} %bitcast.17), channel_id=1, source_target_pairs={{0,224},{32,0},{64,32},{96,64},{128,96},{160,128},{192,160},{224,1... | collective-permute-start | bytes 1228808 | tf_op jit(solution)/shard_map/ppermute | solution.py:282
  15.8 33.5 %collective-permute-start.15 = (bf16[320,640]{1,0:T(8,128)(2,1)S(1)}, bf16[320,640]{1,0:T(8,128)(2,1)S(1)}, u32[]{:S(2)}, u32[]{:S(2)}) collective-permute-start(bf16[320,640]{1,0:T(8,128)(2,1)S(1)} %collective-permute-done.13.r1), channel_id=1, source_target_pairs={{0,32},{32,64},{64,96},{96,128},{128,160},{160,192},{192,224},{224... | collective-permute-start | bytes 1228808 | tf_op jit(solution)/shard_map/ppermute | solution.py:281
  17.6 26.8 %all-to-all-start = ((bf16[8,64,320]{2,1,0:T(8,128)(2,1)}), bf16[8,64,320]{2,1,0:T(8,128)(2,1)S(1)}, u32[]{:S(2)}, u32[]{:S(2)}) async-start(bf16[8,64,320]{2,1,0:T(8,128)(2,1)} %broadcast_in_dim.24), calls=%async_computation | async-start | bytes 786432 | tf_op jit(solution)/shard_map/all_to_all | solution.py:296
  36.6 15.5 %collective-permute-start.2 = (bf16[320,640]{1,0:T(8,128)(2,1)}, bf16[320,640]{1,0:T(8,128)(2,1)}, u32[]{:S(2)}, u32[]{:S(2)}) collective-permute-start(bf16[320,640]{1,0:T(8,128)(2,1)} %refs_0_.1), channel_id=1, source_target_pairs={{0,16},{16,0},{1,17},{17,1},{2,18},{18,2},{3,19},{19,3},{4,20},{20... | collective-permute-start | bytes 1228808 | tf_op jit(solution)/shard_map/ppermute | solution.py:284
  37.6 20.5 %collective-permute-start.3 = (bf16[320,640]{1,0:T(8,128)(2,1)}, bf16[320,640]{1,0:T(8,128)(2,1)}, u32[]{:S(2)}, u32[]{:S(2)}) collective-permute-start(bf16[320,640]{1,0:T(8,128)(2,1)} %refs_2_.1), channel_id=1, source_target_pairs={{0,16},{16,0},{1,17},{17,1},{2,18},{18,2},{3,19},{19,3},{4,20},{20... | collective-permute-start | bytes 1228808 | tf_op jit(solution)/shard_map/ppermute | solution.py:285
  44.5 13.7 %collective-permute-start.1 = (bf16[512,320]{1,0:T(8,128)(2,1)S(1)}, bf16[512,320]{1,0:T(8,128)(2,1)}, u32[]{:S(2)}, u32[]{:S(2)}) collective-permute-start(bf16[512,320]{1,0:T(8,128)(2,1)S(1)} %bitcast.13), channel_id=1, source_target_pairs={{0,1},{1,0},{2,3},{3,2},{4,5},{5,4},{6,7},{7,6},{8,9},{9,8},{10,11... | collective-permute-start | bytes 983048 | tf_op jit(solution)/shard_map/ppermute | solution.py:299
  49.2 34.7 %collective-permute-start.16 = (bf16[320,640]{1,0:T(8,128)(2,1)S(1)}, bf16[320,640]{1,0:T(8,128)(2,1)S(1)}, u32[]{:S(2)}, u32[]{:S(2)}) collective-permute-start(bf16[320,640]{1,0:T(8,128)(2,1)S(1)} %collective-permute-done.14.l1), channel_id=1, source_target_pairs={{0,224},{32,0},{64,32},{96,64},{128,96},{160,128},{192,160},{224,1... | collective-permute-start | bytes 1228808 | tf_op jit(solution)/shard_map/ppermute | solution.py:282
  49.3 34.6 %collective-permute-start.17 = (bf16[320,640]{1,0:T(8,128)(2,1)S(1)}, bf16[320,640]{1,0:T(8,128)(2,1)S(1)}, u32[]{:S(2)}, u32[]{:S(2)}) collective-permute-start(bf16[320,640]{1,0:T(8,128)(2,1)S(1)} %collective-permute-done.15.r2), channel_id=1, source_target_pairs={{0,32},{32,64},{64,96},{96,128},{128,160},{160,192},{192,224},{224... | collective-permute-start | bytes 1228808 | tf_op jit(solution)/shard_map/ppermute | solution.py:281
  52.2 12.2 %collective-permute-start.11 = (bf16[64,320]{1,0:T(8,128)(2,1)S(1)}, bf16[64,320]{1,0:T(8,128)(2,1)S(1)}, u32[]{:S(2)}, u32[]{:S(2)}) collective-permute-start(bf16[64,320]{1,0:T(8,128)(2,1)S(1)} %maximum_maximum_fusion.s_own), channel_id=1, source_target_pairs={{0,16},{16,0},{1,17},{17,1},{2,18},{18,2},{3,19},{19,3},{4,20},{20... | collective-permute-start | bytes 122888 | tf_op jit(solution)/shard_map/ppermute | solution.py:289
  63.4 16.3 %collective-permute-start.10 = (bf16[64,1280]{1,0:T(8,128)(2,1)}, bf16[64,1280]{1,0:T(8,128)(2,1)}, u32[]{:S(2)}, u32[]{:S(2)}) collective-permute-start(bf16[64,1280]{1,0:T(8,128)(2,1)} %get-tuple-element.26), channel_id=1, source_target_pairs={{0,224},{32,0},{64,32},{96,64},{128,96},{160,128},{192,160},{224,1... | collective-permute-start | bytes 491528 | tf_op jit(solution)/shard_map/ppermute | solution.py:331
  68.1 17.3 %all-to-all-start.1 = ((bf16[8,64,128]{2,1,0:T(8,128)(2,1)}), bf16[8,64,128]{2,1,0:T(8,128)(2,1)S(1)}, u32[]{:S(2)}, u32[]{:S(2)}) async-start(bf16[8,64,128]{2,1,0:T(8,128)(2,1)} %shard_map.128), calls=%async_computation.1 | async-start | bytes 262144 | tf_op jit(solution)/shard_map/all_to_all | solution.py:308
  74.1 25.6 %collective-permute-start.4 = (bf16[64,1280]{1,0:T(8,128)(2,1)}, bf16[64,1280]{1,0:T(8,128)(2,1)}, u32[]{:S(2)}, u32[]{:S(2)}) collective-permute-start(bf16[64,1280]{1,0:T(8,128)(2,1)} %get-tuple-element.20), channel_id=1, source_target_pairs={{0,128},{32,160},{64,192},{96,224},{128,0},{160,32},{192,64},{224,... | collective-permute-start | bytes 491528 | tf_op jit(solution)/shard_map/ppermute | solution.py:331
  79.4 20.6 %collective-permute-start.5 = (bf16[64,1280]{1,0:T(8,128)(2,1)}, bf16[64,1280]{1,0:T(8,128)(2,1)}, u32[]{:S(2)}, u32[]{:S(2)}) collective-permute-start(bf16[64,1280]{1,0:T(8,128)(2,1)} %get-tuple-element.21), channel_id=1, source_target_pairs={{0,96},{32,128},{64,160},{96,192},{128,224},{160,0},{192,32},{224,... | collective-permute-start | bytes 491528 | tf_op jit(solution)/shard_map/ppermute | solution.py:331
  79.7 23.6 %collective-permute-start.6 = (bf16[64,1280]{1,0:T(8,128)(2,1)}, bf16[64,1280]{1,0:T(8,128)(2,1)}, u32[]{:S(2)}, u32[]{:S(2)}) collective-permute-start(bf16[64,1280]{1,0:T(8,128)(2,1)} %get-tuple-element.22), channel_id=1, source_target_pairs={{0,160},{32,192},{64,224},{96,0},{128,32},{160,64},{192,96},{224,1... | collective-permute-start | bytes 491528 | tf_op jit(solution)/shard_map/ppermute | solution.py:331
  83.9 40.4 %collective-permute-start.18 = (bf16[320,640]{1,0:T(8,128)(2,1)S(1)}, bf16[320,640]{1,0:T(8,128)(2,1)}, u32[]{:S(2)}, u32[]{:S(2)}) collective-permute-start(bf16[320,640]{1,0:T(8,128)(2,1)S(1)} %collective-permute-done.16.l2), channel_id=1, source_target_pairs={{0,224},{32,0},{64,32},{96,64},{128,96},{160,128},{192,160},{224,1... | collective-permute-start | bytes 1228808 | tf_op jit(solution)/shard_map/ppermute | solution.py:282
  83.9 40.4 %collective-permute-start.19 = (bf16[320,640]{1,0:T(8,128)(2,1)S(1)}, bf16[320,640]{1,0:T(8,128)(2,1)}, u32[]{:S(2)}, u32[]{:S(2)}) collective-permute-start(bf16[320,640]{1,0:T(8,128)(2,1)S(1)} %collective-permute-done.17.r3), channel_id=1, source_target_pairs={{0,32},{32,64},{64,96},{96,128},{128,160},{160,192},{192,224},{224... | collective-permute-start | bytes 1228808 | tf_op jit(solution)/shard_map/ppermute | solution.py:283
  86.9 21.7 %all-to-all-start.2 = ((bf16[16,64,128]{2,1,0:T(8,128)(2,1)}), bf16[16,64,128]{2,1,0:T(8,128)(2,1)S(1)}, u32[]{:S(2)}, u32[]{:S(2)}) async-start(bf16[16,64,128]{2,1,0:T(8,128)(2,1)} %copy-done.4), calls=%async_computation.2 | async-start | bytes 524288 | tf_op jit(solution)/shard_map/all_to_all | solution.py:337
  99.7 14.1 %collective-permute-start.7 = (bf16[64,1280]{1,0:T(8,128)(2,1)}, bf16[64,1280]{1,0:T(8,128)(2,1)}, u32[]{:S(2)}, u32[]{:S(2)}) collective-permute-start(bf16[64,1280]{1,0:T(8,128)(2,1)} %get-tuple-element.23), channel_id=1, source_target_pairs={{0,64},{32,96},{64,128},{96,160},{128,192},{160,224},{192,0},{224,... | collective-permute-start | bytes 491528 | tf_op jit(solution)/shard_map/ppermute | solution.py:331
  100.1 15.6 %collective-permute-start.8 = (bf16[64,1280]{1,0:T(8,128)(2,1)}, bf16[64,1280]{1,0:T(8,128)(2,1)}, u32[]{:S(2)}, u32[]{:S(2)}) collective-permute-start(bf16[64,1280]{1,0:T(8,128)(2,1)} %get-tuple-element.24), channel_id=1, source_target_pairs={{0,192},{32,224},{64,0},{96,32},{128,64},{160,96},{192,128},{224,1... | collective-permute-start | bytes 491528 | tf_op jit(solution)/shard_map/ppermute | solution.py:331
  103.4 15.3 %collective-permute-start.9 = (bf16[64,1280]{1,0:T(8,128)(2,1)}, bf16[64,1280]{1,0:T(8,128)(2,1)}, u32[]{:S(2)}, u32[]{:S(2)}) collective-permute-start(bf16[64,1280]{1,0:T(8,128)(2,1)} %get-tuple-element.25), channel_id=1, source_target_pairs={{0,32},{32,64},{64,96},{96,128},{128,160},{160,192},{192,224},{224... | collective-permute-start | bytes 491528 | tf_op jit(solution)/shard_map/ppermute | solution.py:331
  126.7 4.0 %collective-permute-start.20 = (bf16[8,64,384]{2,1,0:T(8,128)(2,1)S(1)}, bf16[8,64,384]{2,1,0:T(8,128)(2,1)S(1)}, u32[]{:S(2)}, u32[]{:S(2)}) collective-permute-start(bf16[8,64,384]{2,1,0:T(8,128)(2,1)S(1)} %get-tuple-element.32), channel_id=1, source_target_pairs={{0,1},{1,0},{2,3},{3,2},{4,5},{5,4},{6,7},{7,6},{8,9},{9,8},{10,11... | collective-permute-start | bytes 1179656 | tf_op jit(solution)/shard_map/ppermute | solution.py:393
  131.8 16.7 %all-to-all-start.3 = ((bf16[8,64,384]{2,1,0:T(8,128)(2,1)}), bf16[8,64,384]{2,1,0:T(8,128)(2,1)S(1)}, u32[]{:S(2)}, u32[]{:S(2)}) async-start(bf16[8,64,384]{2,1,0:T(8,128)(2,1)} %shard_map.133), calls=%async_computation.3 | async-start | bytes 786432 | tf_op jit(solution)/shard_map/all_to_all | solution.py:395
  148.6 5.4 %collective-permute-start.21 = (bf16[64,320]{1,0:T(8,128)(2,1)S(1)}, bf16[64,320]{1,0:T(8,128)(2,1)S(1)}, u32[]{:S(2)}, u32[]{:S(2)}) collective-permute-start(bf16[64,320]{1,0:T(8,128)(2,1)S(1)} %shard_map.134), channel_id=1, source_target_pairs={{0,0},{1,16},{16,1},{17,17},{2,2},{3,18},{18,3},{19,19},{4,4},{5,2... | collective-permute-start | bytes 122888 | tf_op jit(solution)/shard_map/ppermute | solution.py:401
  (16 other events, 422.1 us)

commit v3 on v2

--- a/solution.py
+++ b/solution.py
@@ -18,8 +18,6 @@
 VMEM_LIMIT = 14 * 1024 * 1024
 PROJECT_LIMIT = 58 * 1024 * 1024
 STATE_LIMIT = 52 * 1024 * 1024
-
-FAR_FIRST = (4, 3, 5, 2, 6, 1, 7)
 
 
 def nt(a, b):
@@ -72,37 +70,25 @@
 
 
 def project_kernel(place, e_own, e_oth, *refs):
-    outs, held, sems = refs[4:12], refs[12:16], refs[16]
+    out, held, sems = refs[4], refs[5:9], refs[9]
     x_own, x_oth, z_own, z_oth = held
     inner = x_own.shape[1]
-    copies = [
-        pltpu.make_async_copy(refs[k], held[k], sems.at[k]) for k in range(4)
-    ]
+    groups, rows = out.shape[:2]
+    copies = [pltpu.make_async_copy(refs[k], held[k], sems.at[k]) for k in range(4)]
     for copy in copies:
         copy.start()
-    rows = outs[0].shape[0]
-    groups = len(outs)
-
-    def turned(ref):
-        blocks = []
-        for k in range(groups):
-            at = lax.rem(place[1] + k, groups) * rows
-            blocks.append(ref[pl.ds(pl.multiple_of(at, rows), rows), :])
-        return jnp.concatenate(blocks, 0)
 
     def run(ea, eb):
-        a = turned(ea)
-        b = turned(eb)
+        a = ea[...]
+        b = eb[...]
         copies[0].wait()
         copies[1].wait()
         px = (nn(a, x_own[...]) + nn(b, x_oth[...])).astype(BF)
-        for k in range(groups):
-            outs[k][:, :inner] = px[k * rows : (k + 1) * rows]
+        out[:, :, :inner] = px.reshape(groups, rows, inner)
         copies[2].wait()
         copies[3].wait()
         pz = (nn(a, z_own[...]) + nn(b, z_oth[...])).astype(BF)
-        for k in range(groups):
-            outs[k][:, inner:] = pz[k * rows : (k + 1) * rows]
+        out[:, :, inner:] = pz.reshape(groups, rows, inner)
 
     @pl.when(place[0] == 1)
     def _():
@@ -119,13 +105,11 @@
         total = total + part[k].astype(F32)
     total = total[:, :64] + total[:, 64:]
     hi, lo = split2(total)
-    both = jnp.concatenate([hi, lo], 1)
-    for k in range(bc.shape[0]):
-        bc[k] = both
+    bc[...] = jnp.concatenate([hi, lo], 1)
     small[...] = total
 
 
-def state_kernel(bc, s, out, dots, cmat, held, sems):
+def state_kernel(place, bc0, bc1, bc2, bc3, s, out, dots, cmat, pieces_ref, held, sems):
     rows = cmat.shape[0]
     chunks = sems.shape[0]
     step = rows // chunks
@@ -137,7 +121,13 @@
     ]
     for copy in copies:
         copy.start()
-    pieces = [bc[t] for t in range(bc.shape[0])]
+    for shift, bc in ((0, bc0), (1, bc1), (2, bc2), (3, bc3)):
+        x = lax.rem(place[2] + shift, 4)
+        for k in range(4):
+            yh = lax.rem(place[3] + k // 2, 2)
+            core = lax.rem(place[4] + k % 2, 2)
+            pieces_ref[(x * 2 + yh) * 2 + core] = bc[k]
+    pieces = [pieces_ref[t] for t in range(16)]
     pieces = [p[:, :32].astype(F32) + p[:, 64:96].astype(F32) for p in pieces]
     b = jnp.concatenate(pieces[:8], 1)
     c = jnp.concatenate(pieces[8:], 1)
@@ -160,14 +150,13 @@
             out[r] = nt(cmat[r].astype(BF), m)
 
 
-def decode_kernel(*refs):
-    parts, (small, dots, g, bias, rate, skip, gain, out) = refs[:8], refs[8:]
+def decode_kernel(part, small, dots, g, bias, rate, skip, gain, out):
     heads = bias.shape[1]
     inner = gain.shape[1]
-    half = parts[0].shape[0] // 2
-    total = parts[0][...].astype(F32)
-    for part in parts[1:]:
-        total = total + part[...].astype(F32)
+    half = part.shape[1] // 2
+    total = part[0].astype(F32)
+    for k in range(1, part.shape[0]):
+        total = total + part[k].astype(F32)
     x_pre = total[:, :inner]
     z_pre = total[:, inner:]
     pick = (
@@ -297,7 +286,9 @@
         jnp.broadcast_to(moved[None], (8,) + moved.shape), ("x", "yh"), 0, 0
     ).reshape(8 * 2 * rows, wide)
     e_oth = lax.ppermute(e_own, "core", pair)
-    place = jnp.stack([(y == core).astype(jnp.int32), lax.axis_index("z")])
+    place = jnp.stack(
+        [(y == core).astype(jnp.int32), lax.axis_index("z"), lax.axis_index("x"), lax.axis_index("yh"), core]
+    )
     part_small = call(
         project_small_kernel,
         jax.ShapeDtypeStruct((8, 2 * rows, 128), BF),
@@ -306,46 +297,40 @@
         flops=2 * 16 * rows * 2 * wide * 128,
     )
     part_small = lax.all_to_all(part_small, "z", 0, 0)
-    blocks = call(
+    part = call(
         project_kernel,
-        tuple(jax.ShapeDtypeStruct((2 * rows, 2 * inner), BF) for _ in range(8)),
-        (
-            place,
-            e_own,
-            e_oth,
-            x_weight,
-            x_oth,
-            z_weight,
-            z_oth,
-        ),
+        jax.ShapeDtypeStruct((8, 2 * rows, 2 * inner), BF),
+        (place, e_own, e_oth, x_weight, x_oth, z_weight, z_oth),
         in_specs=[pl.BlockSpec(memory_space=pltpu.SMEM)]
         + [pl.BlockSpec(memory_space=pltpu.VMEM)] * 2
-        + [pl.BlockSpec(memory_space=pltpu.HBM)] * 4,
-        out_specs=tuple(pl.BlockSpec(memory_space=pltpu.VMEM) for _ in range(8)),
+        + [pl.BlockSpec(memory_space=pl.ANY)] * 4,
+        out_specs=pl.BlockSpec(memory_space=pltpu.VMEM),
         scratch=[pltpu.VMEM((wide, inner), BF)] * 4 + [pltpu.SemaphoreType.DMA((4,))],
         limit=PROJECT_LIMIT,
         flops=2 * 16 * rows * 2 * wide * 2 * inner,
     )
-    parts = [blocks[0]]
-    for k in FAR_FIRST:
-        parts.append(lax.ppermute(blocks[k], "z", [(i, (i + k) % 8) for i in range(8)]))
+    part = lax.all_to_all(part, "z", 0, 0)
     bc, small = call(
         small_kernel,
-        (jax.ShapeDtypeStruct((16, 2 * rows, 128), BF), jax.ShapeDtypeStruct((2 * rows, 64), F32)),
+        (jax.ShapeDtypeStruct((2 * rows, 128), BF), jax.ShapeDtypeStruct((2 * rows, 64), F32)),
         (part_small,),
     )
-    bc_all = lax.all_to_all(bc, TP, 0, 0)
+    bc2 = jnp.stack([bc, lax.ppermute(bc, "core", pair)])
+    bc4 = jnp.concatenate([bc2, lax.ppermute(bc2, "yh", pair)], 0)
+    bc_all = [bc4]
+    for k in (1, 2, 3):
+        bc_all.append(lax.ppermute(bc4, "x", [((i + k) % 4, i) for i in range(4)]))
     g, dots = call(
         state_kernel,
         (jax.ShapeDtypeStruct((rows, 8, inner), F32), jax.ShapeDtypeStruct((rows, 128), F32)),
-        (bc_all, ssm_state),
-        in_specs=[
-            pl.BlockSpec(memory_space=pltpu.VMEM),
-            pl.BlockSpec(memory_space=pl.ANY),
-        ],
+        (place, *bc_all, ssm_state),
+        in_specs=[pl.BlockSpec(memory_space=pltpu.SMEM)]
+        + [pl.BlockSpec(memory_space=pltpu.VMEM)] * 4
+        + [pl.BlockSpec(memory_space=pl.ANY)],
         out_specs=(pl.BlockSpec(memory_space=pltpu.VMEM), pl.BlockSpec(memory_space=pltpu.VMEM)),
         scratch=[
             pltpu.VMEM((rows, 8, 256), F32),
+            pltpu.VMEM((16, 2 * rows, 128), BF),
             pltpu.VMEM(ssm_state.shape, BF),
             pltpu.SemaphoreType.DMA((8,)),
         ],
@@ -356,7 +341,7 @@
         decode_kernel,
         jax.ShapeDtypeStruct((2 * rows, inner), BF),
         (
-            *parts,
+            part,
             small,
             dots,
             g,

time: 156 us -> 188 us (1.21)
  waiting for transfers between devices: 42.8 us -> 90.7 us
  starting transfers between devices: 84.3 us -> 46.1 us
  blocking collectives: 0 us -> 27.4 us
  other arithmetic: 2.98 us -> 0.81 us
    ppermute x4, waiting for transfers between devices: 8.57 us -> 48.6 us  [per_device(): ring_r.append(lax.ppermute(ring_r[-1], 'z', right))]
    all_to_all x0 -> x1, blocking collectives: none -> 27.4 us  [per_device(): lax.all_to_all(jnp.broadcast_to(moved[None], (8,) + moved.shape), ('x', '...]
    all_to_all x2 -> x1, starting transfers between devices: 31.8 us -> 5.61 us  [per_device(): part = lax.all_to_all(part, 'z', 0, 0)]
    ppermute x1, waiting for transfers between devices: 0.01 us -> 18.4 us  [per_device(): small_oth = lax.ppermute(small_own, 'yl', pair)]
    all_to_all x2 -> x1, waiting for transfers between devices: 9.93 us -> 0.01 us  [per_device(): part = lax.all_to_all(part, 'z', 0, 0)]
    ppermute x7 -> x5, starting transfers between devices: 14.7 us -> 5.24 us  [the longest x1 2.28 us: per_device(): bc2 = jnp.stack([bc, lax.ppermute(bc, 'core', pair)])]
    ppermute x1, waiting for transfers between devices: 4.7 us -> 0.01 us  [per_device(): z_oth = lax.ppermute(z_weight, 'yl', pair)]
    ppermute x1, starting transfers between devices: 2.64 us -> 6.8 us  [per_device(): got = lax.ppermute(send, 'core', pair)]
  transfers between devices with their start and end apart: 26 -> 23, of which waited for: 10 -> 13; matrix products, arithmetic and copies ran while one was open for 3% -> 0% of each run, Pallas kernels for 10% -> 7%
where the time goes in v3:
time: 188 us
  waiting for transfers between devices  90.7 us (48%)
  starting transfers between devices  46.1 us (25%)
  blocking collectives  27.4 us (15%)
  Pallas kernels  17.2 us (9%)
  local copies, waits for them, and re-layouts  4.33 us (2%)
    ppermute x4, waiting for transfers between devices, per_device(): ring_r.append(lax.ppermute(ring_r[-1], 'z', right))  48.6 us
    all_to_all x1, blocking collectives, per_device(): lax.all_to_all(jnp.broadcast_to(moved[None], (8,) + moved.shape), ('x', '...  27.4 us
    ppermute x1, waiting for transfers between devices, per_device(): small_oth = lax.ppermute(small_own, 'yl', pair)  18.4 us
    pallas_call x8, Pallas kernels, call(): pl.pallas_call(body, out_shape=out_shape, in_specs=in_specs, out_specs=ou...  17.2 us
    all_to_all x1, waiting for transfers between devices, per_device(): partial_out = lax.all_to_all(paired, ('x', 'yh'), 0, 0)  8.77 us
    ppermute x3, starting transfers between devices, per_device(): ring_l.append(lax.ppermute(ring_l[-1], 'z', left))  6.92 us
    ppermute x1, starting transfers between devices, per_device(): got = lax.ppermute(send, 'core', pair)  6.8 us
    all_to_all x1, starting transfers between devices, per_device(): part_small = lax.all_to_all(part_small, 'z', 0, 0)  6.1 us
  transfers between devices with their start and end apart: 23, of which 13 were waited for; matrix products, arithmetic and copies ran while one was open for 0% of the time, Pallas kernels for 7%

profile of v3, /device:TPU:1, one launch (start us, length us, event | category | flops | bytes accessed | tf_op | source)
XLA Modules:
  0.0 187.9 jit_solution(5692437768416460832)
XLA Ops:
  2.2 27.4 %all_to_all.20 = bf16[8,64,320]{2,1,0:T(8,128)(2,1)S(1)} all-to-all(bf16[8,64,320]{2,1,0:T(8,128)(2,1)S(1)} %broadcast_in_dim.24), channel_id=1, replica_groups=mesh['z'=8,'yl'=2,'x'=4,'yh'=2,'core'=2] {'x','yh'}, dimensions={0} | all-to-all | bytes 655360 | tf_op jit(solution)/shard_map/all_to_all | solution.py:285
  29.6 3.2 %collective-permute-start.1 = (bf16[512,320]{1,0:T(8,128)(2,1)S(1)}, bf16[512,320]{1,0:T(8,128)(2,1)S(1)}, u32[]{:S(2)}, u32[]{:S(2)}) collective-permute-start(bf16[512,320]{1,0:T(8,128)(2,1)S(1)} %bitcast.18), channel_id=1, source_target_pairs={{0,1},{1,0},{2,3},{3,2},{4,5},{5,4},{6,7},{7,6},{8,9},{9,8},{10,11... | collective-permute-start | bytes 983048 | tf_op jit(solution)/shard_map/ppermute | solution.py:288
  35.2 18.4 %collective-permute-done.4.s_oth = bf16[64,320]{1,0:T(8,128)(2,1)S(1)} collective-permute-done((bf16[64,320]{1,0:T(8,128)(2,1)S(1)}, bf16[64,320]{1,0:T(8,128)(2,1)S(1)}, u32[]{:S(2)}, u32[]{:S(2)}) %collective-permute-start.4) | collective-permute-done | bytes 40992 | tf_op jit(solution)/shard_map/ppermute | solution.py:278
  53.6 1.6 shard_map.128
  55.2 6.1 %all-to-all-start.2 = ((bf16[8,64,128]{2,1,0:T(8,128)(2,1)}), bf16[8,64,128]{2,1,0:T(8,128)(2,1)S(1)}, u32[]{:S(2)}, u32[]{:S(2)}) async-start(bf16[8,64,128]{2,1,0:T(8,128)(2,1)} %shard_map.128), calls=%async_computation.2 | async-start | bytes 262144 | tf_op jit(solution)/shard_map/all_to_all | solution.py:299
  62.8 5.2 %shard_map.127 = bf16[8,64,1280]{2,1,0:T(8,128)(2,1)} custom-call(s32[5]{0:T(128)} %copy-done.8, bf16[512,320]{1,0:T(8,128)(2,1)} %bitcast.20, bf16[512,320]{1,0:T(8,128)(2,1)} %copy-done.2, bf16[320,640]{1,0:T(8,128)(2,1)} %refs_0_.1, bf16[320,640]{1,0:T(8,128)(2,1)} %copy-done.15, bf16[320,640]{1,0:T(8,128)(2,1)} %refs_2_.1, bf16[320,640]{1,0:T(8,128)(2,1)} %copy-done.16), custom_call_target="tpu_custom_call" | custom-call | flops 838860800 | bytes 1048576 | tf_op jit(solution)/shard_map/pallas_call | solution.py:38
  69.3 5.6 %all-to-all-start.1 = ((bf16[8,64,1280]{2,1,0:T(8,128)(2,1)}), bf16[8,64,1280]{2,1,0:T(8,128)(2,1)S(1)}, u32[]{:S(2)}, u32[]{:S(2)}) async-start(bf16[8,64,1280]{2,1,0:T(8,128)(2,1)} %shard_map.127), calls=%async_computation.1 | async-start | bytes 2621440 | tf_op jit(solution)/shard_map/all_to_all | solution.py:312
  74.9 1.5 collective-permute-start.11
  77.7 37.2 %collective-permute-done.11.r1 = bf16[320,640]{1,0:T(8,128)(2,1)S(1)} collective-permute-done((bf16[320,640]{1,0:T(8,128)(2,1)S(1)}, bf16[320,640]{1,0:T(8,128)(2,1)S(1)}, u32[]{:S(2)}, u32[]{:S(2)}) %collective-permute-start.11) | collective-permute-done | bytes 409632 | tf_op jit(solution)/shard_map/ppermute | solution.py:270
  114.9 2.7 %collective-permute-start.14 = (bf16[320,640]{1,0:T(8,128)(2,1)S(1)}, bf16[320,640]{1,0:T(8,128)(2,1)}, u32[]{:S(2)}, u32[]{:S(2)}) collective-permute-start(bf16[320,640]{1,0:T(8,128)(2,1)S(1)} %collective-permute-done.12.l1), channel_id=1, source_target_pairs={{0,224},{32,0},{64,32},{96,64},{128,96},{160,128},{192,160},{224,1... | collective-permute-start | bytes 1228808 | tf_op jit(solution)/shard_map/ppermute | solution.py:271
  118.3 7.4 %collective-permute-done.13.r2 = bf16[320,640]{1,0:T(8,128)(2,1)S(1)} collective-permute-done((bf16[320,640]{1,0:T(8,128)(2,1)S(1)}, bf16[320,640]{1,0:T(8,128)(2,1)S(1)}, u32[]{:S(2)}, u32[]{:S(2)}) %collective-permute-start.13) | collective-permute-done | bytes 409632 | tf_op jit(solution)/shard_map/ppermute | solution.py:270
  126.7 2.3 %collective-permute-start.5 = (bf16[64,128]{1,0:T(8,128)(2,1)S(1)}, bf16[64,128]{1,0:T(8,128)(2,1)S(1)}, u32[]{:S(2)}, u32[]{:S(2)}) collective-permute-start(bf16[64,128]{1,0:T(8,128)(2,1)S(1)} %get-tuple-element.12), channel_id=1, source_target_pairs={{0,1},{1,0},{2,3},{3,2},{4,5},{5,4},{6,7},{7,6},{8,9},{9,8},{10,11... | collective-permute-start | bytes 49160 | tf_op jit(solution)/shard_map/ppermute | solution.py:318
  128.9 3.0 %collective-permute-start.16 = (bf16[320,640]{1,0:T(8,128)(2,1)}, bf16[320,640]{1,0:T(8,128)(2,1)}, u32[]{:S(2)}, u32[]{:S(2)}) collective-permute-start(bf16[320,640]{1,0:T(8,128)(2,1)} %collective-permute-done.14.l2), channel_id=1, source_target_pairs={{0,224},{32,0},{64,32},{96,64},{128,96},{160,128},{192,160},{224,1... | collective-permute-start | bytes 1228808 | tf_op jit(solution)/shard_map/ppermute | solution.py:271
  131.9 3.9 %collective-permute-done.15.r3 = bf16[320,640]{1,0:T(8,128)(2,1)} collective-permute-done((bf16[320,640]{1,0:T(8,128)(2,1)S(1)}, bf16[320,640]{1,0:T(8,128)(2,1)}, u32[]{:S(2)}, u32[]{:S(2)}) %collective-permute-start.15) | collective-permute-done | bytes 409632 | tf_op jit(solution)/shard_map/ppermute | solution.py:270
  136.7 3.5 %collective-permute-done.6 = bf16[2,64,128]{2,1,0:T(8,128)(2,1)S(1)} collective-permute-done((bf16[2,64,128]{2,1,0:T(8,128)(2,1)S(1)}, bf16[2,64,128]{2,1,0:T(8,128)(2,1)S(1)}, u32[]{:S(2)}, u32[]{:S(2)}) %collective-permute-start.6) | collective-permute-done | bytes 32800 | tf_op jit(solution)/shard_map/ppermute | solution.py:319
  143.8 1.9 %collective-permute-done.8.bc2 = bf16[4,64,128]{2,1,0:T(8,128)(2,1)S(1)} collective-permute-done((bf16[4,64,128]{2,1,0:T(8,128)(2,1)S(1)}, bf16[4,64,128]{2,1,0:T(8,128)(2,1)S(1)}, u32[]{:S(2)}, u32[]{:S(2)}) %collective-permute-start.8) | collective-permute-done | bytes 65568 | tf_op jit(solution)/shard_map/ppermute | solution.py:322
  147.0 5.6 %shard_map.130 = (f32[32,8,640]{2,1,0:T(8,128)S(1)}, f32[32,128]{1,0:T(8,128)S(1)}) custom-call(s32[5]{0:T(128)S(1)} %copy-done.9, bf16[4,64,128]{2,1,0:T(8,128)(2,1)S(1)} %pad_maximum_fusion.bc0, bf16[4,64,128]{2,1,0:T(8,128)(2,1)S(1)} %collective-permute-done.7.bc1, bf16[4,64,128]{2,1,0:T(8,128)(2,1)S(1)} %collective-permute-done.8.bc2, ...), custom_call_target="tpu_custom_call" | custom-call | flops 83886080 | bytes 1048576 | tf_op jit(solution)/shard_map/pallas_call | solution.py:38
  154.3 2.5 %collective-permute-done.10.other = bf16[64,640]{1,0:T(8,128)(2,1)S(1)} collective-permute-done((bf16[64,640]{1,0:T(8,128)(2,1)S(1)}, bf16[64,640]{1,0:T(8,128)(2,1)S(1)}, u32[]{:S(2)}, u32[]{:S(2)}) %collective-permute-start.10) | collective-permute-done | bytes 81952 | tf_op jit(solution)/shard_map/ppermute | solution.py:354
  156.9 2.6 %shard_map.132 = (f32[8,64,384]{2,1,0:T(8,128)S(1)}, bf16[8,64,384]{2,1,0:T(8,128)(2,1)S(1)}) custom-call(s32[5]{0:T(128)S(1)} %copy-done.9, bf16[64,640]{1,0:T(8,128)(2,1)S(1)} %shard_map.131.mine, bf16[64,640]{1,0:T(8,128)(2,1)S(1)} %collective-permute-done.10.other, f32[1,640]{1,0:T(1,128)S(1)} %reshape.28.gain, bf16[320,640]{1,0:T(8,128)(2,1)S(1)} %bitcast.23, ...), custom_call_target="tpu_custom_call" | custom-call | flops 419430400 | bytes 1048576 | tf_op jit(solution)/shard_map/pallas_call | solution.py:38
  159.5 6.8 %collective-permute-start.18 = (bf16[8,64,384]{2,1,0:T(8,128)(2,1)S(1)}, bf16[8,64,384]{2,1,0:T(8,128)(2,1)S(1)}, u32[]{:S(2)}, u32[]{:S(2)}) collective-permute-start(bf16[8,64,384]{2,1,0:T(8,128)(2,1)S(1)} %get-tuple-element.16), channel_id=1, source_target_pairs={{0,1},{1,0},{2,3},{3,2},{4,5},{5,4},{6,7},{7,6},{8,9},{9,8},{10,11... | collective-permute-start | bytes 1179656 | tf_op jit(solution)/shard_map/ppermute | solution.py:378
  168.7 3.5 %all-to-all-start.3 = ((bf16[8,64,384]{2,1,0:T(8,128)(2,1)}), bf16[8,64,384]{2,1,0:T(8,128)(2,1)S(1)}, u32[]{:S(2)}, u32[]{:S(2)}) async-start(bf16[8,64,384]{2,1,0:T(8,128)(2,1)} %shard_map.133), calls=%async_computation.3 | async-start | bytes 786432 | tf_op jit(solution)/shard_map/all_to_all | solution.py:380
  172.8 8.8 %all-to-all-done.3.part = bf16[8,64,384]{2,1,0:T(8,128)(2,1)S(1)} async-done(((bf16[8,64,384]{2,1,0:T(8,128)(2,1)}), bf16[8,64,384]{2,1,0:T(8,128)(2,1)S(1)}, u32[]{:S(2)}, u32[]{:S(2)}) %all-to-all-start.3) | async-done | bytes 393248 | tf_op jit(solution)/shard_map/all_to_all | solution.py:380
  181.8 3.7 %collective-permute-start.19 = (bf16[64,320]{1,0:T(8,128)(2,1)S(1)}, bf16[64,320]{1,0:T(8,128)(2,1)S(1)}, u32[]{:S(2)}, u32[]{:S(2)}) collective-permute-start(bf16[64,320]{1,0:T(8,128)(2,1)S(1)} %shard_map.134), channel_id=1, source_target_pairs={{0,0},{1,16},{16,1},{17,17},{2,2},{3,18},{18,3},{19,19},{4,4},{5,2... | collective-permute-start | bytes 122888 | tf_op jit(solution)/shard_map/ppermute | solution.py:386
  185.5 1.7 collective-permute-done.19
  (88 shorter events, 20.8 us)
Async XLA Ops:
  1.5 0.7 collective-permute-start
  29.6 24.0 %collective-permute-start.1 = (bf16[512,320]{1,0:T(8,128)(2,1)S(1)}, bf16[512,320]{1,0:T(8,128)(2,1)S(1)}, u32[]{:S(2)}, u32[]{:S(2)}) collective-permute-start(bf16[512,320]{1,0:T(8,128)(2,1)S(1)} %bitcast.18), channel_id=1, source_target_pairs={{0,1},{1,0},{2,3},{3,2},{4,5},{5,4},{6,7},{7,6},{8,9},{9,8},{10,11... | collective-permute-start | bytes 983048 | tf_op jit(solution)/shard_map/ppermute | solution.py:288
  32.9 28.5 %collective-permute-start.2 = (bf16[320,640]{1,0:T(8,128)(2,1)S(1)}, bf16[320,640]{1,0:T(8,128)(2,1)S(1)}, u32[]{:S(2)}, u32[]{:S(2)}) collective-permute-start(bf16[320,640]{1,0:T(8,128)(2,1)S(1)} %copy-done.13), channel_id=1, source_target_pairs={{0,16},{16,0},{1,17},{17,1},{2,18},{18,2},{3,19},{19,3},{4,20},{20... | collective-permute-start | bytes 1228808 | tf_op jit(solution)/shard_map/ppermute | solution.py:273
  33.4 27.9 %collective-permute-start.3 = (bf16[320,640]{1,0:T(8,128)(2,1)S(1)}, bf16[320,640]{1,0:T(8,128)(2,1)S(1)}, u32[]{:S(2)}, u32[]{:S(2)}) collective-permute-start(bf16[320,640]{1,0:T(8,128)(2,1)S(1)} %copy-done.14), channel_id=1, source_target_pairs={{0,16},{16,0},{1,17},{17,1},{2,18},{18,2},{3,19},{19,3},{4,20},{20... | collective-permute-start | bytes 1228808 | tf_op jit(solution)/shard_map/ppermute | solution.py:274
  34.5 19.1 %collective-permute-start.4 = (bf16[64,320]{1,0:T(8,128)(2,1)S(1)}, bf16[64,320]{1,0:T(8,128)(2,1)S(1)}, u32[]{:S(2)}, u32[]{:S(2)}) collective-permute-start(bf16[64,320]{1,0:T(8,128)(2,1)S(1)} %maximum_maximum_fusion.s_own), channel_id=1, source_target_pairs={{0,16},{16,0},{1,17},{17,1},{2,18},{18,2},{3,19},{19,3},{4,20},{20... | collective-permute-start | bytes 122888 | tf_op jit(solution)/shard_map/ppermute | solution.py:278
  55.2 14.0 %all-to-all-start.2 = ((bf16[8,64,128]{2,1,0:T(8,128)(2,1)}), bf16[8,64,128]{2,1,0:T(8,128)(2,1)S(1)}, u32[]{:S(2)}, u32[]{:S(2)}) async-start(bf16[8,64,128]{2,1,0:T(8,128)(2,1)} %shard_map.128), calls=%async_computation.2 | async-start | bytes 262144 | tf_op jit(solution)/shard_map/all_to_all | solution.py:299
  68.1 78.9 %copy-start.9 = (s32[5]{0:T(128)S(1)}, s32[5]{0:T(128)}, u32[]{:S(2)}) copy-start(s32[5]{0:T(128)} %copy-done.8) | copy-start | bytes 64
  69.3 83.4 %all-to-all-start.1 = ((bf16[8,64,1280]{2,1,0:T(8,128)(2,1)}), bf16[8,64,1280]{2,1,0:T(8,128)(2,1)S(1)}, u32[]{:S(2)}, u32[]{:S(2)}) async-start(bf16[8,64,1280]{2,1,0:T(8,128)(2,1)} %shard_map.127), calls=%async_computation.1 | async-start | bytes 2621440 | tf_op jit(solution)/shard_map/all_to_all | solution.py:312
  74.9 40.0 %collective-permute-start.11 = (bf16[320,640]{1,0:T(8,128)(2,1)S(1)}, bf16[320,640]{1,0:T(8,128)(2,1)S(1)}, u32[]{:S(2)}, u32[]{:S(2)}) collective-permute-start(bf16[320,640]{1,0:T(8,128)(2,1)S(1)} %bitcast.21), channel_id=1, source_target_pairs={{0,32},{32,64},{64,96},{96,128},{128,160},{160,192},{192,224},{224... | collective-permute-start | bytes 1228808 | tf_op jit(solution)/shard_map/ppermute | solution.py:270
  76.4 38.5 %collective-permute-start.12 = (bf16[320,640]{1,0:T(8,128)(2,1)S(1)}, bf16[320,640]{1,0:T(8,128)(2,1)S(1)}, u32[]{:S(2)}, u32[]{:S(2)}) collective-permute-start(bf16[320,640]{1,0:T(8,128)(2,1)S(1)} %bitcast.22), channel_id=1, source_target_pairs={{0,224},{32,0},{64,32},{96,64},{128,96},{160,128},{192,160},{224,1... | collective-permute-start | bytes 1228808 | tf_op jit(solution)/shard_map/ppermute | solution.py:271
  114.9 10.8 %collective-permute-start.13 = (bf16[320,640]{1,0:T(8,128)(2,1)S(1)}, bf16[320,640]{1,0:T(8,128)(2,1)S(1)}, u32[]{:S(2)}, u32[]{:S(2)}) collective-permute-start(bf16[320,640]{1,0:T(8,128)(2,1)S(1)} %collective-permute-done.11.r1), channel_id=1, source_target_pairs={{0,32},{32,64},{64,96},{96,128},{128,160},{160,192},{192,224},{224... | collective-permute-start | bytes 1228808 | tf_op jit(solution)/shard_map/ppermute | solution.py:270
  114.9 14.0 %collective-permute-start.14 = (bf16[320,640]{1,0:T(8,128)(2,1)S(1)}, bf16[320,640]{1,0:T(8,128)(2,1)}, u32[]{:S(2)}, u32[]{:S(2)}) collective-permute-start(bf16[320,640]{1,0:T(8,128)(2,1)S(1)} %collective-permute-done.12.l1), channel_id=1, source_target_pairs={{0,224},{32,0},{64,32},{96,64},{128,96},{160,128},{192,160},{224,1... | collective-permute-start | bytes 1228808 | tf_op jit(solution)/shard_map/ppermute | solution.py:271
  125.7 10.1 %collective-permute-start.15 = (bf16[320,640]{1,0:T(8,128)(2,1)S(1)}, bf16[320,640]{1,0:T(8,128)(2,1)}, u32[]{:S(2)}, u32[]{:S(2)}) collective-permute-start(bf16[320,640]{1,0:T(8,128)(2,1)S(1)} %collective-permute-done.13.r2), channel_id=1, source_target_pairs={{0,32},{32,64},{64,96},{96,128},{128,160},{160,192},{192,224},{224... | collective-permute-start | bytes 1228808 | tf_op jit(solution)/shard_map/ppermute | solution.py:270
  126.7 9.2 %collective-permute-start.5 = (bf16[64,128]{1,0:T(8,128)(2,1)S(1)}, bf16[64,128]{1,0:T(8,128)(2,1)S(1)}, u32[]{:S(2)}, u32[]{:S(2)}) collective-permute-start(bf16[64,128]{1,0:T(8,128)(2,1)S(1)} %get-tuple-element.12), channel_id=1, source_target_pairs={{0,1},{1,0},{2,3},{3,2},{4,5},{5,4},{6,7},{7,6},{8,9},{9,8},{10,11... | collective-permute-start | bytes 49160 | tf_op jit(solution)/shard_map/ppermute | solution.py:318
  128.9 25.4 %collective-permute-start.16 = (bf16[320,640]{1,0:T(8,128)(2,1)}, bf16[320,640]{1,0:T(8,128)(2,1)}, u32[]{:S(2)}, u32[]{:S(2)}) collective-permute-start(bf16[320,640]{1,0:T(8,128)(2,1)} %collective-permute-done.14.l2), channel_id=1, source_target_pairs={{0,224},{32,0},{64,32},{96,64},{128,96},{160,128},{192,160},{224,1... | collective-permute-start | bytes 1228808 | tf_op jit(solution)/shard_map/ppermute | solution.py:271
  135.8 18.5 %collective-permute-start.17 = (bf16[320,640]{1,0:T(8,128)(2,1)}, bf16[320,640]{1,0:T(8,128)(2,1)}, u32[]{:S(2)}, u32[]{:S(2)}) collective-permute-start(bf16[320,640]{1,0:T(8,128)(2,1)} %collective-permute-done.15.r3), channel_id=1, source_target_pairs={{0,32},{32,64},{64,96},{96,128},{128,160},{160,192},{192,224},{224... | collective-permute-start | bytes 1228808 | tf_op jit(solution)/shard_map/ppermute | solution.py:272
  135.8 4.4 %collective-permute-start.6 = (bf16[2,64,128]{2,1,0:T(8,128)(2,1)S(1)}, bf16[2,64,128]{2,1,0:T(8,128)(2,1)S(1)}, u32[]{:S(2)}, u32[]{:S(2)}) collective-permute-start(bf16[2,64,128]{2,1,0:T(8,128)(2,1)S(1)} %pad_maximum_fusion.1), channel_id=1, source_target_pairs={{0,2},{2,0},{1,3},{3,1},{4,6},{6,4},{5,7},{7,5},{8,10},{10,8},{9,1... | collective-permute-start | bytes 98312 | tf_op jit(solution)/shard_map/ppermute | solution.py:319
  140.2 3.6 %collective-permute-start.7 = (bf16[4,64,128]{2,1,0:T(8,128)(2,1)S(1)}, bf16[4,64,128]{2,1,0:T(8,128)(2,1)S(1)}, u32[]{:S(2)}, u32[]{:S(2)}) collective-permute-start(bf16[4,64,128]{2,1,0:T(8,128)(2,1)S(1)} %pad_maximum_fusion.bc0), channel_id=1, source_target_pairs={{4,0},{8,4},{12,8},{0,12},{5,1},{9,5},{13,9},{1,13},{6,2},{10,6},{... | collective-permute-start | bytes 196616 | tf_op jit(solution)/shard_map/ppermute | solution.py:322
  141.1 4.6 %collective-permute-start.8 = (bf16[4,64,128]{2,1,0:T(8,128)(2,1)S(1)}, bf16[4,64,128]{2,1,0:T(8,128)(2,1)S(1)}, u32[]{:S(2)}, u32[]{:S(2)}) collective-permute-start(bf16[4,64,128]{2,1,0:T(8,128)(2,1)S(1)} %pad_maximum_fusion.bc0), channel_id=1, source_target_pairs={{8,0},{12,4},{0,8},{4,12},{9,1},{13,5},{1,9},{5,13},{10,2},{14,6},... | collective-permute-start | bytes 196616 | tf_op jit(solution)/shard_map/ppermute | solution.py:322
  142.3 4.7 %collective-permute-start.9 = (bf16[4,64,128]{2,1,0:T(8,128)(2,1)S(1)}, bf16[4,64,128]{2,1,0:T(8,128)(2,1)S(1)}, u32[]{:S(2)}, u32[]{:S(2)}) collective-permute-start(bf16[4,64,128]{2,1,0:T(8,128)(2,1)S(1)} %pad_maximum_fusion.bc0), channel_id=1, source_target_pairs={{12,0},{0,4},{4,8},{8,12},{13,1},{1,5},{5,9},{9,13},{14,2},{2,6},{... | collective-permute-start | bytes 196616 | tf_op jit(solution)/shard_map/ppermute | solution.py:322
  153.5 3.4 %collective-permute-start.10 = (bf16[64,640]{1,0:T(8,128)(2,1)S(1)}, bf16[64,640]{1,0:T(8,128)(2,1)S(1)}, u32[]{:S(2)}, u32[]{:S(2)}) collective-permute-start(bf16[64,640]{1,0:T(8,128)(2,1)S(1)} %shard_map.131.mine), channel_id=1, source_target_pairs={{0,16},{16,0},{1,17},{17,1},{2,18},{18,2},{3,19},{19,3},{4,20},{20... | collective-permute-start | bytes 245768 | tf_op jit(solution)/shard_map/ppermute | solution.py:354
  159.5 8.2 %collective-permute-start.18 = (bf16[8,64,384]{2,1,0:T(8,128)(2,1)S(1)}, bf16[8,64,384]{2,1,0:T(8,128)(2,1)S(1)}, u32[]{:S(2)}, u32[]{:S(2)}) collective-permute-start(bf16[8,64,384]{2,1,0:T(8,128)(2,1)S(1)} %get-tuple-element.16), channel_id=1, source_target_pairs={{0,1},{1,0},{2,3},{3,2},{4,5},{5,4},{6,7},{7,6},{8,9},{9,8},{10,11... | collective-permute-start | bytes 1179656 | tf_op jit(solution)/shard_map/ppermute | solution.py:378
  168.7 12.9 %all-to-all-start.3 = ((bf16[8,64,384]{2,1,0:T(8,128)(2,1)}), bf16[8,64,384]{2,1,0:T(8,128)(2,1)S(1)}, u32[]{:S(2)}, u32[]{:S(2)}) async-start(bf16[8,64,384]{2,1,0:T(8,128)(2,1)} %shard_map.133), calls=%async_computation.3 | async-start | bytes 786432 | tf_op jit(solution)/shard_map/all_to_all | solution.py:380
  181.8 5.4 %collective-permute-start.19 = (bf16[64,320]{1,0:T(8,128)(2,1)S(1)}, bf16[64,320]{1,0:T(8,128)(2,1)S(1)}, u32[]{:S(2)}, u32[]{:S(2)}) collective-permute-start(bf16[64,320]{1,0:T(8,128)(2,1)S(1)} %shard_map.134), channel_id=1, source_target_pairs={{0,0},{1,16},{16,1},{17,17},{2,2},{3,18},{18,3},{19,19},{4,4},{5,2... | collective-permute-start | bytes 122888 | tf_op jit(solution)/shard_map/ppermute | solution.py:386
  (21 other events, 345.7 us)

commit v4 on v3

--- a/solution.py
+++ b/solution.py
@@ -69,34 +69,25 @@
         run(e_oth, e_own)
 
 
-def project_kernel(place, e_own, e_oth, *refs):
-    out, held, sems = refs[4], refs[5:9], refs[9]
-    x_own, x_oth, z_own, z_oth = held
-    inner = x_own.shape[1]
-    groups, rows = out.shape[:2]
-    copies = [pltpu.make_async_copy(refs[k], held[k], sems.at[k]) for k in range(4)]
-    for copy in copies:
-        copy.start()
-
-    def run(ea, eb):
-        a = ea[...]
-        b = eb[...]
-        copies[0].wait()
-        copies[1].wait()
-        px = (nn(a, x_own[...]) + nn(b, x_oth[...])).astype(BF)
-        out[:, :, :inner] = px.reshape(groups, rows, inner)
-        copies[2].wait()
-        copies[3].wait()
-        pz = (nn(a, z_own[...]) + nn(b, z_oth[...])).astype(BF)
-        out[:, :, inner:] = pz.reshape(groups, rows, inner)
-
-    @pl.when(place[0] == 1)
+def project_kernel(place, e_own, e_oth, x_own, x_oth, z_own, z_oth, out, both):
+    depth = x_own.shape[0]
+
+    def fill(ea, eb):
+        both[:, :depth] = ea[...]
+        both[:, depth:] = eb[...]
+
+    @pl.when((pl.program_id(0) == 0) & (place[0] == 1))
     def _():
-        run(e_own, e_oth)
-
-    @pl.when(place[0] == 0)
+        fill(e_own, e_oth)
+
+    @pl.when((pl.program_id(0) == 0) & (place[0] == 0))
     def _():
-        run(e_oth, e_own)
+        fill(e_oth, e_own)
+
+    own = jnp.concatenate([x_own[...], z_own[...]], 1)
+    oth = jnp.concatenate([x_oth[...], z_oth[...]], 1)
+    total = nn(both[...], jnp.concatenate([own, oth], 0))
+    out[...] = total.astype(BF).reshape(out.shape)
 
 
 def small_kernel(part, bc, small):
@@ -157,8 +148,8 @@
     total = part[0].astype(F32)
     for k in range(1, part.shape[0]):
         total = total + part[k].astype(F32)
-    x_pre = total[:, :inner]
-    z_pre = total[:, inner:]
+    x_pre = jnp.concatenate([total[:, k : k + 128] for k in range(0, 2 * inner, 256)], 1)
+    z_pre = jnp.concatenate([total[:, k + 128 : k + 256] for k in range(0, 2 * inner, 256)], 1)
     pick = (
         lax.broadcasted_iota(jnp.int32, (heads, inner), 0)
         == lax.broadcasted_iota(jnp.int32, (heads, inner), 1) // (inner // heads)
@@ -192,13 +183,13 @@
     out[...] = jnp.concatenate([gg1, gg2], 0).astype(BF)
 
 
-def output_kernel(place, mine, other, gain, own, r1, l1, r2, l2, r3, l3, r4, keep, send):
-    same = place[0]
+def output_kernel(place, mine, other, gain, own, r1, l1, r2, l2, r3, l3, r4, out):
     z = place[1]
-    groups, rows, _ = keep.shape
+    groups = out.shape[0] // 2
+    rows = out.shape[1]
     m = mine[...]
     o = other[...]
-    v = jnp.concatenate([jnp.where(same == 1, m, o), jnp.where(same == 1, o, m)], 0)
+    v = jnp.concatenate([jnp.where(place[5] == 0, m, o), jnp.where(place[5] == 0, o, m)], 0)
     raw = v.astype(F32) / gain[...]
     ss = jnp.sum(raw * raw, axis=1, keepdims=True)
     hi = ss.astype(BF).astype(F32)
@@ -208,18 +199,8 @@
     for shift, w in order:
         block = jnp.concatenate([nt(v, w[...]), tail], 1)
         at = lax.rem(z + shift, groups)
-        keep[at] = block[:rows]
-        send[at] = block[rows:].astype(BF)
-
-
-def pair_kernel(keep, got, out):
-    total = keep[...] + got[...].astype(F32)
-    cols = out.shape[2] - 64
-    lane = lax.broadcasted_iota(jnp.int32, total.shape, 2)
-    ss = total[:, :, cols : cols + 1] + total[:, :, cols + 1 : cols + 2]
-    hi = ss.astype(BF).astype(F32)
-    total = jnp.where(lane == cols, hi, jnp.where(lane == cols + 1, ss - hi, total))
-    out[...] = total.astype(BF)
+        out[2 * at] = block[:rows].astype(BF)
+        out[2 * at + 1] = block[rows:].astype(BF)
 
 
 def reduce_kernel(part, out, *, count):
@@ -287,7 +268,7 @@
     ).reshape(8 * 2 * rows, wide)
     e_oth = lax.ppermute(e_own, "core", pair)
     place = jnp.stack(
-        [(y == core).astype(jnp.int32), lax.axis_index("z"), lax.axis_index("x"), lax.axis_index("yh"), core]
+        [(y == core).astype(jnp.int32), lax.axis_index("z"), lax.axis_index("x"), lax.axis_index("yh"), core, y]
     )
     part_small = call(
         project_small_kernel,
@@ -301,11 +282,12 @@
         project_kernel,
         jax.ShapeDtypeStruct((8, 2 * rows, 2 * inner), BF),
         (place, e_own, e_oth, x_weight, x_oth, z_weight, z_oth),
+        grid=(inner // 128,),
         in_specs=[pl.BlockSpec(memory_space=pltpu.SMEM)]
-        + [pl.BlockSpec(memory_space=pltpu.VMEM)] * 2
-        + [pl.BlockSpec(memory_space=pl.ANY)] * 4,
-        out_specs=pl.BlockSpec(memory_space=pltpu.VMEM),
-        scratch=[pltpu.VMEM((wide, inner), BF)] * 4 + [pltpu.SemaphoreType.DMA((4,))],
+        + [pl.BlockSpec((16 * rows, wide), lambda i: (0, 0))] * 2
+        + [pl.BlockSpec((wide, 128), lambda i: (0, i))] * 4,
+        out_specs=pl.BlockSpec((8, 2 * rows, 256), lambda i: (0, 0, i)),
+        scratch=[pltpu.VMEM((16 * rows, 2 * wide), BF)],
         limit=PROJECT_LIMIT,
         flops=2 * 16 * rows * 2 * wide * 2 * inner,
     )
@@ -352,12 +334,9 @@
         ),
     )
     gg_oth = lax.ppermute(gg, "yl", pair)
-    keep, send = call(
+    out_part = call(
         output_kernel,
-        (
-            jax.ShapeDtypeStruct((8, 2 * rows, wide + 64), F32),
-            jax.ShapeDtypeStruct((8, 2 * rows, wide + 64), BF),
-        ),
+        jax.ShapeDtypeStruct((16, 2 * rows, wide + 64), BF),
         (
             place,
             gg,
@@ -375,9 +354,7 @@
         in_smem=1,
         flops=2 * 4 * rows * inner * 8 * wide,
     )
-    got = lax.ppermute(send, "core", pair)
-    paired = call(pair_kernel, jax.ShapeDtypeStruct((8, 2 * rows, wide + 64), BF), (keep, got))
-    partial_out = lax.all_to_all(paired, ("x", "yh"), 0, 0)
+    partial_out = lax.all_to_all(out_part, TP, 0, 0)
     mine = call(
         functools.partial(reduce_kernel, count=float(16 * inner)),
         jax.ShapeDtypeStruct((2 * rows, wide), BF),

time: 188 us -> 192 us (1.021)
  waiting for transfers between devices: 90.7 us -> 93.2 us
    ppermute x1 -> x0, starting transfers between devices: 6.8 us -> none  [per_device(): got = lax.ppermute(send, 'core', pair)]
    all_to_all x1, starting transfers between devices: 3.45 us -> 10.2 us  [per_device(): partial_out = lax.all_to_all(out_part, TP, 0, 0)]
    all_to_all x1, waiting for transfers between devices: 8.77 us -> 13.1 us  [per_device(): partial_out = lax.all_to_all(out_part, TP, 0, 0)]
    pallas_call x8 -> x7, Pallas kernels: 17.2 us -> 17.6 us  [call(): pl.pallas_call(body, out_shape=out_shape, in_specs=in_specs, out_specs=ou...]
  transfers between devices with their start and end apart: 23 -> 22, of which waited for: 13 -> 12; matrix products, arithmetic and copies ran while one was open for 0% -> 0% of each run, Pallas kernels for 7% -> 7%
where the time goes in v4:
time: 192 us
  waiting for transfers between devices  93.2 us (49%)
  starting transfers between devices  47.1 us (25%)
  blocking collectives  27.4 us (14%)
  Pallas kernels  17.6 us (9%)
  local copies, waits for them, and re-layouts  4.33 us (2%)
    ppermute x4, waiting for transfers between devices, per_device(): ring_r.append(lax.ppermute(ring_r[-1], 'z', right))  48.6 us
    all_to_all x1, blocking collectives, per_device(): lax.all_to_all(jnp.broadcast_to(moved[None], (8,) + moved.shape), ('x', '...  27.4 us
    ppermute x1, waiting for transfers between devices, per_device(): small_oth = lax.ppermute(small_own, 'yl', pair)  18.4 us
    pallas_call x7, Pallas kernels, call(): pl.pallas_call(body, out_shape=out_shape, in_specs=in_specs, out_specs=ou...  17.6 us
    all_to_all x1, waiting for transfers between devices, per_device(): partial_out = lax.all_to_all(out_part, TP, 0, 0)  13.1 us
    all_to_all x1, starting transfers between devices, per_device(): partial_out = lax.all_to_all(out_part, TP, 0, 0)  10.2 us
    ppermute x3, starting transfers between devices, per_device(): ring_l.append(lax.ppermute(ring_l[-1], 'z', left))  6.92 us
    all_to_all x1, starting transfers between devices, per_device(): part = lax.all_to_all(part, 'z', 0, 0)  6.15 us
  transfers between devices with their start and end apart: 22, of which 12 were waited for; matrix products, arithmetic and copies ran while one was open for 0% of the time, Pallas kernels for 7%

profile of v4, /device:TPU:1, one launch (start us, length us, event | category | flops | bytes accessed | tf_op | source)
XLA Modules:
  0.0 191.7 jit_solution(1827752423690998580)
XLA Ops:
  2.2 27.4 %all_to_all.20 = bf16[8,64,320]{2,1,0:T(8,128)(2,1)S(1)} all-to-all(bf16[8,64,320]{2,1,0:T(8,128)(2,1)S(1)} %broadcast_in_dim.24), channel_id=1, replica_groups=mesh['z'=8,'yl'=2,'x'=4,'yh'=2,'core'=2] {'x','yh'}, dimensions={0} | all-to-all | bytes 655360 | tf_op jit(solution)/shard_map/all_to_all | solution.py:266
  29.6 3.2 %collective-permute-start.1 = (bf16[512,320]{1,0:T(8,128)(2,1)S(1)}, bf16[512,320]{1,0:T(8,128)(2,1)S(1)}, u32[]{:S(2)}, u32[]{:S(2)}) collective-permute-start(bf16[512,320]{1,0:T(8,128)(2,1)S(1)} %bitcast.19), channel_id=1, source_target_pairs={{0,1},{1,0},{2,3},{3,2},{4,5},{5,4},{6,7},{7,6},{8,9},{9,8},{10,11... | collective-permute-start | bytes 983048 | tf_op jit(solution)/shard_map/ppermute | solution.py:269
  35.2 18.4 %collective-permute-done.4.s_oth = bf16[64,320]{1,0:T(8,128)(2,1)S(1)} collective-permute-done((bf16[64,320]{1,0:T(8,128)(2,1)S(1)}, bf16[64,320]{1,0:T(8,128)(2,1)S(1)}, u32[]{:S(2)}, u32[]{:S(2)}) %collective-permute-start.4) | collective-permute-done | bytes 40992 | tf_op jit(solution)/shard_map/ppermute | solution.py:259
  53.6 1.6 shard_map.128
  55.2 6.1 %all-to-all-start.2 = ((bf16[8,64,128]{2,1,0:T(8,128)(2,1)}), bf16[8,64,128]{2,1,0:T(8,128)(2,1)S(1)}, u32[]{:S(2)}, u32[]{:S(2)}) async-start(bf16[8,64,128]{2,1,0:T(8,128)(2,1)} %shard_map.128), calls=%async_computation.2 | async-start | bytes 262144 | tf_op jit(solution)/shard_map/all_to_all | solution.py:280
  62.9 5.7 %shard_map.127 = bf16[8,64,1280]{2,1,0:T(8,128)(2,1)} custom-call(s32[6]{0:T(128)} %copy-done.8, bf16[512,320]{1,0:T(8,128)(2,1)} %bitcast.21, bf16[512,320]{1,0:T(8,128)(2,1)} %copy-done.2, bf16[320,640]{1,0:T(8,128)(2,1)} %x_own.1, bf16[320,640]{1,0:T(8,128)(2,1)} %copy-done.15, bf16[320,640]{1,0:T(8,128)(2,1)} %z_own.1, bf16[320,640]{1,0:T(8,128)(2,1)} %copy-done.16), custom_call_target="tpu_custom_call" | custom-call | flops 838860800 | bytes 1048576 | tf_op jit(solution)/shard_map/pallas_call | solution.py:38
  69.3 6.1 %all-to-all-start.1 = ((bf16[8,64,1280]{2,1,0:T(8,128)(2,1)}), bf16[8,64,1280]{2,1,0:T(8,128)(2,1)S(1)}, u32[]{:S(2)}, u32[]{:S(2)}) async-start(bf16[8,64,1280]{2,1,0:T(8,128)(2,1)} %shard_map.127), calls=%async_computation.1 | async-start | bytes 2621440 | tf_op jit(solution)/shard_map/all_to_all | solution.py:294
  75.4 1.5 collective-permute-start.11
  78.2 37.2 %collective-permute-done.11.r1 = bf16[320,640]{1,0:T(8,128)(2,1)S(1)} collective-permute-done((bf16[320,640]{1,0:T(8,128)(2,1)S(1)}, bf16[320,640]{1,0:T(8,128)(2,1)S(1)}, u32[]{:S(2)}, u32[]{:S(2)}) %collective-permute-start.11) | collective-permute-done | bytes 409632 | tf_op jit(solution)/shard_map/ppermute | solution.py:251
  115.4 2.7 %collective-permute-start.14 = (bf16[320,640]{1,0:T(8,128)(2,1)S(1)}, bf16[320,640]{1,0:T(8,128)(2,1)}, u32[]{:S(2)}, u32[]{:S(2)}) collective-permute-start(bf16[320,640]{1,0:T(8,128)(2,1)S(1)} %collective-permute-done.12.l1), channel_id=1, source_target_pairs={{0,224},{32,0},{64,32},{96,64},{128,96},{160,128},{192,160},{224,1... | collective-permute-start | bytes 1228808 | tf_op jit(solution)/shard_map/ppermute | solution.py:252
  118.9 7.4 %collective-permute-done.13.r2 = bf16[320,640]{1,0:T(8,128)(2,1)S(1)} collective-permute-done((bf16[320,640]{1,0:T(8,128)(2,1)S(1)}, bf16[320,640]{1,0:T(8,128)(2,1)S(1)}, u32[]{:S(2)}, u32[]{:S(2)}) %collective-permute-start.13) | collective-permute-done | bytes 409632 | tf_op jit(solution)/shard_map/ppermute | solution.py:251
  127.2 2.3 %collective-permute-start.5 = (bf16[64,128]{1,0:T(8,128)(2,1)S(1)}, bf16[64,128]{1,0:T(8,128)(2,1)S(1)}, u32[]{:S(2)}, u32[]{:S(2)}) collective-permute-start(bf16[64,128]{1,0:T(8,128)(2,1)S(1)} %get-tuple-element.10), channel_id=1, source_target_pairs={{0,1},{1,0},{2,3},{3,2},{4,5},{5,4},{6,7},{7,6},{8,9},{9,8},{10,11... | collective-permute-start | bytes 49160 | tf_op jit(solution)/shard_map/ppermute | solution.py:300
  129.5 3.0 %collective-permute-start.16 = (bf16[320,640]{1,0:T(8,128)(2,1)}, bf16[320,640]{1,0:T(8,128)(2,1)}, u32[]{:S(2)}, u32[]{:S(2)}) collective-permute-start(bf16[320,640]{1,0:T(8,128)(2,1)} %collective-permute-done.14.l2), channel_id=1, source_target_pairs={{0,224},{32,0},{64,32},{96,64},{128,96},{160,128},{192,160},{224,1... | collective-permute-start | bytes 1228808 | tf_op jit(solution)/shard_map/ppermute | solution.py:252
  132.4 3.9 %collective-permute-done.15.r3 = bf16[320,640]{1,0:T(8,128)(2,1)} collective-permute-done((bf16[320,640]{1,0:T(8,128)(2,1)S(1)}, bf16[320,640]{1,0:T(8,128)(2,1)}, u32[]{:S(2)}, u32[]{:S(2)}) %collective-permute-start.15) | collective-permute-done | bytes 409632 | tf_op jit(solution)/shard_map/ppermute | solution.py:251
  137.2 3.5 %collective-permute-done.6 = bf16[2,64,128]{2,1,0:T(8,128)(2,1)S(1)} collective-permute-done((bf16[2,64,128]{2,1,0:T(8,128)(2,1)S(1)}, bf16[2,64,128]{2,1,0:T(8,128)(2,1)S(1)}, u32[]{:S(2)}, u32[]{:S(2)}) %collective-permute-start.6) | collective-permute-done | bytes 32800 | tf_op jit(solution)/shard_map/ppermute | solution.py:301
  142.9 1.4 collective-permute-done.7.bc1
  144.3 1.9 %collective-permute-done.8.bc2 = bf16[4,64,128]{2,1,0:T(8,128)(2,1)S(1)} collective-permute-done((bf16[4,64,128]{2,1,0:T(8,128)(2,1)S(1)}, bf16[4,64,128]{2,1,0:T(8,128)(2,1)S(1)}, u32[]{:S(2)}, u32[]{:S(2)}) %collective-permute-start.8) | collective-permute-done | bytes 65568 | tf_op jit(solution)/shard_map/ppermute | solution.py:304
  147.6 5.6 %shard_map.130 = (f32[32,8,640]{2,1,0:T(8,128)S(1)}, f32[32,128]{1,0:T(8,128)S(1)}) custom-call(s32[6]{0:T(128)S(1)} %copy-done.9, bf16[4,64,128]{2,1,0:T(8,128)(2,1)S(1)} %pad_maximum_fusion.bc0, bf16[4,64,128]{2,1,0:T(8,128)(2,1)S(1)} %collective-permute-done.7.bc1, bf16[4,64,128]{2,1,0:T(8,128)(2,1)S(1)} %collective-permute-done.8.bc2, ...), custom_call_target="tpu_custom_call" | custom-call | flops 83886080 | bytes 1048576 | tf_op jit(solution)/shard_map/pallas_call | solution.py:38
  154.8 2.5 %collective-permute-done.10.other = bf16[64,640]{1,0:T(8,128)(2,1)S(1)} collective-permute-done((bf16[64,640]{1,0:T(8,128)(2,1)S(1)}, bf16[64,640]{1,0:T(8,128)(2,1)S(1)}, u32[]{:S(2)}, u32[]{:S(2)}) %collective-permute-start.10) | collective-permute-done | bytes 81952 | tf_op jit(solution)/shard_map/ppermute | solution.py:336
  157.4 3.6 %shard_map.132 = bf16[16,64,384]{2,1,0:T(8,128)(2,1)} custom-call(s32[6]{0:T(128)S(1)} %copy-done.9, bf16[64,640]{1,0:T(8,128)(2,1)S(1)} %shard_map.131.mine, bf16[64,640]{1,0:T(8,128)(2,1)S(1)} %collective-permute-done.10.other, f32[1,640]{1,0:T(1,128)S(1)} %reshape.28.gain, bf16[320,640]{1,0:T(8,128)(2,1)S(1)} %bitcast.24, ...), custom_call_target="tpu_custom_call" | custom-call | flops 419430400 | bytes 1048576 | tf_op jit(solution)/shard_map/pallas_call | solution.py:38
  160.9 10.2 %all-to-all-start.3 = ((bf16[16,64,384]{2,1,0:T(8,128)(2,1)}), bf16[16,64,384]{2,1,0:T(8,128)(2,1)S(1)}, u32[]{:S(2)}, u32[]{:S(2)}) async-start(bf16[16,64,384]{2,1,0:T(8,128)(2,1)} %shard_map.132), calls=%async_computation.3 | async-start | bytes 1572864 | tf_op jit(solution)/shard_map/all_to_all | solution.py:357
  171.8 13.1 %all-to-all-done.3.part = bf16[16,64,384]{2,1,0:T(8,128)(2,1)S(1)} async-done(((bf16[16,64,384]{2,1,0:T(8,128)(2,1)}), bf16[16,64,384]{2,1,0:T(8,128)(2,1)S(1)}, u32[]{:S(2)}, u32[]{:S(2)}) %all-to-all-start.3) | async-done | bytes 786464 | tf_op jit(solution)/shard_map/all_to_all | solution.py:357
  185.1 4.1 %collective-permute-start.18 = (bf16[64,320]{1,0:T(8,128)(2,1)S(1)}, bf16[64,320]{1,0:T(8,128)(2,1)S(1)}, u32[]{:S(2)}, u32[]{:S(2)}) collective-permute-start(bf16[64,320]{1,0:T(8,128)(2,1)S(1)} %shard_map.133), channel_id=1, source_target_pairs={{0,0},{1,16},{16,1},{17,17},{2,2},{3,18},{18,3},{19,19},{4,4},{5,2... | collective-permute-start | bytes 122888 | tf_op jit(solution)/shard_map/ppermute | solution.py:363
  189.2 1.7 collective-permute-done.18
  (85 shorter events, 16.4 us)
Async XLA Ops:
  1.5 0.7 collective-permute-start
  29.6 24.0 %collective-permute-start.1 = (bf16[512,320]{1,0:T(8,128)(2,1)S(1)}, bf16[512,320]{1,0:T(8,128)(2,1)S(1)}, u32[]{:S(2)}, u32[]{:S(2)}) collective-permute-start(bf16[512,320]{1,0:T(8,128)(2,1)S(1)} %bitcast.19), channel_id=1, source_target_pairs={{0,1},{1,0},{2,3},{3,2},{4,5},{5,4},{6,7},{7,6},{8,9},{9,8},{10,11... | collective-permute-start | bytes 983048 | tf_op jit(solution)/shard_map/ppermute | solution.py:269
  32.9 28.5 %collective-permute-start.2 = (bf16[320,640]{1,0:T(8,128)(2,1)S(1)}, bf16[320,640]{1,0:T(8,128)(2,1)S(1)}, u32[]{:S(2)}, u32[]{:S(2)}) collective-permute-start(bf16[320,640]{1,0:T(8,128)(2,1)S(1)} %copy-done.13), channel_id=1, source_target_pairs={{0,16},{16,0},{1,17},{17,1},{2,18},{18,2},{3,19},{19,3},{4,20},{20... | collective-permute-start | bytes 1228808 | tf_op jit(solution)/shard_map/ppermute | solution.py:254
  33.4 27.9 %collective-permute-start.3 = (bf16[320,640]{1,0:T(8,128)(2,1)S(1)}, bf16[320,640]{1,0:T(8,128)(2,1)S(1)}, u32[]{:S(2)}, u32[]{:S(2)}) collective-permute-start(bf16[320,640]{1,0:T(8,128)(2,1)S(1)} %copy-done.14), channel_id=1, source_target_pairs={{0,16},{16,0},{1,17},{17,1},{2,18},{18,2},{3,19},{19,3},{4,20},{20... | collective-permute-start | bytes 1228808 | tf_op jit(solution)/shard_map/ppermute | solution.py:255
  34.5 19.1 %collective-permute-start.4 = (bf16[64,320]{1,0:T(8,128)(2,1)S(1)}, bf16[64,320]{1,0:T(8,128)(2,1)S(1)}, u32[]{:S(2)}, u32[]{:S(2)}) collective-permute-start(bf16[64,320]{1,0:T(8,128)(2,1)S(1)} %maximum_maximum_fusion.s_own), channel_id=1, source_target_pairs={{0,16},{16,0},{1,17},{17,1},{2,18},{18,2},{3,19},{19,3},{4,20},{20... | collective-permute-start | bytes 122888 | tf_op jit(solution)/shard_map/ppermute | solution.py:259
  55.2 14.0 %all-to-all-start.2 = ((bf16[8,64,128]{2,1,0:T(8,128)(2,1)}), bf16[8,64,128]{2,1,0:T(8,128)(2,1)S(1)}, u32[]{:S(2)}, u32[]{:S(2)}) async-start(bf16[8,64,128]{2,1,0:T(8,128)(2,1)} %shard_map.128), calls=%async_computation.2 | async-start | bytes 262144 | tf_op jit(solution)/shard_map/all_to_all | solution.py:280
  68.6 74.3 %copy-start.21 = (f32[640]{0:T(1024)S(1)}, f32[640]{0:T(1024)}, u32[]{:S(2)}) copy-start(f32[640]{0:T(1024)} %param.23) | copy-start | bytes 7684
  68.6 78.9 %copy-start.9 = (s32[6]{0:T(128)S(1)}, s32[6]{0:T(128)}, u32[]{:S(2)}) copy-start(s32[6]{0:T(128)} %copy-done.8) | copy-start | bytes 76
  69.3 83.9 %all-to-all-start.1 = ((bf16[8,64,1280]{2,1,0:T(8,128)(2,1)}), bf16[8,64,1280]{2,1,0:T(8,128)(2,1)S(1)}, u32[]{:S(2)}, u32[]{:S(2)}) async-start(bf16[8,64,1280]{2,1,0:T(8,128)(2,1)} %shard_map.127), calls=%async_computation.1 | async-start | bytes 2621440 | tf_op jit(solution)/shard_map/all_to_all | solution.py:294
  75.4 40.0 %collective-permute-start.11 = (bf16[320,640]{1,0:T(8,128)(2,1)S(1)}, bf16[320,640]{1,0:T(8,128)(2,1)S(1)}, u32[]{:S(2)}, u32[]{:S(2)}) collective-permute-start(bf16[320,640]{1,0:T(8,128)(2,1)S(1)} %bitcast.22), channel_id=1, source_target_pairs={{0,32},{32,64},{64,96},{96,128},{128,160},{160,192},{192,224},{224... | collective-permute-start | bytes 1228808 | tf_op jit(solution)/shard_map/ppermute | solution.py:251
  76.9 38.5 %collective-permute-start.12 = (bf16[320,640]{1,0:T(8,128)(2,1)S(1)}, bf16[320,640]{1,0:T(8,128)(2,1)S(1)}, u32[]{:S(2)}, u32[]{:S(2)}) collective-permute-start(bf16[320,640]{1,0:T(8,128)(2,1)S(1)} %bitcast.23), channel_id=1, source_target_pairs={{0,224},{32,0},{64,32},{96,64},{128,96},{160,128},{192,160},{224,1... | collective-permute-start | bytes 1228808 | tf_op jit(solution)/shard_map/ppermute | solution.py:252
  115.4 10.8 %collective-permute-start.13 = (bf16[320,640]{1,0:T(8,128)(2,1)S(1)}, bf16[320,640]{1,0:T(8,128)(2,1)S(1)}, u32[]{:S(2)}, u32[]{:S(2)}) collective-permute-start(bf16[320,640]{1,0:T(8,128)(2,1)S(1)} %collective-permute-done.11.r1), channel_id=1, source_target_pairs={{0,32},{32,64},{64,96},{96,128},{128,160},{160,192},{192,224},{224... | collective-permute-start | bytes 1228808 | tf_op jit(solution)/shard_map/ppermute | solution.py:251
  115.4 14.0 %collective-permute-start.14 = (bf16[320,640]{1,0:T(8,128)(2,1)S(1)}, bf16[320,640]{1,0:T(8,128)(2,1)}, u32[]{:S(2)}, u32[]{:S(2)}) collective-permute-start(bf16[320,640]{1,0:T(8,128)(2,1)S(1)} %collective-permute-done.12.l1), channel_id=1, source_target_pairs={{0,224},{32,0},{64,32},{96,64},{128,96},{160,128},{192,160},{224,1... | collective-permute-start | bytes 1228808 | tf_op jit(solution)/shard_map/ppermute | solution.py:252
  126.3 10.1 %collective-permute-start.15 = (bf16[320,640]{1,0:T(8,128)(2,1)S(1)}, bf16[320,640]{1,0:T(8,128)(2,1)}, u32[]{:S(2)}, u32[]{:S(2)}) collective-permute-start(bf16[320,640]{1,0:T(8,128)(2,1)S(1)} %collective-permute-done.13.r2), channel_id=1, source_target_pairs={{0,32},{32,64},{64,96},{96,128},{128,160},{160,192},{192,224},{224... | collective-permute-start | bytes 1228808 | tf_op jit(solution)/shard_map/ppermute | solution.py:251
  127.2 9.2 %collective-permute-start.5 = (bf16[64,128]{1,0:T(8,128)(2,1)S(1)}, bf16[64,128]{1,0:T(8,128)(2,1)S(1)}, u32[]{:S(2)}, u32[]{:S(2)}) collective-permute-start(bf16[64,128]{1,0:T(8,128)(2,1)S(1)} %get-tuple-element.10), channel_id=1, source_target_pairs={{0,1},{1,0},{2,3},{3,2},{4,5},{5,4},{6,7},{7,6},{8,9},{9,8},{10,11... | collective-permute-start | bytes 49160 | tf_op jit(solution)/shard_map/ppermute | solution.py:300
  129.5 25.3 %collective-permute-start.16 = (bf16[320,640]{1,0:T(8,128)(2,1)}, bf16[320,640]{1,0:T(8,128)(2,1)}, u32[]{:S(2)}, u32[]{:S(2)}) collective-permute-start(bf16[320,640]{1,0:T(8,128)(2,1)} %collective-permute-done.14.l2), channel_id=1, source_target_pairs={{0,224},{32,0},{64,32},{96,64},{128,96},{160,128},{192,160},{224,1... | collective-permute-start | bytes 1228808 | tf_op jit(solution)/shard_map/ppermute | solution.py:252
  136.4 18.5 %collective-permute-start.17 = (bf16[320,640]{1,0:T(8,128)(2,1)}, bf16[320,640]{1,0:T(8,128)(2,1)}, u32[]{:S(2)}, u32[]{:S(2)}) collective-permute-start(bf16[320,640]{1,0:T(8,128)(2,1)} %collective-permute-done.15.r3), channel_id=1, source_target_pairs={{0,32},{32,64},{64,96},{96,128},{128,160},{160,192},{192,224},{224... | collective-permute-start | bytes 1228808 | tf_op jit(solution)/shard_map/ppermute | solution.py:253
  136.4 4.4 %collective-permute-start.6 = (bf16[2,64,128]{2,1,0:T(8,128)(2,1)S(1)}, bf16[2,64,128]{2,1,0:T(8,128)(2,1)S(1)}, u32[]{:S(2)}, u32[]{:S(2)}) collective-permute-start(bf16[2,64,128]{2,1,0:T(8,128)(2,1)S(1)} %pad_maximum_fusion.1), channel_id=1, source_target_pairs={{0,2},{2,0},{1,3},{3,1},{4,6},{6,4},{5,7},{7,5},{8,10},{10,8},{9,1... | collective-permute-start | bytes 98312 | tf_op jit(solution)/shard_map/ppermute | solution.py:301
  140.7 3.6 %collective-permute-start.7 = (bf16[4,64,128]{2,1,0:T(8,128)(2,1)S(1)}, bf16[4,64,128]{2,1,0:T(8,128)(2,1)S(1)}, u32[]{:S(2)}, u32[]{:S(2)}) collective-permute-start(bf16[4,64,128]{2,1,0:T(8,128)(2,1)S(1)} %pad_maximum_fusion.bc0), channel_id=1, source_target_pairs={{4,0},{8,4},{12,8},{0,12},{5,1},{9,5},{13,9},{1,13},{6,2},{10,6},{... | collective-permute-start | bytes 196616 | tf_op jit(solution)/shard_map/ppermute | solution.py:304
  141.7 4.6 %collective-permute-start.8 = (bf16[4,64,128]{2,1,0:T(8,128)(2,1)S(1)}, bf16[4,64,128]{2,1,0:T(8,128)(2,1)S(1)}, u32[]{:S(2)}, u32[]{:S(2)}) collective-permute-start(bf16[4,64,128]{2,1,0:T(8,128)(2,1)S(1)} %pad_maximum_fusion.bc0), channel_id=1, source_target_pairs={{8,0},{12,4},{0,8},{4,12},{9,1},{13,5},{1,9},{5,13},{10,2},{14,6},... | collective-permute-start | bytes 196616 | tf_op jit(solution)/shard_map/ppermute | solution.py:304
  142.8 4.7 %collective-permute-start.9 = (bf16[4,64,128]{2,1,0:T(8,128)(2,1)S(1)}, bf16[4,64,128]{2,1,0:T(8,128)(2,1)S(1)}, u32[]{:S(2)}, u32[]{:S(2)}) collective-permute-start(bf16[4,64,128]{2,1,0:T(8,128)(2,1)S(1)} %pad_maximum_fusion.bc0), channel_id=1, source_target_pairs={{12,0},{0,4},{4,8},{8,12},{13,1},{1,5},{5,9},{9,13},{14,2},{2,6},{... | collective-permute-start | bytes 196616 | tf_op jit(solution)/shard_map/ppermute | solution.py:304
  154.0 3.4 %collective-permute-start.10 = (bf16[64,640]{1,0:T(8,128)(2,1)S(1)}, bf16[64,640]{1,0:T(8,128)(2,1)S(1)}, u32[]{:S(2)}, u32[]{:S(2)}) collective-permute-start(bf16[64,640]{1,0:T(8,128)(2,1)S(1)} %shard_map.131.mine), channel_id=1, source_target_pairs={{0,16},{16,0},{1,17},{17,1},{2,18},{18,2},{3,19},{19,3},{4,20},{20... | collective-permute-start | bytes 245768 | tf_op jit(solution)/shard_map/ppermute | solution.py:336
  160.9 24.0 %all-to-all-start.3 = ((bf16[16,64,384]{2,1,0:T(8,128)(2,1)}), bf16[16,64,384]{2,1,0:T(8,128)(2,1)S(1)}, u32[]{:S(2)}, u32[]{:S(2)}) async-start(bf16[16,64,384]{2,1,0:T(8,128)(2,1)} %shard_map.132), calls=%async_computation.3 | async-start | bytes 1572864 | tf_op jit(solution)/shard_map/all_to_all | solution.py:357
  185.1 5.9 %collective-permute-start.18 = (bf16[64,320]{1,0:T(8,128)(2,1)S(1)}, bf16[64,320]{1,0:T(8,128)(2,1)S(1)}, u32[]{:S(2)}, u32[]{:S(2)}) collective-permute-start(bf16[64,320]{1,0:T(8,128)(2,1)S(1)} %shard_map.133), channel_id=1, source_target_pairs={{0,0},{1,16},{16,1},{17,17},{2,2},{3,18},{18,3},{19,19},{4,4},{5,2... | collective-permute-start | bytes 122888 | tf_op jit(solution)/shard_map/ppermute | solution.py:363
  (20 other events, 281.9 us)

commit v5 on v3

--- a/solution.py
+++ b/solution.py
@@ -69,34 +69,47 @@
         run(e_oth, e_own)
 
 
-def project_kernel(place, e_own, e_oth, *refs):
-    out, held, sems = refs[4], refs[5:9], refs[9]
-    x_own, x_oth, z_own, z_oth = held
-    inner = x_own.shape[1]
+def project_kernel(place, e_own, e_oth, x_own, x_oth, z_own, z_oth, out, both, held, done, sems):
+    depth, inner = x_own.shape
     groups, rows = out.shape[:2]
-    copies = [pltpu.make_async_copy(refs[k], held[k], sems.at[k]) for k in range(4)]
-    for copy in copies:
-        copy.start()
-
-    def run(ea, eb):
-        a = ea[...]
-        b = eb[...]
-        copies[0].wait()
-        copies[1].wait()
-        px = (nn(a, x_own[...]) + nn(b, x_oth[...])).astype(BF)
-        out[:, :, :inner] = px.reshape(groups, rows, inner)
-        copies[2].wait()
-        copies[3].wait()
-        pz = (nn(a, z_own[...]) + nn(b, z_oth[...])).astype(BF)
-        out[:, :, inner:] = pz.reshape(groups, rows, inner)
+    sources = ((x_own, x_oth), (z_own, z_oth))
+    loads = [
+        [
+            pltpu.make_async_copy(ref, held.at[k, pl.ds(j * depth, depth)], sems.at[2 * k + j])
+            for j, ref in enumerate(refs)
+        ]
+        for k, refs in enumerate(sources)
+    ]
+    for pair in loads:
+        for load in pair:
+            load.start()
+
+    def fill(ea, eb):
+        both[:, :depth] = ea[...]
+        both[:, depth:] = eb[...]
 
     @pl.when(place[0] == 1)
     def _():
-        run(e_own, e_oth)
+        fill(e_own, e_oth)
 
     @pl.when(place[0] == 0)
     def _():
-        run(e_oth, e_own)
+        fill(e_oth, e_own)
+
+    stores = []
+    for k in range(2):
+        for load in loads[k]:
+            load.wait()
+        total = nn(both[...], held[k])
+        done[k] = total.astype(BF).reshape(groups, rows, inner)
+        stores.append(
+            pltpu.make_async_copy(
+                done.at[k], out.at[:, :, pl.ds(k * inner, inner)], sems.at[4 + k]
+            )
+        )
+        stores[k].start()
+    for store in stores:
+        store.wait()
 
 
 def small_kernel(part, bc, small):
@@ -304,8 +317,13 @@
         in_specs=[pl.BlockSpec(memory_space=pltpu.SMEM)]
         + [pl.BlockSpec(memory_space=pltpu.VMEM)] * 2
         + [pl.BlockSpec(memory_space=pl.ANY)] * 4,
-        out_specs=pl.BlockSpec(memory_space=pltpu.VMEM),
-        scratch=[pltpu.VMEM((wide, inner), BF)] * 4 + [pltpu.SemaphoreType.DMA((4,))],
+        out_specs=pl.BlockSpec(memory_space=pl.ANY),
+        scratch=[
+            pltpu.VMEM((16 * rows, 2 * wide), BF),
+            pltpu.VMEM((2, 2 * wide, inner), BF),
+            pltpu.VMEM((2, 8, 2 * rows, inner), BF),
+            pltpu.SemaphoreType.DMA((6,)),
+        ],
         limit=PROJECT_LIMIT,
         flops=2 * 16 * rows * 2 * wide * 2 * inner,
     )

time: 188 us -> 188 us (level)
  no operation moved by 1% of the time
where the time goes in v5:
time: 188 us
  waiting for transfers between devices  91.1 us (48%)
  starting transfers between devices  46 us (24%)
  blocking collectives  27.4 us (15%)
  Pallas kernels  16.9 us (9%)
  local copies, waits for them, and re-layouts  4.33 us (2%)
    ppermute x4, waiting for transfers between devices, per_device(): ring_r.append(lax.ppermute(ring_r[-1], 'z', right))  48.6 us
    all_to_all x1, blocking collectives, per_device(): lax.all_to_all(jnp.broadcast_to(moved[None], (8,) + moved.shape), ('x', '...  27.4 us
    ppermute x1, waiting for transfers between devices, per_device(): small_oth = lax.ppermute(small_own, 'yl', pair)  18.4 us
    pallas_call x8, Pallas kernels, call(): pl.pallas_call(body, out_shape=out_shape, in_specs=in_specs, out_specs=ou...  16.9 us
    all_to_all x1, waiting for transfers between devices, per_device(): partial_out = lax.all_to_all(paired, ('x', 'yh'), 0, 0)  8.77 us
    ppermute x3, starting transfers between devices, per_device(): ring_l.append(lax.ppermute(ring_l[-1], 'z', left))  6.92 us
    ppermute x1, starting transfers between devices, per_device(): got = lax.ppermute(send, 'core', pair)  6.8 us
    all_to_all x1, starting transfers between devices, per_device(): part_small = lax.all_to_all(part_small, 'z', 0, 0)  6.1 us
  transfers between devices with their start and end apart: 23, of which 13 were waited for; matrix products, arithmetic and copies ran while one was open for 0% of the time, Pallas kernels for 7%

profile of v5, /device:TPU:1, one launch (start us, length us, event | category | flops | bytes accessed | tf_op | source)
XLA Modules:
  0.0 187.8 jit_solution(2620817604770460701)
XLA Ops:
  2.2 27.4 %all_to_all.20 = bf16[8,64,320]{2,1,0:T(8,128)(2,1)S(1)} all-to-all(bf16[8,64,320]{2,1,0:T(8,128)(2,1)S(1)} %broadcast_in_dim.24), channel_id=1, replica_groups=mesh['z'=8,'yl'=2,'x'=4,'yh'=2,'core'=2] {'x','yh'}, dimensions={0} | all-to-all | bytes 655360 | tf_op jit(solution)/shard_map/all_to_all | solution.py:298
  29.6 3.2 %collective-permute-start.1 = (bf16[512,320]{1,0:T(8,128)(2,1)S(1)}, bf16[512,320]{1,0:T(8,128)(2,1)S(1)}, u32[]{:S(2)}, u32[]{:S(2)}) collective-permute-start(bf16[512,320]{1,0:T(8,128)(2,1)S(1)} %bitcast.18), channel_id=1, source_target_pairs={{0,1},{1,0},{2,3},{3,2},{4,5},{5,4},{6,7},{7,6},{8,9},{9,8},{10,11... | collective-permute-start | bytes 983048 | tf_op jit(solution)/shard_map/ppermute | solution.py:301
  35.2 18.4 %collective-permute-done.4.s_oth = bf16[64,320]{1,0:T(8,128)(2,1)S(1)} collective-permute-done((bf16[64,320]{1,0:T(8,128)(2,1)S(1)}, bf16[64,320]{1,0:T(8,128)(2,1)S(1)}, u32[]{:S(2)}, u32[]{:S(2)}) %collective-permute-start.4) | collective-permute-done | bytes 40992 | tf_op jit(solution)/shard_map/ppermute | solution.py:291
  53.6 1.6 shard_map.128
  55.2 6.1 %all-to-all-start.2 = ((bf16[8,64,128]{2,1,0:T(8,128)(2,1)}), bf16[8,64,128]{2,1,0:T(8,128)(2,1)S(1)}, u32[]{:S(2)}, u32[]{:S(2)}) async-start(bf16[8,64,128]{2,1,0:T(8,128)(2,1)} %shard_map.128), calls=%async_computation.2 | async-start | bytes 262144 | tf_op jit(solution)/shard_map/all_to_all | solution.py:312
  62.8 4.9 %shard_map.127 = bf16[8,64,1280]{2,1,0:T(8,128)(2,1)} custom-call(s32[5]{0:T(128)} %copy-done.8, bf16[512,320]{1,0:T(8,128)(2,1)} %bitcast.20, bf16[512,320]{1,0:T(8,128)(2,1)} %copy-done.2, bf16[320,640]{1,0:T(8,128)(2,1)} %x_own.1, bf16[320,640]{1,0:T(8,128)(2,1)} %copy-done.15, bf16[320,640]{1,0:T(8,128)(2,1)} %z_own.1, bf16[320,640]{1,0:T(8,128)(2,1)} %copy-done.16), custom_call_target="tpu_custom_call" | custom-call | flops 838860800 | bytes 1048576 | tf_op jit(solution)/shard_map/pallas_call | solution.py:38
  67.8 1.5 all-to-all-done.2.part
  69.3 5.3 %all-to-all-start.1 = ((bf16[8,64,1280]{2,1,0:T(8,128)(2,1)}), bf16[8,64,1280]{2,1,0:T(8,128)(2,1)S(1)}, u32[]{:S(2)}, u32[]{:S(2)}) async-start(bf16[8,64,1280]{2,1,0:T(8,128)(2,1)} %shard_map.127), calls=%async_computation.1 | async-start | bytes 2621440 | tf_op jit(solution)/shard_map/all_to_all | solution.py:330
  77.3 37.2 %collective-permute-done.11.r1 = bf16[320,640]{1,0:T(8,128)(2,1)S(1)} collective-permute-done((bf16[320,640]{1,0:T(8,128)(2,1)S(1)}, bf16[320,640]{1,0:T(8,128)(2,1)S(1)}, u32[]{:S(2)}, u32[]{:S(2)}) %collective-permute-start.11) | collective-permute-done | bytes 409632 | tf_op jit(solution)/shard_map/ppermute | solution.py:283
  114.6 2.7 %collective-permute-start.14 = (bf16[320,640]{1,0:T(8,128)(2,1)S(1)}, bf16[320,640]{1,0:T(8,128)(2,1)}, u32[]{:S(2)}, u32[]{:S(2)}) collective-permute-start(bf16[320,640]{1,0:T(8,128)(2,1)S(1)} %collective-permute-done.12.l1), channel_id=1, source_target_pairs={{0,224},{32,0},{64,32},{96,64},{128,96},{160,128},{192,160},{224,1... | collective-permute-start | bytes 1228808 | tf_op jit(solution)/shard_map/ppermute | solution.py:284
  118.0 7.4 %collective-permute-done.13.r2 = bf16[320,640]{1,0:T(8,128)(2,1)S(1)} collective-permute-done((bf16[320,640]{1,0:T(8,128)(2,1)S(1)}, bf16[320,640]{1,0:T(8,128)(2,1)S(1)}, u32[]{:S(2)}, u32[]{:S(2)}) %collective-permute-start.13) | collective-permute-done | bytes 409632 | tf_op jit(solution)/shard_map/ppermute | solution.py:283
  126.3 2.3 %collective-permute-start.5 = (bf16[64,128]{1,0:T(8,128)(2,1)S(1)}, bf16[64,128]{1,0:T(8,128)(2,1)S(1)}, u32[]{:S(2)}, u32[]{:S(2)}) collective-permute-start(bf16[64,128]{1,0:T(8,128)(2,1)S(1)} %get-tuple-element.12), channel_id=1, source_target_pairs={{0,1},{1,0},{2,3},{3,2},{4,5},{5,4},{6,7},{7,6},{8,9},{9,8},{10,11... | collective-permute-start | bytes 49160 | tf_op jit(solution)/shard_map/ppermute | solution.py:336
  128.6 3.0 %collective-permute-start.16 = (bf16[320,640]{1,0:T(8,128)(2,1)}, bf16[320,640]{1,0:T(8,128)(2,1)}, u32[]{:S(2)}, u32[]{:S(2)}) collective-permute-start(bf16[320,640]{1,0:T(8,128)(2,1)} %collective-permute-done.14.l2), channel_id=1, source_target_pairs={{0,224},{32,0},{64,32},{96,64},{128,96},{160,128},{192,160},{224,1... | collective-permute-start | bytes 1228808 | tf_op jit(solution)/shard_map/ppermute | solution.py:284
  131.6 3.9 %collective-permute-done.15.r3 = bf16[320,640]{1,0:T(8,128)(2,1)} collective-permute-done((bf16[320,640]{1,0:T(8,128)(2,1)S(1)}, bf16[320,640]{1,0:T(8,128)(2,1)}, u32[]{:S(2)}, u32[]{:S(2)}) %collective-permute-start.15) | collective-permute-done | bytes 409632 | tf_op jit(solution)/shard_map/ppermute | solution.py:283
  136.4 3.5 %collective-permute-done.6 = bf16[2,64,128]{2,1,0:T(8,128)(2,1)S(1)} collective-permute-done((bf16[2,64,128]{2,1,0:T(8,128)(2,1)S(1)}, bf16[2,64,128]{2,1,0:T(8,128)(2,1)S(1)}, u32[]{:S(2)}, u32[]{:S(2)}) %collective-permute-start.6) | collective-permute-done | bytes 32800 | tf_op jit(solution)/shard_map/ppermute | solution.py:337
  143.7 1.9 %collective-permute-done.8.bc2 = bf16[4,64,128]{2,1,0:T(8,128)(2,1)S(1)} collective-permute-done((bf16[4,64,128]{2,1,0:T(8,128)(2,1)S(1)}, bf16[4,64,128]{2,1,0:T(8,128)(2,1)S(1)}, u32[]{:S(2)}, u32[]{:S(2)}) %collective-permute-start.8) | collective-permute-done | bytes 65568 | tf_op jit(solution)/shard_map/ppermute | solution.py:340
  146.9 5.6 %shard_map.130 = (f32[32,8,640]{2,1,0:T(8,128)S(1)}, f32[32,128]{1,0:T(8,128)S(1)}) custom-call(s32[5]{0:T(128)S(1)} %copy-done.9, bf16[4,64,128]{2,1,0:T(8,128)(2,1)S(1)} %pad_maximum_fusion.bc0, bf16[4,64,128]{2,1,0:T(8,128)(2,1)S(1)} %collective-permute-done.7.bc1, bf16[4,64,128]{2,1,0:T(8,128)(2,1)S(1)} %collective-permute-done.8.bc2, ...), custom_call_target="tpu_custom_call" | custom-call | flops 83886080 | bytes 1048576 | tf_op jit(solution)/shard_map/pallas_call | solution.py:38
  154.2 2.5 %collective-permute-done.10.other = bf16[64,640]{1,0:T(8,128)(2,1)S(1)} collective-permute-done((bf16[64,640]{1,0:T(8,128)(2,1)S(1)}, bf16[64,640]{1,0:T(8,128)(2,1)S(1)}, u32[]{:S(2)}, u32[]{:S(2)}) %collective-permute-start.10) | collective-permute-done | bytes 81952 | tf_op jit(solution)/shard_map/ppermute | solution.py:372
  156.7 2.7 %shard_map.132 = (f32[8,64,384]{2,1,0:T(8,128)S(1)}, bf16[8,64,384]{2,1,0:T(8,128)(2,1)S(1)}) custom-call(s32[5]{0:T(128)S(1)} %copy-done.9, bf16[64,640]{1,0:T(8,128)(2,1)S(1)} %shard_map.131.mine, bf16[64,640]{1,0:T(8,128)(2,1)S(1)} %collective-permute-done.10.other, f32[1,640]{1,0:T(1,128)S(1)} %reshape.28.gain, bf16[320,640]{1,0:T(8,128)(2,1)S(1)} %bitcast.23, ...), custom_call_target="tpu_custom_call" | custom-call | flops 419430400 | bytes 1048576 | tf_op jit(solution)/shard_map/pallas_call | solution.py:38
  159.4 6.8 %collective-permute-start.18 = (bf16[8,64,384]{2,1,0:T(8,128)(2,1)S(1)}, bf16[8,64,384]{2,1,0:T(8,128)(2,1)S(1)}, u32[]{:S(2)}, u32[]{:S(2)}) collective-permute-start(bf16[8,64,384]{2,1,0:T(8,128)(2,1)S(1)} %get-tuple-element.16), channel_id=1, source_target_pairs={{0,1},{1,0},{2,3},{3,2},{4,5},{5,4},{6,7},{7,6},{8,9},{9,8},{10,11... | collective-permute-start | bytes 1179656 | tf_op jit(solution)/shard_map/ppermute | solution.py:396
  168.6 3.5 %all-to-all-start.3 = ((bf16[8,64,384]{2,1,0:T(8,128)(2,1)}), bf16[8,64,384]{2,1,0:T(8,128)(2,1)S(1)}, u32[]{:S(2)}, u32[]{:S(2)}) async-start(bf16[8,64,384]{2,1,0:T(8,128)(2,1)} %shard_map.133), calls=%async_computation.3 | async-start | bytes 786432 | tf_op jit(solution)/shard_map/all_to_all | solution.py:398
  172.7 8.8 %all-to-all-done.3.part = bf16[8,64,384]{2,1,0:T(8,128)(2,1)S(1)} async-done(((bf16[8,64,384]{2,1,0:T(8,128)(2,1)}), bf16[8,64,384]{2,1,0:T(8,128)(2,1)S(1)}, u32[]{:S(2)}, u32[]{:S(2)}) %all-to-all-start.3) | async-done | bytes 393248 | tf_op jit(solution)/shard_map/all_to_all | solution.py:398
  181.6 3.7 %collective-permute-start.19 = (bf16[64,320]{1,0:T(8,128)(2,1)S(1)}, bf16[64,320]{1,0:T(8,128)(2,1)S(1)}, u32[]{:S(2)}, u32[]{:S(2)}) collective-permute-start(bf16[64,320]{1,0:T(8,128)(2,1)S(1)} %shard_map.134), channel_id=1, source_target_pairs={{0,0},{1,16},{16,1},{17,17},{2,2},{3,18},{18,3},{19,19},{4,4},{5,2... | collective-permute-start | bytes 122888 | tf_op jit(solution)/shard_map/ppermute | solution.py:404
  185.3 1.7 collective-permute-done.19
  (88 shorter events, 21.2 us)
Async XLA Ops:
  1.5 0.7 collective-permute-start
  29.6 24.0 %collective-permute-start.1 = (bf16[512,320]{1,0:T(8,128)(2,1)S(1)}, bf16[512,320]{1,0:T(8,128)(2,1)S(1)}, u32[]{:S(2)}, u32[]{:S(2)}) collective-permute-start(bf16[512,320]{1,0:T(8,128)(2,1)S(1)} %bitcast.18), channel_id=1, source_target_pairs={{0,1},{1,0},{2,3},{3,2},{4,5},{5,4},{6,7},{7,6},{8,9},{9,8},{10,11... | collective-permute-start | bytes 983048 | tf_op jit(solution)/shard_map/ppermute | solution.py:301
  32.9 28.5 %collective-permute-start.2 = (bf16[320,640]{1,0:T(8,128)(2,1)S(1)}, bf16[320,640]{1,0:T(8,128)(2,1)S(1)}, u32[]{:S(2)}, u32[]{:S(2)}) collective-permute-start(bf16[320,640]{1,0:T(8,128)(2,1)S(1)} %copy-done.13), channel_id=1, source_target_pairs={{0,16},{16,0},{1,17},{17,1},{2,18},{18,2},{3,19},{19,3},{4,20},{20... | collective-permute-start | bytes 1228808 | tf_op jit(solution)/shard_map/ppermute | solution.py:286
  33.4 27.9 %collective-permute-start.3 = (bf16[320,640]{1,0:T(8,128)(2,1)S(1)}, bf16[320,640]{1,0:T(8,128)(2,1)S(1)}, u32[]{:S(2)}, u32[]{:S(2)}) collective-permute-start(bf16[320,640]{1,0:T(8,128)(2,1)S(1)} %copy-done.14), channel_id=1, source_target_pairs={{0,16},{16,0},{1,17},{17,1},{2,18},{18,2},{3,19},{19,3},{4,20},{20... | collective-permute-start | bytes 1228808 | tf_op jit(solution)/shard_map/ppermute | solution.py:287
  34.5 19.1 %collective-permute-start.4 = (bf16[64,320]{1,0:T(8,128)(2,1)S(1)}, bf16[64,320]{1,0:T(8,128)(2,1)S(1)}, u32[]{:S(2)}, u32[]{:S(2)}) collective-permute-start(bf16[64,320]{1,0:T(8,128)(2,1)S(1)} %maximum_maximum_fusion.s_own), channel_id=1, source_target_pairs={{0,16},{16,0},{1,17},{17,1},{2,18},{18,2},{3,19},{19,3},{4,20},{20... | collective-permute-start | bytes 122888 | tf_op jit(solution)/shard_map/ppermute | solution.py:291
  55.2 14.0 %all-to-all-start.2 = ((bf16[8,64,128]{2,1,0:T(8,128)(2,1)}), bf16[8,64,128]{2,1,0:T(8,128)(2,1)S(1)}, u32[]{:S(2)}, u32[]{:S(2)}) async-start(bf16[8,64,128]{2,1,0:T(8,128)(2,1)} %shard_map.128), calls=%async_computation.2 | async-start | bytes 262144 | tf_op jit(solution)/shard_map/all_to_all | solution.py:312
  67.8 79.1 %copy-start.9 = (s32[5]{0:T(128)S(1)}, s32[5]{0:T(128)}, u32[]{:S(2)}) copy-start(s32[5]{0:T(128)} %copy-done.8) | copy-start | bytes 64
  69.3 83.2 %all-to-all-start.1 = ((bf16[8,64,1280]{2,1,0:T(8,128)(2,1)}), bf16[8,64,1280]{2,1,0:T(8,128)(2,1)S(1)}, u32[]{:S(2)}, u32[]{:S(2)}) async-start(bf16[8,64,1280]{2,1,0:T(8,128)(2,1)} %shard_map.127), calls=%async_computation.1 | async-start | bytes 2621440 | tf_op jit(solution)/shard_map/all_to_all | solution.py:330
  74.6 40.0 %collective-permute-start.11 = (bf16[320,640]{1,0:T(8,128)(2,1)S(1)}, bf16[320,640]{1,0:T(8,128)(2,1)S(1)}, u32[]{:S(2)}, u32[]{:S(2)}) collective-permute-start(bf16[320,640]{1,0:T(8,128)(2,1)S(1)} %bitcast.21), channel_id=1, source_target_pairs={{0,32},{32,64},{64,96},{96,128},{128,160},{160,192},{192,224},{224... | collective-permute-start | bytes 1228808 | tf_op jit(solution)/shard_map/ppermute | solution.py:283
  76.0 38.5 %collective-permute-start.12 = (bf16[320,640]{1,0:T(8,128)(2,1)S(1)}, bf16[320,640]{1,0:T(8,128)(2,1)S(1)}, u32[]{:S(2)}, u32[]{:S(2)}) collective-permute-start(bf16[320,640]{1,0:T(8,128)(2,1)S(1)} %bitcast.22), channel_id=1, source_target_pairs={{0,224},{32,0},{64,32},{96,64},{128,96},{160,128},{192,160},{224,1... | collective-permute-start | bytes 1228808 | tf_op jit(solution)/shard_map/ppermute | solution.py:284
  114.6 10.8 %collective-permute-start.13 = (bf16[320,640]{1,0:T(8,128)(2,1)S(1)}, bf16[320,640]{1,0:T(8,128)(2,1)S(1)}, u32[]{:S(2)}, u32[]{:S(2)}) collective-permute-start(bf16[320,640]{1,0:T(8,128)(2,1)S(1)} %collective-permute-done.11.r1), channel_id=1, source_target_pairs={{0,32},{32,64},{64,96},{96,128},{128,160},{160,192},{192,224},{224... | collective-permute-start | bytes 1228808 | tf_op jit(solution)/shard_map/ppermute | solution.py:283
  114.6 14.0 %collective-permute-start.14 = (bf16[320,640]{1,0:T(8,128)(2,1)S(1)}, bf16[320,640]{1,0:T(8,128)(2,1)}, u32[]{:S(2)}, u32[]{:S(2)}) collective-permute-start(bf16[320,640]{1,0:T(8,128)(2,1)S(1)} %collective-permute-done.12.l1), channel_id=1, source_target_pairs={{0,224},{32,0},{64,32},{96,64},{128,96},{160,128},{192,160},{224,1... | collective-permute-start | bytes 1228808 | tf_op jit(solution)/shard_map/ppermute | solution.py:284
  125.4 10.1 %collective-permute-start.15 = (bf16[320,640]{1,0:T(8,128)(2,1)S(1)}, bf16[320,640]{1,0:T(8,128)(2,1)}, u32[]{:S(2)}, u32[]{:S(2)}) collective-permute-start(bf16[320,640]{1,0:T(8,128)(2,1)S(1)} %collective-permute-done.13.r2), channel_id=1, source_target_pairs={{0,32},{32,64},{64,96},{96,128},{128,160},{160,192},{192,224},{224... | collective-permute-start | bytes 1228808 | tf_op jit(solution)/shard_map/ppermute | solution.py:283
  126.3 9.2 %collective-permute-start.5 = (bf16[64,128]{1,0:T(8,128)(2,1)S(1)}, bf16[64,128]{1,0:T(8,128)(2,1)S(1)}, u32[]{:S(2)}, u32[]{:S(2)}) collective-permute-start(bf16[64,128]{1,0:T(8,128)(2,1)S(1)} %get-tuple-element.12), channel_id=1, source_target_pairs={{0,1},{1,0},{2,3},{3,2},{4,5},{5,4},{6,7},{7,6},{8,9},{9,8},{10,11... | collective-permute-start | bytes 49160 | tf_op jit(solution)/shard_map/ppermute | solution.py:336
  128.6 25.6 %collective-permute-start.16 = (bf16[320,640]{1,0:T(8,128)(2,1)}, bf16[320,640]{1,0:T(8,128)(2,1)}, u32[]{:S(2)}, u32[]{:S(2)}) collective-permute-start(bf16[320,640]{1,0:T(8,128)(2,1)} %collective-permute-done.14.l2), channel_id=1, source_target_pairs={{0,224},{32,0},{64,32},{96,64},{128,96},{160,128},{192,160},{224,1... | collective-permute-start | bytes 1228808 | tf_op jit(solution)/shard_map/ppermute | solution.py:284
  135.5 18.7 %collective-permute-start.17 = (bf16[320,640]{1,0:T(8,128)(2,1)}, bf16[320,640]{1,0:T(8,128)(2,1)}, u32[]{:S(2)}, u32[]{:S(2)}) collective-permute-start(bf16[320,640]{1,0:T(8,128)(2,1)} %collective-permute-done.15.r3), channel_id=1, source_target_pairs={{0,32},{32,64},{64,96},{96,128},{128,160},{160,192},{192,224},{224... | collective-permute-start | bytes 1228808 | tf_op jit(solution)/shard_map/ppermute | solution.py:285
  135.5 4.4 %collective-permute-start.6 = (bf16[2,64,128]{2,1,0:T(8,128)(2,1)S(1)}, bf16[2,64,128]{2,1,0:T(8,128)(2,1)S(1)}, u32[]{:S(2)}, u32[]{:S(2)}) collective-permute-start(bf16[2,64,128]{2,1,0:T(8,128)(2,1)S(1)} %pad_maximum_fusion.1), channel_id=1, source_target_pairs={{0,2},{2,0},{1,3},{3,1},{4,6},{6,4},{5,7},{7,5},{8,10},{10,8},{9,1... | collective-permute-start | bytes 98312 | tf_op jit(solution)/shard_map/ppermute | solution.py:337
  139.9 3.8 %collective-permute-start.7 = (bf16[4,64,128]{2,1,0:T(8,128)(2,1)S(1)}, bf16[4,64,128]{2,1,0:T(8,128)(2,1)S(1)}, u32[]{:S(2)}, u32[]{:S(2)}) collective-permute-start(bf16[4,64,128]{2,1,0:T(8,128)(2,1)S(1)} %pad_maximum_fusion.bc0), channel_id=1, source_target_pairs={{4,0},{8,4},{12,8},{0,12},{5,1},{9,5},{13,9},{1,13},{6,2},{10,6},{... | collective-permute-start | bytes 196616 | tf_op jit(solution)/shard_map/ppermute | solution.py:340
  141.0 4.6 %collective-permute-start.8 = (bf16[4,64,128]{2,1,0:T(8,128)(2,1)S(1)}, bf16[4,64,128]{2,1,0:T(8,128)(2,1)S(1)}, u32[]{:S(2)}, u32[]{:S(2)}) collective-permute-start(bf16[4,64,128]{2,1,0:T(8,128)(2,1)S(1)} %pad_maximum_fusion.bc0), channel_id=1, source_target_pairs={{8,0},{12,4},{0,8},{4,12},{9,1},{13,5},{1,9},{5,13},{10,2},{14,6},... | collective-permute-start | bytes 196616 | tf_op jit(solution)/shard_map/ppermute | solution.py:340
  142.2 4.7 %collective-permute-start.9 = (bf16[4,64,128]{2,1,0:T(8,128)(2,1)S(1)}, bf16[4,64,128]{2,1,0:T(8,128)(2,1)S(1)}, u32[]{:S(2)}, u32[]{:S(2)}) collective-permute-start(bf16[4,64,128]{2,1,0:T(8,128)(2,1)S(1)} %pad_maximum_fusion.bc0), channel_id=1, source_target_pairs={{12,0},{0,4},{4,8},{8,12},{13,1},{1,5},{5,9},{9,13},{14,2},{2,6},{... | collective-permute-start | bytes 196616 | tf_op jit(solution)/shard_map/ppermute | solution.py:340
  153.3 3.4 %collective-permute-start.10 = (bf16[64,640]{1,0:T(8,128)(2,1)S(1)}, bf16[64,640]{1,0:T(8,128)(2,1)S(1)}, u32[]{:S(2)}, u32[]{:S(2)}) collective-permute-start(bf16[64,640]{1,0:T(8,128)(2,1)S(1)} %shard_map.131.mine), channel_id=1, source_target_pairs={{0,16},{16,0},{1,17},{17,1},{2,18},{18,2},{3,19},{19,3},{4,20},{20... | collective-permute-start | bytes 245768 | tf_op jit(solution)/shard_map/ppermute | solution.py:372
  159.4 8.1 %collective-permute-start.18 = (bf16[8,64,384]{2,1,0:T(8,128)(2,1)S(1)}, bf16[8,64,384]{2,1,0:T(8,128)(2,1)S(1)}, u32[]{:S(2)}, u32[]{:S(2)}) collective-permute-start(bf16[8,64,384]{2,1,0:T(8,128)(2,1)S(1)} %get-tuple-element.16), channel_id=1, source_target_pairs={{0,1},{1,0},{2,3},{3,2},{4,5},{5,4},{6,7},{7,6},{8,9},{9,8},{10,11... | collective-permute-start | bytes 1179656 | tf_op jit(solution)/shard_map/ppermute | solution.py:396
  168.6 12.9 %all-to-all-start.3 = ((bf16[8,64,384]{2,1,0:T(8,128)(2,1)}), bf16[8,64,384]{2,1,0:T(8,128)(2,1)S(1)}, u32[]{:S(2)}, u32[]{:S(2)}) async-start(bf16[8,64,384]{2,1,0:T(8,128)(2,1)} %shard_map.133), calls=%async_computation.3 | async-start | bytes 786432 | tf_op jit(solution)/shard_map/all_to_all | solution.py:398
  181.6 5.4 %collective-permute-start.19 = (bf16[64,320]{1,0:T(8,128)(2,1)S(1)}, bf16[64,320]{1,0:T(8,128)(2,1)S(1)}, u32[]{:S(2)}, u32[]{:S(2)}) collective-permute-start(bf16[64,320]{1,0:T(8,128)(2,1)S(1)} %shard_map.134), channel_id=1, source_target_pairs={{0,0},{1,16},{16,1},{17,17},{2,2},{3,18},{18,3},{19,19},{4,4},{5,2... | collective-permute-start | bytes 122888 | tf_op jit(solution)/shard_map/ppermute | solution.py:404
  (21 other events, 345.9 us)

commit v6 on v5

--- a/solution.py
+++ b/solution.py
@@ -205,7 +205,7 @@
     out[...] = jnp.concatenate([gg1, gg2], 0).astype(BF)
 
 
-def output_kernel(place, mine, other, gain, own, r1, l1, r2, l2, r3, l3, r4, keep, send):
+def output_kernel(place, mine, other, gain, own, r1, l1, r2, l2, r3, l3, r4, l4, keep, send):
     same = place[0]
     z = place[1]
     groups, rows, _ = keep.shape
@@ -217,9 +217,10 @@
     hi = ss.astype(BF).astype(F32)
     lane = lax.broadcasted_iota(jnp.int32, (2 * rows, 64), 1)
     tail = jnp.where(lane == 0, hi, jnp.where(lane == 1, ss - hi, 0.0))
-    order = ((0, own), (7, r1), (1, l1), (6, r2), (2, l2), (5, r3), (3, l3), (4, r4))
+    order = ((0, own), (7, r1), (1, l1), (6, r2), (2, l2), (5, r3), (3, l3), (4, None))
     for shift, w in order:
-        block = jnp.concatenate([nt(v, w[...]), tail], 1)
+        w = jnp.concatenate([r4[...], l4[...]], 0) if w is None else w[...]
+        block = jnp.concatenate([nt(v, w), tail], 1)
         at = lax.rem(z + shift, groups)
         keep[at] = block[:rows]
         send[at] = block[rows:].astype(BF)
@@ -282,7 +283,8 @@
     for _ in range(1, 4):
         ring_r.append(lax.ppermute(ring_r[-1], "z", right))
         ring_l.append(lax.ppermute(ring_l[-1], "z", left))
-    ring_r.append(lax.ppermute(ring_r[-1], "z", right))
+    far_r = lax.ppermute(ring_r[3][: wide // 2], "z", right)
+    far_l = lax.ppermute(ring_l[3][wide // 2 :], "z", left)
     x_oth = lax.ppermute(x_weight, "yl", pair)
     z_oth = lax.ppermute(z_weight, "yl", pair)
     small_own = jnp.concatenate(
@@ -388,7 +390,8 @@
             ring_l[2],
             ring_r[3],
             ring_l[3],
-            ring_r[4],
+            far_r,
+            far_l,
         ),
         in_smem=1,
         flops=2 * 4 * rows * inner * 8 * wide,

time: 188 us -> 187 us (level)
  waiting for transfers between devices: 91.1 us -> 85.5 us
  starting transfers between devices: 46 us -> 48.9 us
    ppermute x1, waiting for transfers between devices: 3.51 us -> 0.01 us  [per_device(): bc4 = jnp.concatenate([bc2, lax.ppermute(bc2, 'yh', pair)], 0)]
    ppermute x0 -> x2, starting transfers between devices: none -> 2.68 us  [the longest x1 2.67 us: per_device(): far_l = lax.ppermute(ring_l[3][wide // 2:], 'z', left)]
    ppermute x4 -> x3, waiting for transfers between devices: 48.6 us -> 46.1 us  [per_device(): ring_r.append(lax.ppermute(ring_r[-1], 'z', right))]
  transfers between devices with their start and end apart: 23 -> 24, of which waited for: 13 -> 13; matrix products, arithmetic and copies ran while one was open for 0% -> 1% of each run, Pallas kernels for 7% -> 7%
where the time goes in v6:
time: 187 us; the launch traced here: 186 us
  waiting for transfers between devices  85.5 us (46%)
  starting transfers between devices  48.9 us (26%)
  blocking collectives  27.4 us (15%)
  Pallas kernels  16.6 us (9%)
  local copies, waits for them, and re-layouts  5.76 us (3%)
    ppermute x3, waiting for transfers between devices, per_device(): ring_r.append(lax.ppermute(ring_r[-1], 'z', right))  46.1 us
    all_to_all x1, blocking collectives, per_device(): lax.all_to_all(jnp.broadcast_to(moved[None], (8,) + moved.shape), ('x', '...  27.4 us
    ppermute x1, waiting for transfers between devices, per_device(): small_oth = lax.ppermute(small_own, 'yl', pair)  18.4 us
    pallas_call x8, Pallas kernels, call(): pl.pallas_call(body, out_shape=out_shape, in_specs=in_specs, out_specs=ou...  16.6 us
    all_to_all x1, waiting for transfers between devices, per_device(): partial_out = lax.all_to_all(paired, ('x', 'yh'), 0, 0)  8.77 us
    ppermute x3, starting transfers between devices, per_device(): ring_l.append(lax.ppermute(ring_l[-1], 'z', left))  7.11 us
    ppermute x1, starting transfers between devices, per_device(): got = lax.ppermute(send, 'core', pair)  6.43 us
    all_to_all x1, starting transfers between devices, per_device(): part_small = lax.all_to_all(part_small, 'z', 0, 0)  6.1 us
  transfers between devices with their start and end apart: 24, of which 13 were waited for; matrix products, arithmetic and copies ran while one was open for 1% of the time, Pallas kernels for 7%

profile of v6, /device:TPU:1, one launch (start us, length us, event | category | flops | bytes accessed | tf_op | source)
XLA Modules:
  0.0 186.4 jit_solution(10682792090159110957)
XLA Ops:
  2.2 27.4 %all_to_all.20 = bf16[8,64,320]{2,1,0:T(8,128)(2,1)S(1)} all-to-all(bf16[8,64,320]{2,1,0:T(8,128)(2,1)S(1)} %broadcast_in_dim.24), channel_id=1, replica_groups=mesh['z'=8,'yl'=2,'x'=4,'yh'=2,'core'=2] {'x','yh'}, dimensions={0} | all-to-all | bytes 655360 | tf_op jit(solution)/shard_map/all_to_all | solution.py:300
  29.6 3.2 %collective-permute-start.1 = (bf16[512,320]{1,0:T(8,128)(2,1)S(1)}, bf16[512,320]{1,0:T(8,128)(2,1)S(1)}, u32[]{:S(2)}, u32[]{:S(2)}) collective-permute-start(bf16[512,320]{1,0:T(8,128)(2,1)S(1)} %bitcast.18), channel_id=1, source_target_pairs={{0,1},{1,0},{2,3},{3,2},{4,5},{5,4},{6,7},{7,6},{8,9},{9,8},{10,11... | collective-permute-start | bytes 983048 | tf_op jit(solution)/shard_map/ppermute | solution.py:303
  35.2 18.4 %collective-permute-done.4.s_oth = bf16[64,320]{1,0:T(8,128)(2,1)S(1)} collective-permute-done((bf16[64,320]{1,0:T(8,128)(2,1)S(1)}, bf16[64,320]{1,0:T(8,128)(2,1)S(1)}, u32[]{:S(2)}, u32[]{:S(2)}) %collective-permute-start.4) | collective-permute-done | bytes 40992 | tf_op jit(solution)/shard_map/ppermute | solution.py:293
  53.6 1.6 shard_map.128
  55.2 6.1 %all-to-all-start.2 = ((bf16[8,64,128]{2,1,0:T(8,128)(2,1)}), bf16[8,64,128]{2,1,0:T(8,128)(2,1)S(1)}, u32[]{:S(2)}, u32[]{:S(2)}) async-start(bf16[8,64,128]{2,1,0:T(8,128)(2,1)} %shard_map.128), calls=%async_computation.2 | async-start | bytes 262144 | tf_op jit(solution)/shard_map/all_to_all | solution.py:314
  62.9 4.9 %shard_map.127 = bf16[8,64,1280]{2,1,0:T(8,128)(2,1)} custom-call(s32[5]{0:T(128)} %copy-done.13, bf16[512,320]{1,0:T(8,128)(2,1)} %bitcast.20, bf16[512,320]{1,0:T(8,128)(2,1)} %copy-done.2, bf16[320,640]{1,0:T(8,128)(2,1)} %x_own.1, bf16[320,640]{1,0:T(8,128)(2,1)} %copy-done.20, bf16[320,640]{1,0:T(8,128)(2,1)} %z_own.1, bf16[320,640]{1,0:T(8,128)(2,1)} %copy-done.21), custom_call_target="tpu_custom_call" | custom-call | flops 838860800 | bytes 1048576 | tf_op jit(solution)/shard_map/pallas_call | solution.py:38
  69.3 5.4 %all-to-all-start.1 = ((bf16[8,64,1280]{2,1,0:T(8,128)(2,1)}), bf16[8,64,1280]{2,1,0:T(8,128)(2,1)S(1)}, u32[]{:S(2)}, u32[]{:S(2)}) async-start(bf16[8,64,1280]{2,1,0:T(8,128)(2,1)} %shard_map.127), calls=%async_computation.1 | async-start | bytes 2621440 | tf_op jit(solution)/shard_map/all_to_all | solution.py:332
  74.6 1.5 collective-permute-start.11
  77.4 37.2 %collective-permute-done.11.r1 = bf16[320,640]{1,0:T(8,128)(2,1)S(1)} collective-permute-done((bf16[320,640]{1,0:T(8,128)(2,1)S(1)}, bf16[320,640]{1,0:T(8,128)(2,1)S(1)}, u32[]{:S(2)}, u32[]{:S(2)}) %collective-permute-start.11) | collective-permute-done | bytes 409632 | tf_op jit(solution)/shard_map/ppermute | solution.py:284
  115.4 2.7 %collective-permute-start.14 = (bf16[320,640]{1,0:T(8,128)(2,1)S(1)}, bf16[320,640]{1,0:T(8,128)(2,1)S(1)}, u32[]{:S(2)}, u32[]{:S(2)}) collective-permute-start(bf16[320,640]{1,0:T(8,128)(2,1)S(1)} %collective-permute-done.12.l1), channel_id=1, source_target_pairs={{0,224},{32,0},{64,32},{96,64},{128,96},{160,128},{192,160},{224,1... | collective-permute-start | bytes 1228808 | tf_op jit(solution)/shard_map/ppermute | solution.py:285
  118.8 6.6 %collective-permute-done.13.r2 = bf16[320,640]{1,0:T(8,128)(2,1)S(1)} collective-permute-done((bf16[320,640]{1,0:T(8,128)(2,1)S(1)}, bf16[320,640]{1,0:T(8,128)(2,1)S(1)}, u32[]{:S(2)}, u32[]{:S(2)}) %collective-permute-start.13) | collective-permute-done | bytes 409632 | tf_op jit(solution)/shard_map/ppermute | solution.py:284
  125.5 3.1 %collective-permute-start.16 = (bf16[320,640]{1,0:T(8,128)(2,1)S(1)}, bf16[320,640]{1,0:T(8,128)(2,1)S(1)}, u32[]{:S(2)}, u32[]{:S(2)}) collective-permute-start(bf16[320,640]{1,0:T(8,128)(2,1)S(1)} %collective-permute-done.14.l2), channel_id=1, source_target_pairs={{0,224},{32,0},{64,32},{96,64},{128,96},{160,128},{192,160},{224,1... | collective-permute-start | bytes 1228808 | tf_op jit(solution)/shard_map/ppermute | solution.py:285
  128.8 2.8 %collective-permute-start.5 = (bf16[64,128]{1,0:T(8,128)(2,1)S(1)}, bf16[64,128]{1,0:T(8,128)(2,1)S(1)}, u32[]{:S(2)}, u32[]{:S(2)}) collective-permute-start(bf16[64,128]{1,0:T(8,128)(2,1)S(1)} %get-tuple-element.12), channel_id=1, source_target_pairs={{0,1},{1,0},{2,3},{3,2},{4,5},{5,4},{6,7},{7,6},{8,9},{9,8},{10,11... | collective-permute-start | bytes 49160 | tf_op jit(solution)/shard_map/ppermute | solution.py:338
  133.2 2.2 %collective-permute-done.15.r3 = bf16[320,640]{1,0:T(8,128)(2,1)S(1)} collective-permute-done((bf16[320,640]{1,0:T(8,128)(2,1)S(1)}, bf16[320,640]{1,0:T(8,128)(2,1)S(1)}, u32[]{:S(2)}, u32[]{:S(2)}) %collective-permute-start.15) | collective-permute-done | bytes 409632 | tf_op jit(solution)/shard_map/ppermute | solution.py:284
  136.9 2.7 %collective-permute-start.18 = (bf16[160,640]{1,0:T(8,128)(2,1)}, bf16[160,640]{1,0:T(8,128)(2,1)}, u32[]{:S(2)}, u32[]{:S(2)}) collective-permute-start(bf16[160,640]{1,0:T(8,128)(2,1)} %slice.9), channel_id=1, source_target_pairs={{0,224},{32,0},{64,32},{96,64},{128,96},{160,128},{192,160},{224,1... | collective-permute-start | bytes 614408 | tf_op jit(solution)/shard_map/ppermute | solution.py:287
  142.8 2.3 %collective-permute-done.8.bc2 = bf16[4,64,128]{2,1,0:T(8,128)(2,1)S(1)} collective-permute-done((bf16[4,64,128]{2,1,0:T(8,128)(2,1)S(1)}, bf16[4,64,128]{2,1,0:T(8,128)(2,1)S(1)}, u32[]{:S(2)}, u32[]{:S(2)}) %collective-permute-start.8) | collective-permute-done | bytes 65568 | tf_op jit(solution)/shard_map/ppermute | solution.py:342
  146.2 5.6 %shard_map.130 = (f32[32,8,640]{2,1,0:T(8,128)S(1)}, f32[32,128]{1,0:T(8,128)S(1)}) custom-call(s32[5]{0:T(128)S(1)} %copy-done.14, bf16[4,64,128]{2,1,0:T(8,128)(2,1)S(1)} %pad_maximum_fusion.bc0, bf16[4,64,128]{2,1,0:T(8,128)(2,1)S(1)} %collective-permute-done.7.bc1, bf16[4,64,128]{2,1,0:T(8,128)(2,1)S(1)} %collective-permute-done.8.bc2, ...), custom_call_target="tpu_custom_call" | custom-call | flops 83886080 | bytes 1048576 | tf_op jit(solution)/shard_map/pallas_call | solution.py:38
  153.6 2.4 %collective-permute-done.10.other = bf16[64,640]{1,0:T(8,128)(2,1)S(1)} collective-permute-done((bf16[64,640]{1,0:T(8,128)(2,1)S(1)}, bf16[64,640]{1,0:T(8,128)(2,1)S(1)}, u32[]{:S(2)}, u32[]{:S(2)}) %collective-permute-start.10) | collective-permute-done | bytes 81952 | tf_op jit(solution)/shard_map/ppermute | solution.py:374
  156.0 2.3 %shard_map.132 = (f32[8,64,384]{2,1,0:T(8,128)S(1)}, bf16[8,64,384]{2,1,0:T(8,128)(2,1)S(1)}) custom-call(s32[5]{0:T(128)S(1)} %copy-done.14, bf16[64,640]{1,0:T(8,128)(2,1)S(1)} %shard_map.131.mine, bf16[64,640]{1,0:T(8,128)(2,1)S(1)} %collective-permute-done.10.other, f32[1,640]{1,0:T(1,128)S(1)} %reshape.28.gain, bf16[320,640]{1,0:T(8,128)(2,1)S(1)} %bitcast.23, ...), custom_call_target="tpu_custom_call" | custom-call | flops 419430400 | bytes 1048576 | tf_op jit(solution)/shard_map/pallas_call | solution.py:38
  158.3 6.4 %collective-permute-start.19 = (bf16[8,64,384]{2,1,0:T(8,128)(2,1)S(1)}, bf16[8,64,384]{2,1,0:T(8,128)(2,1)S(1)}, u32[]{:S(2)}, u32[]{:S(2)}) collective-permute-start(bf16[8,64,384]{2,1,0:T(8,128)(2,1)S(1)} %get-tuple-element.16), channel_id=1, source_target_pairs={{0,1},{1,0},{2,3},{3,2},{4,5},{5,4},{6,7},{7,6},{8,9},{9,8},{10,11... | collective-permute-start | bytes 1179656 | tf_op jit(solution)/shard_map/ppermute | solution.py:399
  167.2 3.5 %all-to-all-start.3 = ((bf16[8,64,384]{2,1,0:T(8,128)(2,1)}), bf16[8,64,384]{2,1,0:T(8,128)(2,1)S(1)}, u32[]{:S(2)}, u32[]{:S(2)}) async-start(bf16[8,64,384]{2,1,0:T(8,128)(2,1)} %shard_map.133), calls=%async_computation.3 | async-start | bytes 786432 | tf_op jit(solution)/shard_map/all_to_all | solution.py:401
  171.3 8.8 %all-to-all-done.3.part = bf16[8,64,384]{2,1,0:T(8,128)(2,1)S(1)} async-done(((bf16[8,64,384]{2,1,0:T(8,128)(2,1)}), bf16[8,64,384]{2,1,0:T(8,128)(2,1)S(1)}, u32[]{:S(2)}, u32[]{:S(2)}) %all-to-all-start.3) | async-done | bytes 393248 | tf_op jit(solution)/shard_map/all_to_all | solution.py:401
  180.3 3.7 %collective-permute-start.20 = (bf16[64,320]{1,0:T(8,128)(2,1)S(1)}, bf16[64,320]{1,0:T(8,128)(2,1)S(1)}, u32[]{:S(2)}, u32[]{:S(2)}) collective-permute-start(bf16[64,320]{1,0:T(8,128)(2,1)S(1)} %shard_map.134), channel_id=1, source_target_pairs={{0,0},{1,16},{16,1},{17,17},{2,2},{3,18},{18,3},{19,19},{4,4},{5,2... | collective-permute-start | bytes 122888 | tf_op jit(solution)/shard_map/ppermute | solution.py:407
  184.0 1.7 collective-permute-done.20
  (102 shorter events, 22.8 us)
Async XLA Ops:
  1.5 0.7 collective-permute-start
  29.6 24.0 %collective-permute-start.1 = (bf16[512,320]{1,0:T(8,128)(2,1)S(1)}, bf16[512,320]{1,0:T(8,128)(2,1)S(1)}, u32[]{:S(2)}, u32[]{:S(2)}) collective-permute-start(bf16[512,320]{1,0:T(8,128)(2,1)S(1)} %bitcast.18), channel_id=1, source_target_pairs={{0,1},{1,0},{2,3},{3,2},{4,5},{5,4},{6,7},{7,6},{8,9},{9,8},{10,11... | collective-permute-start | bytes 983048 | tf_op jit(solution)/shard_map/ppermute | solution.py:303
  32.9 28.5 %collective-permute-start.2 = (bf16[320,640]{1,0:T(8,128)(2,1)S(1)}, bf16[320,640]{1,0:T(8,128)(2,1)S(1)}, u32[]{:S(2)}, u32[]{:S(2)}) collective-permute-start(bf16[320,640]{1,0:T(8,128)(2,1)S(1)} %copy-done.18), channel_id=1, source_target_pairs={{0,16},{16,0},{1,17},{17,1},{2,18},{18,2},{3,19},{19,3},{4,20},{20... | collective-permute-start | bytes 1228808 | tf_op jit(solution)/shard_map/ppermute | solution.py:288
  33.4 27.9 %collective-permute-start.3 = (bf16[320,640]{1,0:T(8,128)(2,1)S(1)}, bf16[320,640]{1,0:T(8,128)(2,1)S(1)}, u32[]{:S(2)}, u32[]{:S(2)}) collective-permute-start(bf16[320,640]{1,0:T(8,128)(2,1)S(1)} %copy-done.19), channel_id=1, source_target_pairs={{0,16},{16,0},{1,17},{17,1},{2,18},{18,2},{3,19},{19,3},{4,20},{20... | collective-permute-start | bytes 1228808 | tf_op jit(solution)/shard_map/ppermute | solution.py:289
  34.5 19.1 %collective-permute-start.4 = (bf16[64,320]{1,0:T(8,128)(2,1)S(1)}, bf16[64,320]{1,0:T(8,128)(2,1)S(1)}, u32[]{:S(2)}, u32[]{:S(2)}) collective-permute-start(bf16[64,320]{1,0:T(8,128)(2,1)S(1)} %maximum_maximum_fusion.s_own), channel_id=1, source_target_pairs={{0,16},{16,0},{1,17},{17,1},{2,18},{18,2},{3,19},{19,3},{4,20},{20... | collective-permute-start | bytes 122888 | tf_op jit(solution)/shard_map/ppermute | solution.py:293
  55.2 14.0 %all-to-all-start.2 = ((bf16[8,64,128]{2,1,0:T(8,128)(2,1)}), bf16[8,64,128]{2,1,0:T(8,128)(2,1)S(1)}, u32[]{:S(2)}, u32[]{:S(2)}) async-start(bf16[8,64,128]{2,1,0:T(8,128)(2,1)} %shard_map.128), calls=%async_computation.2 | async-start | bytes 262144 | tf_op jit(solution)/shard_map/all_to_all | solution.py:314
  69.3 82.5 %all-to-all-start.1 = ((bf16[8,64,1280]{2,1,0:T(8,128)(2,1)}), bf16[8,64,1280]{2,1,0:T(8,128)(2,1)S(1)}, u32[]{:S(2)}, u32[]{:S(2)}) async-start(bf16[8,64,1280]{2,1,0:T(8,128)(2,1)} %shard_map.127), calls=%async_computation.1 | async-start | bytes 2621440 | tf_op jit(solution)/shard_map/all_to_all | solution.py:332
  74.6 40.0 %collective-permute-start.11 = (bf16[320,640]{1,0:T(8,128)(2,1)S(1)}, bf16[320,640]{1,0:T(8,128)(2,1)S(1)}, u32[]{:S(2)}, u32[]{:S(2)}) collective-permute-start(bf16[320,640]{1,0:T(8,128)(2,1)S(1)} %bitcast.21), channel_id=1, source_target_pairs={{0,32},{32,64},{64,96},{96,128},{128,160},{160,192},{192,224},{224... | collective-permute-start | bytes 1228808 | tf_op jit(solution)/shard_map/ppermute | solution.py:284
  76.1 39.3 %collective-permute-start.12 = (bf16[320,640]{1,0:T(8,128)(2,1)S(1)}, bf16[320,640]{1,0:T(8,128)(2,1)S(1)}, u32[]{:S(2)}, u32[]{:S(2)}) collective-permute-start(bf16[320,640]{1,0:T(8,128)(2,1)S(1)} %bitcast.22), channel_id=1, source_target_pairs={{0,224},{32,0},{64,32},{96,64},{128,96},{160,128},{192,160},{224,1... | collective-permute-start | bytes 1228808 | tf_op jit(solution)/shard_map/ppermute | solution.py:285
  114.6 10.8 %collective-permute-start.13 = (bf16[320,640]{1,0:T(8,128)(2,1)S(1)}, bf16[320,640]{1,0:T(8,128)(2,1)S(1)}, u32[]{:S(2)}, u32[]{:S(2)}) collective-permute-start(bf16[320,640]{1,0:T(8,128)(2,1)S(1)} %collective-permute-done.11.r1), channel_id=1, source_target_pairs={{0,32},{32,64},{64,96},{96,128},{128,160},{160,192},{192,224},{224... | collective-permute-start | bytes 1228808 | tf_op jit(solution)/shard_map/ppermute | solution.py:284
  115.4 10.1 %collective-permute-start.14 = (bf16[320,640]{1,0:T(8,128)(2,1)S(1)}, bf16[320,640]{1,0:T(8,128)(2,1)S(1)}, u32[]{:S(2)}, u32[]{:S(2)}) collective-permute-start(bf16[320,640]{1,0:T(8,128)(2,1)S(1)} %collective-permute-done.12.l1), channel_id=1, source_target_pairs={{0,224},{32,0},{64,32},{96,64},{128,96},{160,128},{192,160},{224,1... | collective-permute-start | bytes 1228808 | tf_op jit(solution)/shard_map/ppermute | solution.py:285
  125.5 10.0 %collective-permute-start.15 = (bf16[320,640]{1,0:T(8,128)(2,1)S(1)}, bf16[320,640]{1,0:T(8,128)(2,1)S(1)}, u32[]{:S(2)}, u32[]{:S(2)}) collective-permute-start(bf16[320,640]{1,0:T(8,128)(2,1)S(1)} %collective-permute-done.13.r2), channel_id=1, source_target_pairs={{0,32},{32,64},{64,96},{96,128},{128,160},{160,192},{192,224},{224... | collective-permute-start | bytes 1228808 | tf_op jit(solution)/shard_map/ppermute | solution.py:284
  125.5 10.7 %collective-permute-start.16 = (bf16[320,640]{1,0:T(8,128)(2,1)S(1)}, bf16[320,640]{1,0:T(8,128)(2,1)S(1)}, u32[]{:S(2)}, u32[]{:S(2)}) collective-permute-start(bf16[320,640]{1,0:T(8,128)(2,1)S(1)} %collective-permute-done.14.l2), channel_id=1, source_target_pairs={{0,224},{32,0},{64,32},{96,64},{128,96},{160,128},{192,160},{224,1... | collective-permute-start | bytes 1228808 | tf_op jit(solution)/shard_map/ppermute | solution.py:285
  128.8 3.7 %collective-permute-start.5 = (bf16[64,128]{1,0:T(8,128)(2,1)S(1)}, bf16[64,128]{1,0:T(8,128)(2,1)S(1)}, u32[]{:S(2)}, u32[]{:S(2)}) collective-permute-start(bf16[64,128]{1,0:T(8,128)(2,1)S(1)} %get-tuple-element.12), channel_id=1, source_target_pairs={{0,1},{1,0},{2,3},{3,2},{4,5},{5,4},{6,7},{7,6},{8,9},{9,8},{10,11... | collective-permute-start | bytes 49160 | tf_op jit(solution)/shard_map/ppermute | solution.py:338
  132.5 7.1 %collective-permute-start.6 = (bf16[2,64,128]{2,1,0:T(8,128)(2,1)S(1)}, bf16[2,64,128]{2,1,0:T(8,128)(2,1)S(1)}, u32[]{:S(2)}, u32[]{:S(2)}) collective-permute-start(bf16[2,64,128]{2,1,0:T(8,128)(2,1)S(1)} %pad_maximum_fusion.1), channel_id=1, source_target_pairs={{0,2},{2,0},{1,3},{3,1},{4,6},{6,4},{5,7},{7,5},{8,10},{10,8},{9,1... | collective-permute-start | bytes 98312 | tf_op jit(solution)/shard_map/ppermute | solution.py:339
  136.2 17.4 %collective-permute-start.17 = (bf16[160,640]{1,0:T(8,128)(2,1)}, bf16[160,640]{1,0:T(8,128)(2,1)}, u32[]{:S(2)}, u32[]{:S(2)}) collective-permute-start(bf16[160,640]{1,0:T(8,128)(2,1)} %slice.8), channel_id=1, source_target_pairs={{0,32},{32,64},{64,96},{96,128},{128,160},{160,192},{192,224},{224... | collective-permute-start | bytes 614408 | tf_op jit(solution)/shard_map/ppermute | solution.py:286
  136.9 16.7 %collective-permute-start.18 = (bf16[160,640]{1,0:T(8,128)(2,1)}, bf16[160,640]{1,0:T(8,128)(2,1)}, u32[]{:S(2)}, u32[]{:S(2)}) collective-permute-start(bf16[160,640]{1,0:T(8,128)(2,1)} %slice.9), channel_id=1, source_target_pairs={{0,224},{32,0},{64,32},{96,64},{128,96},{160,128},{192,160},{224,1... | collective-permute-start | bytes 614408 | tf_op jit(solution)/shard_map/ppermute | solution.py:287
  139.6 3.2 %collective-permute-start.7 = (bf16[4,64,128]{2,1,0:T(8,128)(2,1)S(1)}, bf16[4,64,128]{2,1,0:T(8,128)(2,1)S(1)}, u32[]{:S(2)}, u32[]{:S(2)}) collective-permute-start(bf16[4,64,128]{2,1,0:T(8,128)(2,1)S(1)} %pad_maximum_fusion.bc0), channel_id=1, source_target_pairs={{4,0},{8,4},{12,8},{0,12},{5,1},{9,5},{13,9},{1,13},{6,2},{10,6},{... | collective-permute-start | bytes 196616 | tf_op jit(solution)/shard_map/ppermute | solution.py:342
  140.5 4.6 %collective-permute-start.8 = (bf16[4,64,128]{2,1,0:T(8,128)(2,1)S(1)}, bf16[4,64,128]{2,1,0:T(8,128)(2,1)S(1)}, u32[]{:S(2)}, u32[]{:S(2)}) collective-permute-start(bf16[4,64,128]{2,1,0:T(8,128)(2,1)S(1)} %pad_maximum_fusion.bc0), channel_id=1, source_target_pairs={{8,0},{12,4},{0,8},{4,12},{9,1},{13,5},{1,9},{5,13},{10,2},{14,6},... | collective-permute-start | bytes 196616 | tf_op jit(solution)/shard_map/ppermute | solution.py:342
  141.7 4.5 %collective-permute-start.9 = (bf16[4,64,128]{2,1,0:T(8,128)(2,1)S(1)}, bf16[4,64,128]{2,1,0:T(8,128)(2,1)S(1)}, u32[]{:S(2)}, u32[]{:S(2)}) collective-permute-start(bf16[4,64,128]{2,1,0:T(8,128)(2,1)S(1)} %pad_maximum_fusion.bc0), channel_id=1, source_target_pairs={{12,0},{0,4},{4,8},{8,12},{13,1},{1,5},{5,9},{9,13},{14,2},{2,6},{... | collective-permute-start | bytes 196616 | tf_op jit(solution)/shard_map/ppermute | solution.py:342
  152.6 3.4 %collective-permute-start.10 = (bf16[64,640]{1,0:T(8,128)(2,1)S(1)}, bf16[64,640]{1,0:T(8,128)(2,1)S(1)}, u32[]{:S(2)}, u32[]{:S(2)}) collective-permute-start(bf16[64,640]{1,0:T(8,128)(2,1)S(1)} %shard_map.131.mine), channel_id=1, source_target_pairs={{0,16},{16,0},{1,17},{17,1},{2,18},{18,2},{3,19},{19,3},{4,20},{20... | collective-permute-start | bytes 245768 | tf_op jit(solution)/shard_map/ppermute | solution.py:374
  158.3 7.8 %collective-permute-start.19 = (bf16[8,64,384]{2,1,0:T(8,128)(2,1)S(1)}, bf16[8,64,384]{2,1,0:T(8,128)(2,1)S(1)}, u32[]{:S(2)}, u32[]{:S(2)}) collective-permute-start(bf16[8,64,384]{2,1,0:T(8,128)(2,1)S(1)} %get-tuple-element.16), channel_id=1, source_target_pairs={{0,1},{1,0},{2,3},{3,2},{4,5},{5,4},{6,7},{7,6},{8,9},{9,8},{10,11... | collective-permute-start | bytes 1179656 | tf_op jit(solution)/shard_map/ppermute | solution.py:399
  167.2 12.9 %all-to-all-start.3 = ((bf16[8,64,384]{2,1,0:T(8,128)(2,1)}), bf16[8,64,384]{2,1,0:T(8,128)(2,1)S(1)}, u32[]{:S(2)}, u32[]{:S(2)}) async-start(bf16[8,64,384]{2,1,0:T(8,128)(2,1)} %shard_map.133), calls=%async_computation.3 | async-start | bytes 786432 | tf_op jit(solution)/shard_map/all_to_all | solution.py:401
  180.3 5.4 %collective-permute-start.20 = (bf16[64,320]{1,0:T(8,128)(2,1)S(1)}, bf16[64,320]{1,0:T(8,128)(2,1)S(1)}, u32[]{:S(2)}, u32[]{:S(2)}) collective-permute-start(bf16[64,320]{1,0:T(8,128)(2,1)S(1)} %shard_map.134), channel_id=1, source_target_pairs={{0,0},{1,16},{16,1},{17,17},{2,2},{3,18},{18,3},{19,19},{4,4},{5,2... | collective-permute-start | bytes 122888 | tf_op jit(solution)/shard_map/ppermute | solution.py:407
  (27 other events, 475.0 us)

commit v7 on v6

--- a/solution.py
+++ b/solution.py
@@ -18,6 +18,8 @@
 VMEM_LIMIT = 14 * 1024 * 1024
 PROJECT_LIMIT = 58 * 1024 * 1024
 STATE_LIMIT = 52 * 1024 * 1024
+
+SHIFTS = (4, 3, 5, 2, 6, 1, 7)
 
 
 def nt(a, b):
@@ -69,9 +71,10 @@
         run(e_oth, e_own)
 
 
-def project_kernel(place, e_own, e_oth, x_own, x_oth, z_own, z_oth, out, both, held, done, sems):
+def project_kernel(place, e_own, e_oth, x_own, x_oth, z_own, z_oth, *refs):
+    outs, (both, held, done, sems) = refs[:8], refs[8:]
     depth, inner = x_own.shape
-    groups, rows = out.shape[:2]
+    groups, rows = len(outs), outs[0].shape[0]
     sources = ((x_own, x_oth), (z_own, z_oth))
     loads = [
         [
@@ -102,12 +105,15 @@
             load.wait()
         total = nn(both[...], held[k])
         done[k] = total.astype(BF).reshape(groups, rows, inner)
-        stores.append(
-            pltpu.make_async_copy(
-                done.at[k], out.at[:, :, pl.ds(k * inner, inner)], sems.at[4 + k]
+        for j in range(groups):
+            stores.append(
+                pltpu.make_async_copy(
+                    done.at[k, lax.rem(place[1] + j, groups)],
+                    outs[j].at[:, pl.ds(k * inner, inner)],
+                    sems.at[4 + k * groups + j],
+                )
             )
-        )
-        stores[k].start()
+            stores[-1].start()
     for store in stores:
         store.wait()
 
@@ -163,13 +169,14 @@
             out[r] = nt(cmat[r].astype(BF), m)
 
 
-def decode_kernel(part, small, dots, g, bias, rate, skip, gain, out):
+def decode_kernel(*refs):
+    parts, (small, dots, g, bias, rate, skip, gain, out) = refs[:8], refs[8:]
     heads = bias.shape[1]
     inner = gain.shape[1]
-    half = part.shape[1] // 2
-    total = part[0].astype(F32)
-    for k in range(1, part.shape[0]):
-        total = total + part[k].astype(F32)
+    half = parts[0].shape[0] // 2
+    total = parts[0][...].astype(F32)
+    for part in parts[1:]:
+        total = total + part[...].astype(F32)
     x_pre = total[:, :inner]
     z_pre = total[:, inner:]
     pick = (
@@ -312,24 +319,26 @@
         flops=2 * 16 * rows * 2 * wide * 128,
     )
     part_small = lax.all_to_all(part_small, "z", 0, 0)
-    part = call(
+    blocks = call(
         project_kernel,
-        jax.ShapeDtypeStruct((8, 2 * rows, 2 * inner), BF),
+        tuple(jax.ShapeDtypeStruct((2 * rows, 2 * inner), BF) for _ in range(8)),
         (place, e_own, e_oth, x_weight, x_oth, z_weight, z_oth),
         in_specs=[pl.BlockSpec(memory_space=pltpu.SMEM)]
         + [pl.BlockSpec(memory_space=pltpu.VMEM)] * 2
         + [pl.BlockSpec(memory_space=pl.ANY)] * 4,
-        out_specs=pl.BlockSpec(memory_space=pl.ANY),
+        out_specs=tuple(pl.BlockSpec(memory_space=pl.ANY) for _ in range(8)),
         scratch=[
             pltpu.VMEM((16 * rows, 2 * wide), BF),
             pltpu.VMEM((2, 2 * wide, inner), BF),
             pltpu.VMEM((2, 8, 2 * rows, inner), BF),
-            pltpu.SemaphoreType.DMA((6,)),
+            pltpu.SemaphoreType.DMA((20,)),
         ],
         limit=PROJECT_LIMIT,
         flops=2 * 16 * rows * 2 * wide * 2 * inner,
     )
-    part = lax.all_to_all(part, "z", 0, 0)
+    parts = [blocks[0]]
+    for k in SHIFTS:
+        parts.append(lax.ppermute(blocks[k], "z", [(i, (i + k) % 8) for i in range(8)]))
     bc, small = call(
         small_kernel,
         (jax.ShapeDtypeStruct((2 * rows, 128), BF), jax.ShapeDtypeStruct((2 * rows, 64), F32)),
@@ -361,7 +370,7 @@
         decode_kernel,
         jax.ShapeDtypeStruct((2 * rows, inner), BF),
         (
-            part,
+            *parts,
             small,
             dots,
             g,

time: 187 us -> 137 us (0.73)
  waiting for transfers between devices: 85.5 us -> 38.8 us
  blocking collectives: 27.4 us -> 0 us
  starting transfers between devices: 48.9 us -> 74.2 us
  local copies, waits for them, and re-layouts: 5.76 us -> 3.48 us
    ppermute x3, waiting for transfers between devices: 46.1 us -> 0.17 us  [per_device(): ring_r.append(lax.ppermute(ring_r[-1], 'z', right))]
    all_to_all x1 -> x0, blocking collectives: 27.4 us -> none  [per_device(): lax.all_to_all(jnp.broadcast_to(moved[None], (8,) + moved.shape), ('x', '...]
    ppermute x1, waiting for transfers between devices: 18.4 us -> 0.01 us  [per_device(): small_oth = lax.ppermute(small_own, 'yl', pair)]
    all_to_all x1, starting transfers between devices: 5.36 us -> 19.4 us  [per_device(): lax.all_to_all(jnp.broadcast_to(moved[None], (8,) + moved.shape), ('x', '...]
    ppermute x0 -> x7, starting transfers between devices: none -> 13.3 us  [per_device(): lax.ppermute(blocks[k], 'z', [(i, (i + k) % 8) for i in range(8)])]
    ppermute x0 -> x7, waiting for transfers between devices: none -> 12.8 us  [per_device(): lax.ppermute(blocks[k], 'z', [(i, (i + k) % 8) for i in range(8)])]
    all_to_all x1, waiting for transfers between devices: 0.01 us -> 5.05 us  [per_device(): lax.all_to_all(jnp.broadcast_to(moved[None], (8,) + moved.shape), ('x', '...]
    ppermute x1, waiting for transfers between devices: 0.01 us -> 4.82 us  [per_device(): z_oth = lax.ppermute(z_weight, 'yl', pair)]
  transfers between devices with their start and end apart: 24 -> 31, of which waited for: 13 -> 12; matrix products, arithmetic and copies ran while one was open for 1% -> 1% of each run, Pallas kernels for 7% -> 10%
where the time goes in v7:
time: 137 us; the launch traced here: 136 us
  starting transfers between devices  74.2 us (54%)
  waiting for transfers between devices  38.8 us (28%)
  Pallas kernels  16.8 us (12%)
  local copies, waits for them, and re-layouts  3.48 us (3%)
  other arithmetic  1.56 us (1%)
    all_to_all x1, starting transfers between devices, per_device(): lax.all_to_all(jnp.broadcast_to(moved[None], (8,) + moved.shape), ('x', '...  19.4 us
    pallas_call x8, Pallas kernels, call(): pl.pallas_call(body, out_shape=out_shape, in_specs=in_specs, out_specs=ou...  16.8 us
    ppermute x7, starting transfers between devices, per_device(): lax.ppermute(blocks[k], 'z', [(i, (i + k) % 8) for i in range(8)])  13.3 us
    ppermute x7, waiting for transfers between devices, per_device(): lax.ppermute(blocks[k], 'z', [(i, (i + k) % 8) for i in range(8)])  12.8 us
    all_to_all x1, waiting for transfers between devices, per_device(): partial_out = lax.all_to_all(paired, ('x', 'yh'), 0, 0)  8.5 us
    all_to_all x1, starting transfers between devices, per_device(): part_small = lax.all_to_all(part_small, 'z', 0, 0)  6.38 us
    ppermute x3, starting transfers between devices, per_device(): ring_l.append(lax.ppermute(ring_l[-1], 'z', left))  6.35 us
    all_to_all x1, waiting for transfers between devices, per_device(): lax.all_to_all(jnp.broadcast_to(moved[None], (8,) + moved.shape), ('x', '...  5.05 us
  transfers between devices with their start and end apart: 31, of which 12 were waited for; matrix products, arithmetic and copies ran while one was open for 1% of the time, Pallas kernels for 10%

profile of v7, /device:TPU:1, one launch (start us, length us, event | category | flops | bytes accessed | tf_op | source)
XLA Modules:
  0.0 136.0 jit_solution(15053397692425093586)
XLA Ops:
  3.0 19.4 %all-to-all-start = ((bf16[8,64,320]{2,1,0:T(8,128)(2,1)}), bf16[8,64,320]{2,1,0:T(8,128)(2,1)S(1)}, u32[]{:S(2)}, u32[]{:S(2)}) async-start(bf16[8,64,320]{2,1,0:T(8,128)(2,1)} %broadcast_in_dim.24), calls=%async_computation | async-start | bytes 786432 | tf_op jit(solution)/shard_map/all_to_all | solution.py:307
  22.6 2.5 %collective-permute-start.19 = (bf16[320,640]{1,0:T(8,128)(2,1)}, bf16[320,640]{1,0:T(8,128)(2,1)S(1)}, u32[]{:S(2)}, u32[]{:S(2)}) collective-permute-start(bf16[320,640]{1,0:T(8,128)(2,1)} %bitcast.22), channel_id=1, source_target_pairs={{0,224},{32,0},{64,32},{96,64},{128,96},{160,128},{192,160},{224,1... | collective-permute-start | bytes 1228808 | tf_op jit(solution)/shard_map/ppermute | solution.py:292
  25.2 5.1 %all-to-all-done = bf16[8,64,320]{2,1,0:T(8,128)(2,1)S(1)} async-done(((bf16[8,64,320]{2,1,0:T(8,128)(2,1)}), bf16[8,64,320]{2,1,0:T(8,128)(2,1)S(1)}, u32[]{:S(2)}, u32[]{:S(2)}) %all-to-all-start) | async-done | bytes 327712 | tf_op jit(solution)/shard_map/all_to_all | solution.py:307
  30.2 3.2 %collective-permute-start.1 = (bf16[512,320]{1,0:T(8,128)(2,1)S(1)}, bf16[512,320]{1,0:T(8,128)(2,1)S(1)}, u32[]{:S(2)}, u32[]{:S(2)}) collective-permute-start(bf16[512,320]{1,0:T(8,128)(2,1)S(1)} %bitcast.18), channel_id=1, source_target_pairs={{0,1},{1,0},{2,3},{3,2},{4,5},{5,4},{6,7},{7,6},{8,9},{9,8},{10,11... | collective-permute-start | bytes 983048 | tf_op jit(solution)/shard_map/ppermute | solution.py:310
  36.0 2.5 %collective-permute-start.21 = (bf16[320,640]{1,0:T(8,128)(2,1)S(1)}, bf16[320,640]{1,0:T(8,128)(2,1)}, u32[]{:S(2)}, u32[]{:S(2)}) collective-permute-start(bf16[320,640]{1,0:T(8,128)(2,1)S(1)} %collective-permute-done.19.l1), channel_id=1, source_target_pairs={{0,224},{32,0},{64,32},{96,64},{128,96},{160,128},{192,160},{224,1... | collective-permute-start | bytes 1228808 | tf_op jit(solution)/shard_map/ppermute | solution.py:292
  41.0 6.4 %all-to-all-start.1 = ((bf16[8,64,128]{2,1,0:T(8,128)(2,1)}), bf16[8,64,128]{2,1,0:T(8,128)(2,1)S(1)}, u32[]{:S(2)}, u32[]{:S(2)}) async-start(bf16[8,64,128]{2,1,0:T(8,128)(2,1)} %shard_map.128), calls=%async_computation.1 | async-start | bytes 262144 | tf_op jit(solution)/shard_map/all_to_all | solution.py:321
  50.3 4.8 %collective-permute-done.3.z_oth = bf16[320,640]{1,0:T(8,128)(2,1)} collective-permute-done((bf16[320,640]{1,0:T(8,128)(2,1)}, bf16[320,640]{1,0:T(8,128)(2,1)}, u32[]{:S(2)}, u32[]{:S(2)}) %collective-permute-start.3) | collective-permute-done | bytes 409632 | tf_op jit(solution)/shard_map/ppermute | solution.py:296
  55.1 5.0 %shard_map.127 = (bf16[64,1280]{1,0:T(8,128)(2,1)}, bf16[64,1280]{1,0:T(8,128)(2,1)}, bf16[64,1280]{1,0:T(8,128)(2,1)}, bf16[64,1280]{1,0:T(8,128)(2,1)}, bf16[6...) custom-call(s32[5]{0:T(128)} %copy-done.5, ...), custom_call_target="tpu_custom_call" | custom-call | flops 838860800 | bytes 1048576 | tf_op jit(solution)/shard_map/pallas_call | solution.py:40
  60.1 2.7 %collective-permute-start.10 = (bf16[64,1280]{1,0:T(8,128)(2,1)}, bf16[64,1280]{1,0:T(8,128)(2,1)S(1)}, u32[]{:S(2)}, u32[]{:S(2)}) collective-permute-start(bf16[64,1280]{1,0:T(8,128)(2,1)} %get-tuple-element.26), channel_id=1, source_target_pairs={{0,224},{32,0},{64,32},{96,64},{128,96},{160,128},{192,160},{224,1... | collective-permute-start | bytes 491528 | tf_op jit(solution)/shard_map/ppermute | solution.py:341
  64.3 2.4 %collective-permute-start.4 = (bf16[64,1280]{1,0:T(8,128)(2,1)}, bf16[64,1280]{1,0:T(8,128)(2,1)S(1)}, u32[]{:S(2)}, u32[]{:S(2)}) collective-permute-start(bf16[64,1280]{1,0:T(8,128)(2,1)} %get-tuple-element.20), channel_id=1, source_target_pairs={{0,128},{32,160},{64,192},{96,224},{128,0},{160,32},{192,64},{224,... | collective-permute-start | bytes 491528 | tf_op jit(solution)/shard_map/ppermute | solution.py:341
  68.4 2.6 %collective-permute-start.5 = (bf16[64,1280]{1,0:T(8,128)(2,1)}, bf16[64,1280]{1,0:T(8,128)(2,1)S(1)}, u32[]{:S(2)}, u32[]{:S(2)}) collective-permute-start(bf16[64,1280]{1,0:T(8,128)(2,1)} %get-tuple-element.21), channel_id=1, source_target_pairs={{0,96},{32,128},{64,160},{96,192},{128,224},{160,0},{192,32},{224,... | collective-permute-start | bytes 491528 | tf_op jit(solution)/shard_map/ppermute | solution.py:341
  71.1 1.8 %collective-permute-start.6 = (bf16[64,1280]{1,0:T(8,128)(2,1)}, bf16[64,1280]{1,0:T(8,128)(2,1)S(1)}, u32[]{:S(2)}, u32[]{:S(2)}) collective-permute-start(bf16[64,1280]{1,0:T(8,128)(2,1)} %get-tuple-element.22), channel_id=1, source_target_pairs={{0,160},{32,192},{64,224},{96,0},{128,32},{160,64},{192,96},{224,1... | collective-permute-start | bytes 491528 | tf_op jit(solution)/shard_map/ppermute | solution.py:341
  72.9 4.3 %collective-permute-done.4.refs_1_ = bf16[64,1280]{1,0:T(8,128)(2,1)S(1)} collective-permute-done((bf16[64,1280]{1,0:T(8,128)(2,1)}, bf16[64,1280]{1,0:T(8,128)(2,1)S(1)}, u32[]{:S(2)}, u32[]{:S(2)}) %collective-permute-start.4) | collective-permute-done | bytes 163872 | tf_op jit(solution)/shard_map/ppermute | solution.py:341
  78.5 7.9 %collective-permute-done.5.refs_2_ = bf16[64,1280]{1,0:T(8,128)(2,1)S(1)} collective-permute-done((bf16[64,1280]{1,0:T(8,128)(2,1)}, bf16[64,1280]{1,0:T(8,128)(2,1)S(1)}, u32[]{:S(2)}, u32[]{:S(2)}) %collective-permute-start.5) | collective-permute-done | bytes 163872 | tf_op jit(solution)/shard_map/ppermute | solution.py:341
  88.2 3.9 %collective-permute-start.8 = (bf16[64,1280]{1,0:T(8,128)(2,1)}, bf16[64,1280]{1,0:T(8,128)(2,1)S(1)}, u32[]{:S(2)}, u32[]{:S(2)}) collective-permute-start(bf16[64,1280]{1,0:T(8,128)(2,1)} %get-tuple-element.24), channel_id=1, source_target_pairs={{0,192},{32,224},{64,0},{96,32},{128,64},{160,96},{192,128},{224,1... | collective-permute-start | bytes 491528 | tf_op jit(solution)/shard_map/ppermute | solution.py:341
  93.0 2.0 %collective-permute-start.25 = (bf16[160,640]{1,0:T(8,128)(2,1)S(1)}, bf16[160,640]{1,0:T(8,128)(2,1)S(1)}, u32[]{:S(2)}, u32[]{:S(2)}) collective-permute-start(bf16[160,640]{1,0:T(8,128)(2,1)S(1)} %slice.9), channel_id=1, source_target_pairs={{0,224},{32,0},{64,32},{96,64},{128,96},{160,128},{192,160},{224,1... | collective-permute-start | bytes 614408 | tf_op jit(solution)/shard_map/ppermute | solution.py:294
  96.4 5.6 %shard_map.130 = (f32[32,8,640]{2,1,0:T(8,128)S(1)}, f32[32,128]{1,0:T(8,128)S(1)}) custom-call(s32[5]{0:T(128)S(1)} %copy-done.6, bf16[4,64,128]{2,1,0:T(8,128)(2,1)S(1)} %pad_maximum_fusion.bc0, bf16[4,64,128]{2,1,0:T(8,128)(2,1)S(1)} %collective-permute-done.14.bc1, bf16[4,64,128]{2,1,0:T(8,128)(2,1)S(1)} %collective-permute-done.15.bc2, ...), custom_call_target="tpu_custom_call" | custom-call | flops 83886080 | bytes 1048576 | tf_op jit(solution)/shard_map/pallas_call | solution.py:40
  103.6 3.4 %collective-permute-done.17.other = bf16[64,640]{1,0:T(8,128)(2,1)S(1)} collective-permute-done((bf16[64,640]{1,0:T(8,128)(2,1)S(1)}, bf16[64,640]{1,0:T(8,128)(2,1)S(1)}, u32[]{:S(2)}, u32[]{:S(2)}) %collective-permute-start.17) | collective-permute-done | bytes 81952 | tf_op jit(solution)/shard_map/ppermute | solution.py:383
  107.0 2.4 %shard_map.132 = (f32[8,64,384]{2,1,0:T(8,128)S(1)}, bf16[8,64,384]{2,1,0:T(8,128)(2,1)S(1)}) custom-call(s32[5]{0:T(128)S(1)} %copy-done.6, bf16[64,640]{1,0:T(8,128)(2,1)S(1)} %shard_map.131.mine, bf16[64,640]{1,0:T(8,128)(2,1)S(1)} %collective-permute-done.17.other, f32[1,640]{1,0:T(1,128)S(1)} %reshape.28.refs_14_.gain, bf16[320,640]{1,0:T(8,128)(2,1)S(1)} %bitcast.23, ...), custom_call_target="tpu_custom_call" | custom-call | flops 419430400 | bytes 1048576 | tf_op jit(solution)/shard_map/pallas_call | solution.py:40
  109.5 3.7 %collective-permute-start.26 = (bf16[8,64,384]{2,1,0:T(8,128)(2,1)S(1)}, bf16[8,64,384]{2,1,0:T(8,128)(2,1)S(1)}, u32[]{:S(2)}, u32[]{:S(2)}) collective-permute-start(bf16[8,64,384]{2,1,0:T(8,128)(2,1)S(1)} %get-tuple-element.32), channel_id=1, source_target_pairs={{0,1},{1,0},{2,3},{3,2},{4,5},{5,4},{6,7},{7,6},{8,9},{9,8},{10,11... | collective-permute-start | bytes 1179656 | tf_op jit(solution)/shard_map/ppermute | solution.py:408
  115.6 4.5 %all-to-all-start.2 = ((bf16[8,64,384]{2,1,0:T(8,128)(2,1)}), bf16[8,64,384]{2,1,0:T(8,128)(2,1)S(1)}, u32[]{:S(2)}, u32[]{:S(2)}) async-start(bf16[8,64,384]{2,1,0:T(8,128)(2,1)} %shard_map.133), calls=%async_computation.2 | async-start | bytes 786432 | tf_op jit(solution)/shard_map/all_to_all | solution.py:410
  120.8 8.5 %all-to-all-done.2.part = bf16[8,64,384]{2,1,0:T(8,128)(2,1)S(1)} async-done(((bf16[8,64,384]{2,1,0:T(8,128)(2,1)}), bf16[8,64,384]{2,1,0:T(8,128)(2,1)S(1)}, u32[]{:S(2)}, u32[]{:S(2)}) %all-to-all-start.2) | async-done | bytes 393248 | tf_op jit(solution)/shard_map/all_to_all | solution.py:410
  129.4 4.1 %collective-permute-start.27 = (bf16[64,320]{1,0:T(8,128)(2,1)S(1)}, bf16[64,320]{1,0:T(8,128)(2,1)S(1)}, u32[]{:S(2)}, u32[]{:S(2)}) collective-permute-start(bf16[64,320]{1,0:T(8,128)(2,1)S(1)} %shard_map.134), channel_id=1, source_target_pairs={{0,0},{1,16},{16,1},{17,17},{2,2},{3,18},{18,3},{19,19},{4,4},{5,2... | collective-permute-start | bytes 122888 | tf_op jit(solution)/shard_map/ppermute | solution.py:416
  133.6 1.7 %collective-permute-done.27 = bf16[64,320]{1,0:T(8,128)(2,1)S(1)} collective-permute-done((bf16[64,320]{1,0:T(8,128)(2,1)S(1)}, bf16[64,320]{1,0:T(8,128)(2,1)S(1)}, u32[]{:S(2)}, u32[]{:S(2)}) %collective-permute-start.27) | collective-permute-done | bytes 40992 | tf_op jit(solution)/shard_map/ppermute | solution.py:416
  (81 shorter events, 24.6 us)
Async XLA Ops:
  3.0 27.3 %all-to-all-start = ((bf16[8,64,320]{2,1,0:T(8,128)(2,1)}), bf16[8,64,320]{2,1,0:T(8,128)(2,1)S(1)}, u32[]{:S(2)}, u32[]{:S(2)}) async-start(bf16[8,64,320]{2,1,0:T(8,128)(2,1)} %broadcast_in_dim.24), calls=%async_computation | async-start | bytes 786432 | tf_op jit(solution)/shard_map/all_to_all | solution.py:307
  22.4 13.5 %collective-permute-start.18 = (bf16[320,640]{1,0:T(8,128)(2,1)}, bf16[320,640]{1,0:T(8,128)(2,1)S(1)}, u32[]{:S(2)}, u32[]{:S(2)}) collective-permute-start(bf16[320,640]{1,0:T(8,128)(2,1)} %bitcast.21), channel_id=1, source_target_pairs={{0,32},{32,64},{64,96},{96,128},{128,160},{160,192},{192,224},{224... | collective-permute-start | bytes 1228808 | tf_op jit(solution)/shard_map/ppermute | solution.py:291
  22.6 13.4 %collective-permute-start.19 = (bf16[320,640]{1,0:T(8,128)(2,1)}, bf16[320,640]{1,0:T(8,128)(2,1)S(1)}, u32[]{:S(2)}, u32[]{:S(2)}) collective-permute-start(bf16[320,640]{1,0:T(8,128)(2,1)} %bitcast.22), channel_id=1, source_target_pairs={{0,224},{32,0},{64,32},{96,64},{128,96},{160,128},{192,160},{224,1... | collective-permute-start | bytes 1228808 | tf_op jit(solution)/shard_map/ppermute | solution.py:292
  30.2 9.2 %collective-permute-start.1 = (bf16[512,320]{1,0:T(8,128)(2,1)S(1)}, bf16[512,320]{1,0:T(8,128)(2,1)S(1)}, u32[]{:S(2)}, u32[]{:S(2)}) collective-permute-start(bf16[512,320]{1,0:T(8,128)(2,1)S(1)} %bitcast.18), channel_id=1, source_target_pairs={{0,1},{1,0},{2,3},{3,2},{4,5},{5,4},{6,7},{7,6},{8,9},{9,8},{10,11... | collective-permute-start | bytes 983048 | tf_op jit(solution)/shard_map/ppermute | solution.py:310
  35.2 15.1 %collective-permute-start.2 = (bf16[320,640]{1,0:T(8,128)(2,1)}, bf16[320,640]{1,0:T(8,128)(2,1)}, u32[]{:S(2)}, u32[]{:S(2)}) collective-permute-start(bf16[320,640]{1,0:T(8,128)(2,1)} %x_own.1), channel_id=1, source_target_pairs={{0,16},{16,0},{1,17},{17,1},{2,18},{18,2},{3,19},{19,3},{4,20},{20... | collective-permute-start | bytes 1228808 | tf_op jit(solution)/shard_map/ppermute | solution.py:295
  35.9 11.7 %collective-permute-start.20 = (bf16[320,640]{1,0:T(8,128)(2,1)S(1)}, bf16[320,640]{1,0:T(8,128)(2,1)}, u32[]{:S(2)}, u32[]{:S(2)}) collective-permute-start(bf16[320,640]{1,0:T(8,128)(2,1)S(1)} %collective-permute-done.18.r1), channel_id=1, source_target_pairs={{0,32},{32,64},{64,96},{96,128},{128,160},{160,192},{192,224},{224... | collective-permute-start | bytes 1228808 | tf_op jit(solution)/shard_map/ppermute | solution.py:291
  36.0 13.0 %collective-permute-start.21 = (bf16[320,640]{1,0:T(8,128)(2,1)S(1)}, bf16[320,640]{1,0:T(8,128)(2,1)}, u32[]{:S(2)}, u32[]{:S(2)}) collective-permute-start(bf16[320,640]{1,0:T(8,128)(2,1)S(1)} %collective-permute-done.19.l1), channel_id=1, source_target_pairs={{0,224},{32,0},{64,32},{96,64},{128,96},{160,128},{192,160},{224,1... | collective-permute-start | bytes 1228808 | tf_op jit(solution)/shard_map/ppermute | solution.py:292
  38.6 16.6 %collective-permute-start.3 = (bf16[320,640]{1,0:T(8,128)(2,1)}, bf16[320,640]{1,0:T(8,128)(2,1)}, u32[]{:S(2)}, u32[]{:S(2)}) collective-permute-start(bf16[320,640]{1,0:T(8,128)(2,1)} %z_own.1), channel_id=1, source_target_pairs={{0,16},{16,0},{1,17},{17,1},{2,18},{18,2},{3,19},{19,3},{4,20},{20... | collective-permute-start | bytes 1228808 | tf_op jit(solution)/shard_map/ppermute | solution.py:296
  41.0 21.8 %all-to-all-start.1 = ((bf16[8,64,128]{2,1,0:T(8,128)(2,1)}), bf16[8,64,128]{2,1,0:T(8,128)(2,1)S(1)}, u32[]{:S(2)}, u32[]{:S(2)}) async-start(bf16[8,64,128]{2,1,0:T(8,128)(2,1)} %shard_map.128), calls=%async_computation.1 | async-start | bytes 262144 | tf_op jit(solution)/shard_map/all_to_all | solution.py:321
  47.6 40.6 %collective-permute-start.22 = (bf16[320,640]{1,0:T(8,128)(2,1)}, bf16[320,640]{1,0:T(8,128)(2,1)S(1)}, u32[]{:S(2)}, u32[]{:S(2)}) collective-permute-start(bf16[320,640]{1,0:T(8,128)(2,1)} %collective-permute-done.20.r2), channel_id=1, source_target_pairs={{0,32},{32,64},{64,96},{96,128},{128,160},{160,192},{192,224},{224... | collective-permute-start | bytes 1228808 | tf_op jit(solution)/shard_map/ppermute | solution.py:291
  49.0 43.2 %collective-permute-start.23 = (bf16[320,640]{1,0:T(8,128)(2,1)}, bf16[320,640]{1,0:T(8,128)(2,1)S(1)}, u32[]{:S(2)}, u32[]{:S(2)}) collective-permute-start(bf16[320,640]{1,0:T(8,128)(2,1)} %collective-permute-done.21.l2), channel_id=1, source_target_pairs={{0,224},{32,0},{64,32},{96,64},{128,96},{160,128},{192,160},{224,1... | collective-permute-start | bytes 1228808 | tf_op jit(solution)/shard_map/ppermute | solution.py:292
  60.1 8.3 %collective-permute-start.10 = (bf16[64,1280]{1,0:T(8,128)(2,1)}, bf16[64,1280]{1,0:T(8,128)(2,1)S(1)}, u32[]{:S(2)}, u32[]{:S(2)}) collective-permute-start(bf16[64,1280]{1,0:T(8,128)(2,1)} %get-tuple-element.26), channel_id=1, source_target_pairs={{0,224},{32,0},{64,32},{96,64},{128,96},{160,128},{192,160},{224,1... | collective-permute-start | bytes 491528 | tf_op jit(solution)/shard_map/ppermute | solution.py:341
  64.3 12.9 %collective-permute-start.4 = (bf16[64,1280]{1,0:T(8,128)(2,1)}, bf16[64,1280]{1,0:T(8,128)(2,1)S(1)}, u32[]{:S(2)}, u32[]{:S(2)}) collective-permute-start(bf16[64,1280]{1,0:T(8,128)(2,1)} %get-tuple-element.20), channel_id=1, source_target_pairs={{0,128},{32,160},{64,192},{96,224},{128,0},{160,32},{192,64},{224,... | collective-permute-start | bytes 491528 | tf_op jit(solution)/shard_map/ppermute | solution.py:341
  68.4 18.0 %collective-permute-start.5 = (bf16[64,1280]{1,0:T(8,128)(2,1)}, bf16[64,1280]{1,0:T(8,128)(2,1)S(1)}, u32[]{:S(2)}, u32[]{:S(2)}) collective-permute-start(bf16[64,1280]{1,0:T(8,128)(2,1)} %get-tuple-element.21), channel_id=1, source_target_pairs={{0,96},{32,128},{64,160},{96,192},{128,224},{160,0},{192,32},{224,... | collective-permute-start | bytes 491528 | tf_op jit(solution)/shard_map/ppermute | solution.py:341
  71.1 16.5 %collective-permute-start.6 = (bf16[64,1280]{1,0:T(8,128)(2,1)}, bf16[64,1280]{1,0:T(8,128)(2,1)S(1)}, u32[]{:S(2)}, u32[]{:S(2)}) collective-permute-start(bf16[64,1280]{1,0:T(8,128)(2,1)} %get-tuple-element.22), channel_id=1, source_target_pairs={{0,160},{32,192},{64,224},{96,0},{128,32},{160,64},{192,96},{224,1... | collective-permute-start | bytes 491528 | tf_op jit(solution)/shard_map/ppermute | solution.py:341
  77.2 11.0 %collective-permute-start.14 = (bf16[4,64,128]{2,1,0:T(8,128)(2,1)S(1)}, bf16[4,64,128]{2,1,0:T(8,128)(2,1)S(1)}, u32[]{:S(2)}, u32[]{:S(2)}) collective-permute-start(bf16[4,64,128]{2,1,0:T(8,128)(2,1)S(1)} %pad_maximum_fusion.bc0), channel_id=1, source_target_pairs={{4,0},{8,4},{12,8},{0,12},{5,1},{9,5},{13,9},{1,13},{6,2},{10,6},{... | collective-permute-start | bytes 196616 | tf_op jit(solution)/shard_map/ppermute | solution.py:351
  86.4 5.8 %collective-permute-start.15 = (bf16[4,64,128]{2,1,0:T(8,128)(2,1)S(1)}, bf16[4,64,128]{2,1,0:T(8,128)(2,1)S(1)}, u32[]{:S(2)}, u32[]{:S(2)}) collective-permute-start(bf16[4,64,128]{2,1,0:T(8,128)(2,1)S(1)} %pad_maximum_fusion.bc0), channel_id=1, source_target_pairs={{8,0},{12,4},{0,8},{4,12},{9,1},{13,5},{1,9},{5,13},{10,2},{14,6},... | collective-permute-start | bytes 196616 | tf_op jit(solution)/shard_map/ppermute | solution.py:351
  88.2 13.8 %collective-permute-start.7 = (bf16[64,1280]{1,0:T(8,128)(2,1)}, bf16[64,1280]{1,0:T(8,128)(2,1)S(1)}, u32[]{:S(2)}, u32[]{:S(2)}) collective-permute-start(bf16[64,1280]{1,0:T(8,128)(2,1)} %get-tuple-element.23), channel_id=1, source_target_pairs={{0,64},{32,96},{64,128},{96,160},{128,192},{160,224},{192,0},{224,... | collective-permute-start | bytes 491528 | tf_op jit(solution)/shard_map/ppermute | solution.py:341
  88.2 13.8 %collective-permute-start.8 = (bf16[64,1280]{1,0:T(8,128)(2,1)}, bf16[64,1280]{1,0:T(8,128)(2,1)S(1)}, u32[]{:S(2)}, u32[]{:S(2)}) collective-permute-start(bf16[64,1280]{1,0:T(8,128)(2,1)} %get-tuple-element.24), channel_id=1, source_target_pairs={{0,192},{32,224},{64,0},{96,32},{128,64},{160,96},{192,128},{224,1... | collective-permute-start | bytes 491528 | tf_op jit(solution)/shard_map/ppermute | solution.py:341
  92.1 10.4 %collective-permute-start.9 = (bf16[64,1280]{1,0:T(8,128)(2,1)}, bf16[64,1280]{1,0:T(8,128)(2,1)S(1)}, u32[]{:S(2)}, u32[]{:S(2)}) collective-permute-start(bf16[64,1280]{1,0:T(8,128)(2,1)} %get-tuple-element.25), channel_id=1, source_target_pairs={{0,32},{32,64},{64,96},{96,128},{128,160},{160,192},{192,224},{224... | collective-permute-start | bytes 491528 | tf_op jit(solution)/shard_map/ppermute | solution.py:341
  92.2 14.8 %collective-permute-start.24 = (bf16[160,640]{1,0:T(8,128)(2,1)S(1)}, bf16[160,640]{1,0:T(8,128)(2,1)S(1)}, u32[]{:S(2)}, u32[]{:S(2)}) collective-permute-start(bf16[160,640]{1,0:T(8,128)(2,1)S(1)} %slice.8), channel_id=1, source_target_pairs={{0,32},{32,64},{64,96},{96,128},{128,160},{160,192},{192,224},{224... | collective-permute-start | bytes 614408 | tf_op jit(solution)/shard_map/ppermute | solution.py:293
  93.0 14.0 %collective-permute-start.25 = (bf16[160,640]{1,0:T(8,128)(2,1)S(1)}, bf16[160,640]{1,0:T(8,128)(2,1)S(1)}, u32[]{:S(2)}, u32[]{:S(2)}) collective-permute-start(bf16[160,640]{1,0:T(8,128)(2,1)S(1)} %slice.9), channel_id=1, source_target_pairs={{0,224},{32,0},{64,32},{96,64},{128,96},{160,128},{192,160},{224,1... | collective-permute-start | bytes 614408 | tf_op jit(solution)/shard_map/ppermute | solution.py:294
  115.6 13.7 %all-to-all-start.2 = ((bf16[8,64,384]{2,1,0:T(8,128)(2,1)}), bf16[8,64,384]{2,1,0:T(8,128)(2,1)S(1)}, u32[]{:S(2)}, u32[]{:S(2)}) async-start(bf16[8,64,384]{2,1,0:T(8,128)(2,1)} %shard_map.133), calls=%async_computation.2 | async-start | bytes 786432 | tf_op jit(solution)/shard_map/all_to_all | solution.py:410
  129.4 5.9 %collective-permute-start.27 = (bf16[64,320]{1,0:T(8,128)(2,1)S(1)}, bf16[64,320]{1,0:T(8,128)(2,1)S(1)}, u32[]{:S(2)}, u32[]{:S(2)}) collective-permute-start(bf16[64,320]{1,0:T(8,128)(2,1)S(1)} %shard_map.134), channel_id=1, source_target_pairs={{0,0},{1,16},{16,1},{17,17},{2,2},{3,18},{18,3},{19,19},{4,4},{5,2... | collective-permute-start | bytes 122888 | tf_op jit(solution)/shard_map/ppermute | solution.py:416
  (17 other events, 534.8 us)

commit v8 on v7

--- a/solution.py
+++ b/solution.py
@@ -141,10 +141,10 @@
     for copy in copies:
         copy.start()
     for shift, bc in ((0, bc0), (1, bc1), (2, bc2), (3, bc3)):
-        x = lax.rem(place[2] + shift, 4)
+        x = lax.rem(place[0] + shift, 4)
         for k in range(4):
-            yh = lax.rem(place[3] + k // 2, 2)
-            core = lax.rem(place[4] + k % 2, 2)
+            yh = lax.rem(place[1] + k // 2, 2)
+            core = lax.rem(place[2] + k % 2, 2)
             pieces_ref[(x * 2 + yh) * 2 + core] = bc[k]
     pieces = [pieces_ref[t] for t in range(16)]
     pieces = [p[:, :32].astype(F32) + p[:, 64:96].astype(F32) for p in pieces]
@@ -213,8 +213,8 @@
 
 
 def output_kernel(place, mine, other, gain, own, r1, l1, r2, l2, r3, l3, r4, l4, keep, send):
-    same = place[0]
-    z = place[1]
+    z = place[0]
+    same = place[1]
     groups, rows, _ = keep.shape
     m = mine[...]
     o = other[...]
@@ -308,9 +308,11 @@
         jnp.broadcast_to(moved[None], (8,) + moved.shape), ("x", "yh"), 0, 0
     ).reshape(8 * 2 * rows, wide)
     e_oth = lax.ppermute(e_own, "core", pair)
-    place = jnp.stack(
-        [(y == core).astype(jnp.int32), lax.axis_index("z"), lax.axis_index("x"), lax.axis_index("yh"), core]
-    )
+    same = (y == core).astype(jnp.int32)
+    z = lax.axis_index("z")
+    place = jnp.stack([same, z])
+    plane = jnp.stack([lax.axis_index("x"), lax.axis_index("yh"), core])
+    turned = jnp.stack([z, same])
     part_small = call(
         project_small_kernel,
         jax.ShapeDtypeStruct((8, 2 * rows, 128), BF),
@@ -352,7 +354,7 @@
     g, dots = call(
         state_kernel,
         (jax.ShapeDtypeStruct((rows, 8, inner), F32), jax.ShapeDtypeStruct((rows, 128), F32)),
-        (place, *bc_all, ssm_state),
+        (plane, *bc_all, ssm_state),
         in_specs=[pl.BlockSpec(memory_space=pltpu.SMEM)]
         + [pl.BlockSpec(memory_space=pltpu.VMEM)] * 4
         + [pl.BlockSpec(memory_space=pl.ANY)],
@@ -388,7 +390,7 @@
             jax.ShapeDtypeStruct((8, 2 * rows, wide + 64), BF),
         ),
         (
-            place,
+            turned,
             gg,
             gg_oth,
             gain,

time: 137 us -> 138 us (level)
  Pallas kernels: 16.8 us -> 18.4 us
    pallas_call x8, Pallas kernels: 16.8 us -> 18.4 us  [call(): pl.pallas_call(body, out_shape=out_shape, in_specs=in_specs, out_specs=ou...]
  transfers between devices with their start and end apart: 31 -> 31, of which waited for: 12 -> 11; matrix products, arithmetic and copies ran while one was open for 1% -> 1% of each run, Pallas kernels for 10% -> 11%
where the time goes in v8:
time: 138 us
  starting transfers between devices  74.9 us (54%)
  waiting for transfers between devices  38 us (28%)
  Pallas kernels  18.4 us (13%)
  local copies, waits for them, and re-layouts  3.47 us (3%)
  other arithmetic  1.79 us (1%)
    all_to_all x1, starting transfers between devices, per_device(): lax.all_to_all(jnp.broadcast_to(moved[None], (8,) + moved.shape), ('x', '...  19.4 us
    pallas_call x8, Pallas kernels, call(): pl.pallas_call(body, out_shape=out_shape, in_specs=in_specs, out_specs=ou...  18.4 us
    ppermute x7, starting transfers between devices, per_device(): lax.ppermute(blocks[k], 'z', [(i, (i + k) % 8) for i in range(8)])  13.3 us
    ppermute x7, waiting for transfers between devices, per_device(): lax.ppermute(blocks[k], 'z', [(i, (i + k) % 8) for i in range(8)])  12.9 us
    all_to_all x1, waiting for transfers between devices, per_device(): partial_out = lax.all_to_all(paired, ('x', 'yh'), 0, 0)  8.5 us
    all_to_all x1, starting transfers between devices, per_device(): part_small = lax.all_to_all(part_small, 'z', 0, 0)  6.38 us
    ppermute x3, starting transfers between devices, per_device(): ring_l.append(lax.ppermute(ring_l[-1], 'z', left))  6.35 us
    all_to_all x1, waiting for transfers between devices, per_device(): lax.all_to_all(jnp.broadcast_to(moved[None], (8,) + moved.shape), ('x', '...  5.05 us
  transfers between devices with their start and end apart: 31, of which 11 were waited for; matrix products, arithmetic and copies ran while one was open for 1% of the time, Pallas kernels for 11%

profile of v8, /device:TPU:1, one launch (start us, length us, event | category | flops | bytes accessed | tf_op | source)
XLA Modules:
  0.0 137.8 jit_solution(18331934839268479592)
XLA Ops:
  2.9 19.4 %all-to-all-start = ((bf16[8,64,320]{2,1,0:T(8,128)(2,1)}), bf16[8,64,320]{2,1,0:T(8,128)(2,1)S(1)}, u32[]{:S(2)}, u32[]{:S(2)}) async-start(bf16[8,64,320]{2,1,0:T(8,128)(2,1)} %broadcast_in_dim.24), calls=%async_computation | async-start | bytes 786432 | tf_op jit(solution)/shard_map/all_to_all | solution.py:307
  22.6 2.5 %collective-permute-start.19 = (bf16[320,640]{1,0:T(8,128)(2,1)}, bf16[320,640]{1,0:T(8,128)(2,1)S(1)}, u32[]{:S(2)}, u32[]{:S(2)}) collective-permute-start(bf16[320,640]{1,0:T(8,128)(2,1)} %bitcast.22), channel_id=1, source_target_pairs={{0,224},{32,0},{64,32},{96,64},{128,96},{160,128},{192,160},{224,1... | collective-permute-start | bytes 1228808 | tf_op jit(solution)/shard_map/ppermute | solution.py:292
  25.1 5.1 %all-to-all-done = bf16[8,64,320]{2,1,0:T(8,128)(2,1)S(1)} async-done(((bf16[8,64,320]{2,1,0:T(8,128)(2,1)}), bf16[8,64,320]{2,1,0:T(8,128)(2,1)S(1)}, u32[]{:S(2)}, u32[]{:S(2)}) %all-to-all-start) | async-done | bytes 327712 | tf_op jit(solution)/shard_map/all_to_all | solution.py:307
  30.2 3.2 %collective-permute-start.1 = (bf16[512,320]{1,0:T(8,128)(2,1)S(1)}, bf16[512,320]{1,0:T(8,128)(2,1)S(1)}, u32[]{:S(2)}, u32[]{:S(2)}) collective-permute-start(bf16[512,320]{1,0:T(8,128)(2,1)S(1)} %bitcast.18), channel_id=1, source_target_pairs={{0,1},{1,0},{2,3},{3,2},{4,5},{5,4},{6,7},{7,6},{8,9},{9,8},{10,11... | collective-permute-start | bytes 983048 | tf_op jit(solution)/shard_map/ppermute | solution.py:310
  36.0 2.5 %collective-permute-start.21 = (bf16[320,640]{1,0:T(8,128)(2,1)S(1)}, bf16[320,640]{1,0:T(8,128)(2,1)}, u32[]{:S(2)}, u32[]{:S(2)}) collective-permute-start(bf16[320,640]{1,0:T(8,128)(2,1)S(1)} %collective-permute-done.19.l1), channel_id=1, source_target_pairs={{0,224},{32,0},{64,32},{96,64},{128,96},{160,128},{192,160},{224,1... | collective-permute-start | bytes 1228808 | tf_op jit(solution)/shard_map/ppermute | solution.py:292
  41.0 6.4 %all-to-all-start.1 = ((bf16[8,64,128]{2,1,0:T(8,128)(2,1)}), bf16[8,64,128]{2,1,0:T(8,128)(2,1)S(1)}, u32[]{:S(2)}, u32[]{:S(2)}) async-start(bf16[8,64,128]{2,1,0:T(8,128)(2,1)} %shard_map.128), calls=%async_computation.1 | async-start | bytes 262144 | tf_op jit(solution)/shard_map/all_to_all | solution.py:323
  50.2 4.8 %collective-permute-done.3.z_oth = bf16[320,640]{1,0:T(8,128)(2,1)} collective-permute-done((bf16[320,640]{1,0:T(8,128)(2,1)}, bf16[320,640]{1,0:T(8,128)(2,1)}, u32[]{:S(2)}, u32[]{:S(2)}) %collective-permute-start.3) | collective-permute-done | bytes 409632 | tf_op jit(solution)/shard_map/ppermute | solution.py:296
  55.1 5.0 %shard_map.127 = (bf16[64,1280]{1,0:T(8,128)(2,1)}, bf16[64,1280]{1,0:T(8,128)(2,1)}, bf16[64,1280]{1,0:T(8,128)(2,1)}, bf16[64,1280]{1,0:T(8,128)(2,1)}, bf16[6...) custom-call(s32[2]{0:T(128)} %copy-done.11, ...), custom_call_target="tpu_custom_call" | custom-call | flops 838860800 | bytes 1048576 | tf_op jit(solution)/shard_map/pallas_call | solution.py:40
  60.1 2.7 %collective-permute-start.10 = (bf16[64,1280]{1,0:T(8,128)(2,1)}, bf16[64,1280]{1,0:T(8,128)(2,1)S(1)}, u32[]{:S(2)}, u32[]{:S(2)}) collective-permute-start(bf16[64,1280]{1,0:T(8,128)(2,1)} %get-tuple-element.26), channel_id=1, source_target_pairs={{0,224},{32,0},{64,32},{96,64},{128,96},{160,128},{192,160},{224,1... | collective-permute-start | bytes 491528 | tf_op jit(solution)/shard_map/ppermute | solution.py:343
  64.4 2.4 %collective-permute-start.4 = (bf16[64,1280]{1,0:T(8,128)(2,1)}, bf16[64,1280]{1,0:T(8,128)(2,1)S(1)}, u32[]{:S(2)}, u32[]{:S(2)}) collective-permute-start(bf16[64,1280]{1,0:T(8,128)(2,1)} %get-tuple-element.20), channel_id=1, source_target_pairs={{0,128},{32,160},{64,192},{96,224},{128,0},{160,32},{192,64},{224,... | collective-permute-start | bytes 491528 | tf_op jit(solution)/shard_map/ppermute | solution.py:343
  68.5 2.6 %collective-permute-start.5 = (bf16[64,1280]{1,0:T(8,128)(2,1)}, bf16[64,1280]{1,0:T(8,128)(2,1)S(1)}, u32[]{:S(2)}, u32[]{:S(2)}) collective-permute-start(bf16[64,1280]{1,0:T(8,128)(2,1)} %get-tuple-element.21), channel_id=1, source_target_pairs={{0,96},{32,128},{64,160},{96,192},{128,224},{160,0},{192,32},{224,... | collective-permute-start | bytes 491528 | tf_op jit(solution)/shard_map/ppermute | solution.py:343
  71.2 1.8 %collective-permute-start.6 = (bf16[64,1280]{1,0:T(8,128)(2,1)}, bf16[64,1280]{1,0:T(8,128)(2,1)S(1)}, u32[]{:S(2)}, u32[]{:S(2)}) collective-permute-start(bf16[64,1280]{1,0:T(8,128)(2,1)} %get-tuple-element.22), channel_id=1, source_target_pairs={{0,160},{32,192},{64,224},{96,0},{128,32},{160,64},{192,96},{224,1... | collective-permute-start | bytes 491528 | tf_op jit(solution)/shard_map/ppermute | solution.py:343
  73.0 4.3 %collective-permute-done.4.refs_1_ = bf16[64,1280]{1,0:T(8,128)(2,1)S(1)} collective-permute-done((bf16[64,1280]{1,0:T(8,128)(2,1)}, bf16[64,1280]{1,0:T(8,128)(2,1)S(1)}, u32[]{:S(2)}, u32[]{:S(2)}) %collective-permute-start.4) | collective-permute-done | bytes 163872 | tf_op jit(solution)/shard_map/ppermute | solution.py:343
  78.5 7.9 %collective-permute-done.5.refs_2_ = bf16[64,1280]{1,0:T(8,128)(2,1)S(1)} collective-permute-done((bf16[64,1280]{1,0:T(8,128)(2,1)}, bf16[64,1280]{1,0:T(8,128)(2,1)S(1)}, u32[]{:S(2)}, u32[]{:S(2)}) %collective-permute-start.5) | collective-permute-done | bytes 163872 | tf_op jit(solution)/shard_map/ppermute | solution.py:343
  88.9 3.9 %collective-permute-start.8 = (bf16[64,1280]{1,0:T(8,128)(2,1)}, bf16[64,1280]{1,0:T(8,128)(2,1)}, u32[]{:S(2)}, u32[]{:S(2)}) collective-permute-start(bf16[64,1280]{1,0:T(8,128)(2,1)} %get-tuple-element.24), channel_id=1, source_target_pairs={{0,192},{32,224},{64,0},{96,32},{128,64},{160,96},{192,128},{224,1... | collective-permute-start | bytes 491528 | tf_op jit(solution)/shard_map/ppermute | solution.py:343
  93.8 2.7 %collective-permute-start.25 = (bf16[160,640]{1,0:T(8,128)(2,1)S(1)}, bf16[160,640]{1,0:T(8,128)(2,1)S(1)}, u32[]{:S(2)}, u32[]{:S(2)}) collective-permute-start(bf16[160,640]{1,0:T(8,128)(2,1)S(1)} %slice.9), channel_id=1, source_target_pairs={{0,224},{32,0},{64,32},{96,64},{128,96},{160,128},{192,160},{224,1... | collective-permute-start | bytes 614408 | tf_op jit(solution)/shard_map/ppermute | solution.py:294
  96.6 6.1 %shard_map.130 = (f32[32,8,640]{2,1,0:T(8,128)S(1)}, f32[32,128]{1,0:T(8,128)S(1)}) custom-call(s32[3]{0:T(128)S(1)} %pad_add_fusion.2.place, bf16[4,64,128]{2,1,0:T(8,128)(2,1)S(1)} %pad_maximum_fusion.bc0, bf16[4,64,128]{2,1,0:T(8,128)(2,1)S(1)} %collective-permute-done.14.bc1, bf16[4,64,128]{2,1,0:T(8,128)(2,1)} %collective-permute-done.15.bc2, ...), custom_call_target="tpu_custom_call" | custom-call | flops 83886080 | bytes 1048576 | tf_op jit(solution)/shard_map/pallas_call | solution.py:40
  103.5 1.8 %shard_map.131.mine = bf16[64,640]{1,0:T(8,128)(2,1)S(1)} custom-call(bf16[64,1280]{1,0:T(8,128)(2,1)S(1)} %copy-done.4, bf16[64,1280]{1,0:T(8,128)(2,1)S(1)} %collective-permute-done.4.refs_1_, bf16[64,1280]{1,0:T(8,128)(2,1)S(1)} %copy-done.6, bf16[64,1280]{1,0:T(8,128)(2,1)S(1)} %copy-done.8, bf16[64,1280]{1,0:T(8,128)(2,1)} %collective-permute-done.7.refs_4_, ...), custom_call_target="tpu_custom_call" | custom-call | flops 1048576 | bytes 1048576 | tf_op jit(solution)/shard_map/pallas_call | solution.py:40
  105.5 3.2 %collective-permute-done.17.other = bf16[64,640]{1,0:T(8,128)(2,1)S(1)} collective-permute-done((bf16[64,640]{1,0:T(8,128)(2,1)S(1)}, bf16[64,640]{1,0:T(8,128)(2,1)S(1)}, u32[]{:S(2)}, u32[]{:S(2)}) %collective-permute-start.17) | collective-permute-done | bytes 81952 | tf_op jit(solution)/shard_map/ppermute | solution.py:385
  108.7 2.4 %shard_map.132 = (f32[8,64,384]{2,1,0:T(8,128)S(1)}, bf16[8,64,384]{2,1,0:T(8,128)(2,1)S(1)}) custom-call(s32[2]{0:T(128)S(1)} %pad_add_fusion.place, bf16[64,640]{1,0:T(8,128)(2,1)S(1)} %shard_map.131.mine, bf16[64,640]{1,0:T(8,128)(2,1)S(1)} %collective-permute-done.17.other, f32[1,640]{1,0:T(1,128)S(1)} %reshape.28.refs_14_.gain, ...), custom_call_target="tpu_custom_call" | custom-call | flops 419430400 | bytes 1048576 | tf_op jit(solution)/shard_map/pallas_call | solution.py:40
  111.1 3.9 %collective-permute-start.26 = (bf16[8,64,384]{2,1,0:T(8,128)(2,1)S(1)}, bf16[8,64,384]{2,1,0:T(8,128)(2,1)S(1)}, u32[]{:S(2)}, u32[]{:S(2)}) collective-permute-start(bf16[8,64,384]{2,1,0:T(8,128)(2,1)S(1)} %get-tuple-element.32), channel_id=1, source_target_pairs={{0,1},{1,0},{2,3},{3,2},{4,5},{5,4},{6,7},{7,6},{8,9},{9,8},{10,11... | collective-permute-start | bytes 1179656 | tf_op jit(solution)/shard_map/ppermute | solution.py:410
  117.4 4.5 %all-to-all-start.2 = ((bf16[8,64,384]{2,1,0:T(8,128)(2,1)}), bf16[8,64,384]{2,1,0:T(8,128)(2,1)S(1)}, u32[]{:S(2)}, u32[]{:S(2)}) async-start(bf16[8,64,384]{2,1,0:T(8,128)(2,1)} %shard_map.133), calls=%async_computation.2 | async-start | bytes 786432 | tf_op jit(solution)/shard_map/all_to_all | solution.py:412
  122.6 8.5 %all-to-all-done.2.part = bf16[8,64,384]{2,1,0:T(8,128)(2,1)S(1)} async-done(((bf16[8,64,384]{2,1,0:T(8,128)(2,1)}), bf16[8,64,384]{2,1,0:T(8,128)(2,1)S(1)}, u32[]{:S(2)}, u32[]{:S(2)}) %all-to-all-start.2) | async-done | bytes 393248 | tf_op jit(solution)/shard_map/all_to_all | solution.py:412
  131.2 4.1 %collective-permute-start.27 = (bf16[64,320]{1,0:T(8,128)(2,1)S(1)}, bf16[64,320]{1,0:T(8,128)(2,1)S(1)}, u32[]{:S(2)}, u32[]{:S(2)}) collective-permute-start(bf16[64,320]{1,0:T(8,128)(2,1)S(1)} %shard_map.134), channel_id=1, source_target_pairs={{0,0},{1,16},{16,1},{17,17},{2,2},{3,18},{18,3},{19,19},{4,4},{5,2... | collective-permute-start | bytes 122888 | tf_op jit(solution)/shard_map/ppermute | solution.py:418
  (93 shorter events, 25.1 us)
Async XLA Ops:
  2.9 27.3 %all-to-all-start = ((bf16[8,64,320]{2,1,0:T(8,128)(2,1)}), bf16[8,64,320]{2,1,0:T(8,128)(2,1)S(1)}, u32[]{:S(2)}, u32[]{:S(2)}) async-start(bf16[8,64,320]{2,1,0:T(8,128)(2,1)} %broadcast_in_dim.24), calls=%async_computation | async-start | bytes 786432 | tf_op jit(solution)/shard_map/all_to_all | solution.py:307
  22.4 13.5 %collective-permute-start.18 = (bf16[320,640]{1,0:T(8,128)(2,1)}, bf16[320,640]{1,0:T(8,128)(2,1)S(1)}, u32[]{:S(2)}, u32[]{:S(2)}) collective-permute-start(bf16[320,640]{1,0:T(8,128)(2,1)} %bitcast.21), channel_id=1, source_target_pairs={{0,32},{32,64},{64,96},{96,128},{128,160},{160,192},{192,224},{224... | collective-permute-start | bytes 1228808 | tf_op jit(solution)/shard_map/ppermute | solution.py:291
  22.6 13.4 %collective-permute-start.19 = (bf16[320,640]{1,0:T(8,128)(2,1)}, bf16[320,640]{1,0:T(8,128)(2,1)S(1)}, u32[]{:S(2)}, u32[]{:S(2)}) collective-permute-start(bf16[320,640]{1,0:T(8,128)(2,1)} %bitcast.22), channel_id=1, source_target_pairs={{0,224},{32,0},{64,32},{96,64},{128,96},{160,128},{192,160},{224,1... | collective-permute-start | bytes 1228808 | tf_op jit(solution)/shard_map/ppermute | solution.py:292
  30.2 9.2 %collective-permute-start.1 = (bf16[512,320]{1,0:T(8,128)(2,1)S(1)}, bf16[512,320]{1,0:T(8,128)(2,1)S(1)}, u32[]{:S(2)}, u32[]{:S(2)}) collective-permute-start(bf16[512,320]{1,0:T(8,128)(2,1)S(1)} %bitcast.18), channel_id=1, source_target_pairs={{0,1},{1,0},{2,3},{3,2},{4,5},{5,4},{6,7},{7,6},{8,9},{9,8},{10,11... | collective-permute-start | bytes 983048 | tf_op jit(solution)/shard_map/ppermute | solution.py:310
  35.1 15.1 %collective-permute-start.2 = (bf16[320,640]{1,0:T(8,128)(2,1)}, bf16[320,640]{1,0:T(8,128)(2,1)}, u32[]{:S(2)}, u32[]{:S(2)}) collective-permute-start(bf16[320,640]{1,0:T(8,128)(2,1)} %x_own.1), channel_id=1, source_target_pairs={{0,16},{16,0},{1,17},{17,1},{2,18},{18,2},{3,19},{19,3},{4,20},{20... | collective-permute-start | bytes 1228808 | tf_op jit(solution)/shard_map/ppermute | solution.py:295
  35.8 11.7 %collective-permute-start.20 = (bf16[320,640]{1,0:T(8,128)(2,1)S(1)}, bf16[320,640]{1,0:T(8,128)(2,1)}, u32[]{:S(2)}, u32[]{:S(2)}) collective-permute-start(bf16[320,640]{1,0:T(8,128)(2,1)S(1)} %collective-permute-done.18.r1), channel_id=1, source_target_pairs={{0,32},{32,64},{64,96},{96,128},{128,160},{160,192},{192,224},{224... | collective-permute-start | bytes 1228808 | tf_op jit(solution)/shard_map/ppermute | solution.py:291
  36.0 13.0 %collective-permute-start.21 = (bf16[320,640]{1,0:T(8,128)(2,1)S(1)}, bf16[320,640]{1,0:T(8,128)(2,1)}, u32[]{:S(2)}, u32[]{:S(2)}) collective-permute-start(bf16[320,640]{1,0:T(8,128)(2,1)S(1)} %collective-permute-done.19.l1), channel_id=1, source_target_pairs={{0,224},{32,0},{64,32},{96,64},{128,96},{160,128},{192,160},{224,1... | collective-permute-start | bytes 1228808 | tf_op jit(solution)/shard_map/ppermute | solution.py:292
  38.5 16.6 %collective-permute-start.3 = (bf16[320,640]{1,0:T(8,128)(2,1)}, bf16[320,640]{1,0:T(8,128)(2,1)}, u32[]{:S(2)}, u32[]{:S(2)}) collective-permute-start(bf16[320,640]{1,0:T(8,128)(2,1)} %z_own.1), channel_id=1, source_target_pairs={{0,16},{16,0},{1,17},{17,1},{2,18},{18,2},{3,19},{19,3},{4,20},{20... | collective-permute-start | bytes 1228808 | tf_op jit(solution)/shard_map/ppermute | solution.py:296
  41.0 21.8 %all-to-all-start.1 = ((bf16[8,64,128]{2,1,0:T(8,128)(2,1)}), bf16[8,64,128]{2,1,0:T(8,128)(2,1)S(1)}, u32[]{:S(2)}, u32[]{:S(2)}) async-start(bf16[8,64,128]{2,1,0:T(8,128)(2,1)} %shard_map.128), calls=%async_computation.1 | async-start | bytes 262144 | tf_op jit(solution)/shard_map/all_to_all | solution.py:323
  47.6 41.4 %collective-permute-start.22 = (bf16[320,640]{1,0:T(8,128)(2,1)}, bf16[320,640]{1,0:T(8,128)(2,1)S(1)}, u32[]{:S(2)}, u32[]{:S(2)}) collective-permute-start(bf16[320,640]{1,0:T(8,128)(2,1)} %collective-permute-done.20.r2), channel_id=1, source_target_pairs={{0,32},{32,64},{64,96},{96,128},{128,160},{160,192},{192,224},{224... | collective-permute-start | bytes 1228808 | tf_op jit(solution)/shard_map/ppermute | solution.py:291
  48.9 43.9 %collective-permute-start.23 = (bf16[320,640]{1,0:T(8,128)(2,1)}, bf16[320,640]{1,0:T(8,128)(2,1)S(1)}, u32[]{:S(2)}, u32[]{:S(2)}) collective-permute-start(bf16[320,640]{1,0:T(8,128)(2,1)} %collective-permute-done.21.l2), channel_id=1, source_target_pairs={{0,224},{32,0},{64,32},{96,64},{128,96},{160,128},{192,160},{224,1... | collective-permute-start | bytes 1228808 | tf_op jit(solution)/shard_map/ppermute | solution.py:292
  60.1 8.3 %collective-permute-start.10 = (bf16[64,1280]{1,0:T(8,128)(2,1)}, bf16[64,1280]{1,0:T(8,128)(2,1)S(1)}, u32[]{:S(2)}, u32[]{:S(2)}) collective-permute-start(bf16[64,1280]{1,0:T(8,128)(2,1)} %get-tuple-element.26), channel_id=1, source_target_pairs={{0,224},{32,0},{64,32},{96,64},{128,96},{160,128},{192,160},{224,1... | collective-permute-start | bytes 491528 | tf_op jit(solution)/shard_map/ppermute | solution.py:343
  64.4 12.9 %collective-permute-start.4 = (bf16[64,1280]{1,0:T(8,128)(2,1)}, bf16[64,1280]{1,0:T(8,128)(2,1)S(1)}, u32[]{:S(2)}, u32[]{:S(2)}) collective-permute-start(bf16[64,1280]{1,0:T(8,128)(2,1)} %get-tuple-element.20), channel_id=1, source_target_pairs={{0,128},{32,160},{64,192},{96,224},{128,0},{160,32},{192,64},{224,... | collective-permute-start | bytes 491528 | tf_op jit(solution)/shard_map/ppermute | solution.py:343
  68.5 18.0 %collective-permute-start.5 = (bf16[64,1280]{1,0:T(8,128)(2,1)}, bf16[64,1280]{1,0:T(8,128)(2,1)S(1)}, u32[]{:S(2)}, u32[]{:S(2)}) collective-permute-start(bf16[64,1280]{1,0:T(8,128)(2,1)} %get-tuple-element.21), channel_id=1, source_target_pairs={{0,96},{32,128},{64,160},{96,192},{128,224},{160,0},{192,32},{224,... | collective-permute-start | bytes 491528 | tf_op jit(solution)/shard_map/ppermute | solution.py:343
  71.2 16.5 %collective-permute-start.6 = (bf16[64,1280]{1,0:T(8,128)(2,1)}, bf16[64,1280]{1,0:T(8,128)(2,1)S(1)}, u32[]{:S(2)}, u32[]{:S(2)}) collective-permute-start(bf16[64,1280]{1,0:T(8,128)(2,1)} %get-tuple-element.22), channel_id=1, source_target_pairs={{0,160},{32,192},{64,224},{96,0},{128,32},{160,64},{192,96},{224,1... | collective-permute-start | bytes 491528 | tf_op jit(solution)/shard_map/ppermute | solution.py:343
  77.3 11.7 %collective-permute-start.14 = (bf16[4,64,128]{2,1,0:T(8,128)(2,1)S(1)}, bf16[4,64,128]{2,1,0:T(8,128)(2,1)S(1)}, u32[]{:S(2)}, u32[]{:S(2)}) collective-permute-start(bf16[4,64,128]{2,1,0:T(8,128)(2,1)S(1)} %pad_maximum_fusion.bc0), channel_id=1, source_target_pairs={{4,0},{8,4},{12,8},{0,12},{5,1},{9,5},{13,9},{1,13},{6,2},{10,6},{... | collective-permute-start | bytes 196616 | tf_op jit(solution)/shard_map/ppermute | solution.py:353
  86.5 7.2 %collective-permute-start.15 = (bf16[4,64,128]{2,1,0:T(8,128)(2,1)S(1)}, bf16[4,64,128]{2,1,0:T(8,128)(2,1)}, u32[]{:S(2)}, u32[]{:S(2)}) collective-permute-start(bf16[4,64,128]{2,1,0:T(8,128)(2,1)S(1)} %pad_maximum_fusion.bc0), channel_id=1, source_target_pairs={{8,0},{12,4},{0,8},{4,12},{9,1},{13,5},{1,9},{5,13},{10,2},{14,6},... | collective-permute-start | bytes 196616 | tf_op jit(solution)/shard_map/ppermute | solution.py:353
  88.9 13.8 %collective-permute-start.7 = (bf16[64,1280]{1,0:T(8,128)(2,1)}, bf16[64,1280]{1,0:T(8,128)(2,1)}, u32[]{:S(2)}, u32[]{:S(2)}) collective-permute-start(bf16[64,1280]{1,0:T(8,128)(2,1)} %get-tuple-element.23), channel_id=1, source_target_pairs={{0,64},{32,96},{64,128},{96,160},{128,192},{160,224},{192,0},{224,... | collective-permute-start | bytes 491528 | tf_op jit(solution)/shard_map/ppermute | solution.py:343
  88.9 13.8 %collective-permute-start.8 = (bf16[64,1280]{1,0:T(8,128)(2,1)}, bf16[64,1280]{1,0:T(8,128)(2,1)}, u32[]{:S(2)}, u32[]{:S(2)}) collective-permute-start(bf16[64,1280]{1,0:T(8,128)(2,1)} %get-tuple-element.24), channel_id=1, source_target_pairs={{0,192},{32,224},{64,0},{96,32},{128,64},{160,96},{192,128},{224,1... | collective-permute-start | bytes 491528 | tf_op jit(solution)/shard_map/ppermute | solution.py:343
  92.8 10.6 %collective-permute-start.9 = (bf16[64,1280]{1,0:T(8,128)(2,1)}, bf16[64,1280]{1,0:T(8,128)(2,1)}, u32[]{:S(2)}, u32[]{:S(2)}) collective-permute-start(bf16[64,1280]{1,0:T(8,128)(2,1)} %get-tuple-element.25), channel_id=1, source_target_pairs={{0,32},{32,64},{64,96},{96,128},{128,160},{160,192},{192,224},{224... | collective-permute-start | bytes 491528 | tf_op jit(solution)/shard_map/ppermute | solution.py:343
  93.7 15.0 %collective-permute-start.24 = (bf16[160,640]{1,0:T(8,128)(2,1)S(1)}, bf16[160,640]{1,0:T(8,128)(2,1)S(1)}, u32[]{:S(2)}, u32[]{:S(2)}) collective-permute-start(bf16[160,640]{1,0:T(8,128)(2,1)S(1)} %slice.8), channel_id=1, source_target_pairs={{0,32},{32,64},{64,96},{96,128},{128,160},{160,192},{192,224},{224... | collective-permute-start | bytes 614408 | tf_op jit(solution)/shard_map/ppermute | solution.py:293
  93.8 14.9 %collective-permute-start.25 = (bf16[160,640]{1,0:T(8,128)(2,1)S(1)}, bf16[160,640]{1,0:T(8,128)(2,1)S(1)}, u32[]{:S(2)}, u32[]{:S(2)}) collective-permute-start(bf16[160,640]{1,0:T(8,128)(2,1)S(1)} %slice.9), channel_id=1, source_target_pairs={{0,224},{32,0},{64,32},{96,64},{128,96},{160,128},{192,160},{224,1... | collective-permute-start | bytes 614408 | tf_op jit(solution)/shard_map/ppermute | solution.py:294
  117.4 13.7 %all-to-all-start.2 = ((bf16[8,64,384]{2,1,0:T(8,128)(2,1)}), bf16[8,64,384]{2,1,0:T(8,128)(2,1)S(1)}, u32[]{:S(2)}, u32[]{:S(2)}) async-start(bf16[8,64,384]{2,1,0:T(8,128)(2,1)} %shard_map.133), calls=%async_computation.2 | async-start | bytes 786432 | tf_op jit(solution)/shard_map/all_to_all | solution.py:412
  131.2 5.9 %collective-permute-start.27 = (bf16[64,320]{1,0:T(8,128)(2,1)S(1)}, bf16[64,320]{1,0:T(8,128)(2,1)S(1)}, u32[]{:S(2)}, u32[]{:S(2)}) collective-permute-start(bf16[64,320]{1,0:T(8,128)(2,1)S(1)} %shard_map.134), channel_id=1, source_target_pairs={{0,0},{1,16},{16,1},{17,17},{2,2},{3,18},{18,3},{19,19},{4,4},{5,2... | collective-permute-start | bytes 122888 | tf_op jit(solution)/shard_map/ppermute | solution.py:418
  (22 other events, 390.4 us)

commit v9 on v8

--- a/solution.py
+++ b/solution.py
@@ -19,7 +19,7 @@
 PROJECT_LIMIT = 58 * 1024 * 1024
 STATE_LIMIT = 52 * 1024 * 1024
 
-SHIFTS = (4, 3, 5, 2, 6, 1, 7)
+SHIFTS = (3, 2, 5, 6, 1, 7)
 
 
 def nt(a, b):
@@ -116,6 +116,10 @@
             stores[-1].start()
     for store in stores:
         store.wait()
+
+
+def join_kernel(own, passed, out):
+    out[...] = (own[...].astype(F32) + passed[...].astype(F32)).astype(BF)
 
 
 def small_kernel(part, bc, small):
@@ -170,7 +174,7 @@
 
 
 def decode_kernel(*refs):
-    parts, (small, dots, g, bias, rate, skip, gain, out) = refs[:8], refs[8:]
+    parts, (small, dots, g, bias, rate, skip, gain, out) = refs[:7], refs[7:]
     heads = bias.shape[1]
     inner = gain.shape[1]
     half = parts[0].shape[0] // 2
@@ -338,6 +342,9 @@
         limit=PROJECT_LIMIT,
         flops=2 * 16 * rows * 2 * wide * 2 * inner,
     )
+    blocks = list(blocks)
+    passed = lax.ppermute(blocks[4], "z", left)
+    blocks[5] = call(join_kernel, jax.ShapeDtypeStruct(blocks[5].shape, BF), (blocks[5], passed))
     parts = [blocks[0]]
     for k in SHIFTS:
         parts.append(lax.ppermute(blocks[k], "z", [(i, (i + k) % 8) for i in range(8)]))

time: 138 us -> 146 us (1.058)
  the two profiles are of different devices: /device:TPU:1 before, /device:TPU:33 now
where the time goes in v9:
time: 146 us; the launch traced here: 145 us
  starting transfers between devices  72.2 us (49%)
  waiting for transfers between devices  46.6 us (32%)
  Pallas kernels  18.4 us (13%)
  local copies, waits for them, and re-layouts  5.04 us (3%)
  other arithmetic  1.79 us (1%)
    pallas_call x9, Pallas kernels, call(): pl.pallas_call(body, out_shape=out_shape, in_specs=in_specs, out_specs=ou...  18.4 us
    ppermute x6, waiting for transfers between devices, per_device(): lax.ppermute(blocks[k], 'z', [(i, (i + k) % 8) for i in range(8)])  17.8 us
    ppermute x6, starting transfers between devices, per_device(): lax.ppermute(blocks[k], 'z', [(i, (i + k) % 8) for i in range(8)])  14.4 us
    all_to_all x1, starting transfers between devices, per_device(): lax.all_to_all(jnp.broadcast_to(moved[None], (8,) + moved.shape), ('x', '...  10.6 us
    all_to_all x1, waiting for transfers between devices, per_device(): partial_out = lax.all_to_all(paired, ('x', 'yh'), 0, 0)  8.5 us
    all_to_all x1, starting transfers between devices, per_device(): part_small = lax.all_to_all(part_small, 'z', 0, 0)  7.43 us
    ppermute x3, starting transfers between devices, per_device(): ring_r.append(lax.ppermute(ring_r[-1], 'z', right))  6.96 us
    ppermute x1, starting transfers between devices, per_device(): got = lax.ppermute(send, 'core', pair)  6.93 us
  transfers between devices with their start and end apart: 31, of which 11 were waited for; matrix products, arithmetic and copies ran while one was open for 1% of the time, Pallas kernels for 10%

profile of v9, /device:TPU:33, one launch (start us, length us, event | category | flops | bytes accessed | tf_op | source)
XLA Modules:
  0.0 145.3 jit_solution(13379438024448518143)
XLA Ops:
  1.5 4.4 %collective-permute-start = (bf16[64,320]{1,0:T(8,128)(2,1)S(1)}, bf16[64,320]{1,0:T(8,128)(2,1)S(1)}, u32[]{:S(2)}, u32[]{:S(2)}) collective-permute-start(bf16[64,320]{1,0:T(8,128)(2,1)S(1)} %convolution_convert_fusion), channel_id=1, source_target_pairs={{0,0},{1,1},{2,32},{3,33},{4,64},{5,65},{6,96},{7,97},{8,128},{9,1... | collective-permute-start | bytes 122888 | tf_op jit(solution)/shard_map/ppermute | solution.py:310
  5.8 2.9 %collective-permute-done = bf16[64,320]{1,0:T(8,128)(2,1)S(1)} collective-permute-done((bf16[64,320]{1,0:T(8,128)(2,1)S(1)}, bf16[64,320]{1,0:T(8,128)(2,1)S(1)}, u32[]{:S(2)}, u32[]{:S(2)}) %collective-permute-start) | collective-permute-done | bytes 40992 | tf_op jit(solution)/shard_map/ppermute | solution.py:310
  9.5 10.6 %all-to-all-start = ((bf16[8,64,320]{2,1,0:T(8,128)(2,1)}), bf16[8,64,320]{2,1,0:T(8,128)(2,1)S(1)}, u32[]{:S(2)}, u32[]{:S(2)}) async-start(bf16[8,64,320]{2,1,0:T(8,128)(2,1)} %broadcast_in_dim.24), calls=%async_computation | async-start | bytes 786432 | tf_op jit(solution)/shard_map/all_to_all | solution.py:311
  20.1 2.8 %collective-permute-start.18 = (bf16[320,640]{1,0:T(8,128)(2,1)}, bf16[320,640]{1,0:T(8,128)(2,1)S(1)}, u32[]{:S(2)}, u32[]{:S(2)}) collective-permute-start(bf16[320,640]{1,0:T(8,128)(2,1)} %bitcast.21), channel_id=1, source_target_pairs={{0,32},{32,64},{64,96},{96,128},{128,160},{160,192},{192,224},{224... | collective-permute-start | bytes 1228808 | tf_op jit(solution)/shard_map/ppermute | solution.py:295
  23.0 4.9 %all-to-all-done = bf16[8,64,320]{2,1,0:T(8,128)(2,1)S(1)} async-done(((bf16[8,64,320]{2,1,0:T(8,128)(2,1)}), bf16[8,64,320]{2,1,0:T(8,128)(2,1)S(1)}, u32[]{:S(2)}, u32[]{:S(2)}) %all-to-all-start) | async-done | bytes 327712 | tf_op jit(solution)/shard_map/all_to_all | solution.py:311
  27.9 3.2 %collective-permute-start.1 = (bf16[512,320]{1,0:T(8,128)(2,1)S(1)}, bf16[512,320]{1,0:T(8,128)(2,1)S(1)}, u32[]{:S(2)}, u32[]{:S(2)}) collective-permute-start(bf16[512,320]{1,0:T(8,128)(2,1)S(1)} %bitcast.18), channel_id=1, source_target_pairs={{0,1},{1,0},{2,3},{3,2},{4,5},{5,4},{6,7},{7,6},{8,9},{9,8},{10,11... | collective-permute-start | bytes 983048 | tf_op jit(solution)/shard_map/ppermute | solution.py:314
  33.5 2.9 %collective-permute-start.20 = (bf16[320,640]{1,0:T(8,128)(2,1)S(1)}, bf16[320,640]{1,0:T(8,128)(2,1)}, u32[]{:S(2)}, u32[]{:S(2)}) collective-permute-start(bf16[320,640]{1,0:T(8,128)(2,1)S(1)} %collective-permute-done.18.r1), channel_id=1, source_target_pairs={{0,32},{32,64},{64,96},{96,128},{128,160},{160,192},{192,224},{224... | collective-permute-start | bytes 1228808 | tf_op jit(solution)/shard_map/ppermute | solution.py:295
  38.9 7.4 %all-to-all-start.1 = ((bf16[8,64,128]{2,1,0:T(8,128)(2,1)}), bf16[8,64,128]{2,1,0:T(8,128)(2,1)S(1)}, u32[]{:S(2)}, u32[]{:S(2)}) async-start(bf16[8,64,128]{2,1,0:T(8,128)(2,1)} %shard_map.129), calls=%async_computation.1 | async-start | bytes 262144 | tf_op jit(solution)/shard_map/all_to_all | solution.py:327
  47.9 4.9 %collective-permute-done.3.z_oth = bf16[320,640]{1,0:T(8,128)(2,1)} collective-permute-done((bf16[320,640]{1,0:T(8,128)(2,1)}, bf16[320,640]{1,0:T(8,128)(2,1)}, u32[]{:S(2)}, u32[]{:S(2)}) %collective-permute-start.3) | collective-permute-done | bytes 409632 | tf_op jit(solution)/shard_map/ppermute | solution.py:300
  52.8 5.0 %shard_map.127 = (bf16[64,1280]{1,0:T(8,128)(2,1)}, bf16[64,1280]{1,0:T(8,128)(2,1)}, bf16[64,1280]{1,0:T(8,128)(2,1)}, bf16[64,1280]{1,0:T(8,128)(2,1)}, bf16[6...) custom-call(s32[2]{0:T(128)} %copy-done.12, ...), custom_call_target="tpu_custom_call" | custom-call | flops 838860800 | bytes 1048576 | tf_op jit(solution)/shard_map/pallas_call | solution.py:40
  60.8 2.5 %collective-permute-start.10 = (bf16[64,1280]{1,0:T(8,128)(2,1)}, bf16[64,1280]{1,0:T(8,128)(2,1)S(1)}, u32[]{:S(2)}, u32[]{:S(2)}) collective-permute-start(bf16[64,1280]{1,0:T(8,128)(2,1)} %get-tuple-element.26), channel_id=1, source_target_pairs={{0,224},{32,0},{64,32},{96,64},{128,96},{160,128},{192,160},{224,1... | collective-permute-start | bytes 491528 | tf_op jit(solution)/shard_map/ppermute | solution.py:350
  65.2 2.5 %collective-permute-start.4 = (bf16[64,1280]{1,0:T(8,128)(2,1)}, bf16[64,1280]{1,0:T(8,128)(2,1)S(1)}, u32[]{:S(2)}, u32[]{:S(2)}) collective-permute-start(bf16[64,1280]{1,0:T(8,128)(2,1)} %get-tuple-element.20), channel_id=1, source_target_pairs={{0,96},{32,128},{64,160},{96,192},{128,224},{160,0},{192,32},{224,... | collective-permute-start | bytes 491528 | tf_op jit(solution)/shard_map/ppermute | solution.py:350
  71.3 5.8 %collective-permute-done.4.refs_1_ = bf16[64,1280]{1,0:T(8,128)(2,1)S(1)} collective-permute-done((bf16[64,1280]{1,0:T(8,128)(2,1)}, bf16[64,1280]{1,0:T(8,128)(2,1)S(1)}, u32[]{:S(2)}, u32[]{:S(2)}) %collective-permute-start.4) | collective-permute-done | bytes 163872 | tf_op jit(solution)/shard_map/ppermute | solution.py:350
  77.8 7.3 %collective-permute-done.5.refs_2_ = bf16[64,1280]{1,0:T(8,128)(2,1)S(1)} collective-permute-done((bf16[64,1280]{1,0:T(8,128)(2,1)}, bf16[64,1280]{1,0:T(8,128)(2,1)S(1)}, u32[]{:S(2)}, u32[]{:S(2)}) %collective-permute-start.5) | collective-permute-done | bytes 163872 | tf_op jit(solution)/shard_map/ppermute | solution.py:350
  86.8 5.1 %collective-permute-start.8 = (bf16[64,1280]{1,0:T(8,128)(2,1)}, bf16[64,1280]{1,0:T(8,128)(2,1)}, u32[]{:S(2)}, u32[]{:S(2)}) collective-permute-start(bf16[64,1280]{1,0:T(8,128)(2,1)} %get-tuple-element.24), channel_id=1, source_target_pairs={{0,192},{32,224},{64,0},{96,32},{128,64},{160,96},{192,128},{224,1... | collective-permute-start | bytes 491528 | tf_op jit(solution)/shard_map/ppermute | solution.py:350
  91.9 2.7 %collective-permute-start.7 = (bf16[64,1280]{1,0:T(8,128)(2,1)S(1)}, bf16[64,1280]{1,0:T(8,128)(2,1)}, u32[]{:S(2)}, u32[]{:S(2)}) collective-permute-start(bf16[64,1280]{1,0:T(8,128)(2,1)S(1)} %shard_map.128), channel_id=1, source_target_pairs={{0,160},{32,192},{64,224},{96,0},{128,32},{160,64},{192,96},{224,1... | collective-permute-start | bytes 491528 | tf_op jit(solution)/shard_map/ppermute | solution.py:350
  97.0 6.1 %shard_map.131 = (f32[32,8,640]{2,1,0:T(8,128)S(1)}, f32[32,128]{1,0:T(8,128)S(1)}) custom-call(s32[3]{0:T(128)S(1)} %pad_add_fusion.2.place, bf16[4,64,128]{2,1,0:T(8,128)(2,1)S(1)} %pad_maximum_fusion.bc0, bf16[4,64,128]{2,1,0:T(8,128)(2,1)S(1)} %collective-permute-done.14.bc1, bf16[4,64,128]{2,1,0:T(8,128)(2,1)} %collective-permute-done.15.bc2, ...), custom_call_target="tpu_custom_call" | custom-call | flops 83886080 | bytes 1048576 | tf_op jit(solution)/shard_map/pallas_call | solution.py:40
  103.2 4.6 %collective-permute-done.7.refs_3_ = bf16[64,1280]{1,0:T(8,128)(2,1)} collective-permute-done((bf16[64,1280]{1,0:T(8,128)(2,1)S(1)}, bf16[64,1280]{1,0:T(8,128)(2,1)}, u32[]{:S(2)}, u32[]{:S(2)}) %collective-permute-start.7) | collective-permute-done | bytes 163872 | tf_op jit(solution)/shard_map/ppermute | solution.py:350
  109.8 3.6 %collective-permute-done.17.other = bf16[64,640]{1,0:T(8,128)(2,1)S(1)} collective-permute-done((bf16[64,640]{1,0:T(8,128)(2,1)S(1)}, bf16[64,640]{1,0:T(8,128)(2,1)S(1)}, u32[]{:S(2)}, u32[]{:S(2)}) %collective-permute-start.17) | collective-permute-done | bytes 81952 | tf_op jit(solution)/shard_map/ppermute | solution.py:392
  115.9 6.9 %collective-permute-start.26 = (bf16[8,64,384]{2,1,0:T(8,128)(2,1)S(1)}, bf16[8,64,384]{2,1,0:T(8,128)(2,1)S(1)}, u32[]{:S(2)}, u32[]{:S(2)}) collective-permute-start(bf16[8,64,384]{2,1,0:T(8,128)(2,1)S(1)} %get-tuple-element.32), channel_id=1, source_target_pairs={{0,1},{1,0},{2,3},{3,2},{4,5},{5,4},{6,7},{7,6},{8,9},{9,8},{10,11... | collective-permute-start | bytes 1179656 | tf_op jit(solution)/shard_map/ppermute | solution.py:417
  125.2 4.6 %all-to-all-start.2 = ((bf16[8,64,384]{2,1,0:T(8,128)(2,1)}), bf16[8,64,384]{2,1,0:T(8,128)(2,1)S(1)}, u32[]{:S(2)}, u32[]{:S(2)}) async-start(bf16[8,64,384]{2,1,0:T(8,128)(2,1)} %shard_map.134), calls=%async_computation.2 | async-start | bytes 786432 | tf_op jit(solution)/shard_map/all_to_all | solution.py:419
  130.5 8.5 %all-to-all-done.2.part = bf16[8,64,384]{2,1,0:T(8,128)(2,1)S(1)} async-done(((bf16[8,64,384]{2,1,0:T(8,128)(2,1)}), bf16[8,64,384]{2,1,0:T(8,128)(2,1)S(1)}, u32[]{:S(2)}, u32[]{:S(2)}) %all-to-all-start.2) | async-done | bytes 393248 | tf_op jit(solution)/shard_map/all_to_all | solution.py:419
  139.2 2.8 %collective-permute-start.27 = (bf16[64,320]{1,0:T(8,128)(2,1)S(1)}, bf16[64,320]{1,0:T(8,128)(2,1)S(1)}, u32[]{:S(2)}, u32[]{:S(2)}) collective-permute-start(bf16[64,320]{1,0:T(8,128)(2,1)S(1)} %shard_map.135), channel_id=1, source_target_pairs={{0,0},{1,16},{16,1},{17,17},{2,2},{3,18},{18,3},{19,19},{4,4},{5,2... | collective-permute-start | bytes 122888 | tf_op jit(solution)/shard_map/ppermute | solution.py:425
  142.0 2.6 %collective-permute-done.27 = bf16[64,320]{1,0:T(8,128)(2,1)S(1)} collective-permute-done((bf16[64,320]{1,0:T(8,128)(2,1)S(1)}, bf16[64,320]{1,0:T(8,128)(2,1)S(1)}, u32[]{:S(2)}, u32[]{:S(2)}) %collective-permute-start.27) | collective-permute-done | bytes 40992 | tf_op jit(solution)/shard_map/ppermute | solution.py:425
  (96 shorter events, 29.7 us)
Async XLA Ops:
  9.5 18.4 %all-to-all-start = ((bf16[8,64,320]{2,1,0:T(8,128)(2,1)}), bf16[8,64,320]{2,1,0:T(8,128)(2,1)S(1)}, u32[]{:S(2)}, u32[]{:S(2)}) async-start(bf16[8,64,320]{2,1,0:T(8,128)(2,1)} %broadcast_in_dim.24), calls=%async_computation | async-start | bytes 786432 | tf_op jit(solution)/shard_map/all_to_all | solution.py:311
  20.1 13.4 %collective-permute-start.18 = (bf16[320,640]{1,0:T(8,128)(2,1)}, bf16[320,640]{1,0:T(8,128)(2,1)S(1)}, u32[]{:S(2)}, u32[]{:S(2)}) collective-permute-start(bf16[320,640]{1,0:T(8,128)(2,1)} %bitcast.21), channel_id=1, source_target_pairs={{0,32},{32,64},{64,96},{96,128},{128,160},{160,192},{192,224},{224... | collective-permute-start | bytes 1228808 | tf_op jit(solution)/shard_map/ppermute | solution.py:295
  22.9 13.5 %collective-permute-start.19 = (bf16[320,640]{1,0:T(8,128)(2,1)}, bf16[320,640]{1,0:T(8,128)(2,1)S(1)}, u32[]{:S(2)}, u32[]{:S(2)}) collective-permute-start(bf16[320,640]{1,0:T(8,128)(2,1)} %bitcast.22), channel_id=1, source_target_pairs={{0,224},{32,0},{64,32},{96,64},{128,96},{160,128},{192,160},{224,1... | collective-permute-start | bytes 1228808 | tf_op jit(solution)/shard_map/ppermute | solution.py:296
  27.9 9.4 %collective-permute-start.1 = (bf16[512,320]{1,0:T(8,128)(2,1)S(1)}, bf16[512,320]{1,0:T(8,128)(2,1)S(1)}, u32[]{:S(2)}, u32[]{:S(2)}) collective-permute-start(bf16[512,320]{1,0:T(8,128)(2,1)S(1)} %bitcast.18), channel_id=1, source_target_pairs={{0,1},{1,0},{2,3},{3,2},{4,5},{5,4},{6,7},{7,6},{8,9},{9,8},{10,11... | collective-permute-start | bytes 983048 | tf_op jit(solution)/shard_map/ppermute | solution.py:314
  32.7 15.2 %collective-permute-start.2 = (bf16[320,640]{1,0:T(8,128)(2,1)}, bf16[320,640]{1,0:T(8,128)(2,1)}, u32[]{:S(2)}, u32[]{:S(2)}) collective-permute-start(bf16[320,640]{1,0:T(8,128)(2,1)} %x_own.1), channel_id=1, source_target_pairs={{0,16},{16,0},{1,17},{17,1},{2,18},{18,2},{3,19},{19,3},{4,20},{20... | collective-permute-start | bytes 1228808 | tf_op jit(solution)/shard_map/ppermute | solution.py:299
  33.5 12.9 %collective-permute-start.20 = (bf16[320,640]{1,0:T(8,128)(2,1)S(1)}, bf16[320,640]{1,0:T(8,128)(2,1)}, u32[]{:S(2)}, u32[]{:S(2)}) collective-permute-start(bf16[320,640]{1,0:T(8,128)(2,1)S(1)} %collective-permute-done.18.r1), channel_id=1, source_target_pairs={{0,32},{32,64},{64,96},{96,128},{128,160},{160,192},{192,224},{224... | collective-permute-start | bytes 1228808 | tf_op jit(solution)/shard_map/ppermute | solution.py:295
  36.4 11.3 %collective-permute-start.21 = (bf16[320,640]{1,0:T(8,128)(2,1)S(1)}, bf16[320,640]{1,0:T(8,128)(2,1)}, u32[]{:S(2)}, u32[]{:S(2)}) collective-permute-start(bf16[320,640]{1,0:T(8,128)(2,1)S(1)} %collective-permute-done.19.l1), channel_id=1, source_target_pairs={{0,224},{32,0},{64,32},{96,64},{128,96},{160,128},{192,160},{224,1... | collective-permute-start | bytes 1228808 | tf_op jit(solution)/shard_map/ppermute | solution.py:296
  36.4 16.4 %collective-permute-start.3 = (bf16[320,640]{1,0:T(8,128)(2,1)}, bf16[320,640]{1,0:T(8,128)(2,1)}, u32[]{:S(2)}, u32[]{:S(2)}) collective-permute-start(bf16[320,640]{1,0:T(8,128)(2,1)} %z_own.1), channel_id=1, source_target_pairs={{0,16},{16,0},{1,17},{17,1},{2,18},{18,2},{3,19},{19,3},{4,20},{20... | collective-permute-start | bytes 1228808 | tf_op jit(solution)/shard_map/ppermute | solution.py:300
  38.9 20.3 %all-to-all-start.1 = ((bf16[8,64,128]{2,1,0:T(8,128)(2,1)}), bf16[8,64,128]{2,1,0:T(8,128)(2,1)S(1)}, u32[]{:S(2)}, u32[]{:S(2)}) async-start(bf16[8,64,128]{2,1,0:T(8,128)(2,1)} %shard_map.129), calls=%async_computation.1 | async-start | bytes 262144 | tf_op jit(solution)/shard_map/all_to_all | solution.py:327
  46.4 45.5 %collective-permute-start.22 = (bf16[320,640]{1,0:T(8,128)(2,1)}, bf16[320,640]{1,0:T(8,128)(2,1)S(1)}, u32[]{:S(2)}, u32[]{:S(2)}) collective-permute-start(bf16[320,640]{1,0:T(8,128)(2,1)} %collective-permute-done.20.r2), channel_id=1, source_target_pairs={{0,32},{32,64},{64,96},{96,128},{128,160},{160,192},{192,224},{224... | collective-permute-start | bytes 1228808 | tf_op jit(solution)/shard_map/ppermute | solution.py:295
  47.7 44.2 %collective-permute-start.23 = (bf16[320,640]{1,0:T(8,128)(2,1)}, bf16[320,640]{1,0:T(8,128)(2,1)S(1)}, u32[]{:S(2)}, u32[]{:S(2)}) collective-permute-start(bf16[320,640]{1,0:T(8,128)(2,1)} %collective-permute-done.21.l2), channel_id=1, source_target_pairs={{0,224},{32,0},{64,32},{96,64},{128,96},{160,128},{192,160},{224,1... | collective-permute-start | bytes 1228808 | tf_op jit(solution)/shard_map/ppermute | solution.py:296
  60.8 8.6 %collective-permute-start.10 = (bf16[64,1280]{1,0:T(8,128)(2,1)}, bf16[64,1280]{1,0:T(8,128)(2,1)S(1)}, u32[]{:S(2)}, u32[]{:S(2)}) collective-permute-start(bf16[64,1280]{1,0:T(8,128)(2,1)} %get-tuple-element.26), channel_id=1, source_target_pairs={{0,224},{32,0},{64,32},{96,64},{128,96},{160,128},{192,160},{224,1... | collective-permute-start | bytes 491528 | tf_op jit(solution)/shard_map/ppermute | solution.py:350
  65.2 11.9 %collective-permute-start.4 = (bf16[64,1280]{1,0:T(8,128)(2,1)}, bf16[64,1280]{1,0:T(8,128)(2,1)S(1)}, u32[]{:S(2)}, u32[]{:S(2)}) collective-permute-start(bf16[64,1280]{1,0:T(8,128)(2,1)} %get-tuple-element.20), channel_id=1, source_target_pairs={{0,96},{32,128},{64,160},{96,192},{128,224},{160,0},{192,32},{224,... | collective-permute-start | bytes 491528 | tf_op jit(solution)/shard_map/ppermute | solution.py:350
  67.9 17.2 %collective-permute-start.5 = (bf16[64,1280]{1,0:T(8,128)(2,1)}, bf16[64,1280]{1,0:T(8,128)(2,1)S(1)}, u32[]{:S(2)}, u32[]{:S(2)}) collective-permute-start(bf16[64,1280]{1,0:T(8,128)(2,1)} %get-tuple-element.21), channel_id=1, source_target_pairs={{0,64},{32,96},{64,128},{96,160},{128,192},{160,224},{192,0},{224,... | collective-permute-start | bytes 491528 | tf_op jit(solution)/shard_map/ppermute | solution.py:350
  69.5 17.3 %collective-permute-start.14 = (bf16[4,64,128]{2,1,0:T(8,128)(2,1)S(1)}, bf16[4,64,128]{2,1,0:T(8,128)(2,1)S(1)}, u32[]{:S(2)}, u32[]{:S(2)}) collective-permute-start(bf16[4,64,128]{2,1,0:T(8,128)(2,1)S(1)} %pad_maximum_fusion.bc0), channel_id=1, source_target_pairs={{4,0},{8,4},{12,8},{0,12},{5,1},{9,5},{13,9},{1,13},{6,2},{10,6},{... | collective-permute-start | bytes 196616 | tf_op jit(solution)/shard_map/ppermute | solution.py:360
  77.8 17.6 %collective-permute-start.15 = (bf16[4,64,128]{2,1,0:T(8,128)(2,1)S(1)}, bf16[4,64,128]{2,1,0:T(8,128)(2,1)}, u32[]{:S(2)}, u32[]{:S(2)}) collective-permute-start(bf16[4,64,128]{2,1,0:T(8,128)(2,1)S(1)} %pad_maximum_fusion.bc0), channel_id=1, source_target_pairs={{8,0},{12,4},{0,8},{4,12},{9,1},{13,5},{1,9},{5,13},{10,2},{14,6},... | collective-permute-start | bytes 196616 | tf_op jit(solution)/shard_map/ppermute | solution.py:360
  85.8 9.7 %collective-permute-start.16 = (bf16[4,64,128]{2,1,0:T(8,128)(2,1)S(1)}, bf16[4,64,128]{2,1,0:T(8,128)(2,1)}, u32[]{:S(2)}, u32[]{:S(2)}) collective-permute-start(bf16[4,64,128]{2,1,0:T(8,128)(2,1)S(1)} %pad_maximum_fusion.bc0), channel_id=1, source_target_pairs={{12,0},{0,4},{4,8},{8,12},{13,1},{1,5},{5,9},{9,13},{14,2},{2,6},{... | collective-permute-start | bytes 196616 | tf_op jit(solution)/shard_map/ppermute | solution.py:360
  86.8 16.4 %collective-permute-start.8 = (bf16[64,1280]{1,0:T(8,128)(2,1)}, bf16[64,1280]{1,0:T(8,128)(2,1)}, u32[]{:S(2)}, u32[]{:S(2)}) collective-permute-start(bf16[64,1280]{1,0:T(8,128)(2,1)} %get-tuple-element.24), channel_id=1, source_target_pairs={{0,192},{32,224},{64,0},{96,32},{128,64},{160,96},{192,128},{224,1... | collective-permute-start | bytes 491528 | tf_op jit(solution)/shard_map/ppermute | solution.py:350
  91.9 11.3 %collective-permute-start.9 = (bf16[64,1280]{1,0:T(8,128)(2,1)}, bf16[64,1280]{1,0:T(8,128)(2,1)}, u32[]{:S(2)}, u32[]{:S(2)}) collective-permute-start(bf16[64,1280]{1,0:T(8,128)(2,1)} %get-tuple-element.25), channel_id=1, source_target_pairs={{0,32},{32,64},{64,96},{96,128},{128,160},{160,192},{192,224},{224... | collective-permute-start | bytes 491528 | tf_op jit(solution)/shard_map/ppermute | solution.py:350
  91.9 15.9 %collective-permute-start.7 = (bf16[64,1280]{1,0:T(8,128)(2,1)S(1)}, bf16[64,1280]{1,0:T(8,128)(2,1)}, u32[]{:S(2)}, u32[]{:S(2)}) collective-permute-start(bf16[64,1280]{1,0:T(8,128)(2,1)S(1)} %shard_map.128), channel_id=1, source_target_pairs={{0,160},{32,192},{64,224},{96,0},{128,32},{160,64},{192,96},{224,1... | collective-permute-start | bytes 491528 | tf_op jit(solution)/shard_map/ppermute | solution.py:350
  95.4 18.1 %collective-permute-start.24 = (bf16[160,640]{1,0:T(8,128)(2,1)S(1)}, bf16[160,640]{1,0:T(8,128)(2,1)S(1)}, u32[]{:S(2)}, u32[]{:S(2)}) collective-permute-start(bf16[160,640]{1,0:T(8,128)(2,1)S(1)} %slice.8), channel_id=1, source_target_pairs={{0,32},{32,64},{64,96},{96,128},{128,160},{160,192},{192,224},{224... | collective-permute-start | bytes 614408 | tf_op jit(solution)/shard_map/ppermute | solution.py:297
  95.5 17.9 %collective-permute-start.25 = (bf16[160,640]{1,0:T(8,128)(2,1)S(1)}, bf16[160,640]{1,0:T(8,128)(2,1)S(1)}, u32[]{:S(2)}, u32[]{:S(2)}) collective-permute-start(bf16[160,640]{1,0:T(8,128)(2,1)S(1)} %slice.9), channel_id=1, source_target_pairs={{0,224},{32,0},{64,32},{96,64},{128,96},{160,128},{192,160},{224,1... | collective-permute-start | bytes 614408 | tf_op jit(solution)/shard_map/ppermute | solution.py:298
  115.9 8.3 %collective-permute-start.26 = (bf16[8,64,384]{2,1,0:T(8,128)(2,1)S(1)}, bf16[8,64,384]{2,1,0:T(8,128)(2,1)S(1)}, u32[]{:S(2)}, u32[]{:S(2)}) collective-permute-start(bf16[8,64,384]{2,1,0:T(8,128)(2,1)S(1)} %get-tuple-element.32), channel_id=1, source_target_pairs={{0,1},{1,0},{2,3},{3,2},{4,5},{5,4},{6,7},{7,6},{8,9},{9,8},{10,11... | collective-permute-start | bytes 1179656 | tf_op jit(solution)/shard_map/ppermute | solution.py:417
  125.2 13.8 %all-to-all-start.2 = ((bf16[8,64,384]{2,1,0:T(8,128)(2,1)}), bf16[8,64,384]{2,1,0:T(8,128)(2,1)S(1)}, u32[]{:S(2)}, u32[]{:S(2)}) async-start(bf16[8,64,384]{2,1,0:T(8,128)(2,1)} %shard_map.134), calls=%async_computation.2 | async-start | bytes 786432 | tf_op jit(solution)/shard_map/all_to_all | solution.py:419
  (23 other events, 469.0 us)

commit v10 on v9

--- a/solution.py
+++ b/solution.py
@@ -216,7 +216,7 @@
     out[...] = jnp.concatenate([gg1, gg2], 0).astype(BF)
 
 
-def output_kernel(place, mine, other, gain, own, r1, l1, r2, l2, r3, l3, r4, l4, keep, send):
+def output_kernel(place, mine, other, gain, own, r1, l1, r2, l2, r3, l3, r4, keep, send):
     z = place[0]
     same = place[1]
     groups, rows, _ = keep.shape
@@ -228,10 +228,9 @@
     hi = ss.astype(BF).astype(F32)
     lane = lax.broadcasted_iota(jnp.int32, (2 * rows, 64), 1)
     tail = jnp.where(lane == 0, hi, jnp.where(lane == 1, ss - hi, 0.0))
-    order = ((0, own), (7, r1), (1, l1), (6, r2), (2, l2), (5, r3), (3, l3), (4, None))
+    order = ((0, own), (7, r1), (1, l1), (6, r2), (2, l2), (5, r3), (3, l3), (4, r4))
     for shift, w in order:
-        w = jnp.concatenate([r4[...], l4[...]], 0) if w is None else w[...]
-        block = jnp.concatenate([nt(v, w), tail], 1)
+        block = jnp.concatenate([nt(v, w[...]), tail], 1)
         at = lax.rem(z + shift, groups)
         keep[at] = block[:rows]
         send[at] = block[rows:].astype(BF)
@@ -294,8 +293,7 @@
     for _ in range(1, 4):
         ring_r.append(lax.ppermute(ring_r[-1], "z", right))
         ring_l.append(lax.ppermute(ring_l[-1], "z", left))
-    far_r = lax.ppermute(ring_r[3][: wide // 2], "z", right)
-    far_l = lax.ppermute(ring_l[3][wide // 2 :], "z", left)
+    ring_r.append(lax.ppermute(ring_r[3], "z", right))
     x_oth = lax.ppermute(x_weight, "yl", pair)
     z_oth = lax.ppermute(z_weight, "yl", pair)
     small_own = jnp.concatenate(
@@ -408,8 +406,7 @@
             ring_l[2],
             ring_r[3],
             ring_l[3],
-            far_r,
-            far_l,
+            ring_r[4],
         ),
         in_smem=1,
         flops=2 * 4 * rows * inner * 8 * wide,

time: 146 us -> 153 us (1.048)
  the two profiles are of different devices: /device:TPU:33 before, /device:TPU:1 now
where the time goes in v10:
time: 153 us
  starting transfers between devices  73.7 us (48%)
  waiting for transfers between devices  47 us (31%)
  Pallas kernels  18.3 us (12%)
  local copies, waits for them, and re-layouts  9.72 us (6%)
  other arithmetic  2.59 us (2%)
    ppermute x1, waiting for transfers between devices, per_device(): small_oth = lax.ppermute(small_own, 'yl', pair)  20.8 us
    all_to_all x1, starting transfers between devices, per_device(): lax.all_to_all(jnp.broadcast_to(moved[None], (8,) + moved.shape), ('x', '...  20.5 us
    pallas_call x9, Pallas kernels, call(): pl.pallas_call(body, out_shape=out_shape, in_specs=in_specs, out_specs=ou...  18.3 us
    ppermute x6, starting transfers between devices, per_device(): lax.ppermute(blocks[k], 'z', [(i, (i + k) % 8) for i in range(8)])  8.86 us
    all_to_all x1, waiting for transfers between devices, per_device(): partial_out = lax.all_to_all(paired, ('x', 'yh'), 0, 0)  8.5 us
    unnamed x48, local copies, waits for them, and re-layouts  7.35 us
    ppermute x1, starting transfers between devices, per_device(): got = lax.ppermute(send, 'core', pair)  6.9 us
    ppermute x6, waiting for transfers between devices, per_device(): lax.ppermute(blocks[k], 'z', [(i, (i + k) % 8) for i in range(8)])  6.89 us
  transfers between devices with their start and end apart: 30, of which 10 were waited for; matrix products, arithmetic and copies ran while one was open for 2% of the time, Pallas kernels for 10%

profile of v10, /device:TPU:1, one launch (start us, length us, event | category | flops | bytes accessed | tf_op | source)
XLA Modules:
  0.0 152.7 jit_solution(6347615953594067506)
XLA Ops:
  0.0 2.5 %collective-permute-start.18 = (bf16[320,640]{1,0:T(8,128)(2,1)}, bf16[320,640]{1,0:T(8,128)(2,1)S(1)}, u32[]{:S(2)}, u32[]{:S(2)}) collective-permute-start(bf16[320,640]{1,0:T(8,128)(2,1)} %bitcast.21), channel_id=1, source_target_pairs={{0,32},{32,64},{64,96},{96,128},{128,160},{160,192},{192,224},{224... | collective-permute-start | bytes 1228808 | tf_op jit(solution)/shard_map/ppermute | solution.py:294
  5.1 20.5 %all-to-all-start = ((bf16[8,64,320]{2,1,0:T(8,128)(2,1)}), bf16[8,64,320]{2,1,0:T(8,128)(2,1)S(1)}, u32[]{:S(2)}, u32[]{:S(2)}) async-start(bf16[8,64,320]{2,1,0:T(8,128)(2,1)} %broadcast_in_dim.24), calls=%async_computation | async-start | bytes 786432 | tf_op jit(solution)/shard_map/all_to_all | solution.py:309
  25.6 2.1 %collective-permute-start.19 = (bf16[320,640]{1,0:T(8,128)(2,1)}, bf16[320,640]{1,0:T(8,128)(2,1)S(1)}, u32[]{:S(2)}, u32[]{:S(2)}) collective-permute-start(bf16[320,640]{1,0:T(8,128)(2,1)} %bitcast.22), channel_id=1, source_target_pairs={{0,224},{32,0},{64,32},{96,64},{128,96},{160,128},{192,160},{224,1... | collective-permute-start | bytes 1228808 | tf_op jit(solution)/shard_map/ppermute | solution.py:295
  30.8 20.8 %collective-permute-done.11.s_oth = bf16[64,320]{1,0:T(8,128)(2,1)S(1)} collective-permute-done((bf16[64,320]{1,0:T(8,128)(2,1)S(1)}, bf16[64,320]{1,0:T(8,128)(2,1)S(1)}, u32[]{:S(2)}, u32[]{:S(2)}) %collective-permute-start.11) | collective-permute-done | bytes 40992 | tf_op jit(solution)/shard_map/ppermute | solution.py:302
  54.3 2.1 %shard_map.129 = bf16[8,64,128]{2,1,0:T(8,128)(2,1)} custom-call(s32[2]{0:T(128)S(1)} %pad_add_fusion.1.place.flag, bf16[512,320]{1,0:T(8,128)(2,1)S(1)} %bitcast.19, bf16[512,320]{1,0:T(8,128)(2,1)} %collective-permute-done.1.e_oth, bf16[64,320]{1,0:T(8,128)(2,1)S(1)} %maximum_maximum_fusion.s_own, bf16[64,320]{1,0:T(8,128)(2,1)S(1)} %collective-permute-done.11.s_oth), custom_call_target="tpu_custom_call" | custom-call | flops 83886080 | bytes 1048576 | tf_op jit(solution)/shard_map/pallas_call | solution.py:40
  56.4 4.6 %all-to-all-start.1 = ((bf16[8,64,128]{2,1,0:T(8,128)(2,1)}), bf16[8,64,128]{2,1,0:T(8,128)(2,1)S(1)}, u32[]{:S(2)}, u32[]{:S(2)}) async-start(bf16[8,64,128]{2,1,0:T(8,128)(2,1)} %shard_map.129), calls=%async_computation.1 | async-start | bytes 262144 | tf_op jit(solution)/shard_map/all_to_all | solution.py:325
  61.0 5.0 %shard_map.127 = (bf16[64,1280]{1,0:T(8,128)(2,1)}, bf16[64,1280]{1,0:T(8,128)(2,1)}, bf16[64,1280]{1,0:T(8,128)(2,1)}, bf16[64,1280]{1,0:T(8,128)(2,1)}, bf16[6...) custom-call(s32[2]{0:T(128)} %copy-done.19, ...), custom_call_target="tpu_custom_call" | custom-call | flops 838860800 | bytes 1048576 | tf_op jit(solution)/shard_map/pallas_call | solution.py:40
  66.0 2.7 %collective-permute-start.6 = (bf16[64,1280]{1,0:T(8,128)(2,1)}, bf16[64,1280]{1,0:T(8,128)(2,1)S(1)}, u32[]{:S(2)}, u32[]{:S(2)}) collective-permute-start(bf16[64,1280]{1,0:T(8,128)(2,1)} %get-tuple-element.23), channel_id=1, source_target_pairs={{0,224},{32,0},{64,32},{96,64},{128,96},{160,128},{192,160},{224,1... | collective-permute-start | bytes 491528 | tf_op jit(solution)/shard_map/ppermute | solution.py:344
  71.6 3.6 %collective-permute-start.4 = (bf16[64,1280]{1,0:T(8,128)(2,1)}, bf16[64,1280]{1,0:T(8,128)(2,1)S(1)}, u32[]{:S(2)}, u32[]{:S(2)}) collective-permute-start(bf16[64,1280]{1,0:T(8,128)(2,1)} %get-tuple-element.20), channel_id=1, source_target_pairs={{0,96},{32,128},{64,160},{96,192},{128,224},{160,0},{192,32},{224,... | collective-permute-start | bytes 491528 | tf_op jit(solution)/shard_map/ppermute | solution.py:348
  76.5 3.6 %collective-permute-start.13 = (bf16[2,64,128]{2,1,0:T(8,128)(2,1)S(1)}, bf16[2,64,128]{2,1,0:T(8,128)(2,1)S(1)}, u32[]{:S(2)}, u32[]{:S(2)}) collective-permute-start(bf16[2,64,128]{2,1,0:T(8,128)(2,1)S(1)} %pad_maximum_fusion.1), channel_id=1, source_target_pairs={{0,2},{2,0},{1,3},{3,1},{4,6},{6,4},{5,7},{7,5},{8,10},{10,8},{9,1... | collective-permute-start | bytes 98312 | tf_op jit(solution)/shard_map/ppermute | solution.py:355
  81.7 2.2 %collective-permute-start.23 = (bf16[320,640]{1,0:T(8,128)(2,1)S(1)}, bf16[320,640]{1,0:T(8,128)(2,1)S(1)}, u32[]{:S(2)}, u32[]{:S(2)}) collective-permute-start(bf16[320,640]{1,0:T(8,128)(2,1)S(1)} %collective-permute-done.21.l2), channel_id=1, source_target_pairs={{0,224},{32,0},{64,32},{96,64},{128,96},{160,128},{192,160},{224,1... | collective-permute-start | bytes 1228808 | tf_op jit(solution)/shard_map/ppermute | solution.py:295
  84.6 2.4 %collective-permute-start.14 = (bf16[4,64,128]{2,1,0:T(8,128)(2,1)S(1)}, bf16[4,64,128]{2,1,0:T(8,128)(2,1)S(1)}, u32[]{:S(2)}, u32[]{:S(2)}) collective-permute-start(bf16[4,64,128]{2,1,0:T(8,128)(2,1)S(1)} %pad_maximum_fusion.bc0), channel_id=1, source_target_pairs={{4,0},{8,4},{12,8},{0,12},{5,1},{9,5},{13,9},{1,13},{6,2},{10,6},{... | collective-permute-start | bytes 196616 | tf_op jit(solution)/shard_map/ppermute | solution.py:358
  88.3 5.1 %collective-permute-done.5.refs_2_ = bf16[64,1280]{1,0:T(8,128)(2,1)S(1)} collective-permute-done((bf16[64,1280]{1,0:T(8,128)(2,1)}, bf16[64,1280]{1,0:T(8,128)(2,1)S(1)}, u32[]{:S(2)}, u32[]{:S(2)}) %collective-permute-start.5) | collective-permute-done | bytes 163872 | tf_op jit(solution)/shard_map/ppermute | solution.py:348
  99.9 2.6 %collective-permute-start.7 = (bf16[64,1280]{1,0:T(8,128)(2,1)S(1)}, bf16[64,1280]{1,0:T(8,128)(2,1)}, u32[]{:S(2)}, u32[]{:S(2)}) collective-permute-start(bf16[64,1280]{1,0:T(8,128)(2,1)S(1)} %shard_map.128), channel_id=1, source_target_pairs={{0,160},{32,192},{64,224},{96,0},{128,32},{160,64},{192,96},{224,1... | collective-permute-start | bytes 491528 | tf_op jit(solution)/shard_map/ppermute | solution.py:348
  105.8 5.6 %shard_map.131 = (f32[32,8,640]{2,1,0:T(8,128)S(1)}, f32[32,128]{1,0:T(8,128)S(1)}) custom-call(s32[3]{0:T(128)S(1)} %pad_add_fusion.2.place, bf16[4,64,128]{2,1,0:T(8,128)(2,1)S(1)} %pad_maximum_fusion.bc0, bf16[4,64,128]{2,1,0:T(8,128)(2,1)S(1)} %copy-done.12, bf16[4,64,128]{2,1,0:T(8,128)(2,1)S(1)} %copy-done.14, bf16[4,64,128]{2,1,0:T(8,128)(2,1)S(1)} %copy-done.16, ...), custom_call_target="tpu_custom_call" | custom-call | flops 83886080 | bytes 1048576 | tf_op jit(solution)/shard_map/pallas_call | solution.py:40
  111.5 1.8 %collective-permute-done.7.refs_3_ = bf16[64,1280]{1,0:T(8,128)(2,1)} collective-permute-done((bf16[64,1280]{1,0:T(8,128)(2,1)S(1)}, bf16[64,1280]{1,0:T(8,128)(2,1)}, u32[]{:S(2)}, u32[]{:S(2)}) %collective-permute-start.7) | collective-permute-done | bytes 163872 | tf_op jit(solution)/shard_map/ppermute | solution.py:348
  113.4 1.8 %shard_map.132.mine = bf16[64,640]{1,0:T(8,128)(2,1)S(1)} custom-call(bf16[64,1280]{1,0:T(8,128)(2,1)S(1)} %copy-done.4, bf16[64,1280]{1,0:T(8,128)(2,1)S(1)} %copy-done.8, bf16[64,1280]{1,0:T(8,128)(2,1)S(1)} %copy-done.10, bf16[64,1280]{1,0:T(8,128)(2,1)} %collective-permute-done.7.refs_3_, bf16[64,1280]{1,0:T(8,128)(2,1)} %collective-permute-done.8.refs_4_, ...), custom_call_target="tpu_custom_call" | custom-call | flops 1048576 | bytes 1048576 | tf_op jit(solution)/shard_map/pallas_call | solution.py:40
  115.4 3.3 %collective-permute-done.17.other = bf16[64,640]{1,0:T(8,128)(2,1)S(1)} collective-permute-done((bf16[64,640]{1,0:T(8,128)(2,1)S(1)}, bf16[64,640]{1,0:T(8,128)(2,1)S(1)}, u32[]{:S(2)}, u32[]{:S(2)}) %collective-permute-start.17) | collective-permute-done | bytes 81952 | tf_op jit(solution)/shard_map/ppermute | solution.py:390
  118.7 2.4 %shard_map.133 = (f32[8,64,384]{2,1,0:T(8,128)S(1)}, bf16[8,64,384]{2,1,0:T(8,128)(2,1)S(1)}) custom-call(s32[2]{0:T(128)S(1)} %pad_add_fusion.place, bf16[64,640]{1,0:T(8,128)(2,1)S(1)} %shard_map.132.mine, bf16[64,640]{1,0:T(8,128)(2,1)S(1)} %collective-permute-done.17.other, f32[1,640]{1,0:T(1,128)S(1)} %reshape.28.refs_13_.gain, ...), custom_call_target="tpu_custom_call" | custom-call | flops 419430400 | bytes 1048576 | tf_op jit(solution)/shard_map/pallas_call | solution.py:40
  121.1 6.9 %collective-permute-start.25 = (bf16[8,64,384]{2,1,0:T(8,128)(2,1)S(1)}, bf16[8,64,384]{2,1,0:T(8,128)(2,1)S(1)}, u32[]{:S(2)}, u32[]{:S(2)}) collective-permute-start(bf16[8,64,384]{2,1,0:T(8,128)(2,1)S(1)} %get-tuple-element.32), channel_id=1, source_target_pairs={{0,1},{1,0},{2,3},{3,2},{4,5},{5,4},{6,7},{7,6},{8,9},{9,8},{10,11... | collective-permute-start | bytes 1179656 | tf_op jit(solution)/shard_map/ppermute | solution.py:414
  130.4 6.0 %all-to-all-start.2 = ((bf16[8,64,384]{2,1,0:T(8,128)(2,1)}), bf16[8,64,384]{2,1,0:T(8,128)(2,1)S(1)}, u32[]{:S(2)}, u32[]{:S(2)}) async-start(bf16[8,64,384]{2,1,0:T(8,128)(2,1)} %shard_map.134), calls=%async_computation.2 | async-start | bytes 786432 | tf_op jit(solution)/shard_map/all_to_all | solution.py:416
  137.1 8.5 %all-to-all-done.2.part = bf16[8,64,384]{2,1,0:T(8,128)(2,1)S(1)} async-done(((bf16[8,64,384]{2,1,0:T(8,128)(2,1)}), bf16[8,64,384]{2,1,0:T(8,128)(2,1)S(1)}, u32[]{:S(2)}, u32[]{:S(2)}) %all-to-all-start.2) | async-done | bytes 393248 | tf_op jit(solution)/shard_map/all_to_all | solution.py:416
  145.7 2.5 %collective-permute-start.26 = (bf16[64,320]{1,0:T(8,128)(2,1)S(1)}, bf16[64,320]{1,0:T(8,128)(2,1)S(1)}, u32[]{:S(2)}, u32[]{:S(2)}) collective-permute-start(bf16[64,320]{1,0:T(8,128)(2,1)S(1)} %shard_map.135), channel_id=1, source_target_pairs={{0,0},{1,16},{16,1},{17,17},{2,2},{3,18},{18,3},{19,19},{4,4},{5,2... | collective-permute-start | bytes 122888 | tf_op jit(solution)/shard_map/ppermute | solution.py:422
  148.2 2.9 %collective-permute-done.26 = bf16[64,320]{1,0:T(8,128)(2,1)S(1)} collective-permute-done((bf16[64,320]{1,0:T(8,128)(2,1)S(1)}, bf16[64,320]{1,0:T(8,128)(2,1)S(1)}, u32[]{:S(2)}, u32[]{:S(2)}) %collective-permute-start.26) | collective-permute-done | bytes 40992 | tf_op jit(solution)/shard_map/ppermute | solution.py:422
  (108 shorter events, 30.2 us)
Async XLA Ops:
  0.0 29.2 %collective-permute-start.18 = (bf16[320,640]{1,0:T(8,128)(2,1)}, bf16[320,640]{1,0:T(8,128)(2,1)S(1)}, u32[]{:S(2)}, u32[]{:S(2)}) collective-permute-start(bf16[320,640]{1,0:T(8,128)(2,1)} %bitcast.21), channel_id=1, source_target_pairs={{0,32},{32,64},{64,96},{96,128},{128,160},{160,192},{192,224},{224... | collective-permute-start | bytes 1228808 | tf_op jit(solution)/shard_map/ppermute | solution.py:294
  5.1 46.6 %all-to-all-start = ((bf16[8,64,320]{2,1,0:T(8,128)(2,1)}), bf16[8,64,320]{2,1,0:T(8,128)(2,1)S(1)}, u32[]{:S(2)}, u32[]{:S(2)}) async-start(bf16[8,64,320]{2,1,0:T(8,128)(2,1)} %broadcast_in_dim.24), calls=%async_computation | async-start | bytes 786432 | tf_op jit(solution)/shard_map/all_to_all | solution.py:309
  25.6 27.2 %collective-permute-start.19 = (bf16[320,640]{1,0:T(8,128)(2,1)}, bf16[320,640]{1,0:T(8,128)(2,1)S(1)}, u32[]{:S(2)}, u32[]{:S(2)}) collective-permute-start(bf16[320,640]{1,0:T(8,128)(2,1)} %bitcast.22), channel_id=1, source_target_pairs={{0,224},{32,0},{64,32},{96,64},{128,96},{160,128},{192,160},{224,1... | collective-permute-start | bytes 1228808 | tf_op jit(solution)/shard_map/ppermute | solution.py:295
  27.6 33.3 %collective-permute-start.2 = (bf16[320,640]{1,0:T(8,128)(2,1)}, bf16[320,640]{1,0:T(8,128)(2,1)}, u32[]{:S(2)}, u32[]{:S(2)}) collective-permute-start(bf16[320,640]{1,0:T(8,128)(2,1)} %x_own.1), channel_id=1, source_target_pairs={{0,16},{16,0},{1,17},{17,1},{2,18},{18,2},{3,19},{19,3},{4,20},{20... | collective-permute-start | bytes 1228808 | tf_op jit(solution)/shard_map/ppermute | solution.py:297
  28.1 32.8 %collective-permute-start.3 = (bf16[320,640]{1,0:T(8,128)(2,1)}, bf16[320,640]{1,0:T(8,128)(2,1)}, u32[]{:S(2)}, u32[]{:S(2)}) collective-permute-start(bf16[320,640]{1,0:T(8,128)(2,1)} %z_own.1), channel_id=1, source_target_pairs={{0,16},{16,0},{1,17},{17,1},{2,18},{18,2},{3,19},{19,3},{4,20},{20... | collective-permute-start | bytes 1228808 | tf_op jit(solution)/shard_map/ppermute | solution.py:298
  29.2 24.8 %collective-permute-start.20 = (bf16[320,640]{1,0:T(8,128)(2,1)S(1)}, bf16[320,640]{1,0:T(8,128)(2,1)S(1)}, u32[]{:S(2)}, u32[]{:S(2)}) collective-permute-start(bf16[320,640]{1,0:T(8,128)(2,1)S(1)} %collective-permute-done.18.r1), channel_id=1, source_target_pairs={{0,32},{32,64},{64,96},{96,128},{128,160},{160,192},{192,224},{224... | collective-permute-start | bytes 1228808 | tf_op jit(solution)/shard_map/ppermute | solution.py:294
  30.0 21.6 %collective-permute-start.11 = (bf16[64,320]{1,0:T(8,128)(2,1)S(1)}, bf16[64,320]{1,0:T(8,128)(2,1)S(1)}, u32[]{:S(2)}, u32[]{:S(2)}) collective-permute-start(bf16[64,320]{1,0:T(8,128)(2,1)S(1)} %maximum_maximum_fusion.s_own), channel_id=1, source_target_pairs={{0,16},{16,0},{1,17},{17,1},{2,18},{18,2},{3,19},{19,3},{4,20},{20... | collective-permute-start | bytes 122888 | tf_op jit(solution)/shard_map/ppermute | solution.py:302
  52.7 23.7 %collective-permute-start.21 = (bf16[320,640]{1,0:T(8,128)(2,1)S(1)}, bf16[320,640]{1,0:T(8,128)(2,1)S(1)}, u32[]{:S(2)}, u32[]{:S(2)}) collective-permute-start(bf16[320,640]{1,0:T(8,128)(2,1)S(1)} %collective-permute-done.19.l1), channel_id=1, source_target_pairs={{0,224},{32,0},{64,32},{96,64},{128,96},{160,128},{192,160},{224,1... | collective-permute-start | bytes 1228808 | tf_op jit(solution)/shard_map/ppermute | solution.py:295
  53.9 30.0 %collective-permute-start.22 = (bf16[320,640]{1,0:T(8,128)(2,1)S(1)}, bf16[320,640]{1,0:T(8,128)(2,1)}, u32[]{:S(2)}, u32[]{:S(2)}) collective-permute-start(bf16[320,640]{1,0:T(8,128)(2,1)S(1)} %collective-permute-done.20.r2), channel_id=1, source_target_pairs={{0,32},{32,64},{64,96},{96,128},{128,160},{160,192},{192,224},{224... | collective-permute-start | bytes 1228808 | tf_op jit(solution)/shard_map/ppermute | solution.py:294
  56.4 12.4 %all-to-all-start.1 = ((bf16[8,64,128]{2,1,0:T(8,128)(2,1)}), bf16[8,64,128]{2,1,0:T(8,128)(2,1)S(1)}, u32[]{:S(2)}, u32[]{:S(2)}) async-start(bf16[8,64,128]{2,1,0:T(8,128)(2,1)} %shard_map.129), calls=%async_computation.1 | async-start | bytes 262144 | tf_op jit(solution)/shard_map/all_to_all | solution.py:325
  66.0 5.7 %collective-permute-start.6 = (bf16[64,1280]{1,0:T(8,128)(2,1)}, bf16[64,1280]{1,0:T(8,128)(2,1)S(1)}, u32[]{:S(2)}, u32[]{:S(2)}) collective-permute-start(bf16[64,1280]{1,0:T(8,128)(2,1)} %get-tuple-element.23), channel_id=1, source_target_pairs={{0,224},{32,0},{64,32},{96,64},{128,96},{160,128},{192,160},{224,1... | collective-permute-start | bytes 491528 | tf_op jit(solution)/shard_map/ppermute | solution.py:344
  68.9 6.3 %collective-permute-start.12 = (bf16[64,128]{1,0:T(8,128)(2,1)S(1)}, bf16[64,128]{1,0:T(8,128)(2,1)S(1)}, u32[]{:S(2)}, u32[]{:S(2)}) collective-permute-start(bf16[64,128]{1,0:T(8,128)(2,1)S(1)} %get-tuple-element.28), channel_id=1, source_target_pairs={{0,1},{1,0},{2,3},{3,2},{4,5},{5,4},{6,7},{7,6},{8,9},{9,8},{10,11... | collective-permute-start | bytes 49160 | tf_op jit(solution)/shard_map/ppermute | solution.py:354
  70.7 13.3 %collective-permute-start.10 = (bf16[64,1280]{1,0:T(8,128)(2,1)}, bf16[64,1280]{1,0:T(8,128)(2,1)S(1)}, u32[]{:S(2)}, u32[]{:S(2)}) collective-permute-start(bf16[64,1280]{1,0:T(8,128)(2,1)} %get-tuple-element.26), channel_id=1, source_target_pairs={{0,224},{32,0},{64,32},{96,64},{128,96},{160,128},{192,160},{224,1... | collective-permute-start | bytes 491528 | tf_op jit(solution)/shard_map/ppermute | solution.py:348
  71.6 15.4 %collective-permute-start.4 = (bf16[64,1280]{1,0:T(8,128)(2,1)}, bf16[64,1280]{1,0:T(8,128)(2,1)S(1)}, u32[]{:S(2)}, u32[]{:S(2)}) collective-permute-start(bf16[64,1280]{1,0:T(8,128)(2,1)} %get-tuple-element.20), channel_id=1, source_target_pairs={{0,96},{32,128},{64,160},{96,192},{128,224},{160,0},{192,32},{224,... | collective-permute-start | bytes 491528 | tf_op jit(solution)/shard_map/ppermute | solution.py:348
  75.3 18.1 %collective-permute-start.5 = (bf16[64,1280]{1,0:T(8,128)(2,1)}, bf16[64,1280]{1,0:T(8,128)(2,1)S(1)}, u32[]{:S(2)}, u32[]{:S(2)}) collective-permute-start(bf16[64,1280]{1,0:T(8,128)(2,1)} %get-tuple-element.21), channel_id=1, source_target_pairs={{0,64},{32,96},{64,128},{96,160},{128,192},{160,224},{192,0},{224,... | collective-permute-start | bytes 491528 | tf_op jit(solution)/shard_map/ppermute | solution.py:348
  81.7 37.0 %collective-permute-start.23 = (bf16[320,640]{1,0:T(8,128)(2,1)S(1)}, bf16[320,640]{1,0:T(8,128)(2,1)S(1)}, u32[]{:S(2)}, u32[]{:S(2)}) collective-permute-start(bf16[320,640]{1,0:T(8,128)(2,1)S(1)} %collective-permute-done.21.l2), channel_id=1, source_target_pairs={{0,224},{32,0},{64,32},{96,64},{128,96},{160,128},{192,160},{224,1... | collective-permute-start | bytes 1228808 | tf_op jit(solution)/shard_map/ppermute | solution.py:295
  83.9 34.7 %collective-permute-start.24 = (bf16[320,640]{1,0:T(8,128)(2,1)}, bf16[320,640]{1,0:T(8,128)(2,1)}, u32[]{:S(2)}, u32[]{:S(2)}) collective-permute-start(bf16[320,640]{1,0:T(8,128)(2,1)} %collective-permute-done.22.r3), channel_id=1, source_target_pairs={{0,32},{32,64},{64,96},{96,128},{128,160},{160,192},{192,224},{224... | collective-permute-start | bytes 1228808 | tf_op jit(solution)/shard_map/ppermute | solution.py:296
  84.6 11.4 %collective-permute-start.14 = (bf16[4,64,128]{2,1,0:T(8,128)(2,1)S(1)}, bf16[4,64,128]{2,1,0:T(8,128)(2,1)S(1)}, u32[]{:S(2)}, u32[]{:S(2)}) collective-permute-start(bf16[4,64,128]{2,1,0:T(8,128)(2,1)S(1)} %pad_maximum_fusion.bc0), channel_id=1, source_target_pairs={{4,0},{8,4},{12,8},{0,12},{5,1},{9,5},{13,9},{1,13},{6,2},{10,6},{... | collective-permute-start | bytes 196616 | tf_op jit(solution)/shard_map/ppermute | solution.py:358
  87.7 9.5 %collective-permute-start.15 = (bf16[4,64,128]{2,1,0:T(8,128)(2,1)S(1)}, bf16[4,64,128]{2,1,0:T(8,128)(2,1)S(1)}, u32[]{:S(2)}, u32[]{:S(2)}) collective-permute-start(bf16[4,64,128]{2,1,0:T(8,128)(2,1)S(1)} %pad_maximum_fusion.bc0), channel_id=1, source_target_pairs={{8,0},{12,4},{0,8},{4,12},{9,1},{13,5},{1,9},{5,13},{10,2},{14,6},... | collective-permute-start | bytes 196616 | tf_op jit(solution)/shard_map/ppermute | solution.py:358
  96.6 14.8 %collective-permute-start.8 = (bf16[64,1280]{1,0:T(8,128)(2,1)}, bf16[64,1280]{1,0:T(8,128)(2,1)}, u32[]{:S(2)}, u32[]{:S(2)}) collective-permute-start(bf16[64,1280]{1,0:T(8,128)(2,1)} %get-tuple-element.24), channel_id=1, source_target_pairs={{0,192},{32,224},{64,0},{96,32},{128,64},{160,96},{192,128},{224,1... | collective-permute-start | bytes 491528 | tf_op jit(solution)/shard_map/ppermute | solution.py:348
  97.8 13.7 %collective-permute-start.9 = (bf16[64,1280]{1,0:T(8,128)(2,1)}, bf16[64,1280]{1,0:T(8,128)(2,1)}, u32[]{:S(2)}, u32[]{:S(2)}) collective-permute-start(bf16[64,1280]{1,0:T(8,128)(2,1)} %get-tuple-element.25), channel_id=1, source_target_pairs={{0,32},{32,64},{64,96},{96,128},{128,160},{160,192},{192,224},{224... | collective-permute-start | bytes 491528 | tf_op jit(solution)/shard_map/ppermute | solution.py:348
  99.9 13.4 %collective-permute-start.7 = (bf16[64,1280]{1,0:T(8,128)(2,1)S(1)}, bf16[64,1280]{1,0:T(8,128)(2,1)}, u32[]{:S(2)}, u32[]{:S(2)}) collective-permute-start(bf16[64,1280]{1,0:T(8,128)(2,1)S(1)} %shard_map.128), channel_id=1, source_target_pairs={{0,160},{32,192},{64,224},{96,0},{128,32},{160,64},{192,96},{224,1... | collective-permute-start | bytes 491528 | tf_op jit(solution)/shard_map/ppermute | solution.py:348
  121.1 8.2 %collective-permute-start.25 = (bf16[8,64,384]{2,1,0:T(8,128)(2,1)S(1)}, bf16[8,64,384]{2,1,0:T(8,128)(2,1)S(1)}, u32[]{:S(2)}, u32[]{:S(2)}) collective-permute-start(bf16[8,64,384]{2,1,0:T(8,128)(2,1)S(1)} %get-tuple-element.32), channel_id=1, source_target_pairs={{0,1},{1,0},{2,3},{3,2},{4,5},{5,4},{6,7},{7,6},{8,9},{9,8},{10,11... | collective-permute-start | bytes 1179656 | tf_op jit(solution)/shard_map/ppermute | solution.py:414
  130.4 15.2 %all-to-all-start.2 = ((bf16[8,64,384]{2,1,0:T(8,128)(2,1)}), bf16[8,64,384]{2,1,0:T(8,128)(2,1)S(1)}, u32[]{:S(2)}, u32[]{:S(2)}) async-start(bf16[8,64,384]{2,1,0:T(8,128)(2,1)} %shard_map.134), calls=%async_computation.2 | async-start | bytes 786432 | tf_op jit(solution)/shard_map/all_to_all | solution.py:416
  (30 other events, 284.5 us)

commit v11 on v10

--- a/solution.py
+++ b/solution.py
@@ -255,6 +255,12 @@
     out[...] = (total[:, :cols] * lax.rsqrt(ss / count + 1e-05)).astype(BF)
 
 
+def final_kernel(counts, own, back, out):
+    total = (own[...].astype(F32) + back[...].astype(F32)).reshape(out.shape)
+    live = lax.broadcasted_iota(jnp.int32, out.shape, 1) < counts[0]
+    out[...] = jnp.where(live, total, 0.0).astype(BF)
+
+
 def per_device(
     token_ids,
     row_counts,
@@ -420,9 +426,12 @@
         (partial_out,),
     )
     back = lax.ppermute(mine, ("yl", "core"), [(0, 0), (1, 2), (2, 1), (3, 3)])
-    result = (own_embed.astype(F32) + back.astype(F32)).reshape(2, rows, wide)
-    live = jnp.arange(rows, dtype=jnp.int32) < row_counts[0]
-    return jnp.where(live[None, :, None], result, 0.0).astype(BF)
+    return call(
+        final_kernel,
+        jax.ShapeDtypeStruct((2, rows, wide), BF),
+        (row_counts, own_embed, back),
+        in_smem=1,
+    )
 
 
 def solution(mesh):

time: 153 us -> 152 us (level)
  blocking collectives: 0 us -> 14.7 us
  waiting for transfers between devices: 47 us -> 36 us
  starting transfers between devices: 73.7 us -> 71 us
    all_to_all x0 -> x1, blocking collectives: none -> 14.7 us  [per_device(): partial_out = lax.all_to_all(paired, ('x', 'yh'), 0, 0)]
    all_to_all x1 -> x0, waiting for transfers between devices: 8.5 us -> none  [per_device(): partial_out = lax.all_to_all(paired, ('x', 'yh'), 0, 0)]
    all_to_all x1 -> x0, starting transfers between devices: 6.03 us -> none  [per_device(): partial_out = lax.all_to_all(paired, ('x', 'yh'), 0, 0)]
    ppermute x1, waiting for transfers between devices: 2.93 us -> 1.38 us  [per_device(): back = lax.ppermute(mine, ('yl', 'core'), [(0, 0), (1, 2), (2, 1), (3, 3)])]
    unnamed x48 -> x38, local copies, waits for them, and re-layouts: 7.35 us -> 5.89 us
    pallas_call x9 -> x10, Pallas kernels: 18.3 us -> 18.9 us  [call(): pl.pallas_call(body, out_shape=out_shape, in_specs=in_specs, out_specs=ou...]
  transfers between devices with their start and end apart: 30 -> 29, of which waited for: 10 -> 8; matrix products, arithmetic and copies ran while one was open for 2% -> 3% of each run, Pallas kernels for 10% -> 10%
where the time goes in v11:
time: 152 us; the launch traced here: 151 us
  starting transfers between devices  71 us (47%)
  waiting for transfers between devices  36 us (24%)
  Pallas kernels  18.9 us (12%)
  blocking collectives  14.7 us (10%)
  local copies, waits for them, and re-layouts  8.26 us (5%)
    ppermute x1, waiting for transfers between devices, per_device(): small_oth = lax.ppermute(small_own, 'yl', pair)  20.7 us
    all_to_all x1, starting transfers between devices, per_device(): lax.all_to_all(jnp.broadcast_to(moved[None], (8,) + moved.shape), ('x', '...  20.5 us
    pallas_call x10, Pallas kernels, call(): pl.pallas_call(body, out_shape=out_shape, in_specs=in_specs, out_specs=ou...  18.9 us
    all_to_all x1, blocking collectives, per_device(): partial_out = lax.all_to_all(paired, ('x', 'yh'), 0, 0)  14.7 us
    ppermute x6, starting transfers between devices, per_device(): lax.ppermute(blocks[k], 'z', [(i, (i + k) % 8) for i in range(8)])  8.18 us
    ppermute x1, starting transfers between devices, per_device(): got = lax.ppermute(send, 'core', pair)  8.09 us
    ppermute x6, waiting for transfers between devices, per_device(): lax.ppermute(blocks[k], 'z', [(i, (i + k) % 8) for i in range(8)])  6.99 us
    unnamed x38, local copies, waits for them, and re-layouts  5.89 us
  transfers between devices with their start and end apart: 29, of which 8 were waited for; matrix products, arithmetic and copies ran while one was open for 3% of the time, Pallas kernels for 10%

profile of v11, /device:TPU:1, one launch (start us, length us, event | category | flops | bytes accessed | tf_op | source)
XLA Modules:
  0.0 151.1 jit_solution(3830365879000816087)
XLA Ops:
  0.0 2.5 %collective-permute-start.18 = (bf16[320,640]{1,0:T(8,128)(2,1)}, bf16[320,640]{1,0:T(8,128)(2,1)S(1)}, u32[]{:S(2)}, u32[]{:S(2)}) collective-permute-start(bf16[320,640]{1,0:T(8,128)(2,1)} %bitcast.18), channel_id=1, source_target_pairs={{0,32},{32,64},{64,96},{96,128},{128,160},{160,192},{192,224},{224... | collective-permute-start | bytes 1228808 | tf_op jit(solution)/shard_map/ppermute | solution.py:300
  5.1 20.5 %all-to-all-start = ((bf16[8,64,320]{2,1,0:T(8,128)(2,1)}), bf16[8,64,320]{2,1,0:T(8,128)(2,1)S(1)}, u32[]{:S(2)}, u32[]{:S(2)}) async-start(bf16[8,64,320]{2,1,0:T(8,128)(2,1)} %broadcast_in_dim.4), calls=%async_computation | async-start | bytes 786432 | tf_op jit(solution)/shard_map/all_to_all | solution.py:315
  25.7 2.0 %collective-permute-start.19 = (bf16[320,640]{1,0:T(8,128)(2,1)}, bf16[320,640]{1,0:T(8,128)(2,1)S(1)}, u32[]{:S(2)}, u32[]{:S(2)}) collective-permute-start(bf16[320,640]{1,0:T(8,128)(2,1)} %bitcast.19), channel_id=1, source_target_pairs={{0,224},{32,0},{64,32},{96,64},{128,96},{160,128},{192,160},{224,1... | collective-permute-start | bytes 1228808 | tf_op jit(solution)/shard_map/ppermute | solution.py:301
  30.9 20.7 %collective-permute-done.11.s_oth = bf16[64,320]{1,0:T(8,128)(2,1)S(1)} collective-permute-done((bf16[64,320]{1,0:T(8,128)(2,1)S(1)}, bf16[64,320]{1,0:T(8,128)(2,1)S(1)}, u32[]{:S(2)}, u32[]{:S(2)}) %collective-permute-start.11) | collective-permute-done | bytes 40992 | tf_op jit(solution)/shard_map/ppermute | solution.py:308
  54.3 2.1 %shard_map.129 = bf16[8,64,128]{2,1,0:T(8,128)(2,1)} custom-call(s32[2]{0:T(128)S(1)} %pad_add_fusion.1.place.flag, bf16[512,320]{1,0:T(8,128)(2,1)S(1)} %bitcast.16, bf16[512,320]{1,0:T(8,128)(2,1)} %collective-permute-done.1.e_oth, bf16[64,320]{1,0:T(8,128)(2,1)S(1)} %maximum_maximum_fusion.s_own, bf16[64,320]{1,0:T(8,128)(2,1)S(1)} %collective-permute-done.11.s_oth), custom_call_target="tpu_custom_call" | custom-call | flops 83886080 | bytes 1048576 | tf_op jit(solution)/shard_map/pallas_call | solution.py:40
  56.4 4.6 %all-to-all-start.1 = ((bf16[8,64,128]{2,1,0:T(8,128)(2,1)}), bf16[8,64,128]{2,1,0:T(8,128)(2,1)S(1)}, u32[]{:S(2)}, u32[]{:S(2)}) async-start(bf16[8,64,128]{2,1,0:T(8,128)(2,1)} %shard_map.129), calls=%async_computation.1 | async-start | bytes 262144 | tf_op jit(solution)/shard_map/all_to_all | solution.py:331
  61.1 5.0 %shard_map.127 = (bf16[64,1280]{1,0:T(8,128)(2,1)}, bf16[64,1280]{1,0:T(8,128)(2,1)}, bf16[64,1280]{1,0:T(8,128)(2,1)}, bf16[64,1280]{1,0:T(8,128)(2,1)}, bf16[6...) custom-call(s32[2]{0:T(128)} %copy-done.15, ...), custom_call_target="tpu_custom_call" | custom-call | flops 838860800 | bytes 1048576 | tf_op jit(solution)/shard_map/pallas_call | solution.py:40
  66.1 2.7 %collective-permute-start.6 = (bf16[64,1280]{1,0:T(8,128)(2,1)}, bf16[64,1280]{1,0:T(8,128)(2,1)S(1)}, u32[]{:S(2)}, u32[]{:S(2)}) collective-permute-start(bf16[64,1280]{1,0:T(8,128)(2,1)} %get-tuple-element.23), channel_id=1, source_target_pairs={{0,224},{32,0},{64,32},{96,64},{128,96},{160,128},{192,160},{224,1... | collective-permute-start | bytes 491528 | tf_op jit(solution)/shard_map/ppermute | solution.py:350
  69.0 1.8 %collective-permute-start.12 = (bf16[64,128]{1,0:T(8,128)(2,1)S(1)}, bf16[64,128]{1,0:T(8,128)(2,1)S(1)}, u32[]{:S(2)}, u32[]{:S(2)}) collective-permute-start(bf16[64,128]{1,0:T(8,128)(2,1)S(1)} %get-tuple-element.28), channel_id=1, source_target_pairs={{0,1},{1,0},{2,3},{3,2},{4,5},{5,4},{6,7},{7,6},{8,9},{9,8},{10,11... | collective-permute-start | bytes 49160 | tf_op jit(solution)/shard_map/ppermute | solution.py:360
  71.7 3.7 %collective-permute-start.4 = (bf16[64,1280]{1,0:T(8,128)(2,1)}, bf16[64,1280]{1,0:T(8,128)(2,1)S(1)}, u32[]{:S(2)}, u32[]{:S(2)}) collective-permute-start(bf16[64,1280]{1,0:T(8,128)(2,1)} %get-tuple-element.20), channel_id=1, source_target_pairs={{0,96},{32,128},{64,160},{96,192},{128,224},{160,0},{192,32},{224,... | collective-permute-start | bytes 491528 | tf_op jit(solution)/shard_map/ppermute | solution.py:354
  76.6 3.7 %collective-permute-start.13 = (bf16[2,64,128]{2,1,0:T(8,128)(2,1)S(1)}, bf16[2,64,128]{2,1,0:T(8,128)(2,1)S(1)}, u32[]{:S(2)}, u32[]{:S(2)}) collective-permute-start(bf16[2,64,128]{2,1,0:T(8,128)(2,1)S(1)} %pad_maximum_fusion.1), channel_id=1, source_target_pairs={{0,2},{2,0},{1,3},{3,1},{4,6},{6,4},{5,7},{7,5},{8,10},{10,8},{9,1... | collective-permute-start | bytes 98312 | tf_op jit(solution)/shard_map/ppermute | solution.py:361
  81.8 2.2 %collective-permute-start.23 = (bf16[320,640]{1,0:T(8,128)(2,1)S(1)}, bf16[320,640]{1,0:T(8,128)(2,1)S(1)}, u32[]{:S(2)}, u32[]{:S(2)}) collective-permute-start(bf16[320,640]{1,0:T(8,128)(2,1)S(1)} %collective-permute-done.21.l2), channel_id=1, source_target_pairs={{0,224},{32,0},{64,32},{96,64},{128,96},{160,128},{192,160},{224,1... | collective-permute-start | bytes 1228808 | tf_op jit(solution)/shard_map/ppermute | solution.py:301
  84.8 2.4 %collective-permute-start.14 = (bf16[4,64,128]{2,1,0:T(8,128)(2,1)S(1)}, bf16[4,64,128]{2,1,0:T(8,128)(2,1)S(1)}, u32[]{:S(2)}, u32[]{:S(2)}) collective-permute-start(bf16[4,64,128]{2,1,0:T(8,128)(2,1)S(1)} %pad_maximum_fusion.bc0), channel_id=1, source_target_pairs={{4,0},{8,4},{12,8},{0,12},{5,1},{9,5},{13,9},{1,13},{6,2},{10,6},{... | collective-permute-start | bytes 196616 | tf_op jit(solution)/shard_map/ppermute | solution.py:364
  88.4 5.1 %collective-permute-done.5.refs_2_ = bf16[64,1280]{1,0:T(8,128)(2,1)S(1)} collective-permute-done((bf16[64,1280]{1,0:T(8,128)(2,1)}, bf16[64,1280]{1,0:T(8,128)(2,1)S(1)}, u32[]{:S(2)}, u32[]{:S(2)}) %collective-permute-start.5) | collective-permute-done | bytes 163872 | tf_op jit(solution)/shard_map/ppermute | solution.py:354
  97.7 1.7 %collective-permute-done.16.bc3 = bf16[4,64,128]{2,1,0:T(8,128)(2,1)S(1)} collective-permute-done((bf16[4,64,128]{2,1,0:T(8,128)(2,1)S(1)}, bf16[4,64,128]{2,1,0:T(8,128)(2,1)S(1)}, u32[]{:S(2)}, u32[]{:S(2)}) %collective-permute-start.16) | collective-permute-done | bytes 65568 | tf_op jit(solution)/shard_map/ppermute | solution.py:364
  100.1 2.2 %collective-permute-start.7 = (bf16[64,1280]{1,0:T(8,128)(2,1)}, bf16[64,1280]{1,0:T(8,128)(2,1)}, u32[]{:S(2)}, u32[]{:S(2)}) collective-permute-start(bf16[64,1280]{1,0:T(8,128)(2,1)} %shard_map.128), channel_id=1, source_target_pairs={{0,160},{32,192},{64,224},{96,0},{128,32},{160,64},{192,96},{224,1... | collective-permute-start | bytes 491528 | tf_op jit(solution)/shard_map/ppermute | solution.py:354
  104.9 5.6 %shard_map.131 = (f32[32,8,640]{2,1,0:T(8,128)S(1)}, f32[32,128]{1,0:T(8,128)S(1)}) custom-call(s32[3]{0:T(128)S(1)} %pad_add_fusion.2.place, bf16[4,64,128]{2,1,0:T(8,128)(2,1)S(1)} %pad_maximum_fusion.bc0, bf16[4,64,128]{2,1,0:T(8,128)(2,1)S(1)} %collective-permute-done.14.bc1, bf16[4,64,128]{2,1,0:T(8,128)(2,1)S(1)} %copy-done.12, ...), custom_call_target="tpu_custom_call" | custom-call | flops 83886080 | bytes 1048576 | tf_op jit(solution)/shard_map/pallas_call | solution.py:40
  110.5 1.9 %collective-permute-done.7.refs_3_ = bf16[64,1280]{1,0:T(8,128)(2,1)} collective-permute-done((bf16[64,1280]{1,0:T(8,128)(2,1)}, bf16[64,1280]{1,0:T(8,128)(2,1)}, u32[]{:S(2)}, u32[]{:S(2)}) %collective-permute-start.7) | collective-permute-done | bytes 163872 | tf_op jit(solution)/shard_map/ppermute | solution.py:354
  112.4 1.8 %shard_map.132.mine = bf16[64,640]{1,0:T(8,128)(2,1)S(1)} custom-call(bf16[64,1280]{1,0:T(8,128)(2,1)S(1)} %copy-done.4, bf16[64,1280]{1,0:T(8,128)(2,1)S(1)} %copy-done.8, bf16[64,1280]{1,0:T(8,128)(2,1)S(1)} %copy-done.10, bf16[64,1280]{1,0:T(8,128)(2,1)} %collective-permute-done.7.refs_3_, bf16[64,1280]{1,0:T(8,128)(2,1)} %collective-permute-done.8.refs_4_, ...), custom_call_target="tpu_custom_call" | custom-call | flops 1048576 | bytes 1048576 | tf_op jit(solution)/shard_map/pallas_call | solution.py:40
  115.8 2.2 %collective-permute-done.17.other = bf16[64,640]{1,0:T(8,128)(2,1)S(1)} collective-permute-done((bf16[64,640]{1,0:T(8,128)(2,1)S(1)}, bf16[64,640]{1,0:T(8,128)(2,1)S(1)}, u32[]{:S(2)}, u32[]{:S(2)}) %collective-permute-start.17) | collective-permute-done | bytes 81952 | tf_op jit(solution)/shard_map/ppermute | solution.py:396
  118.1 2.4 %shard_map.133 = (f32[8,64,384]{2,1,0:T(8,128)S(1)}, bf16[8,64,384]{2,1,0:T(8,128)(2,1)S(1)}) custom-call(s32[2]{0:T(128)S(1)} %pad_add_fusion.place, bf16[64,640]{1,0:T(8,128)(2,1)S(1)} %shard_map.132.mine, bf16[64,640]{1,0:T(8,128)(2,1)S(1)} %collective-permute-done.17.other, f32[1,640]{1,0:T(1,128)S(1)} %reshape.21.refs_13_.gain, ...), custom_call_target="tpu_custom_call" | custom-call | flops 419430400 | bytes 1048576 | tf_op jit(solution)/shard_map/pallas_call | solution.py:40
  120.4 8.1 %collective-permute-start.25 = (bf16[8,64,384]{2,1,0:T(8,128)(2,1)S(1)}, bf16[8,64,384]{2,1,0:T(8,128)(2,1)S(1)}, u32[]{:S(2)}, u32[]{:S(2)}) collective-permute-start(bf16[8,64,384]{2,1,0:T(8,128)(2,1)S(1)} %get-tuple-element.32), channel_id=1, source_target_pairs={{0,1},{1,0},{2,3},{3,2},{4,5},{5,4},{6,7},{7,6},{8,9},{9,8},{10,11... | collective-permute-start | bytes 1179656 | tf_op jit(solution)/shard_map/ppermute | solution.py:420
  130.2 14.7 %all_to_all.15.part = bf16[8,64,384]{2,1,0:T(8,128)(2,1)S(1)} all-to-all(bf16[8,64,384]{2,1,0:T(8,128)(2,1)S(1)} %shard_map.134), channel_id=1, replica_groups=mesh['z'=8,'yl'=2,'x'=4,'yh'=2,'core'=2] {'x','yh'}, dimensions={0} | all-to-all | bytes 786432 | tf_op jit(solution)/shard_map/all_to_all | solution.py:422
  145.1 3.4 %collective-permute-start.26 = (bf16[64,320]{1,0:T(8,128)(2,1)S(1)}, bf16[64,320]{1,0:T(8,128)(2,1)S(1)}, u32[]{:S(2)}, u32[]{:S(2)}) collective-permute-start(bf16[64,320]{1,0:T(8,128)(2,1)S(1)} %shard_map.135), channel_id=1, source_target_pairs={{0,0},{1,16},{16,1},{17,17},{2,2},{3,18},{18,3},{19,19},{4,4},{5,2... | collective-permute-start | bytes 122888 | tf_op jit(solution)/shard_map/ppermute | solution.py:428
  (95 shorter events, 27.1 us)
Async XLA Ops:
  0.0 29.2 %collective-permute-start.18 = (bf16[320,640]{1,0:T(8,128)(2,1)}, bf16[320,640]{1,0:T(8,128)(2,1)S(1)}, u32[]{:S(2)}, u32[]{:S(2)}) collective-permute-start(bf16[320,640]{1,0:T(8,128)(2,1)} %bitcast.18), channel_id=1, source_target_pairs={{0,32},{32,64},{64,96},{96,128},{128,160},{160,192},{192,224},{224... | collective-permute-start | bytes 1228808 | tf_op jit(solution)/shard_map/ppermute | solution.py:300
  5.1 46.5 %all-to-all-start = ((bf16[8,64,320]{2,1,0:T(8,128)(2,1)}), bf16[8,64,320]{2,1,0:T(8,128)(2,1)S(1)}, u32[]{:S(2)}, u32[]{:S(2)}) async-start(bf16[8,64,320]{2,1,0:T(8,128)(2,1)} %broadcast_in_dim.4), calls=%async_computation | async-start | bytes 786432 | tf_op jit(solution)/shard_map/all_to_all | solution.py:315
  25.7 27.1 %collective-permute-start.19 = (bf16[320,640]{1,0:T(8,128)(2,1)}, bf16[320,640]{1,0:T(8,128)(2,1)S(1)}, u32[]{:S(2)}, u32[]{:S(2)}) collective-permute-start(bf16[320,640]{1,0:T(8,128)(2,1)} %bitcast.19), channel_id=1, source_target_pairs={{0,224},{32,0},{64,32},{96,64},{128,96},{160,128},{192,160},{224,1... | collective-permute-start | bytes 1228808 | tf_op jit(solution)/shard_map/ppermute | solution.py:301
  27.7 33.4 %collective-permute-start.2 = (bf16[320,640]{1,0:T(8,128)(2,1)}, bf16[320,640]{1,0:T(8,128)(2,1)}, u32[]{:S(2)}, u32[]{:S(2)}) collective-permute-start(bf16[320,640]{1,0:T(8,128)(2,1)} %x_own.1), channel_id=1, source_target_pairs={{0,16},{16,0},{1,17},{17,1},{2,18},{18,2},{3,19},{19,3},{4,20},{20... | collective-permute-start | bytes 1228808 | tf_op jit(solution)/shard_map/ppermute | solution.py:303
  28.2 32.8 %collective-permute-start.3 = (bf16[320,640]{1,0:T(8,128)(2,1)}, bf16[320,640]{1,0:T(8,128)(2,1)}, u32[]{:S(2)}, u32[]{:S(2)}) collective-permute-start(bf16[320,640]{1,0:T(8,128)(2,1)} %z_own.1), channel_id=1, source_target_pairs={{0,16},{16,0},{1,17},{17,1},{2,18},{18,2},{3,19},{19,3},{4,20},{20... | collective-permute-start | bytes 1228808 | tf_op jit(solution)/shard_map/ppermute | solution.py:304
  29.2 24.8 %collective-permute-start.20 = (bf16[320,640]{1,0:T(8,128)(2,1)S(1)}, bf16[320,640]{1,0:T(8,128)(2,1)S(1)}, u32[]{:S(2)}, u32[]{:S(2)}) collective-permute-start(bf16[320,640]{1,0:T(8,128)(2,1)S(1)} %collective-permute-done.18.r1), channel_id=1, source_target_pairs={{0,32},{32,64},{64,96},{96,128},{128,160},{160,192},{192,224},{224... | collective-permute-start | bytes 1228808 | tf_op jit(solution)/shard_map/ppermute | solution.py:300
  30.1 21.5 %collective-permute-start.11 = (bf16[64,320]{1,0:T(8,128)(2,1)S(1)}, bf16[64,320]{1,0:T(8,128)(2,1)S(1)}, u32[]{:S(2)}, u32[]{:S(2)}) collective-permute-start(bf16[64,320]{1,0:T(8,128)(2,1)S(1)} %maximum_maximum_fusion.s_own), channel_id=1, source_target_pairs={{0,16},{16,0},{1,17},{17,1},{2,18},{18,2},{3,19},{19,3},{4,20},{20... | collective-permute-start | bytes 122888 | tf_op jit(solution)/shard_map/ppermute | solution.py:308
  52.8 23.8 %collective-permute-start.21 = (bf16[320,640]{1,0:T(8,128)(2,1)S(1)}, bf16[320,640]{1,0:T(8,128)(2,1)S(1)}, u32[]{:S(2)}, u32[]{:S(2)}) collective-permute-start(bf16[320,640]{1,0:T(8,128)(2,1)S(1)} %collective-permute-done.19.l1), channel_id=1, source_target_pairs={{0,224},{32,0},{64,32},{96,64},{128,96},{160,128},{192,160},{224,1... | collective-permute-start | bytes 1228808 | tf_op jit(solution)/shard_map/ppermute | solution.py:301
  54.0 30.0 %collective-permute-start.22 = (bf16[320,640]{1,0:T(8,128)(2,1)S(1)}, bf16[320,640]{1,0:T(8,128)(2,1)}, u32[]{:S(2)}, u32[]{:S(2)}) collective-permute-start(bf16[320,640]{1,0:T(8,128)(2,1)S(1)} %collective-permute-done.20.r2), channel_id=1, source_target_pairs={{0,32},{32,64},{64,96},{96,128},{128,160},{160,192},{192,224},{224... | collective-permute-start | bytes 1228808 | tf_op jit(solution)/shard_map/ppermute | solution.py:300
  56.4 12.4 %all-to-all-start.1 = ((bf16[8,64,128]{2,1,0:T(8,128)(2,1)}), bf16[8,64,128]{2,1,0:T(8,128)(2,1)S(1)}, u32[]{:S(2)}, u32[]{:S(2)}) async-start(bf16[8,64,128]{2,1,0:T(8,128)(2,1)} %shard_map.129), calls=%async_computation.1 | async-start | bytes 262144 | tf_op jit(solution)/shard_map/all_to_all | solution.py:331
  66.1 5.6 %collective-permute-start.6 = (bf16[64,1280]{1,0:T(8,128)(2,1)}, bf16[64,1280]{1,0:T(8,128)(2,1)S(1)}, u32[]{:S(2)}, u32[]{:S(2)}) collective-permute-start(bf16[64,1280]{1,0:T(8,128)(2,1)} %get-tuple-element.23), channel_id=1, source_target_pairs={{0,224},{32,0},{64,32},{96,64},{128,96},{160,128},{192,160},{224,1... | collective-permute-start | bytes 491528 | tf_op jit(solution)/shard_map/ppermute | solution.py:350
  69.0 6.4 %collective-permute-start.12 = (bf16[64,128]{1,0:T(8,128)(2,1)S(1)}, bf16[64,128]{1,0:T(8,128)(2,1)S(1)}, u32[]{:S(2)}, u32[]{:S(2)}) collective-permute-start(bf16[64,128]{1,0:T(8,128)(2,1)S(1)} %get-tuple-element.28), channel_id=1, source_target_pairs={{0,1},{1,0},{2,3},{3,2},{4,5},{5,4},{6,7},{7,6},{8,9},{9,8},{10,11... | collective-permute-start | bytes 49160 | tf_op jit(solution)/shard_map/ppermute | solution.py:360
  70.8 13.3 %collective-permute-start.10 = (bf16[64,1280]{1,0:T(8,128)(2,1)}, bf16[64,1280]{1,0:T(8,128)(2,1)S(1)}, u32[]{:S(2)}, u32[]{:S(2)}) collective-permute-start(bf16[64,1280]{1,0:T(8,128)(2,1)} %get-tuple-element.26), channel_id=1, source_target_pairs={{0,224},{32,0},{64,32},{96,64},{128,96},{160,128},{192,160},{224,1... | collective-permute-start | bytes 491528 | tf_op jit(solution)/shard_map/ppermute | solution.py:354
  71.7 15.5 %collective-permute-start.4 = (bf16[64,1280]{1,0:T(8,128)(2,1)}, bf16[64,1280]{1,0:T(8,128)(2,1)S(1)}, u32[]{:S(2)}, u32[]{:S(2)}) collective-permute-start(bf16[64,1280]{1,0:T(8,128)(2,1)} %get-tuple-element.20), channel_id=1, source_target_pairs={{0,96},{32,128},{64,160},{96,192},{128,224},{160,0},{192,32},{224,... | collective-permute-start | bytes 491528 | tf_op jit(solution)/shard_map/ppermute | solution.py:354
  75.4 18.1 %collective-permute-start.5 = (bf16[64,1280]{1,0:T(8,128)(2,1)}, bf16[64,1280]{1,0:T(8,128)(2,1)S(1)}, u32[]{:S(2)}, u32[]{:S(2)}) collective-permute-start(bf16[64,1280]{1,0:T(8,128)(2,1)} %get-tuple-element.21), channel_id=1, source_target_pairs={{0,64},{32,96},{64,128},{96,160},{128,192},{160,224},{192,0},{224,... | collective-permute-start | bytes 491528 | tf_op jit(solution)/shard_map/ppermute | solution.py:354
  81.8 36.2 %collective-permute-start.23 = (bf16[320,640]{1,0:T(8,128)(2,1)S(1)}, bf16[320,640]{1,0:T(8,128)(2,1)S(1)}, u32[]{:S(2)}, u32[]{:S(2)}) collective-permute-start(bf16[320,640]{1,0:T(8,128)(2,1)S(1)} %collective-permute-done.21.l2), channel_id=1, source_target_pairs={{0,224},{32,0},{64,32},{96,64},{128,96},{160,128},{192,160},{224,1... | collective-permute-start | bytes 1228808 | tf_op jit(solution)/shard_map/ppermute | solution.py:301
  84.1 34.0 %collective-permute-start.24 = (bf16[320,640]{1,0:T(8,128)(2,1)}, bf16[320,640]{1,0:T(8,128)(2,1)}, u32[]{:S(2)}, u32[]{:S(2)}) collective-permute-start(bf16[320,640]{1,0:T(8,128)(2,1)} %collective-permute-done.22.r3), channel_id=1, source_target_pairs={{0,32},{32,64},{64,96},{96,128},{128,160},{160,192},{192,224},{224... | collective-permute-start | bytes 1228808 | tf_op jit(solution)/shard_map/ppermute | solution.py:302
  84.8 12.2 %collective-permute-start.14 = (bf16[4,64,128]{2,1,0:T(8,128)(2,1)S(1)}, bf16[4,64,128]{2,1,0:T(8,128)(2,1)S(1)}, u32[]{:S(2)}, u32[]{:S(2)}) collective-permute-start(bf16[4,64,128]{2,1,0:T(8,128)(2,1)S(1)} %pad_maximum_fusion.bc0), channel_id=1, source_target_pairs={{4,0},{8,4},{12,8},{0,12},{5,1},{9,5},{13,9},{1,13},{6,2},{10,6},{... | collective-permute-start | bytes 196616 | tf_op jit(solution)/shard_map/ppermute | solution.py:364
  87.8 9.3 %collective-permute-start.15 = (bf16[4,64,128]{2,1,0:T(8,128)(2,1)S(1)}, bf16[4,64,128]{2,1,0:T(8,128)(2,1)S(1)}, u32[]{:S(2)}, u32[]{:S(2)}) collective-permute-start(bf16[4,64,128]{2,1,0:T(8,128)(2,1)S(1)} %pad_maximum_fusion.bc0), channel_id=1, source_target_pairs={{8,0},{12,4},{0,8},{4,12},{9,1},{13,5},{1,9},{5,13},{10,2},{14,6},... | collective-permute-start | bytes 196616 | tf_op jit(solution)/shard_map/ppermute | solution.py:364
  96.9 13.5 %collective-permute-start.8 = (bf16[64,1280]{1,0:T(8,128)(2,1)}, bf16[64,1280]{1,0:T(8,128)(2,1)}, u32[]{:S(2)}, u32[]{:S(2)}) collective-permute-start(bf16[64,1280]{1,0:T(8,128)(2,1)} %get-tuple-element.24), channel_id=1, source_target_pairs={{0,192},{32,224},{64,0},{96,32},{128,64},{160,96},{192,128},{224,1... | collective-permute-start | bytes 491528 | tf_op jit(solution)/shard_map/ppermute | solution.py:354
  97.7 12.7 %collective-permute-start.9 = (bf16[64,1280]{1,0:T(8,128)(2,1)}, bf16[64,1280]{1,0:T(8,128)(2,1)}, u32[]{:S(2)}, u32[]{:S(2)}) collective-permute-start(bf16[64,1280]{1,0:T(8,128)(2,1)} %get-tuple-element.25), channel_id=1, source_target_pairs={{0,32},{32,64},{64,96},{96,128},{128,160},{160,192},{192,224},{224... | collective-permute-start | bytes 491528 | tf_op jit(solution)/shard_map/ppermute | solution.py:354
  100.1 12.3 %collective-permute-start.7 = (bf16[64,1280]{1,0:T(8,128)(2,1)}, bf16[64,1280]{1,0:T(8,128)(2,1)}, u32[]{:S(2)}, u32[]{:S(2)}) collective-permute-start(bf16[64,1280]{1,0:T(8,128)(2,1)} %shard_map.128), channel_id=1, source_target_pairs={{0,160},{32,192},{64,224},{96,0},{128,32},{160,64},{192,96},{224,1... | collective-permute-start | bytes 491528 | tf_op jit(solution)/shard_map/ppermute | solution.py:354
  120.4 9.4 %collective-permute-start.25 = (bf16[8,64,384]{2,1,0:T(8,128)(2,1)S(1)}, bf16[8,64,384]{2,1,0:T(8,128)(2,1)S(1)}, u32[]{:S(2)}, u32[]{:S(2)}) collective-permute-start(bf16[8,64,384]{2,1,0:T(8,128)(2,1)S(1)} %get-tuple-element.32), channel_id=1, source_target_pairs={{0,1},{1,0},{2,3},{3,2},{4,5},{5,4},{6,7},{7,6},{8,9},{9,8},{10,11... | collective-permute-start | bytes 1179656 | tf_op jit(solution)/shard_map/ppermute | solution.py:420
  145.1 5.4 %collective-permute-start.26 = (bf16[64,320]{1,0:T(8,128)(2,1)S(1)}, bf16[64,320]{1,0:T(8,128)(2,1)S(1)}, u32[]{:S(2)}, u32[]{:S(2)}) collective-permute-start(bf16[64,320]{1,0:T(8,128)(2,1)S(1)} %shard_map.135), channel_id=1, source_target_pairs={{0,0},{1,16},{16,1},{17,17},{2,2},{3,18},{18,3},{19,19},{4,4},{5,2... | collective-permute-start | bytes 122888 | tf_op jit(solution)/shard_map/ppermute | solution.py:428
  (24 other events, 544.0 us)
